TPU v7x, 128 devices: a whole 4x4x4 slice. The times are simulated.
128 devices in a mesh: row: 8 (over z, x_lo), col: 16 (over y, x_hi, core).
Axes of the slice: x: 4 (x_hi: 2, x_lo: 2; x = x_hi * 2 + x_lo), y: 4, z: 4, core: 2. Of those that a mesh axis runs over, the one named last changes fastest.
Arguments:
- tensor_blocks: bfloat16 [8, 384, 6, 128, 128], P('row', 'col'), may hold values from -6 to 6
- block_list: int32 [8, 384, 2], P('row', 'col'), may hold values from 0 to 15, as said below
- occ_green: bfloat16 [2048, 2048], P(('row', 'col')), may hold values from -0.125 to 0.125
- virt_green: bfloat16 [2048, 2048], P(None, ('row', 'col')), may hold values from -0.125 to 0.125
Outputs:
- polarizability: float32 [8, 6, 6], P('row')
Inputs may be any that keep to these rules, and one draw needn't show every extreme that they name: `block_list`: within the 24 blocks of one device the (m, l) pairs are distinct, every atom block occurs as l once or twice and as m once or twice, so at most 2 blocks of one device share an l, and some l is shared by exactly 2.
All inputs are finite; a program needn't handle non-finite values.
Results may differ from a plain program's by a relative error of at most 0.006.
Values may be sent and summed in bfloat16 or wider, within the bound.
No kernel may reach another device: no remote copies, remote signals or barrier semaphores. Data moves between devices by JAX's collectives and lax.ppermute only.
A program may use at most 128 MiB of HBM per device.

v0:
```python
import jax
import jax.numpy as jnp
from jax import lax
from jax.sharding import PartitionSpec as P

CAP = 2


def shards(tensor_blocks, block_list, occ_green, virt_green):
    col_count = lax.axis_size("col")
    blocks = tensor_blocks[0]
    pairs = block_list[0]
    held = blocks.shape[0]
    width = blocks.shape[-1]
    target = pairs[:, 1]
    first_blocks = pairs[:, 0]
    places = jnp.arange(held)
    slot_rank = jnp.sum(
        (target[None, :] == target[:, None]) & (places[None, :] < places[:, None]), axis=1
    )
    select = (target[:, None, None] == jnp.arange(col_count)[None, :, None]) & (
        slot_rank[:, None, None] == jnp.arange(CAP)[None, None, :]
    )
    send_blocks = jnp.einsum(
        "tdk,tpab->dkpab", select.astype(jnp.bfloat16), blocks, preferred_element_type=jnp.float32
    ).astype(jnp.bfloat16)
    send_first = jnp.sum(select.astype(jnp.int32) * (first_blocks + 1)[:, None, None], axis=0) - 1
    recv_blocks, recv_first = (
        lax.all_to_all(send_blocks, "col", split_axis=0, concat_axis=0, tiled=True),
        lax.all_to_all(send_first, "col", split_axis=0, concat_axis=0, tiled=True),
    )
    slot_total = recv_blocks.shape[0] * recv_blocks.shape[1]
    flat_blocks = recv_blocks.reshape(slot_total, recv_blocks.shape[2], width, width)
    placing = (recv_first.reshape(slot_total)[:, None] == jnp.arange(col_count)[None, :]).astype(
        jnp.bfloat16
    )
    dense_parts = jnp.einsum(
        "sm,spab->pmab", placing, flat_blocks, preferred_element_type=jnp.float32
    )
    dense_tensor = dense_parts.astype(jnp.bfloat16).reshape(
        flat_blocks.shape[1], col_count * width, width
    )
    basis_total = dense_tensor.shape[1]
    occ_half = jnp.einsum(
        "nm,pml->pnl",
        lax.all_gather(occ_green, ("row", "col"), axis=0, tiled=True),
        dense_tensor,
        preferred_element_type=jnp.float32,
    ).astype(jnp.bfloat16)
    turned = lax.all_to_all(occ_half, "col", split_axis=1, concat_axis=2, tiled=True)
    both_sides = jnp.einsum(
        "pnl,ls->pns",
        turned,
        lax.all_gather(virt_green, ("row", "col"), axis=1, tiled=True),
        preferred_element_type=jnp.float32,
    ).astype(jnp.bfloat16)
    partial_polar = jnp.einsum(
        "pns,qsn->pq", both_sides, dense_tensor, preferred_element_type=jnp.float32
    )
    polar_total = lax.psum(partial_polar, "col")
    return (polar_total / float(basis_total))[None]


def solution(mesh):
    in_specs = (
        P("row", "col", None, None, None),
        P("row", "col", None),
        P(("row", "col"), None),
        P(None, ("row", "col")),
    )
    out_specs = P("row", None, None)
    return jax.shard_map(shards, mesh=mesh, in_specs=in_specs, out_specs=out_specs, check_vma=False)
```

profile of v0, /device:TPU:2, one launch (start us, length us, event | category | flops | bytes accessed | tf_op | source)
XLA Modules:
  0.0 585.3 jit_solution(11802510145233425043)
XLA Ops:
  6.5 0.7 all-gather.3.cloned.1.call-update
  7.3 0.7 all-gather.5.cloned.1.call-update
  8.0 0.8 add_bitcast_fusion.1
  9.1 0.7 copy.44
  9.8 6.1 %all-to-all-start.1 = ((s32[16,1,2]{2,1,0:T(1,128)}), s32[16,1,2]{2,1,0:T(1,128)S(1)}, u32[]{:S(2)}, u32[]{:S(2)}) async-start(s32[16,1,2]{2,1,0:T(1,128)} %copy.44), calls=%async_computation.1 | async-start | bytes 16384 | tf_op jit(solution)/shard_map/all_to_all | solution.py:30
  15.9 6.1 %fusion.11 = bf16[16,2,6,128,128]{4,0,3,2,1:T(8,128)(2,1)S(1)} fusion(bf16[24,6,128,128]{3,2,1,0:T(8,128)(2,1)} %bitcast.54, pred[24,2]{0,1:T(4,128)(4,1)S(1)} %iota_compare_fusion.3, pred[24,16]{0,1:T(8,128)(4,1)S(1)} %iota_compare_fusion.2), kind=kOutput, calls=%fused_computation.11 | convolution fusion | flops 154141440 | bytes 11010480 | tf_op jit(solution)/shard_map/tdk,tpab->dkpab/dot_general | solution.py:24
  22.1 4.3 copy.43
  26.4 7.3 %all-to-all-start = ((bf16[16,2,6,128,128]{4,3,2,1,0:T(8,128)(2,1)}), bf16[16,2,6,128,128]{4,3,2,1,0:T(8,128)(2,1)}, u32[]{:S(2)}, u32[]{:S(2)}) async-start(bf16[16,2,6,128,128]{4,3,2,1,0:T(8,128)(2,1)} %copy.43), calls=%async_computation | async-start | bytes 12582912 | tf_op jit(solution)/shard_map/all_to_all | solution.py:29
  34.2 0.7 reduce.3
  34.9 77.1 %all-to-all-done = bf16[16,2,6,128,128]{4,3,2,1,0:T(8,128)(2,1)} async-done(((bf16[16,2,6,128,128]{4,3,2,1,0:T(8,128)(2,1)}), bf16[16,2,6,128,128]{4,3,2,1,0:T(8,128)(2,1)}, u32[]{:S(2)}, u32[]{:S(2)}) %all-to-all-start) | async-done | bytes 6291488 | tf_op jit(solution)/shard_map/all_to_all | solution.py:29
  112.1 6.6 %convert_bitcast_fusion = bf16[6,16,128,128]{3,1,2,0:T(8,128)(2,1)S(1)} fusion(bf16[32,6,128,128]{3,2,1,0:T(8,128)(2,1)} %bitcast.6, s32[32]{0:T(128)S(1)} %eq.73), kind=kOutput, calls=%fused_computation.14 | convolution fusion | flops 102236672 | bytes 9437312 | tf_op jit(solution)/shard_map/sm,spab->pmab/dot_general | solution.py:37
  118.6 0.8 copy.46
  119.5 161.6 %all-gather.3.cloned.1.call-done = bf16[2048,2048]{1,0:T(8,128)(2,1)} async-done(((bf16[16,2048]{1,0:T(8,128)(2,1)}), bf16[2048,2048]{1,0:T(8,128)(2,1)}) %all-gather.3.cloned.1.call-update) | async-done | bytes 8388624 | tf_op jit(solution)/shard_map/all_gather | solution.py:46
  281.1 10.3 %fusion.20 = bf16[6,2048,128]{1,2,0:T(8,128)(2,1)} fusion(bf16[6,2048,128]{2,1,0:T(8,128)(2,1)S(1)} %bitcast.52, bf16[2048,2048]{1,0:T(8,128)(2,1)} %all-gather.3.cloned.1.call-done), kind=kOutput, calls=%fused_computation.15 | convolution fusion | flops 6444023808 | bytes 14680064 | tf_op jit(solution)/shard_map/nm,pml->pnl/dot_general | solution.py:44
  291.4 6.4 %copy.48 = bf16[6,2048,128]{2,0,1:T(8,128)(2,1)} copy(bf16[6,2048,128]{1,2,0:T(8,128)(2,1)} %fusion.20) | data formatting | bytes 6291456 | tf_op jit(solution)/shard_map/convert_element_type | solution.py:49
  297.8 4.8 all-to-all-start.2
  302.6 5.1 copy.53
  307.6 50.6 %all-to-all-done.2 = bf16[6,2048,128]{2,0,1:T(8,128)(2,1)} async-done(((bf16[6,2048,128]{2,0,1:T(8,128)(2,1)}), bf16[6,2048,128]{2,0,1:T(8,128)(2,1)}, u32[]{:S(2)}, u32[]{:S(2)}) %all-to-all-start.2) | async-done | bytes 3145760 | tf_op jit(solution)/shard_map/all_to_all | solution.py:50
  358.2 5.4 copy.50
  363.6 163.8 %all-gather.5.cloned.1.call-done = bf16[2048,2048]{0,1:T(8,128)(2,1)} async-done(((bf16[2048,16]{0,1:T(8,128)(2,1)}), bf16[2048,2048]{0,1:T(8,128)(2,1)}) %all-gather.5.cloned.1.call-update) | async-done | bytes 8388624 | tf_op jit(solution)/shard_map/all_gather | solution.py:54
  527.4 9.3 %fusion.17 = bf16[6,128,2048]{2,1,0:T(8,128)(2,1)S(1)} fusion(bf16[6,128,2048]{1,2,0:T(8,128)(2,1)S(1)} %bitcast.55, bf16[2048,2048]{0,1:T(8,128)(2,1)} %all-gather.5.cloned.1.call-done), kind=kOutput, calls=%fused_computation.13 | convolution fusion | flops 6444023808 | bytes 14680064 | tf_op jit(solution)/shard_map/pnl,ls->pns/dot_general | solution.py:51
  536.7 5.7 fusion.25
  542.5 35.4 %psum.7 = f32[6,6]{1,0:T(8,128)S(1)} all-reduce(f32[6,6]{1,0:T(8,128)S(1)} %fusion.25), channel_id=1, replica_groups=mesh['row'=8,'col'=16] {'col'}, use_global_device_ids=true, to_apply=%region_2.0 | all-reduce | flops 36 | bytes 288 | tf_op jit(solution)/shard_map/psum | solution.py:60
  577.9 0.6 copy.54
  (13 shorter events, 1.0 us)
Async XLA Ops:
  6.5 274.6 %all-gather.3.cloned.1.call-start = ((), (), s32[]{:S(2)}) async-start(), calls=%async_computation.3 | async-start | bytes 8454144 | tf_op jit(solution)/shard_map/all_gather | solution.py:46
  7.3 520.2 %all-gather.5.cloned.1.call-start = ((), (), s32[]{:S(2)}) async-start(), calls=%async_computation.4 | async-start | bytes 8454144 | tf_op jit(solution)/shard_map/all_gather | solution.py:54
  9.8 16.6 %all-to-all-start.1 = ((s32[16,1,2]{2,1,0:T(1,128)}), s32[16,1,2]{2,1,0:T(1,128)S(1)}, u32[]{:S(2)}, u32[]{:S(2)}) async-start(s32[16,1,2]{2,1,0:T(1,128)} %copy.44), calls=%async_computation.1 | async-start | bytes 16384 | tf_op jit(solution)/shard_map/all_to_all | solution.py:30
  26.4 85.7 %all-to-all-start = ((bf16[16,2,6,128,128]{4,3,2,1,0:T(8,128)(2,1)}), bf16[16,2,6,128,128]{4,3,2,1,0:T(8,128)(2,1)}, u32[]{:S(2)}, u32[]{:S(2)}) async-start(bf16[16,2,6,128,128]{4,3,2,1,0:T(8,128)(2,1)} %copy.43), calls=%async_computation | async-start | bytes 12582912 | tf_op jit(solution)/shard_map/all_to_all | solution.py:29
  297.8 60.4 %all-to-all-start.2 = ((bf16[6,2048,128]{2,0,1:T(8,128)(2,1)}), bf16[6,2048,128]{2,0,1:T(8,128)(2,1)}, u32[]{:S(2)}, u32[]{:S(2)}) async-start(bf16[6,2048,128]{2,0,1:T(8,128)(2,1)} %copy.48), calls=%async_computation.2 | async-start | bytes 8388608 | tf_op jit(solution)/shard_map/all_to_all | solution.py:50
  527.4 9.3 %copy-start = (bf16[6,2048,128]{1,0,2:T(8,128)(2,1)S(1)}, bf16[6,2048,128]{1,0,2:T(8,128)(2,1)}, u32[]{:S(2)}) copy-start(bf16[6,2048,128]{1,0,2:T(8,128)(2,1)} %copy.53) | copy-start | bytes 9437188
Sparse Core Ops, SparseCore 0:
  9.1 271.9 all-gather.2
  282.8 244.5 all-gather.4
where the time goes:
time: 586 us; the launch traced here: 585 us
  waiting for transfers between devices  455 us (78%)
  matrix products  38 us (6%)
  blocking collectives  35.4 us (6%)
  local copies, waits for them, and re-layouts  23.9 us (4%)
  starting transfers between devices  18.2 us (3%)
  between operations  13.5 us (2%)
    all_gather x1, waiting for transfers between devices, shards(): lax.all_gather(virt_green, ('row', 'col'), axis=1, tiled=True)  164 us
    all_gather x1, waiting for transfers between devices, shards(): lax.all_gather(occ_green, ('row', 'col'), axis=0, tiled=True)  162 us
    all_to_all x1, waiting for transfers between devices, shards(): lax.all_to_all(send_blocks, 'col', split_axis=0, concat_axis=0, tiled=True)  77.1 us
    all_to_all x1, waiting for transfers between devices, shards(): lax.all_to_all(occ_half, 'col', split_axis=1, concat_axis=2, tiled=True)  50.6 us
    psum x1, blocking collectives, shards(): polar_total = lax.psum(partial_polar, 'col')  35.4 us
  transfers between devices with their start and end apart: 5, of which 4 were waited for; matrix products, arithmetic and copies ran while one was open for 8% of the time, Pallas kernels for 0%

commit v1 on v0

v1 whole, which is shorter than its diff:
```python
import functools

import jax
import jax.numpy as jnp
from jax import lax
from jax.experimental import pallas as pl
from jax.experimental.pallas import tpu as pltpu
from jax.sharding import Mesh
from jax.sharding import PartitionSpec as P

CAP = 2
CHUNKS = 2
AXES = ("z", "xl", "y", "xh", "core")
SIZES = (4, 2, 4, 2, 2)
COL = ("y", "xh", "core")
ROW = ("z", "xl")
PLANE = ("xl", "y", "xh")


def moved(axis, to):
    where = AXES.index(axis)
    stride = 1
    for size in SIZES[where + 1 :]:
        stride *= size
    total = 1
    for size in SIZES:
        total *= size
    pairs = []
    for device in range(total):
        k = device // stride % SIZES[where]
        pairs.append((device, device + (to(k) - k) * stride))
    return pairs


def permute(x, axis, to):
    return lax.ppermute(x, AXES, moved(axis, to))


def up(x):
    return permute(x, "z", lambda k: (k + 1) % 4)


def down(x):
    return permute(x, "z", lambda k: (k - 1) % 4)


def other_core(x):
    return permute(x, "core", lambda k: 1 - k)


def pick_kernel(chunks, pairs_ref, blocks_ref, *refs):
    out_refs = refs[:chunks]
    first_ref, count, sems = refs[chunks:]
    held = blocks_ref.shape[0]
    depth = blocks_ref.shape[1] // chunks
    owners = first_ref.shape[0]
    for d in range(owners):
        count[d] = 0
        for k in range(CAP):
            first_ref[d, k] = -1
    copies = []
    for t in range(held):
        l = pairs_ref[t, 1]
        k = count[l]
        count[l] = k + 1
        first_ref[l, k] = pairs_ref[t, 0]
        for c in range(chunks):
            copy = pltpu.make_async_copy(
                blocks_ref.at[t, pl.ds(c * depth, depth)], out_refs[c].at[l, k], sems.at[t, c]
            )
            copy.start()
            copies.append(copy)
    for copy in copies:
        copy.wait()


def pick(pairs, blocks, owners):
    held, aux, width, _ = blocks.shape
    depth = aux // CHUNKS
    out = jax.ShapeDtypeStruct((owners, CAP, depth, width, width), blocks.dtype)
    return pl.pallas_call(
        functools.partial(pick_kernel, CHUNKS),
        out_shape=[out] * CHUNKS + [jax.ShapeDtypeStruct((owners, CAP), jnp.int32)],
        in_specs=[
            pl.BlockSpec(memory_space=pltpu.SMEM),
            pl.BlockSpec(memory_space=pl.ANY),
        ],
        out_specs=[pl.BlockSpec(memory_space=pl.ANY)] * CHUNKS
        + [pl.BlockSpec(memory_space=pltpu.SMEM)],
        scratch_shapes=[
            pltpu.SMEM((owners,), jnp.int32),
            pltpu.SemaphoreType.DMA((held, CHUNKS)),
        ],
        cost_estimate=pl.CostEstimate(flops=0, bytes_accessed=4 * blocks.size, transcendentals=0),
        name="pick",
    )(pairs, blocks)


def place_kernel(first_ref, blocks_ref, out_ref, total):
    slots, width = blocks_ref.shape[0], blocks_ref.shape[-1]
    total[...] = jnp.zeros_like(total)

    def body(s, carry):
        m = first_ref[s]

        @pl.when(m >= 0)
        def _():
            rows = pl.ds(pl.multiple_of(m * width, width), width)
            total[rows, :] += blocks_ref[s, 0].astype(jnp.float32)

        return carry

    lax.fori_loop(0, slots, body, 0)
    out_ref[...] = total[...].astype(out_ref.dtype)


def place(first, blocks, rows):
    slots, depth, width, _ = blocks.shape
    return pl.pallas_call(
        place_kernel,
        out_shape=jax.ShapeDtypeStruct((rows, depth * width), blocks.dtype),
        grid_spec=pltpu.PrefetchScalarGridSpec(
            num_scalar_prefetch=1,
            grid=(depth,),
            in_specs=[pl.BlockSpec((slots, 1, width, width), lambda p, first: (0, p, 0, 0))],
            out_specs=pl.BlockSpec((rows, width), lambda p, first: (0, p)),
            scratch_shapes=[pltpu.VMEM((rows, width), jnp.float32)],
        ),
        compiler_params=pltpu.CompilerParams(vmem_limit_bytes=32 * 1024 * 1024),
        cost_estimate=pl.CostEstimate(
            flops=blocks.size, bytes_accessed=4 * blocks.size, transcendentals=0
        ),
        name="place",
    )(first, blocks)


def lay_kernel(*refs):
    pieces, out_ref, sems = refs[:-2], refs[-2], refs[-1]
    z, core = lax.axis_index("z"), lax.axis_index("core")
    half = out_ref.shape[1] // 2
    full = out_ref.shape[1]
    spots = [
        (0, 0, full),
        (3, 0, full),
        (1, 0, full),
        (2, 0, half),
        (2, half, half),
    ]
    copies = []
    for side in range(2):
        for i, (dz, start, size) in enumerate(spots):
            n = side * len(spots) + i
            copy = pltpu.make_async_copy(
                pieces[n],
                out_ref.at[(z + dz) % 4, pl.ds(start, size), (core + side) % 2],
                sems.at[n],
            )
            copy.start()
            copies.append(copy)
    for copy in copies:
        copy.wait()


def lay(pieces):
    plane, rows, columns = pieces[0].shape
    return pl.pallas_call(
        lay_kernel,
        out_shape=jax.ShapeDtypeStruct((4, plane, 2, rows, columns), pieces[0].dtype),
        in_specs=[pl.BlockSpec(memory_space=pl.ANY)] * len(pieces),
        out_specs=pl.BlockSpec(memory_space=pl.ANY),
        scratch_shapes=[pltpu.SemaphoreType.DMA((len(pieces),))],
        cost_estimate=pl.CostEstimate(
            flops=0, bytes_accessed=32 * pieces[0].size, transcendentals=0
        ),
        name="lay",
    )(*pieces).reshape(8 * plane * rows, columns)


def plane_gather(shard):
    count = 16
    copies = jnp.broadcast_to(shard[None], (count, *shard.shape))
    return lax.all_to_all(copies, PLANE, split_axis=0, concat_axis=0, tiled=True)


def z_gather(mine):
    half = mine.shape[0] // 2
    from_below, from_above = up(mine), down(mine)
    far_low, far_high = up(from_below[:half]), down(from_above[half:])
    pieces = [mine, from_below, from_above, far_low, far_high]
    return lay(pieces + [other_core(p) for p in pieces])


def pair_kernel(x_ref, y_ref, out_ref):
    width = x_ref.shape[1]
    aux_x, aux_y = x_ref.shape[2] // width, y_ref.shape[0] // width

    @pl.when(pl.program_id(0) == 0)
    def _():
        out_ref[...] = jnp.zeros_like(out_ref)

    for p in range(aux_x):
        x = x_ref[0, :, p * width : (p + 1) * width].astype(jnp.float32)
        for q in range(aux_y):
            y = y_ref[q * width : (q + 1) * width, :].astype(jnp.float32)
            out_ref[p * aux_y + q] += (x * y).reshape(width // 8, 8, width).sum(axis=0)


def pair_sums(x, y):
    blocks, width, _ = x.shape
    aux_x, aux_y = x.shape[2] // width, y.shape[0] // width
    sums = pl.pallas_call(
        pair_kernel,
        out_shape=jax.ShapeDtypeStruct((aux_x * aux_y, 8, width), jnp.float32),
        grid=(blocks,),
        in_specs=[
            pl.BlockSpec((1, width, aux_x * width), lambda k: (k, 0, 0)),
            pl.BlockSpec((aux_y * width, width), lambda k: (0, k)),
        ],
        out_specs=pl.BlockSpec((aux_x * aux_y, 8, width), lambda k: (0, 0, 0)),
        cost_estimate=pl.CostEstimate(
            flops=2 * x.size * aux_y, bytes_accessed=2 * (x.size + y.size), transcendentals=0
        ),
        name="pair",
    )(x, y)
    return sums.sum(axis=(1, 2)).reshape(aux_x, aux_y)


def col_sum(x):
    x = x + other_core(x)
    x = x + permute(x, "xh", lambda k: 1 - k)
    x = x + permute(x, "y", lambda k: k ^ 1)
    return x + permute(x, "y", lambda k: k ^ 2)


def shards(tensor_blocks, block_list, occ_green, virt_green):
    col_count = lax.axis_size(COL)
    blocks = tensor_blocks[0]
    width = blocks.shape[-1]
    basis_total = occ_green.shape[1]

    both = jnp.concatenate([occ_green, virt_green.T], axis=0)
    both_plane = plane_gather(both)
    shard_rows = occ_green.shape[0]
    occ = z_gather(both_plane[:, :shard_rows])
    virt_t = z_gather(both_plane[:, shard_rows:])

    *picked, send_first = pick(block_list[0], blocks, col_count)
    recv = [
        lax.all_to_all(part, COL, split_axis=0, concat_axis=0, tiled=True) for part in picked
    ]
    recv_first = lax.all_to_all(
        send_first[:, None], COL, split_axis=0, concat_axis=0, tiled=True
    ).reshape(-1)

    dense, turned = [], []
    for part in recv:
        part = part.reshape(-1, *part.shape[2:])
        dense.append(place(recv_first, part, basis_total))
        half = jnp.dot(occ, dense[-1], preferred_element_type=jnp.float32).astype(jnp.bfloat16)
        half = half.reshape(col_count, width, -1)
        turned.append(lax.all_to_all(half, COL, split_axis=0, concat_axis=0, tiled=True))

    virt_half = jnp.concatenate(
        [
            lax.dot_general(
                d, virt_t, (((0,), (0,)), ((), ())), preferred_element_type=jnp.float32
            ).astype(jnp.bfloat16)
            for d in dense
        ],
        axis=0,
    )
    sums = jnp.concatenate([pair_sums(x, virt_half) for x in turned], axis=0)
    return (col_sum(sums) / float(basis_total))[None]


def solution(mesh):
    fine = Mesh(mesh.devices.reshape(SIZES), AXES)
    in_specs = (
        P(ROW, COL, None, None, None),
        P(ROW, COL, None),
        P(ROW + COL, None),
        P(None, ROW + COL),
    )
    return jax.shard_map(
        shards, mesh=fine, in_specs=in_specs, out_specs=P(ROW, None, None), check_vma=False
    )
```

time: 586 us -> 882 us (1.51)
  Pallas kernels: 0 us -> 682 us
  waiting for transfers between devices: 455 us -> 55.6 us
  starting transfers between devices: 18.2 us -> 54.8 us
  between operations: 13.5 us -> 0.26 us
    pallas_call x0 -> x7, Pallas kernels: none -> 682 us  [the longest x2 511 us: lay(): pl.pallas_call(lay_kernel, out_shape=jax.ShapeDtypeStruct((4, plane, 2, r...]
    all_gather x2 -> x0, waiting for transfers between devices: 325 us -> none  [the longest x1 164 us: shards(): lax.all_gather(virt_green, ('row', 'col'), axis=1, tiled=True)]
    all_to_all x3 -> x5, waiting for transfers between devices: 128 us -> 37.7 us  [the longest x2 30.2 us: shards(): lax.all_to_all(part, COL, split_axis=0, concat_axis=0, tiled=True)]
    psum x1 -> x0, blocking collectives: 35.4 us -> none  [shards(): polar_total = lax.psum(partial_polar, 'col')]
    all_to_all x0 -> x1, blocking collectives: none -> 31.5 us  [plane_gather(): lax.all_to_all(copies, PLANE, split_axis=0, concat_axis=0, tiled=True)]
    ppermute x0 -> x22, starting transfers between devices: none -> 26.5 us  [permute(): return lax.ppermute(x, AXES, moved(axis, to))]
    ppermute x0 -> x22, waiting for transfers between devices: none -> 17.9 us  [permute(): return lax.ppermute(x, AXES, moved(axis, to))]
    convert_element_type x3 -> x0, local copies, waits for them, and re-layouts: 11.6 us -> none  [the longest x1 6.4 us: shards(): occ_half = jnp.einsum('nm,pml->pnl', lax.all_gather(occ_green, ('row', 'c...]
  transfers between devices with their start and end apart: 5 -> 27, of which waited for: 4 -> 8; matrix products, arithmetic and copies ran while one was open for 8% -> 5% of each run, Pallas kernels for 0% -> 60%
where the time goes in v1:
time: 882 us; the launch traced here: 880 us
  Pallas kernels  682 us (77%)
  waiting for transfers between devices  55.6 us (6%)
  starting transfers between devices  54.8 us (6%)
  matrix products  32.3 us (4%)
  blocking collectives  31.5 us (4%)
  local copies, waits for them, and re-layouts  17.9 us (2%)
    pallas_call x2, Pallas kernels, lay(): pl.pallas_call(lay_kernel, out_shape=jax.ShapeDtypeStruct((4, plane, 2, r...  511 us
    pallas_call x1, Pallas kernels, pick(): pl.pallas_call(functools.partial(pick_kernel, CHUNKS), out_shape=[out] *...  146 us
    all_to_all x1, blocking collectives, plane_gather(): lax.all_to_all(copies, PLANE, split_axis=0, concat_axis=0, tiled=True)  31.5 us
    all_to_all x2, waiting for transfers between devices, shards(): lax.all_to_all(part, COL, split_axis=0, concat_axis=0, tiled=True)  30.2 us
    ppermute x22, starting transfers between devices, permute(): return lax.ppermute(x, AXES, moved(axis, to))  26.5 us
    pallas_call x2, Pallas kernels, pair_sums(): pl.pallas_call(pair_kernel, out_shape=jax.ShapeDtypeStruct((aux_x * aux_y...  19.8 us
    dot_general x2, matrix products, shards(): jnp.dot(occ, dense[-1], preferred_element_type=jnp.float32)  18.6 us
    ppermute x22, waiting for transfers between devices, permute(): return lax.ppermute(x, AXES, moved(axis, to))  17.9 us
  transfers between devices with their start and end apart: 27, of which 8 were waited for; matrix products, arithmetic and copies ran while one was open for 5% of the time, Pallas kernels for 60%

profile of v1, /device:TPU:2, one launch (start us, length us, event | category | flops | bytes accessed | tf_op | source)
XLA Modules:
  0.0 879.7 jit_solution(3787443306965071054)
XLA Ops:
  1.4 146.0 %pick.1 = (bf16[16,2,3,128,128]{4,3,2,1,0:T(8,128)(2,1)}, bf16[16,2,3,128,128]{4,3,2,1,0:T(8,128)(2,1)}, s32[16,2]{1,0:T(8,128)}) custom-call(s32[24,2]{1,0:T(8,128)} %copy.13.pairs_ref, bf16[24,6,128,128]{3,2,1,0:T(8,128)(2,1)} %bitcast.28), custom_call_target="tpu_custom_call" | custom-call | bytes 9437184 | tf_op jit(solution)/shard_map/pick/pallas_call | solution.py:81
  147.4 6.1 all-to-all-start.1
  153.6 7.5 all-to-all-done.1
  161.4 31.5 %all_to_all.30 = bf16[16,32,2048]{2,1,0:T(8,128)(2,1)} all-to-all(bf16[16,32,2048]{2,1,0:T(8,128)(2,1)S(1)} %broadcast_in_dim.12), channel_id=1, replica_groups=mesh['z'=4,'xl'=2,'y'=4,'xh'=2,'core'=2] {'xl','y','xh'}, dimensions={0} | all-to-all | bytes 4194304 | tf_op jit(solution)/shard_map/all_to_all | solution.py:182
  192.9 3.8 all-to-all-start.2
  196.7 3.1 fusion.1
  203.8 3.2 collective-permute-start.10
  207.1 30.2 %all-to-all-done.2 = bf16[16,2,3,128,128]{4,3,2,1,0:T(8,128)(2,1)S(1)} async-done(((bf16[16,2,3,128,128]{4,3,2,1,0:T(8,128)(2,1)}), bf16[16,2,3,128,128]{4,3,2,1,0:T(8,128)(2,1)S(1)}, u32[]{:S(2)}, u32[]{:S(2)}) %all-to-all-start.2) | async-done | bytes 3145760 | tf_op jit(solution)/shard_map/all_to_all | solution.py:249
  238.9 3.7 all-to-all-start.4
  251.2 10.4 %collective-permute-done.2.refs_3_ = bf16[8,16,2048]{2,1,0:T(8,128)(2,1)} collective-permute-done((bf16[8,16,2048]{2,1,0:T(8,128)(2,1)S(1)}, bf16[8,16,2048]{2,1,0:T(8,128)(2,1)}, u32[]{:S(2)}, u32[]{:S(2)}) %collective-permute-start.2) | collective-permute-done | bytes 524320 | tf_op jit(solution)/shard_map/ppermute | solution.py:36
  265.3 3.0 place.2
  277.1 255.3 %lay.2 = bf16[4,16,2,16,2048]{4,3,2,1,0:T(8,128)(2,1)} custom-call(bf16[16,16,2048]{2,1,0:T(8,128)(2,1)} %get-tuple-element.12.refs_0_, bf16[16,16,2048]{2,1,0:T(8,128)(2,1)} %collective-permute-done.refs_1_, bf16[16,16,2048]{2,1,0:T(8,128)(2,1)} %collective-permute-done.1.refs_2_, bf16[8,16,2048]{2,1,0:T(8,128)(2,1)} %collective-permute-done.2.refs_3_, ...), custom_call_target="tpu_custom_call" | custom-call | bytes 16777216 | tf_op jit(solution)/shard_map/lay/pallas_call | solution.py:166
  532.4 9.5 %convolution_convert_fusion.3 = bf16[2048,384]{1,0:T(8,128)(2,1)} fusion(bf16[2048,2048]{1,0:T(8,128)(2,1)} %bitcast.24, bf16[2048,384]{1,0:T(8,128)(2,1)} %copy-done.2), kind=kOutput, calls=%fused_computation.4 | convolution fusion | flops 3222011904 | bytes 11534336 | tf_op jit(solution)/shard_map/dot_general | solution.py:259
  541.9 7.1 all-to-all-start.3
  549.8 3.0 place.3
  554.0 255.3 %lay.3 = bf16[4,16,2,16,2048]{4,3,2,1,0:T(8,128)(2,1)} custom-call(bf16[16,16,2048]{2,1,0:T(8,128)(2,1)} %get-tuple-element.11.refs_0_, bf16[16,16,2048]{2,1,0:T(8,128)(2,1)} %collective-permute-done.9.refs_1_, bf16[16,16,2048]{2,1,0:T(8,128)(2,1)} %collective-permute-done.10.refs_2_, bf16[8,16,2048]{2,1,0:T(8,128)(2,1)} %collective-permute-done.11.refs_3_, ...), custom_call_target="tpu_custom_call" | custom-call | bytes 16777216 | tf_op jit(solution)/shard_map/lay/pallas_call | solution.py:166
  809.4 9.1 %convolution_convert_fusion = bf16[2048,384]{1,0:T(8,128)(2,1)} fusion(bf16[2048,2048]{1,0:T(8,128)(2,1)} %bitcast.25, bf16[2048,384]{1,0:T(8,128)(2,1)S(1)} %copy-done.5), kind=kOutput, calls=%fused_computation.1 | convolution fusion | flops 3222011904 | bytes 11534336 | tf_op jit(solution)/shard_map/dot_general | solution.py:259
  818.5 7.5 all-to-all-start.5
  826.0 6.9 convolution_convert_fusion.2
  832.8 6.9 convolution_convert_fusion.1
  841.7 9.9 %pair.2 = f32[18,8,128]{2,1,0:T(8,128)} custom-call(bf16[16,128,384]{2,1,0:T(8,128)(2,1)} %all-to-all-done.3.x_ref, bf16[768,2048]{1,0:T(8,128)(2,1)} %pad_maximum_fusion.y_ref), custom_call_target="tpu_custom_call" | custom-call | flops 9437184 | bytes 4718592 | tf_op jit(solution)/shard_map/pair/pallas_call | solution.py:211
  852.8 9.9 %pair.3 = f32[18,8,128]{2,1,0:T(8,128)} custom-call(bf16[16,128,384]{2,1,0:T(8,128)(2,1)} %all-to-all-done.5.x_ref, bf16[768,2048]{1,0:T(8,128)(2,1)} %pad_maximum_fusion.y_ref), custom_call_target="tpu_custom_call" | custom-call | flops 9437184 | bytes 4718592 | tf_op jit(solution)/shard_map/pair/pallas_call | solution.py:211
  865.2 3.4 collective-permute-start.19
  874.0 3.4 collective-permute-start.21
  (80 shorter events, 43.6 us)
Async XLA Ops:
  147.4 13.7 %all-to-all-start.1 = ((s32[16,1,2]{2,1,0:T(1,128)}), s32[16,1,2]{2,1,0:T(1,128)S(1)}, u32[]{:S(2)}, u32[]{:S(2)}) async-start(s32[16,1,2]{2,1,0:T(1,128)} %bitcast.32), calls=%async_computation.1 | async-start | bytes 16384 | tf_op jit(solution)/shard_map/all_to_all | solution.py:251
  192.9 44.4 %all-to-all-start.2 = ((bf16[16,2,3,128,128]{4,3,2,1,0:T(8,128)(2,1)}), bf16[16,2,3,128,128]{4,3,2,1,0:T(8,128)(2,1)S(1)}, u32[]{:S(2)}, u32[]{:S(2)}) async-start(bf16[16,2,3,128,128]{4,3,2,1,0:T(8,128)(2,1)} %get-tuple-element.9), calls=%async_computation.2 | async-start | bytes 6291456 | tf_op jit(solution)/shard_map/all_to_all | solution.py:249
  199.8 43.1 %collective-permute-start = (bf16[16,16,2048]{2,1,0:T(8,128)(2,1)}, bf16[16,16,2048]{2,1,0:T(8,128)(2,1)}, u32[]{:S(2)}, u32[]{:S(2)}) collective-permute-start(bf16[16,16,2048]{2,1,0:T(8,128)(2,1)} %get-tuple-element.12.refs_0_), channel_id=1, source_target_pairs={{0,32},{1,33},{2,34},{3,35},{4,36},{5,37},{6,38},{7,39},{8,40},{9,... | collective-permute-start | bytes 3145736 | tf_op jit(solution)/shard_map/ppermute | solution.py:36
  201.7 44.3 %collective-permute-start.1 = (bf16[16,16,2048]{2,1,0:T(8,128)(2,1)}, bf16[16,16,2048]{2,1,0:T(8,128)(2,1)}, u32[]{:S(2)}, u32[]{:S(2)}) collective-permute-start(bf16[16,16,2048]{2,1,0:T(8,128)(2,1)} %get-tuple-element.12.refs_0_), channel_id=1, source_target_pairs={{0,96},{1,97},{2,98},{3,99},{4,100},{5,101},{6,102},{7,103},{8,104... | collective-permute-start | bytes 3145736 | tf_op jit(solution)/shard_map/ppermute | solution.py:36
  203.8 46.8 %collective-permute-start.9 = (bf16[16,16,2048]{2,1,0:T(8,128)(2,1)}, bf16[16,16,2048]{2,1,0:T(8,128)(2,1)}, u32[]{:S(2)}, u32[]{:S(2)}) collective-permute-start(bf16[16,16,2048]{2,1,0:T(8,128)(2,1)} %get-tuple-element.11.refs_0_), channel_id=1, source_target_pairs={{0,32},{1,33},{2,34},{3,35},{4,36},{5,37},{6,38},{7,39},{8,40},{9,... | collective-permute-start | bytes 3145736 | tf_op jit(solution)/shard_map/ppermute | solution.py:36
  203.8 46.8 %collective-permute-start.10 = (bf16[16,16,2048]{2,1,0:T(8,128)(2,1)}, bf16[16,16,2048]{2,1,0:T(8,128)(2,1)}, u32[]{:S(2)}, u32[]{:S(2)}) collective-permute-start(bf16[16,16,2048]{2,1,0:T(8,128)(2,1)} %get-tuple-element.11.refs_0_), channel_id=1, source_target_pairs={{0,96},{1,97},{2,98},{3,99},{4,100},{5,101},{6,102},{7,103},{8,104... | collective-permute-start | bytes 3145736 | tf_op jit(solution)/shard_map/ppermute | solution.py:36
  238.9 303.0 %all-to-all-start.4 = ((bf16[16,2,3,128,128]{4,3,2,1,0:T(8,128)(2,1)}), bf16[16,2,3,128,128]{4,3,2,1,0:T(8,128)(2,1)S(1)}, u32[]{:S(2)}, u32[]{:S(2)}) async-start(bf16[16,2,3,128,128]{4,3,2,1,0:T(8,128)(2,1)} %get-tuple-element.10), calls=%async_computation.4 | async-start | bytes 6291456 | tf_op jit(solution)/shard_map/all_to_all | solution.py:249
  242.6 30.6 %collective-permute-start.4 = (bf16[16,16,2048]{2,1,0:T(8,128)(2,1)}, bf16[16,16,2048]{2,1,0:T(8,128)(2,1)}, u32[]{:S(2)}, u32[]{:S(2)}) collective-permute-start(bf16[16,16,2048]{2,1,0:T(8,128)(2,1)} %get-tuple-element.12.refs_0_), channel_id=1, source_target_pairs={{0,1},{1,0},{2,3},{3,2},{4,5},{5,4},{6,7},{7,6},{8,9},{9,8},{10,11... | collective-permute-start | bytes 3145736 | tf_op jit(solution)/shard_map/ppermute | solution.py:36
  244.0 17.6 %collective-permute-start.2 = (bf16[8,16,2048]{2,1,0:T(8,128)(2,1)S(1)}, bf16[8,16,2048]{2,1,0:T(8,128)(2,1)}, u32[]{:S(2)}, u32[]{:S(2)}) collective-permute-start(bf16[8,16,2048]{2,1,0:T(8,128)(2,1)S(1)} %slice.25), channel_id=1, source_target_pairs={{0,32},{1,33},{2,34},{3,35},{4,36},{5,37},{6,38},{7,39},{8,40},{9,... | collective-permute-start | bytes 1572872 | tf_op jit(solution)/shard_map/ppermute | solution.py:36
  247.1 14.5 %collective-permute-start.3 = (bf16[8,16,2048]{2,1,0:T(8,128)(2,1)S(1)}, bf16[8,16,2048]{2,1,0:T(8,128)(2,1)}, u32[]{:S(2)}, u32[]{:S(2)}) collective-permute-start(bf16[8,16,2048]{2,1,0:T(8,128)(2,1)S(1)} %slice.26), channel_id=1, source_target_pairs={{0,96},{1,97},{2,98},{3,99},{4,100},{5,101},{6,102},{7,103},{8,104... | collective-permute-start | bytes 1572872 | tf_op jit(solution)/shard_map/ppermute | solution.py:36
  250.6 25.9 %collective-permute-start.5 = (bf16[16,16,2048]{2,1,0:T(8,128)(2,1)}, bf16[16,16,2048]{2,1,0:T(8,128)(2,1)}, u32[]{:S(2)}, u32[]{:S(2)}) collective-permute-start(bf16[16,16,2048]{2,1,0:T(8,128)(2,1)} %collective-permute-done.refs_1_), channel_id=1, source_target_pairs={{0,1},{1,0},{2,3},{3,2},{4,5},{5,4},{6,7},{7,6},{8,9},{9,8},{10,11... | collective-permute-start | bytes 3145736 | tf_op jit(solution)/shard_map/ppermute | solution.py:36
  250.6 25.9 %collective-permute-start.6 = (bf16[16,16,2048]{2,1,0:T(8,128)(2,1)}, bf16[16,16,2048]{2,1,0:T(8,128)(2,1)}, u32[]{:S(2)}, u32[]{:S(2)}) collective-permute-start(bf16[16,16,2048]{2,1,0:T(8,128)(2,1)} %collective-permute-done.1.refs_2_), channel_id=1, source_target_pairs={{0,1},{1,0},{2,3},{3,2},{4,5},{5,4},{6,7},{7,6},{8,9},{9,8},{10,11... | collective-permute-start | bytes 3145736 | tf_op jit(solution)/shard_map/ppermute | solution.py:36
  261.6 11.7 %collective-permute-start.7 = (bf16[8,16,2048]{2,1,0:T(8,128)(2,1)}, bf16[8,16,2048]{2,1,0:T(8,128)(2,1)}, u32[]{:S(2)}, u32[]{:S(2)}) collective-permute-start(bf16[8,16,2048]{2,1,0:T(8,128)(2,1)} %collective-permute-done.2.refs_3_), channel_id=1, source_target_pairs={{0,1},{1,0},{2,3},{3,2},{4,5},{5,4},{6,7},{7,6},{8,9},{9,8},{10,11... | collective-permute-start | bytes 1572872 | tf_op jit(solution)/shard_map/ppermute | solution.py:36
  261.6 13.1 %collective-permute-start.8 = (bf16[8,16,2048]{2,1,0:T(8,128)(2,1)}, bf16[8,16,2048]{2,1,0:T(8,128)(2,1)}, u32[]{:S(2)}, u32[]{:S(2)}) collective-permute-start(bf16[8,16,2048]{2,1,0:T(8,128)(2,1)} %collective-permute-done.3.refs_4_), channel_id=1, source_target_pairs={{0,1},{1,0},{2,3},{3,2},{4,5},{5,4},{6,7},{7,6},{8,9},{9,8},{10,11... | collective-permute-start | bytes 1572872 | tf_op jit(solution)/shard_map/ppermute | solution.py:36
  273.2 280.8 %collective-permute-start.13 = (bf16[16,16,2048]{2,1,0:T(8,128)(2,1)}, bf16[16,16,2048]{2,1,0:T(8,128)(2,1)}, u32[]{:S(2)}, u32[]{:S(2)}) collective-permute-start(bf16[16,16,2048]{2,1,0:T(8,128)(2,1)} %get-tuple-element.11.refs_0_), channel_id=1, source_target_pairs={{0,1},{1,0},{2,3},{3,2},{4,5},{5,4},{6,7},{7,6},{8,9},{9,8},{10,11... | collective-permute-start | bytes 3145736 | tf_op jit(solution)/shard_map/ppermute | solution.py:36
  273.3 275.7 %collective-permute-start.11 = (bf16[8,16,2048]{2,1,0:T(8,128)(2,1)}, bf16[8,16,2048]{2,1,0:T(8,128)(2,1)}, u32[]{:S(2)}, u32[]{:S(2)}) collective-permute-start(bf16[8,16,2048]{2,1,0:T(8,128)(2,1)} %slice.28), channel_id=1, source_target_pairs={{0,32},{1,33},{2,34},{3,35},{4,36},{5,37},{6,38},{7,39},{8,40},{9,... | collective-permute-start | bytes 1572872 | tf_op jit(solution)/shard_map/ppermute | solution.py:36
  274.7 274.9 %collective-permute-start.12 = (bf16[8,16,2048]{2,1,0:T(8,128)(2,1)}, bf16[8,16,2048]{2,1,0:T(8,128)(2,1)}, u32[]{:S(2)}, u32[]{:S(2)}) collective-permute-start(bf16[8,16,2048]{2,1,0:T(8,128)(2,1)} %slice.29), channel_id=1, source_target_pairs={{0,96},{1,97},{2,98},{3,99},{4,100},{5,101},{6,102},{7,103},{8,104... | collective-permute-start | bytes 1572872 | tf_op jit(solution)/shard_map/ppermute | solution.py:36
  276.5 277.5 %collective-permute-start.14 = (bf16[16,16,2048]{2,1,0:T(8,128)(2,1)}, bf16[16,16,2048]{2,1,0:T(8,128)(2,1)}, u32[]{:S(2)}, u32[]{:S(2)}) collective-permute-start(bf16[16,16,2048]{2,1,0:T(8,128)(2,1)} %collective-permute-done.9.refs_1_), channel_id=1, source_target_pairs={{0,1},{1,0},{2,3},{3,2},{4,5},{5,4},{6,7},{7,6},{8,9},{9,8},{10,11... | collective-permute-start | bytes 3145736 | tf_op jit(solution)/shard_map/ppermute | solution.py:36
  276.6 277.5 %collective-permute-start.15 = (bf16[16,16,2048]{2,1,0:T(8,128)(2,1)}, bf16[16,16,2048]{2,1,0:T(8,128)(2,1)}, u32[]{:S(2)}, u32[]{:S(2)}) collective-permute-start(bf16[16,16,2048]{2,1,0:T(8,128)(2,1)} %collective-permute-done.10.refs_2_), channel_id=1, source_target_pairs={{0,1},{1,0},{2,3},{3,2},{4,5},{5,4},{6,7},{7,6},{8,9},{9,8},{10,11... | collective-permute-start | bytes 3145736 | tf_op jit(solution)/shard_map/ppermute | solution.py:36
  541.9 276.6 %all-to-all-start.3 = ((bf16[16,128,384]{2,1,0:T(8,128)(2,1)}), bf16[16,128,384]{2,1,0:T(8,128)(2,1)}, u32[]{:S(2)}, u32[]{:S(2)}) async-start(bf16[16,128,384]{2,1,0:T(8,128)(2,1)} %bitcast.29), calls=%async_computation.3 | async-start | bytes 3145728 | tf_op jit(solution)/shard_map/all_to_all | solution.py:261
  549.0 5.0 collective-permute-start.16
  818.5 34.3 %all-to-all-start.5 = ((bf16[16,128,384]{2,1,0:T(8,128)(2,1)}), bf16[16,128,384]{2,1,0:T(8,128)(2,1)}, u32[]{:S(2)}, u32[]{:S(2)}) async-start(bf16[16,128,384]{2,1,0:T(8,128)(2,1)} %bitcast.30), calls=%async_computation.5 | async-start | bytes 3145728 | tf_op jit(solution)/shard_map/all_to_all | solution.py:261
  865.2 5.2 collective-permute-start.19
  874.0 5.1 collective-permute-start.21
  (11 other events, 585.1 us)

commit v2 on v1

--- a/solution.py
+++ b/solution.py
@@ -14,7 +14,6 @@
 SIZES = (4, 2, 4, 2, 2)
 COL = ("y", "xh", "core")
 ROW = ("z", "xl")
-PLANE = ("xl", "y", "xh")
 
 
 def moved(axis, to):
@@ -50,28 +49,30 @@
 
 def pick_kernel(chunks, pairs_ref, blocks_ref, *refs):
     out_refs = refs[:chunks]
-    first_ref, count, sems = refs[chunks:]
+    stage, count, in_sems, out_sems = refs[chunks:]
     held = blocks_ref.shape[0]
     depth = blocks_ref.shape[1] // chunks
-    owners = first_ref.shape[0]
-    for d in range(owners):
+    loads = [
+        pltpu.make_async_copy(blocks_ref.at[t], stage.at[t], in_sems.at[t]) for t in range(held)
+    ]
+    for load in loads:
+        load.start()
+    for d in range(count.shape[0]):
         count[d] = 0
-        for k in range(CAP):
-            first_ref[d, k] = -1
-    copies = []
+    stores = []
     for t in range(held):
         l = pairs_ref[t, 1]
         k = count[l]
         count[l] = k + 1
-        first_ref[l, k] = pairs_ref[t, 0]
+        loads[t].wait()
         for c in range(chunks):
-            copy = pltpu.make_async_copy(
-                blocks_ref.at[t, pl.ds(c * depth, depth)], out_refs[c].at[l, k], sems.at[t, c]
+            store = pltpu.make_async_copy(
+                stage.at[t, pl.ds(c * depth, depth)], out_refs[c].at[l, k], out_sems.at[t, c]
             )
-            copy.start()
-            copies.append(copy)
-    for copy in copies:
-        copy.wait()
+            store.start()
+            stores.append(store)
+    for store in stores:
+        store.wait()
 
 
 def pick(pairs, blocks, owners):
@@ -80,20 +81,31 @@
     out = jax.ShapeDtypeStruct((owners, CAP, depth, width, width), blocks.dtype)
     return pl.pallas_call(
         functools.partial(pick_kernel, CHUNKS),
-        out_shape=[out] * CHUNKS + [jax.ShapeDtypeStruct((owners, CAP), jnp.int32)],
+        out_shape=[out] * CHUNKS,
         in_specs=[
             pl.BlockSpec(memory_space=pltpu.SMEM),
             pl.BlockSpec(memory_space=pl.ANY),
         ],
-        out_specs=[pl.BlockSpec(memory_space=pl.ANY)] * CHUNKS
-        + [pl.BlockSpec(memory_space=pltpu.SMEM)],
+        out_specs=[pl.BlockSpec(memory_space=pl.ANY)] * CHUNKS,
         scratch_shapes=[
+            pltpu.VMEM(blocks.shape, blocks.dtype),
             pltpu.SMEM((owners,), jnp.int32),
+            pltpu.SemaphoreType.DMA((held,)),
             pltpu.SemaphoreType.DMA((held, CHUNKS)),
         ],
+        compiler_params=pltpu.CompilerParams(vmem_limit_bytes=8 * 1024 * 1024),
         cost_estimate=pl.CostEstimate(flops=0, bytes_accessed=4 * blocks.size, transcendentals=0),
         name="pick",
     )(pairs, blocks)
+
+
+def firsts_for_me(all_pairs):
+    hit = all_pairs[:, :, 1] == lax.axis_index(COL)
+    places = jnp.arange(all_pairs.shape[1])
+    before = places[None, :] < places[:, None]
+    rank = jnp.sum(hit[:, None, :] & before[None], axis=2)
+    chosen = hit[:, :, None] & (rank[:, :, None] == jnp.arange(CAP))
+    return jnp.sum(jnp.where(chosen, all_pairs[:, :, :1] + 1, 0), axis=1).reshape(-1) - 1
 
 
 def place_kernel(first_ref, blocks_ref, out_ref, total):
@@ -126,7 +138,7 @@
             out_specs=pl.BlockSpec((rows, width), lambda p, first: (0, p)),
             scratch_shapes=[pltpu.VMEM((rows, width), jnp.float32)],
         ),
-        compiler_params=pltpu.CompilerParams(vmem_limit_bytes=32 * 1024 * 1024),
+        compiler_params=pltpu.CompilerParams(vmem_limit_bytes=8 * 1024 * 1024),
         cost_estimate=pl.CostEstimate(
             flops=blocks.size, bytes_accessed=4 * blocks.size, transcendentals=0
         ),
@@ -134,75 +146,93 @@
     )(first, blocks)
 
 
-def lay_kernel(*refs):
-    pieces, out_ref, sems = refs[:-2], refs[-2], refs[-1]
-    z, core = lax.axis_index("z"), lax.axis_index("core")
-    half = out_ref.shape[1] // 2
-    full = out_ref.shape[1]
-    spots = [
-        (0, 0, full),
-        (3, 0, full),
-        (1, 0, full),
-        (2, 0, half),
-        (2, half, half),
-    ]
-    copies = []
-    for side in range(2):
-        for i, (dz, start, size) in enumerate(spots):
-            n = side * len(spots) + i
-            copy = pltpu.make_async_copy(
-                pieces[n],
-                out_ref.at[(z + dz) % 4, pl.ds(start, size), (core + side) % 2],
-                sems.at[n],
-            )
-            copy.start()
-            copies.append(copy)
-    for copy in copies:
-        copy.wait()
-
-
-def lay(pieces):
-    plane, rows, columns = pieces[0].shape
-    return pl.pallas_call(
-        lay_kernel,
-        out_shape=jax.ShapeDtypeStruct((4, plane, 2, rows, columns), pieces[0].dtype),
+def lay_kernel(spots, *refs):
+    pieces, out_ref, sem = refs[:-2], refs[-2], refs[-1]
+    z, y, core = lax.axis_index("z"), lax.axis_index("y"), lax.axis_index("core")
+    x = 2 * lax.axis_index("xh") + lax.axis_index("xl")
+    for piece, (side, dz, chips) in zip(pieces, spots, strict=True):
+        for i, (dx, dy) in enumerate(chips):
+            to_x = (x + dx) % 4
+            pltpu.make_async_copy(
+                piece.at[i],
+                out_ref.at[(z + dz) % 4, to_x % 2, (y + dy) % 4, to_x // 2, (core + side) % 2],
+                sem,
+            ).start()
+    pltpu.make_async_copy(out_ref, out_ref, sem).wait()
+
+
+def lay(spots, pieces):
+    _, rows, columns = pieces[0].shape
+    out = pl.pallas_call(
+        functools.partial(lay_kernel, spots),
+        out_shape=jax.ShapeDtypeStruct((*SIZES, rows, columns), pieces[0].dtype),
         in_specs=[pl.BlockSpec(memory_space=pl.ANY)] * len(pieces),
-        out_specs=pl.BlockSpec(memory_space=pl.ANY),
-        scratch_shapes=[pltpu.SemaphoreType.DMA((len(pieces),))],
+        out_specs=pl.BlockSpec(memory_space=pltpu.VMEM),
+        scratch_shapes=[pltpu.SemaphoreType.DMA],
+        compiler_params=pltpu.CompilerParams(vmem_limit_bytes=12 * 1024 * 1024),
         cost_estimate=pl.CostEstimate(
-            flops=0, bytes_accessed=32 * pieces[0].size, transcendentals=0
+            flops=0, bytes_accessed=512 * rows * columns, transcendentals=0
         ),
         name="lay",
-    )(*pieces).reshape(8 * plane * rows, columns)
-
-
-def plane_gather(shard):
-    count = 16
-    copies = jnp.broadcast_to(shard[None], (count, *shard.shape))
-    return lax.all_to_all(copies, PLANE, split_axis=0, concat_axis=0, tiled=True)
-
-
-def z_gather(mine):
+    )(*pieces)
+    return out.reshape(-1, columns)
+
+
+def ring(x, move):
+    return jnp.concatenate([x, move(x, 1), move(x, -1), move(x, 2)], axis=0)
+
+
+FROM = (0, -1, 1, 2)
+
+
+def y_move(x, by):
+    return permute(x, "y", lambda k: (k + by) % 4)
+
+
+def x_move(x, by):
+    pairs = []
+    for device in range(128):
+        xl, xh = device // 16 % 2, device // 2 % 2
+        to = (2 * xh + xl + by) % 4
+        pairs.append((device, device + (to % 2 - xl) * 16 + (to // 2 - xh) * 2))
+    return lax.ppermute(x, AXES, pairs)
+
+
+def gather(shard, chips, first, second):
+    mine = ring(ring(shard[None], first), second)
     half = mine.shape[0] // 2
     from_below, from_above = up(mine), down(mine)
     far_low, far_high = up(from_below[:half]), down(from_above[half:])
     pieces = [mine, from_below, from_above, far_low, far_high]
-    return lay(pieces + [other_core(p) for p in pieces])
+    spots = [(0, chips), (-1, chips), (1, chips), (2, chips[:half]), (2, chips[half:])]
+    spots = [(side, dz, those) for side in range(2) for dz, those in spots]
+    return lay(spots, pieces + [other_core(p) for p in pieces])
 
 
 def pair_kernel(x_ref, y_ref, out_ref):
     width = x_ref.shape[1]
     aux_x, aux_y = x_ref.shape[2] // width, y_ref.shape[0] // width
+    step = 16
 
     @pl.when(pl.program_id(0) == 0)
     def _():
         out_ref[...] = jnp.zeros_like(out_ref)
 
-    for p in range(aux_x):
-        x = x_ref[0, :, p * width : (p + 1) * width].astype(jnp.float32)
-        for q in range(aux_y):
-            y = y_ref[q * width : (q + 1) * width, :].astype(jnp.float32)
-            out_ref[p * aux_y + q] += (x * y).reshape(width // 8, 8, width).sum(axis=0)
+    def body(r, totals):
+        rows = pl.multiple_of(r * step, step)
+        ys = [y_ref[pl.ds(rows + q * width, step), :].astype(jnp.float32) for q in range(aux_y)]
+        news = []
+        for p in range(aux_x):
+            x = x_ref[0, pl.ds(rows, step), p * width : (p + 1) * width].astype(jnp.float32)
+            for q in range(aux_y):
+                xy = x * ys[q]
+                news.append(totals[p * aux_y + q] + (xy[:8] + xy[8:]))
+        return tuple(news)
+
+    zero = jnp.zeros((8, width), jnp.float32)
+    totals = lax.fori_loop(0, width // step, body, (zero,) * (aux_x * aux_y), unroll=2)
+    for i, total in enumerate(totals):
+        out_ref[i] += total
 
 
 def pair_sums(x, y):
@@ -238,19 +268,18 @@
     width = blocks.shape[-1]
     basis_total = occ_green.shape[1]
 
-    both = jnp.concatenate([occ_green, virt_green.T], axis=0)
-    both_plane = plane_gather(both)
-    shard_rows = occ_green.shape[0]
-    occ = z_gather(both_plane[:, :shard_rows])
-    virt_t = z_gather(both_plane[:, shard_rows:])
-
-    *picked, send_first = pick(block_list[0], blocks, col_count)
+    all_pairs = lax.all_gather(block_list[0], COL, axis=0)
+    recv_first = firsts_for_me(all_pairs)
+
+    by_xy = tuple((dx, dy) for dx in FROM for dy in FROM)
+    by_yx = tuple((dx, dy) for dy in FROM for dx in FROM)
+    occ = gather(occ_green, by_xy, y_move, x_move)
+    virt_t = gather(virt_green.T, by_yx, x_move, y_move)
+
+    picked = pick(block_list[0], blocks, col_count)
     recv = [
         lax.all_to_all(part, COL, split_axis=0, concat_axis=0, tiled=True) for part in picked
     ]
-    recv_first = lax.all_to_all(
-        send_first[:, None], COL, split_axis=0, concat_axis=0, tiled=True
-    ).reshape(-1)
 
     dense, turned = [], []
     for part in recv:

time: 882 us -> 277 us (0.31)
  Pallas kernels: 682 us -> 48.3 us
  waiting for transfers between devices: 55.6 us -> 74 us
  local copies, waits for them, and re-layouts: 17.9 us -> 31.7 us
  starting transfers between devices: 54.8 us -> 67.5 us
  blocking collectives: 31.5 us -> 21.7 us
    pallas_call x2, Pallas kernels: 511 us -> 6.68 us  [lay(): pl.pallas_call(functools.partial(lay_kernel, spots), out_shape=jax.ShapeD...]
    pallas_call x1, Pallas kernels: 146 us -> 13.9 us  [pick(): pl.pallas_call(functools.partial(pick_kernel, CHUNKS), out_shape=[out] *...]
    ppermute x22 -> x28, waiting for transfers between devices: 17.9 us -> 66.2 us  [permute(): return lax.ppermute(x, AXES, moved(axis, to))]
    all_to_all x1 -> x0, blocking collectives: 31.5 us -> none  [plane_gather(): lax.all_to_all(copies, PLANE, split_axis=0, concat_axis=0, tiled=True)]
    all_to_all x2, waiting for transfers between devices: 30.2 us -> 0.01 us  [shards(): lax.all_to_all(part, COL, split_axis=0, concat_axis=0, tiled=True)]
    all_gather x0 -> x1, blocking collectives: none -> 21.7 us  [shards(): all_pairs = lax.all_gather(block_list[0], COL, axis=0)]
    unnamed x16 -> x38, local copies, waits for them, and re-layouts: 5.91 us -> 21 us
    ppermute x0 -> x6, starting transfers between devices: none -> 13.5 us  [x_move(): return lax.ppermute(x, AXES, pairs)]
  transfers between devices with their start and end apart: 27 -> 38, of which waited for: 8 -> 12; matrix products, arithmetic and copies ran while one was open for 5% -> 18% of each run, Pallas kernels for 60% -> 14%
where the time goes in v2:
time: 277 us; the launch traced here: 274 us
  waiting for transfers between devices  74 us (27%)
  starting transfers between devices  67.5 us (24%)
  Pallas kernels  48.3 us (17%)
  local copies, waits for them, and re-layouts  31.7 us (11%)
  matrix products  24.9 us (9%)
  blocking collectives  21.7 us (8%)
  other arithmetic  5.7 us (2%)
    ppermute x28, waiting for transfers between devices, permute(): return lax.ppermute(x, AXES, moved(axis, to))  66.2 us
    ppermute x28, starting transfers between devices, permute(): return lax.ppermute(x, AXES, moved(axis, to))  35.4 us
    all_gather x1, blocking collectives, shards(): all_pairs = lax.all_gather(block_list[0], COL, axis=0)  21.7 us
    unnamed x38, local copies, waits for them, and re-layouts  21 us
    pallas_call x2, Pallas kernels, pair_sums(): pl.pallas_call(pair_kernel, out_shape=jax.ShapeDtypeStruct((aux_x * aux_y...  20.1 us
    pallas_call x1, Pallas kernels, pick(): pl.pallas_call(functools.partial(pick_kernel, CHUNKS), out_shape=[out] *...  13.9 us
    dot_general x2, matrix products, shards(): lax.dot_general(d, virt_t, (((0,), (0,)), ((), ())), preferred_element_ty...  13.8 us
    ppermute x6, starting transfers between devices, x_move(): return lax.ppermute(x, AXES, pairs)  13.5 us
  transfers between devices with their start and end apart: 38, of which 12 were waited for; matrix products, arithmetic and copies ran while one was open for 18% of the time, Pallas kernels for 14%

profile of v2, /device:TPU:2, one launch (start us, length us, event | category | flops | bytes accessed | tf_op | source)
XLA Modules:
  0.0 274.1 jit_solution(15323967564358091940)
XLA Ops:
  10.5 13.9 %pick.1 = (bf16[16,2,3,128,128]{4,3,2,1,0:T(8,128)(2,1)S(1)}, bf16[16,2,3,128,128]{4,3,2,1,0:T(8,128)(2,1)S(1)}) custom-call(s32[24,2]{1,0:T(8,128)S(1)} %copy.15.pairs_ref, bf16[24,6,128,128]{3,2,1,0:T(8,128)(2,1)S(1)} %bitcast.33), custom_call_target="tpu_custom_call" | custom-call | bytes 9437184 | tf_op jit(solution)/shard_map/pick/pallas_call | solution.py:82
  27.6 4.3 %all-to-all-start = ((bf16[16,2,3,128,128]{4,3,2,1,0:T(8,128)(2,1)}), bf16[16,2,3,128,128]{4,3,2,1,0:T(8,128)(2,1)S(1)}, u32[]{:S(2)}, u32[]{:S(2)}) async-start(bf16[16,2,3,128,128]{4,3,2,1,0:T(8,128)(2,1)} %copy-done.5), calls=%async_computation | async-start | bytes 6291456 | tf_op jit(solution)/shard_map/all_to_all | solution.py:281
  33.2 3.4 %collective-permute-start.2 = (bf16[1,16,2048]{2,1,0:T(8,128)(2,1)S(1)}, bf16[1,16,2048]{2,1,0:T(8,128)(2,1)S(1)}, u32[]{:S(2)}, u32[]{:S(2)}) collective-permute-start(bf16[1,16,2048]{2,1,0:T(8,128)(2,1)S(1)} %bitcast.40), channel_id=1, source_target_pairs={{0,8},{1,9},{2,10},{3,11},{4,12},{5,13},{6,14},{7,15},{8,0},{9,1},... | collective-permute-start | bytes 196616 | tf_op jit(solution)/shard_map/ppermute | solution.py:35
  40.0 28.0 %collective-permute-done.2 = bf16[1,16,2048]{2,1,0:T(8,128)(2,1)S(1)} collective-permute-done((bf16[1,16,2048]{2,1,0:T(8,128)(2,1)S(1)}, bf16[1,16,2048]{2,1,0:T(8,128)(2,1)S(1)}, u32[]{:S(2)}, u32[]{:S(2)}) %collective-permute-start.2) | collective-permute-done | bytes 65568 | tf_op jit(solution)/shard_map/ppermute | solution.py:35
  68.9 6.6 %collective-permute-start.3 = (bf16[4,16,2048]{2,1,0:T(8,128)(2,1)S(1)}, bf16[4,16,2048]{2,1,0:T(8,128)(2,1)S(1)}, u32[]{:S(2)}, u32[]{:S(2)}) collective-permute-start(bf16[4,16,2048]{2,1,0:T(8,128)(2,1)S(1)} %pad_maximum_fusion.1), channel_id=1, source_target_pairs={{0,16},{1,17},{2,18},{3,19},{4,20},{5,21},{6,22},{7,23},{8,24},{9,... | collective-permute-start | bytes 786440 | tf_op jit(solution)/shard_map/ppermute | solution.py:198
  85.4 4.6 %collective-permute-done.5 = bf16[4,16,2048]{2,1,0:T(8,128)(2,1)S(1)} collective-permute-done((bf16[4,16,2048]{2,1,0:T(8,128)(2,1)S(1)}, bf16[4,16,2048]{2,1,0:T(8,128)(2,1)S(1)}, u32[]{:S(2)}, u32[]{:S(2)}) %collective-permute-start.5) | collective-permute-done | bytes 262176 | tf_op jit(solution)/shard_map/ppermute | solution.py:198
  100.3 4.6 %all-to-all-start.2 = ((bf16[16,2,3,128,128]{4,3,2,1,0:T(8,128)(2,1)}), bf16[16,2,3,128,128]{4,3,2,1,0:T(8,128)(2,1)}, u32[]{:S(2)}, u32[]{:S(2)}) async-start(bf16[16,2,3,128,128]{4,3,2,1,0:T(8,128)(2,1)} %copy-done.4), calls=%async_computation.2 | async-start | bytes 6291456 | tf_op jit(solution)/shard_map/all_to_all | solution.py:281
  104.9 14.3 %collective-permute-done.6.refs_1_ = bf16[16,16,2048]{2,1,0:T(8,128)(2,1)} collective-permute-done((bf16[16,16,2048]{2,1,0:T(8,128)(2,1)}, bf16[16,16,2048]{2,1,0:T(8,128)(2,1)}, u32[]{:S(2)}, u32[]{:S(2)}) %collective-permute-start.6) | collective-permute-done | bytes 1048608 | tf_op jit(solution)/shard_map/ppermute | solution.py:35
  126.3 15.4 %collective-permute-done.21.refs_1_ = bf16[16,16,2048]{2,1,0:T(8,128)(2,1)} collective-permute-done((bf16[16,16,2048]{2,1,0:T(8,128)(2,1)}, bf16[16,16,2048]{2,1,0:T(8,128)(2,1)}, u32[]{:S(2)}, u32[]{:S(2)}) %collective-permute-start.21) | collective-permute-done | bytes 1048608 | tf_op jit(solution)/shard_map/ppermute | solution.py:35
  142.2 21.7 %all_gather.3 = s32[16,24,2]{1,2,0:T(2,128)S(1)} all-gather(s32[1,24,2]{1,2,0:T(2,128)S(1)} %copy-done.12), channel_id=1, replica_groups=mesh['z'=4,'xl'=2,'y'=4,'xh'=2,'core'=2] {'y','xh','core'}, dimensions={0}, use_global_device_ids=true | all-gather | bytes 3264 | tf_op jit(solution)/shard_map/all_gather | solution.py:271
  173.2 3.4 %lay.2 = bf16[4,2,4,2,2,16,2048]{6,5,4,3,2,1,0:T(8,128)(2,1)S(1)} custom-call(bf16[16,16,2048]{2,1,0:T(8,128)(2,1)} %constant_dynamic-update-slice_fusion.refs_0_, bf16[16,16,2048]{2,1,0:T(8,128)(2,1)} %collective-permute-done.6.refs_1_, bf16[16,16,2048]{2,1,0:T(8,128)(2,1)} %collective-permute-done.7.refs_2_, ...), custom_call_target="tpu_custom_call" | custom-call | bytes 16777216 | tf_op jit(solution)/shard_map/lay/pallas_call | solution.py:166
  180.9 5.6 %convolution_convert_fusion.3 = bf16[2048,384]{1,0:T(8,128)(2,1)} fusion(bf16[2048,2048]{1,0:T(8,128)(2,1)S(1)} %bitcast.29, bf16[2048,384]{1,0:T(8,128)(2,1)S(1)} %place.2), kind=kOutput, calls=%fused_computation.4 | convolution fusion | flops 3222011904 | bytes 11534336 | tf_op jit(solution)/shard_map/dot_general | solution.py:288
  186.5 4.4 %all-to-all-start.1 = ((bf16[16,128,384]{2,1,0:T(8,128)(2,1)}), bf16[16,128,384]{2,1,0:T(8,128)(2,1)}, u32[]{:S(2)}, u32[]{:S(2)}) async-start(bf16[16,128,384]{2,1,0:T(8,128)(2,1)} %bitcast.7), calls=%async_computation.1 | async-start | bytes 3145728 | tf_op jit(solution)/shard_map/all_to_all | solution.py:290
  193.8 3.2 %lay.3 = bf16[4,2,4,2,2,16,2048]{6,5,4,3,2,1,0:T(8,128)(2,1)S(1)} custom-call(bf16[16,16,2048]{2,1,0:T(8,128)(2,1)} %constant_dynamic-update-slice_fusion.7.refs_0_, bf16[16,16,2048]{2,1,0:T(8,128)(2,1)} %collective-permute-done.21.refs_1_, bf16[16,16,2048]{2,1,0:T(8,128)(2,1)} %collective-permute-done.22.refs_2_, ...), custom_call_target="tpu_custom_call" | custom-call | bytes 16777216 | tf_op jit(solution)/shard_map/lay/pallas_call | solution.py:166
  197.1 4.2 %copy-done.2 = bf16[4,2,4,2,2,16,2048]{6,5,4,3,2,1,0:T(8,128)(2,1)} copy-done((bf16[4,2,4,2,2,16,2048]{6,5,4,3,2,1,0:T(8,128)(2,1)}, bf16[4,2,4,2,2,16,2048]{6,5,4,3,2,1,0:T(8,128)(2,1)S(1)}, u32[]{:S(2)}) %copy-start.2) | copy-done | bytes 8388632
  201.4 4.5 %place.3 = bf16[2048,384]{1,0:T(8,128)(2,1)S(1)} custom-call(s32[32]{0:T(128)S(1)} %sub.7.first_ref, bf16[32,3,128,128]{3,2,1,0:T(8,128)(2,1)} %bitcast.12.blocks_ref), custom_call_target="tpu_custom_call" | custom-call | flops 1572864 | bytes 6291456 | tf_op jit(solution)/shard_map/place/pallas_call | solution.py:131
  207.1 5.5 %convolution_convert_fusion = bf16[2048,384]{1,0:T(8,128)(2,1)} fusion(bf16[2048,2048]{1,0:T(8,128)(2,1)S(1)} %bitcast.30, bf16[2048,384]{1,0:T(8,128)(2,1)S(1)} %place.3), kind=kOutput, calls=%fused_computation.1 | convolution fusion | flops 3222011904 | bytes 11534336 | tf_op jit(solution)/shard_map/dot_general | solution.py:288
  214.7 5.2 %all-to-all-start.3 = ((bf16[16,128,384]{2,1,0:T(8,128)(2,1)}), bf16[16,128,384]{2,1,0:T(8,128)(2,1)}, u32[]{:S(2)}, u32[]{:S(2)}) async-start(bf16[16,128,384]{2,1,0:T(8,128)(2,1)} %bitcast.13), calls=%async_computation.3 | async-start | bytes 3145728 | tf_op jit(solution)/shard_map/all_to_all | solution.py:290
  219.9 7.0 %convolution_convert_fusion.2 = bf16[384,2048]{1,0:T(8,128)(2,1)S(1)} fusion(bf16[2048,384]{1,0:T(8,128)(2,1)S(1)} %copy-done.7, bf16[2048,2048]{1,0:T(8,128)(2,1)} %bitcast.31), kind=kOutput, calls=%fused_computation.3 | convolution fusion | flops 3222011904 | bytes 11534336 | tf_op jit(solution)/shard_map/dot_general | solution.py:294
  226.9 6.9 %convolution_convert_fusion.1 = bf16[384,2048]{1,0:T(8,128)(2,1)S(1)} fusion(bf16[2048,384]{1,0:T(8,128)(2,1)S(1)} %copy-done.9, bf16[2048,2048]{1,0:T(8,128)(2,1)} %bitcast.32), kind=kOutput, calls=%fused_computation.2 | convolution fusion | flops 3222011904 | bytes 11534336 | tf_op jit(solution)/shard_map/dot_general | solution.py:294
  235.8 10.1 %pair.2 = f32[18,8,128]{2,1,0:T(8,128)} custom-call(bf16[16,128,384]{2,1,0:T(8,128)(2,1)} %all-to-all-done.1.x_ref, bf16[768,2048]{1,0:T(8,128)(2,1)} %pad_maximum_fusion.y_ref), custom_call_target="tpu_custom_call" | custom-call | flops 9437184 | bytes 4718592 | tf_op jit(solution)/shard_map/pair/pallas_call | solution.py:241
  247.1 10.1 %pair.3 = f32[18,8,128]{2,1,0:T(8,128)} custom-call(bf16[16,128,384]{2,1,0:T(8,128)(2,1)} %all-to-all-done.3.x_ref, bf16[768,2048]{1,0:T(8,128)(2,1)} %pad_maximum_fusion.y_ref), custom_call_target="tpu_custom_call" | custom-call | flops 9437184 | bytes 4718592 | tf_op jit(solution)/shard_map/pair/pallas_call | solution.py:241
  259.6 3.4 %collective-permute-start.31 = (f32[6,6]{1,0:T(8,128)S(1)}, f32[6,6]{1,0:T(8,128)S(1)}, u32[]{:S(2)}, u32[]{:S(2)}) collective-permute-start(f32[6,6]{1,0:T(8,128)S(1)} %fusion.1), channel_id=1, source_target_pairs={{0,2},{1,3},{2,0},{3,1},{4,6},{5,7},{6,4},{7,5},{8,10},{9,11},{10,... | collective-permute-start | bytes 440 | tf_op jit(solution)/shard_map/ppermute | solution.py:35
  268.4 3.4 %collective-permute-start.33 = (f32[6,6]{1,0:T(8,128)S(1)}, f32[6,6]{1,0:T(8,128)S(1)}, u32[]{:S(2)}, u32[]{:S(2)}) collective-permute-start(f32[6,6]{1,0:T(8,128)S(1)} %add.32), channel_id=1, source_target_pairs={{0,8},{1,9},{2,10},{3,11},{4,12},{5,13},{6,14},{7,15},{8,0},{9,1},... | collective-permute-start | bytes 440 | tf_op jit(solution)/shard_map/ppermute | solution.py:35
  (130 shorter events, 79.9 us)
Async XLA Ops:
  0.0 33.2 %collective-permute-start.15 = (bf16[1,16,2048]{2,1,0:T(8,128)(2,1)}, bf16[1,16,2048]{2,1,0:T(8,128)(2,1)S(1)}, u32[]{:S(2)}, u32[]{:S(2)}) collective-permute-start(bf16[1,16,2048]{2,1,0:T(8,128)(2,1)} %bitcast.34), channel_id=1, source_target_pairs={{0,16},{1,17},{2,18},{3,19},{4,20},{5,21},{6,22},{7,23},{8,24},{9,... | collective-permute-start | bytes 196616 | tf_op jit(solution)/shard_map/ppermute | solution.py:198
  1.5 35.2 %collective-permute-start.16 = (bf16[1,16,2048]{2,1,0:T(8,128)(2,1)}, bf16[1,16,2048]{2,1,0:T(8,128)(2,1)S(1)}, u32[]{:S(2)}, u32[]{:S(2)}) collective-permute-start(bf16[1,16,2048]{2,1,0:T(8,128)(2,1)} %bitcast.35), channel_id=1, source_target_pairs={{0,18},{1,19},{2,16},{3,17},{4,22},{5,23},{6,20},{7,21},{8,26},{9,... | collective-permute-start | bytes 196616 | tf_op jit(solution)/shard_map/ppermute | solution.py:198
  2.0 34.6 %collective-permute-start.17 = (bf16[1,16,2048]{2,1,0:T(8,128)(2,1)}, bf16[1,16,2048]{2,1,0:T(8,128)(2,1)S(1)}, u32[]{:S(2)}, u32[]{:S(2)}) collective-permute-start(bf16[1,16,2048]{2,1,0:T(8,128)(2,1)} %bitcast.36), channel_id=1, source_target_pairs={{0,2},{1,3},{2,0},{3,1},{4,6},{5,7},{6,4},{7,5},{8,10},{9,11},{10,... | collective-permute-start | bytes 196616 | tf_op jit(solution)/shard_map/ppermute | solution.py:198
  4.2 35.9 %collective-permute-start = (bf16[1,16,2048]{2,1,0:T(8,128)(2,1)}, bf16[1,16,2048]{2,1,0:T(8,128)(2,1)S(1)}, u32[]{:S(2)}, u32[]{:S(2)}) collective-permute-start(bf16[1,16,2048]{2,1,0:T(8,128)(2,1)} %bitcast.38), channel_id=1, source_target_pairs={{0,4},{1,5},{2,6},{3,7},{4,8},{5,9},{6,10},{7,11},{8,12},{9,13},{1... | collective-permute-start | bytes 196616 | tf_op jit(solution)/shard_map/ppermute | solution.py:35
  5.7 34.3 %collective-permute-start.1 = (bf16[1,16,2048]{2,1,0:T(8,128)(2,1)}, bf16[1,16,2048]{2,1,0:T(8,128)(2,1)}, u32[]{:S(2)}, u32[]{:S(2)}) collective-permute-start(bf16[1,16,2048]{2,1,0:T(8,128)(2,1)} %bitcast.39), channel_id=1, source_target_pairs={{0,12},{1,13},{2,14},{3,15},{4,0},{5,1},{6,2},{7,3},{8,4},{9,5},{1... | collective-permute-start | bytes 196616 | tf_op jit(solution)/shard_map/ppermute | solution.py:35
  27.6 72.6 %all-to-all-start = ((bf16[16,2,3,128,128]{4,3,2,1,0:T(8,128)(2,1)}), bf16[16,2,3,128,128]{4,3,2,1,0:T(8,128)(2,1)S(1)}, u32[]{:S(2)}, u32[]{:S(2)}) async-start(bf16[16,2,3,128,128]{4,3,2,1,0:T(8,128)(2,1)} %copy-done.5), calls=%async_computation | async-start | bytes 6291456 | tf_op jit(solution)/shard_map/all_to_all | solution.py:281
  33.2 34.8 %collective-permute-start.2 = (bf16[1,16,2048]{2,1,0:T(8,128)(2,1)S(1)}, bf16[1,16,2048]{2,1,0:T(8,128)(2,1)S(1)}, u32[]{:S(2)}, u32[]{:S(2)}) collective-permute-start(bf16[1,16,2048]{2,1,0:T(8,128)(2,1)S(1)} %bitcast.40), channel_id=1, source_target_pairs={{0,8},{1,9},{2,10},{3,11},{4,12},{5,13},{6,14},{7,15},{8,0},{9,1},... | collective-permute-start | bytes 196616 | tf_op jit(solution)/shard_map/ppermute | solution.py:35
  36.7 58.1 %collective-permute-start.18 = (bf16[4,16,2048]{2,1,0:T(8,128)(2,1)S(1)}, bf16[4,16,2048]{2,1,0:T(8,128)(2,1)S(1)}, u32[]{:S(2)}, u32[]{:S(2)}) collective-permute-start(bf16[4,16,2048]{2,1,0:T(8,128)(2,1)S(1)} %pad_maximum_fusion.2), channel_id=1, source_target_pairs={{0,4},{1,5},{2,6},{3,7},{4,8},{5,9},{6,10},{7,11},{8,12},{9,13},{1... | collective-permute-start | bytes 786440 | tf_op jit(solution)/shard_map/ppermute | solution.py:35
  37.4 58.2 %collective-permute-start.19 = (bf16[4,16,2048]{2,1,0:T(8,128)(2,1)S(1)}, bf16[4,16,2048]{2,1,0:T(8,128)(2,1)S(1)}, u32[]{:S(2)}, u32[]{:S(2)}) collective-permute-start(bf16[4,16,2048]{2,1,0:T(8,128)(2,1)S(1)} %pad_maximum_fusion.2), channel_id=1, source_target_pairs={{0,12},{1,13},{2,14},{3,15},{4,0},{5,1},{6,2},{7,3},{8,4},{9,5},{1... | collective-permute-start | bytes 786440 | tf_op jit(solution)/shard_map/ppermute | solution.py:35
  40.0 56.3 %collective-permute-start.20 = (bf16[4,16,2048]{2,1,0:T(8,128)(2,1)S(1)}, bf16[4,16,2048]{2,1,0:T(8,128)(2,1)S(1)}, u32[]{:S(2)}, u32[]{:S(2)}) collective-permute-start(bf16[4,16,2048]{2,1,0:T(8,128)(2,1)S(1)} %pad_maximum_fusion.2), channel_id=1, source_target_pairs={{0,8},{1,9},{2,10},{3,11},{4,12},{5,13},{6,14},{7,15},{8,0},{9,1},... | collective-permute-start | bytes 786440 | tf_op jit(solution)/shard_map/ppermute | solution.py:35
  90.8 28.4 %collective-permute-start.6 = (bf16[16,16,2048]{2,1,0:T(8,128)(2,1)}, bf16[16,16,2048]{2,1,0:T(8,128)(2,1)}, u32[]{:S(2)}, u32[]{:S(2)}) collective-permute-start(bf16[16,16,2048]{2,1,0:T(8,128)(2,1)} %constant_dynamic-update-slice_fusion.refs_0_), channel_id=1, source_target_pairs={{0,32},{1,33},{2,34},{3,35},{4,36},{5,37},{6,38},{7,39},{8,40},{9,... | collective-permute-start | bytes 3145736 | tf_op jit(solution)/shard_map/ppermute | solution.py:35
  92.7 28.4 %collective-permute-start.7 = (bf16[16,16,2048]{2,1,0:T(8,128)(2,1)}, bf16[16,16,2048]{2,1,0:T(8,128)(2,1)}, u32[]{:S(2)}, u32[]{:S(2)}) collective-permute-start(bf16[16,16,2048]{2,1,0:T(8,128)(2,1)} %constant_dynamic-update-slice_fusion.refs_0_), channel_id=1, source_target_pairs={{0,96},{1,97},{2,98},{3,99},{4,100},{5,101},{6,102},{7,103},{8,104... | collective-permute-start | bytes 3145736 | tf_op jit(solution)/shard_map/ppermute | solution.py:35
  97.0 44.7 %collective-permute-start.21 = (bf16[16,16,2048]{2,1,0:T(8,128)(2,1)}, bf16[16,16,2048]{2,1,0:T(8,128)(2,1)}, u32[]{:S(2)}, u32[]{:S(2)}) collective-permute-start(bf16[16,16,2048]{2,1,0:T(8,128)(2,1)} %constant_dynamic-update-slice_fusion.7.refs_0_), channel_id=1, source_target_pairs={{0,32},{1,33},{2,34},{3,35},{4,36},{5,37},{6,38},{7,39},{8,40},{9,... | collective-permute-start | bytes 3145736 | tf_op jit(solution)/shard_map/ppermute | solution.py:35
  97.0 44.7 %collective-permute-start.22 = (bf16[16,16,2048]{2,1,0:T(8,128)(2,1)}, bf16[16,16,2048]{2,1,0:T(8,128)(2,1)}, u32[]{:S(2)}, u32[]{:S(2)}) collective-permute-start(bf16[16,16,2048]{2,1,0:T(8,128)(2,1)} %constant_dynamic-update-slice_fusion.7.refs_0_), channel_id=1, source_target_pairs={{0,96},{1,97},{2,98},{3,99},{4,100},{5,101},{6,102},{7,103},{8,104... | collective-permute-start | bytes 3145736 | tf_op jit(solution)/shard_map/ppermute | solution.py:35
  100.3 86.2 %all-to-all-start.2 = ((bf16[16,2,3,128,128]{4,3,2,1,0:T(8,128)(2,1)}), bf16[16,2,3,128,128]{4,3,2,1,0:T(8,128)(2,1)}, u32[]{:S(2)}, u32[]{:S(2)}) async-start(bf16[16,2,3,128,128]{4,3,2,1,0:T(8,128)(2,1)} %copy-done.4), calls=%async_computation.2 | async-start | bytes 6291456 | tf_op jit(solution)/shard_map/all_to_all | solution.py:281
  121.1 42.9 %collective-permute-start.8 = (bf16[8,16,2048]{2,1,0:T(8,128)(2,1)}, bf16[8,16,2048]{2,1,0:T(8,128)(2,1)}, u32[]{:S(2)}, u32[]{:S(2)}) collective-permute-start(bf16[8,16,2048]{2,1,0:T(8,128)(2,1)} %slice.24), channel_id=1, source_target_pairs={{0,32},{1,33},{2,34},{3,35},{4,36},{5,37},{6,38},{7,39},{8,40},{9,... | collective-permute-start | bytes 1572872 | tf_op jit(solution)/shard_map/ppermute | solution.py:35
  123.0 41.4 %collective-permute-start.9 = (bf16[8,16,2048]{2,1,0:T(8,128)(2,1)}, bf16[8,16,2048]{2,1,0:T(8,128)(2,1)}, u32[]{:S(2)}, u32[]{:S(2)}) collective-permute-start(bf16[8,16,2048]{2,1,0:T(8,128)(2,1)} %slice.25), channel_id=1, source_target_pairs={{0,96},{1,97},{2,98},{3,99},{4,100},{5,101},{6,102},{7,103},{8,104... | collective-permute-start | bytes 1572872 | tf_op jit(solution)/shard_map/ppermute | solution.py:35
  126.3 42.8 %collective-permute-start.10 = (bf16[16,16,2048]{2,1,0:T(8,128)(2,1)}, bf16[16,16,2048]{2,1,0:T(8,128)(2,1)}, u32[]{:S(2)}, u32[]{:S(2)}) collective-permute-start(bf16[16,16,2048]{2,1,0:T(8,128)(2,1)} %constant_dynamic-update-slice_fusion.refs_0_), channel_id=1, source_target_pairs={{0,1},{1,0},{2,3},{3,2},{4,5},{5,4},{6,7},{7,6},{8,9},{9,8},{10,11... | collective-permute-start | bytes 3145736 | tf_op jit(solution)/shard_map/ppermute | solution.py:35
  141.7 27.7 %collective-permute-start.11 = (bf16[16,16,2048]{2,1,0:T(8,128)(2,1)}, bf16[16,16,2048]{2,1,0:T(8,128)(2,1)}, u32[]{:S(2)}, u32[]{:S(2)}) collective-permute-start(bf16[16,16,2048]{2,1,0:T(8,128)(2,1)} %collective-permute-done.6.refs_1_), channel_id=1, source_target_pairs={{0,1},{1,0},{2,3},{3,2},{4,5},{5,4},{6,7},{7,6},{8,9},{9,8},{10,11... | collective-permute-start | bytes 3145736 | tf_op jit(solution)/shard_map/ppermute | solution.py:35
  141.7 29.0 %collective-permute-start.12 = (bf16[16,16,2048]{2,1,0:T(8,128)(2,1)}, bf16[16,16,2048]{2,1,0:T(8,128)(2,1)}, u32[]{:S(2)}, u32[]{:S(2)}) collective-permute-start(bf16[16,16,2048]{2,1,0:T(8,128)(2,1)} %collective-permute-done.7.refs_2_), channel_id=1, source_target_pairs={{0,1},{1,0},{2,3},{3,2},{4,5},{5,4},{6,7},{7,6},{8,9},{9,8},{10,11... | collective-permute-start | bytes 3145736 | tf_op jit(solution)/shard_map/ppermute | solution.py:35
  169.1 22.4 %collective-permute-start.25 = (bf16[16,16,2048]{2,1,0:T(8,128)(2,1)}, bf16[16,16,2048]{2,1,0:T(8,128)(2,1)}, u32[]{:S(2)}, u32[]{:S(2)}) collective-permute-start(bf16[16,16,2048]{2,1,0:T(8,128)(2,1)} %constant_dynamic-update-slice_fusion.7.refs_0_), channel_id=1, source_target_pairs={{0,1},{1,0},{2,3},{3,2},{4,5},{5,4},{6,7},{7,6},{8,9},{9,8},{10,11... | collective-permute-start | bytes 3145736 | tf_op jit(solution)/shard_map/ppermute | solution.py:35
  169.4 21.5 %collective-permute-start.23 = (bf16[8,16,2048]{2,1,0:T(8,128)(2,1)}, bf16[8,16,2048]{2,1,0:T(8,128)(2,1)}, u32[]{:S(2)}, u32[]{:S(2)}) collective-permute-start(bf16[8,16,2048]{2,1,0:T(8,128)(2,1)} %slice.28), channel_id=1, source_target_pairs={{0,32},{1,33},{2,34},{3,35},{4,36},{5,37},{6,38},{7,39},{8,40},{9,... | collective-permute-start | bytes 1572872 | tf_op jit(solution)/shard_map/ppermute | solution.py:35
  186.5 28.2 %all-to-all-start.1 = ((bf16[16,128,384]{2,1,0:T(8,128)(2,1)}), bf16[16,128,384]{2,1,0:T(8,128)(2,1)}, u32[]{:S(2)}, u32[]{:S(2)}) async-start(bf16[16,128,384]{2,1,0:T(8,128)(2,1)} %bitcast.7), calls=%async_computation.1 | async-start | bytes 3145728 | tf_op jit(solution)/shard_map/all_to_all | solution.py:290
  214.7 32.4 %all-to-all-start.3 = ((bf16[16,128,384]{2,1,0:T(8,128)(2,1)}), bf16[16,128,384]{2,1,0:T(8,128)(2,1)}, u32[]{:S(2)}, u32[]{:S(2)}) async-start(bf16[16,128,384]{2,1,0:T(8,128)(2,1)} %bitcast.13), calls=%async_computation.3 | async-start | bytes 3145728 | tf_op jit(solution)/shard_map/all_to_all | solution.py:290
  (27 other events, 219.9 us)

commit v3 on v2

v3 whole, which is shorter than its diff:
```python
import functools

import jax
import jax.numpy as jnp
from jax import lax
from jax.experimental import pallas as pl
from jax.experimental.pallas import tpu as pltpu
from jax.sharding import Mesh
from jax.sharding import PartitionSpec as P

CAP = 2
CHUNKS = 2
NOTE = 16
AXES = ("z", "xl", "y", "xh", "core")
SIZES = (4, 2, 4, 2, 2)
COL = ("y", "xh", "core")
ROW = ("z", "xl")


def moved(axis, to):
    where = AXES.index(axis)
    stride = 1
    for size in SIZES[where + 1 :]:
        stride *= size
    total = 1
    for size in SIZES:
        total *= size
    pairs = []
    for device in range(total):
        k = device // stride % SIZES[where]
        pairs.append((device, device + (to(k) - k) * stride))
    return pairs


def permute(x, axis, to):
    return lax.ppermute(x, AXES, moved(axis, to))


def up(x):
    return permute(x, "z", lambda k: (k + 1) % 4)


def down(x):
    return permute(x, "z", lambda k: (k - 1) % 4)


def other_core(x):
    return permute(x, "core", lambda k: 1 - k)


def pick_kernel(pairs_ref, blocks_ref, out_ref, count, first):
    held, rows, width = blocks_ref.shape
    owners = count.shape[0]
    for d in range(owners):
        count[d] = 0
        for k in range(CAP):
            first[d, k] = 0

    def body(t, carry):
        l = pairs_ref[t, 1]
        k = count[l]
        count[l] = k + 1
        first[l, k] = pairs_ref[t, 0] + 1
        out_ref[l, pl.ds(pl.multiple_of(k * rows, rows), rows), :] = blocks_ref[t]
        return carry

    lax.fori_loop(0, held, body, 0)
    which = lax.broadcasted_iota(jnp.int32, (NOTE, width), 0)
    for d in range(owners):
        note = jnp.zeros((NOTE, width), jnp.float32)
        for k in range(CAP):
            note = jnp.where(which == k, first[d, k].astype(jnp.float32), note)
        out_ref[d, CAP * rows :, :] = note.astype(out_ref.dtype)


def pick(pairs, blocks, owners):
    held, aux, width, _ = blocks.shape
    rows = aux * width
    return pl.pallas_call(
        pick_kernel,
        out_shape=jax.ShapeDtypeStruct((owners, CAP * rows + NOTE, width), blocks.dtype),
        in_specs=[
            pl.BlockSpec(memory_space=pltpu.SMEM),
            pl.BlockSpec(memory_space=pltpu.VMEM),
        ],
        out_specs=pl.BlockSpec(memory_space=pltpu.VMEM),
        scratch_shapes=[
            pltpu.SMEM((owners,), jnp.int32),
            pltpu.SMEM((owners, CAP), jnp.int32),
        ],
        compiler_params=pltpu.CompilerParams(vmem_limit_bytes=16 * 1024 * 1024),
        cost_estimate=pl.CostEstimate(flops=0, bytes_accessed=4 * blocks.size, transcendentals=0),
        name="pick",
    )(pairs, blocks.reshape(held, rows, width))


def place_kernel(first_ref, *refs):
    slot_refs, out_ref, total = refs[:CAP], refs[CAP], refs[CAP + 1]
    width = total.shape[1]
    total[...] = jnp.zeros_like(total)

    def body(s, carry):
        for k, slots in enumerate(slot_refs):
            m = first_ref[s * CAP + k]

            @pl.when(m >= 0)
            def _():
                rows = pl.ds(pl.multiple_of(m * width, width), width)
                total[rows, :] += slots[s].astype(jnp.float32)

        return carry

    lax.fori_loop(0, slot_refs[0].shape[0], body, 0)
    out_ref[...] = total[...].astype(out_ref.dtype)


def place(first, recv, start, depth, aux, rows):
    senders, _, width = recv.shape

    def slot(k):
        return pl.BlockSpec((senders, width, width), lambda p, first: (0, k * aux + start + p, 0))

    size = senders * CAP * depth * width * width
    return pl.pallas_call(
        place_kernel,
        out_shape=jax.ShapeDtypeStruct((rows, depth * width), recv.dtype),
        grid_spec=pltpu.PrefetchScalarGridSpec(
            num_scalar_prefetch=1,
            grid=(depth,),
            in_specs=[slot(k) for k in range(CAP)],
            out_specs=pl.BlockSpec((rows, width), lambda p, first: (0, p)),
            scratch_shapes=[pltpu.VMEM((rows, width), jnp.float32)],
        ),
        compiler_params=pltpu.CompilerParams(vmem_limit_bytes=8 * 1024 * 1024),
        cost_estimate=pl.CostEstimate(flops=size, bytes_accessed=4 * size, transcendentals=0),
        name="place",
    )(first, *[recv] * CAP)


def lay_kernel(spots, *refs):
    pieces, out_ref, sem = refs[:-2], refs[-2], refs[-1]
    z, y, core = lax.axis_index("z"), lax.axis_index("y"), lax.axis_index("core")
    x = 2 * lax.axis_index("xh") + lax.axis_index("xl")
    for piece, (side, dz, chips) in zip(pieces, spots, strict=True):
        for i, (dx, dy) in enumerate(chips):
            to_x = (x + dx) % 4
            pltpu.make_async_copy(
                piece.at[i],
                out_ref.at[(z + dz) % 4, to_x % 2, (y + dy) % 4, to_x // 2, (core + side) % 2],
                sem,
            ).start()
    pltpu.make_async_copy(out_ref, out_ref, sem).wait()


def lay(spots, pieces):
    _, rows, columns = pieces[0].shape
    out = pl.pallas_call(
        functools.partial(lay_kernel, spots),
        out_shape=jax.ShapeDtypeStruct((*SIZES, rows, columns), pieces[0].dtype),
        in_specs=[pl.BlockSpec(memory_space=pl.ANY)] * len(pieces),
        out_specs=pl.BlockSpec(memory_space=pltpu.VMEM),
        scratch_shapes=[pltpu.SemaphoreType.DMA],
        compiler_params=pltpu.CompilerParams(vmem_limit_bytes=12 * 1024 * 1024),
        cost_estimate=pl.CostEstimate(
            flops=0, bytes_accessed=512 * rows * columns, transcendentals=0
        ),
        name="lay",
    )(*pieces)
    return out.reshape(-1, columns)


def ring(x, move):
    return jnp.concatenate([x, move(x, 1), move(x, -1), move(x, 2)], axis=0)


FROM = (0, -1, 1, 2)


def y_move(x, by):
    return permute(x, "y", lambda k: (k + by) % 4)


def x_move(x, by):
    pairs = []
    for device in range(128):
        xl, xh = device // 16 % 2, device // 2 % 2
        to = (2 * xh + xl + by) % 4
        pairs.append((device, device + (to % 2 - xl) * 16 + (to // 2 - xh) * 2))
    return lax.ppermute(x, AXES, pairs)


def plane_gather(shard, first, second):
    return ring(ring(shard[None], first), second)


def z_near(mine):
    return up(mine), down(mine)


def z_far(mine, near):
    half = mine.shape[0] // 2
    return up(near[0][:half]), down(near[1][half:])


def assemble(mine, near, far, chips):
    half = mine.shape[0] // 2
    pieces = [mine, *near, *far]
    spots = [(0, chips), (-1, chips), (1, chips), (2, chips[:half]), (2, chips[half:])]
    spots = [(side, dz, those) for side in range(2) for dz, those in spots]
    return lay(spots, pieces + [other_core(p) for p in pieces])


def pair_kernel(x_ref, *refs):
    y_refs, out_ref = refs[:-1], refs[-1]
    blocks, width, _ = x_ref.shape
    aux_x = x_ref.shape[2] // width
    same = lax.broadcasted_iota(jnp.int32, (width, width), 0) == lax.broadcasted_iota(
        jnp.int32, (width, width), 1
    )
    x = jnp.concatenate(
        [
            jnp.concatenate(
                [x_ref[k, :, p * width : (p + 1) * width] for k in range(blocks)], axis=1
            )
            for p in range(aux_x)
        ],
        axis=0,
    )
    done = 0
    for y_ref in y_refs:
        products = lax.dot_general(
            x, y_ref[...], (((1,), (1,)), ((), ())), preferred_element_type=jnp.float32
        )
        aux_y = y_ref.shape[0] // width
        for q in range(aux_y):
            for p in range(aux_x):
                tile = products[p * width : (p + 1) * width, q * width : (q + 1) * width]
                tile = jnp.where(same, tile, 0.0).reshape(width // 8, 8, width)
                out_ref[(done + q) * aux_x + p] = tile.sum(axis=0)
        done += aux_y


def pair_sums(x, ys):
    _, width, _ = x.shape
    aux_x, aux_y = x.shape[2] // width, sum(y.shape[0] for y in ys) // width
    sums = pl.pallas_call(
        pair_kernel,
        out_shape=jax.ShapeDtypeStruct((aux_y * aux_x, 8, width), jnp.float32),
        in_specs=[pl.BlockSpec(memory_space=pltpu.VMEM)] * (1 + len(ys)),
        out_specs=pl.BlockSpec(memory_space=pltpu.VMEM),
        compiler_params=pltpu.CompilerParams(vmem_limit_bytes=16 * 1024 * 1024),
        cost_estimate=pl.CostEstimate(
            flops=2 * x.size * aux_y, bytes_accessed=6 * x.size, transcendentals=0
        ),
        name="pair",
    )(x, *ys)
    return sums.sum(axis=(1, 2)).reshape(aux_y, aux_x).T


def col_sum(x):
    x = x + other_core(x)
    x = x + permute(x, "xh", lambda k: 1 - k)
    x = x + permute(x, "y", lambda k: k ^ 1)
    return x + permute(x, "y", lambda k: k ^ 2)


def shards(tensor_blocks, block_list, occ_green, virt_green):
    col_count = lax.axis_size(COL)
    blocks = tensor_blocks[0]
    aux, width = blocks.shape[1], blocks.shape[-1]
    depth = aux // CHUNKS
    basis_total = occ_green.shape[1]

    by_xy = tuple((dx, dy) for dx in FROM for dy in FROM)
    by_yx = tuple((dx, dy) for dy in FROM for dx in FROM)
    occ_plane = plane_gather(occ_green, y_move, x_move)
    occ_near = z_near(occ_plane)
    occ_near, virt_shard = lax.optimization_barrier((occ_near, virt_green.T))
    occ_far = z_far(occ_plane, occ_near)
    virt_plane = plane_gather(virt_shard, x_move, y_move)
    occ_far, virt_plane = lax.optimization_barrier((occ_far, virt_plane))
    virt_near = z_near(virt_plane)
    virt_far = z_far(virt_plane, virt_near)
    occ = assemble(occ_plane, occ_near, occ_far, by_xy)
    virt_t = assemble(virt_plane, virt_near, virt_far, by_yx)

    picked = pick(block_list[0], blocks, col_count)
    recv = lax.all_to_all(picked, COL, split_axis=0, concat_axis=0, tiled=True)
    notes = CAP * aux * width
    recv_first = recv[:, notes : notes + CAP, 0].astype(jnp.int32).reshape(-1) - 1

    dense, turned = [], []
    for c in range(CHUNKS):
        dense.append(place(recv_first, recv, c * depth, depth, aux, basis_total))
        half = jnp.dot(occ, dense[-1], preferred_element_type=jnp.float32).astype(jnp.bfloat16)
        half = half.reshape(col_count, width, -1)
        turned.append(lax.all_to_all(half, COL, split_axis=0, concat_axis=0, tiled=True))

    virt_half = [
        lax.dot_general(
            d, virt_t, (((0,), (0,)), ((), ())), preferred_element_type=jnp.float32
        ).astype(jnp.bfloat16)
        for d in dense
    ]
    sums = jnp.concatenate([pair_sums(x, virt_half) for x in turned], axis=0)
    return (col_sum(sums) / float(basis_total))[None]


def solution(mesh):
    fine = Mesh(mesh.devices.reshape(SIZES), AXES)
    in_specs = (
        P(ROW, COL, None, None, None),
        P(ROW, COL, None),
        P(ROW + COL, None),
        P(None, ROW + COL),
    )
    return jax.shard_map(
        shards, mesh=fine, in_specs=in_specs, out_specs=P(ROW, None, None), check_vma=False
    )
```

time: 277 us -> 290 us (1.047)
  waiting for transfers between devices: 74 us -> 139 us
  blocking collectives: 21.7 us -> 0 us
  Pallas kernels: 48.3 us -> 32 us
  starting transfers between devices: 67.5 us -> 54.6 us
  matrix products: 24.9 us -> 34 us
  local copies, waits for them, and re-layouts: 31.7 us -> 24.8 us
  other arithmetic: 5.7 us -> 1.76 us
    ppermute x6, waiting for transfers between devices: 5.79 us -> 81.4 us  [x_move(): return lax.ppermute(x, AXES, pairs)]
    pallas_call x3, Pallas kernels: 34 us -> 4.95 us  [the longest x2 3.59 us: pair_sums(): pl.pallas_call(pair_kernel, out_shape=jax.ShapeDtypeStruct((aux_y * aux_x...]
    all_gather x1 -> x0, blocking collectives: 21.7 us -> none  [shards(): all_pairs = lax.all_gather(block_list[0], COL, axis=0)]
    ppermute x28, waiting for transfers between devices: 66.2 us -> 52.5 us  [permute(): return lax.ppermute(x, AXES, moved(axis, to))]
    pallas_call x2, Pallas kernels: 6.68 us -> 17.4 us  [lay(): pl.pallas_call(functools.partial(lay_kernel, spots), out_shape=jax.ShapeD...]
    dot_general x2, matrix products: 11.1 us -> 19.1 us  [shards(): jnp.dot(occ, dense[-1], preferred_element_type=jnp.float32)]
    ppermute x28, starting transfers between devices: 35.4 us -> 29.2 us  [permute(): return lax.ppermute(x, AXES, moved(axis, to))]
    slice x4, local copies, waits for them, and re-layouts: 7.6 us -> 2.78 us  [z_far(): return (up(near[0][:half]), down(near[1][half:]))]
  transfers between devices with their start and end apart: 38 -> 37, of which waited for: 12 -> 18; matrix products, arithmetic and copies ran while one was open for 18% -> 15% of each run, Pallas kernels for 14% -> 11%
where the time goes in v3:
time: 290 us; the launch traced here: 287 us
  waiting for transfers between devices  139 us (48%)
  starting transfers between devices  54.6 us (19%)
  matrix products  34 us (12%)
  Pallas kernels  32 us (11%)
  local copies, waits for them, and re-layouts  24.8 us (9%)
    ppermute x6, waiting for transfers between devices, x_move(): return lax.ppermute(x, AXES, pairs)  81.4 us
    ppermute x28, waiting for transfers between devices, permute(): return lax.ppermute(x, AXES, moved(axis, to))  52.5 us
    ppermute x28, starting transfers between devices, permute(): return lax.ppermute(x, AXES, moved(axis, to))  29.2 us
    unnamed x36, local copies, waits for them, and re-layouts  19.6 us
    dot_general x2, matrix products, shards(): jnp.dot(occ, dense[-1], preferred_element_type=jnp.float32)  19.1 us
    pallas_call x2, Pallas kernels, lay(): pl.pallas_call(functools.partial(lay_kernel, spots), out_shape=jax.ShapeD...  17.4 us
    dot_general x2, matrix products, shards(): lax.dot_general(d, virt_t, (((0,), (0,)), ((), ())), preferred_element_ty...  14.9 us
    all_to_all x2, starting transfers between devices, shards(): lax.all_to_all(half, COL, split_axis=0, concat_axis=0, tiled=True)  11.8 us
  transfers between devices with their start and end apart: 37, of which 18 were waited for; matrix products, arithmetic and copies ran while one was open for 15% of the time, Pallas kernels for 11%

profile of v3, /device:TPU:2, one launch (start us, length us, event | category | flops | bytes accessed | tf_op | source)
XLA Modules:
  0.0 286.9 jit_solution(8386191413752140501)
XLA Ops:
  12.4 4.8 %all-to-all-start = ((bf16[16,1552,128]{2,1,0:T(8,128)(2,1)}), bf16[16,1552,128]{2,1,0:T(8,128)(2,1)}, u32[]{:S(2)}, u32[]{:S(2)}) async-start(bf16[16,1552,128]{2,1,0:T(8,128)(2,1)} %copy-done), calls=%async_computation | async-start | bytes 12713984 | tf_op jit(solution)/shard_map/all_to_all | solution.py:288
  22.7 72.6 %collective-permute-done.3 = bf16[4,16,2048]{2,1,0:T(8,128)(2,1)S(1)} collective-permute-done((bf16[4,16,2048]{2,1,0:T(8,128)(2,1)S(1)}, bf16[4,16,2048]{2,1,0:T(8,128)(2,1)S(1)}, u32[]{:S(2)}, u32[]{:S(2)}) %collective-permute-start.3) | collective-permute-done | bytes 262176 | tf_op jit(solution)/shard_map/ppermute | solution.py:189
  95.4 6.7 %collective-permute-done.5 = bf16[4,16,2048]{2,1,0:T(8,128)(2,1)S(1)} collective-permute-done((bf16[4,16,2048]{2,1,0:T(8,128)(2,1)S(1)}, bf16[4,16,2048]{2,1,0:T(8,128)(2,1)S(1)}, u32[]{:S(2)}, u32[]{:S(2)}) %collective-permute-start.5) | collective-permute-done | bytes 262176 | tf_op jit(solution)/shard_map/ppermute | solution.py:189
  106.4 22.9 %collective-permute-done.6.refs_1_ = bf16[16,16,2048]{2,1,0:T(8,128)(2,1)S(1)} collective-permute-done((bf16[16,16,2048]{2,1,0:T(8,128)(2,1)S(1)}, bf16[16,16,2048]{2,1,0:T(8,128)(2,1)S(1)}, u32[]{:S(2)}, u32[]{:S(2)}) %collective-permute-start.6) | collective-permute-done | bytes 1048608 | tf_op jit(solution)/shard_map/ppermute | solution.py:36
  144.7 3.0 %collective-permute-start.9 = (bf16[8,16,2048]{2,1,0:T(8,128)(2,1)S(1)}, bf16[8,16,2048]{2,1,0:T(8,128)(2,1)S(1)}, u32[]{:S(2)}, u32[]{:S(2)}) collective-permute-start(bf16[8,16,2048]{2,1,0:T(8,128)(2,1)S(1)} %slice.16), channel_id=1, source_target_pairs={{0,96},{1,97},{2,98},{3,99},{4,100},{5,101},{6,102},{7,103},{8,104... | collective-permute-start | bytes 1572872 | tf_op jit(solution)/shard_map/ppermute | solution.py:36
  150.7 4.9 %collective-permute-done.15 = bf16[4,16,2048]{2,1,0:T(8,128)(2,1)S(1)} collective-permute-done((bf16[4,16,2048]{2,1,0:T(8,128)(2,1)S(1)}, bf16[4,16,2048]{2,1,0:T(8,128)(2,1)S(1)}, u32[]{:S(2)}, u32[]{:S(2)}) %collective-permute-start.15) | collective-permute-done | bytes 262176 | tf_op jit(solution)/shard_map/ppermute | solution.py:36
  163.0 12.9 %lay.2 = bf16[4,2,4,2,2,16,2048]{6,5,4,3,2,1,0:T(8,128)(2,1)S(1)} custom-call(bf16[16,16,2048]{2,1,0:T(8,128)(2,1)S(1)} %constant_dynamic-update-slice_fusion.refs_0_, bf16[16,16,2048]{2,1,0:T(8,128)(2,1)S(1)} %collective-permute-done.6.refs_1_, bf16[16,16,2048]{2,1,0:T(8,128)(2,1)S(1)} %collective-permute-done.7.refs_2_, ...), custom_call_target="tpu_custom_call" | custom-call | bytes 16777216 | tf_op jit(solution)/shard_map/lay/pallas_call | solution.py:157
  175.9 3.3 %copy-done.1 = bf16[4,2,4,2,2,16,2048]{6,5,4,3,2,1,0:T(8,128)(2,1)} copy-done((bf16[4,2,4,2,2,16,2048]{6,5,4,3,2,1,0:T(8,128)(2,1)}, bf16[4,2,4,2,2,16,2048]{6,5,4,3,2,1,0:T(8,128)(2,1)S(1)}, u32[]{:S(2)}) %copy-start.1) | copy-done | bytes 8388632
  179.2 4.2 %collective-permute-done.21.refs_1_ = bf16[16,16,2048]{2,1,0:T(8,128)(2,1)S(1)} collective-permute-done((bf16[16,16,2048]{2,1,0:T(8,128)(2,1)}, bf16[16,16,2048]{2,1,0:T(8,128)(2,1)S(1)}, u32[]{:S(2)}, u32[]{:S(2)}) %collective-permute-start.21) | collective-permute-done | bytes 1048608 | tf_op jit(solution)/shard_map/ppermute | solution.py:36
  186.1 3.2 %collective-permute-start.24 = (bf16[8,16,2048]{2,1,0:T(8,128)(2,1)}, bf16[8,16,2048]{2,1,0:T(8,128)(2,1)}, u32[]{:S(2)}, u32[]{:S(2)}) collective-permute-start(bf16[8,16,2048]{2,1,0:T(8,128)(2,1)} %slice.22), channel_id=1, source_target_pairs={{0,96},{1,97},{2,98},{3,99},{4,100},{5,101},{6,102},{7,103},{8,104... | collective-permute-start | bytes 1572872 | tf_op jit(solution)/shard_map/ppermute | solution.py:36
  191.0 4.3 %place.2 = bf16[2048,384]{1,0:T(8,128)(2,1)S(1)} custom-call(s32[32]{0:T(128)S(1)} %sub.7.first_ref, bf16[16,1552,128]{2,1,0:T(8,128)(2,1)} %all-to-all-done.refs_0_.refs_1_, bf16[16,1552,128]{2,1,0:T(8,128)(2,1)} %all-to-all-done.refs_0_.refs_1_), custom_call_target="tpu_custom_call" | custom-call | flops 1572864 | bytes 6291456 | tf_op jit(solution)/shard_map/place/pallas_call | solution.py:124
  195.4 9.6 %convolution_convert_fusion.3 = bf16[2048,384]{1,0:T(8,128)(2,1)} fusion(bf16[2048,2048]{1,0:T(8,128)(2,1)} %bitcast.23, bf16[2048,384]{1,0:T(8,128)(2,1)S(1)} %place.2), kind=kOutput, calls=%fused_computation.3 | convolution fusion | flops 3222011904 | bytes 11534336 | tf_op jit(solution)/shard_map/dot_general | solution.py:295
  205.0 4.5 %all-to-all-start.1 = ((bf16[16,128,384]{2,1,0:T(8,128)(2,1)}), bf16[16,128,384]{2,1,0:T(8,128)(2,1)S(1)}, u32[]{:S(2)}, u32[]{:S(2)}) async-start(bf16[16,128,384]{2,1,0:T(8,128)(2,1)} %bitcast.28), calls=%async_computation.1 | async-start | bytes 3145728 | tf_op jit(solution)/shard_map/all_to_all | solution.py:297
  212.5 4.6 %lay.3 = bf16[4,2,4,2,2,16,2048]{6,5,4,3,2,1,0:T(8,128)(2,1)S(1)} custom-call(bf16[16,16,2048]{2,1,0:T(8,128)(2,1)} %constant_dynamic-update-slice_fusion.7.refs_0_, bf16[16,16,2048]{2,1,0:T(8,128)(2,1)S(1)} %collective-permute-done.21.refs_1_, bf16[16,16,2048]{2,1,0:T(8,128)(2,1)} %collective-permute-done.22.refs_2_, ...), custom_call_target="tpu_custom_call" | custom-call | bytes 16777216 | tf_op jit(solution)/shard_map/lay/pallas_call | solution.py:157
  217.1 3.3 %copy-done.2 = bf16[4,2,4,2,2,16,2048]{6,5,4,3,2,1,0:T(8,128)(2,1)} copy-done((bf16[4,2,4,2,2,16,2048]{6,5,4,3,2,1,0:T(8,128)(2,1)}, bf16[4,2,4,2,2,16,2048]{6,5,4,3,2,1,0:T(8,128)(2,1)S(1)}, u32[]{:S(2)}) %copy-start.2) | copy-done | bytes 8388632
  220.4 5.2 %place.3 = bf16[2048,384]{1,0:T(8,128)(2,1)} custom-call(s32[32]{0:T(128)S(1)} %sub.7.first_ref, bf16[16,1552,128]{2,1,0:T(8,128)(2,1)} %all-to-all-done.refs_0_.refs_1_, bf16[16,1552,128]{2,1,0:T(8,128)(2,1)} %all-to-all-done.refs_0_.refs_1_), custom_call_target="tpu_custom_call" | custom-call | flops 1572864 | bytes 6291456 | tf_op jit(solution)/shard_map/place/pallas_call | solution.py:124
  225.6 9.5 %convolution_convert_fusion = bf16[2048,384]{1,0:T(8,128)(2,1)} fusion(bf16[2048,2048]{1,0:T(8,128)(2,1)} %bitcast.24, bf16[2048,384]{1,0:T(8,128)(2,1)} %place.3), kind=kOutput, calls=%fused_computation | convolution fusion | flops 3222011904 | bytes 11534336 | tf_op jit(solution)/shard_map/dot_general | solution.py:295
  235.1 7.3 %all-to-all-start.2 = ((bf16[16,128,384]{2,1,0:T(8,128)(2,1)}), bf16[16,128,384]{2,1,0:T(8,128)(2,1)S(1)}, u32[]{:S(2)}, u32[]{:S(2)}) async-start(bf16[16,128,384]{2,1,0:T(8,128)(2,1)} %bitcast.29), calls=%async_computation.2 | async-start | bytes 3145728 | tf_op jit(solution)/shard_map/all_to_all | solution.py:297
  242.4 7.4 %convolution_convert_fusion.1.refs_1_ = bf16[384,2048]{1,0:T(8,128)(2,1)S(1)} fusion(bf16[2048,384]{1,0:T(8,128)(2,1)} %place.3, bf16[2048,2048]{1,0:T(8,128)(2,1)} %bitcast.25), kind=kOutput, calls=%fused_computation.1 | convolution fusion | flops 3222011904 | bytes 11534336 | tf_op jit(solution)/shard_map/dot_general | solution.py:300
  249.9 7.4 %convolution_convert_fusion.2.refs_0_ = bf16[384,2048]{1,0:T(8,128)(2,1)S(1)} fusion(bf16[2048,384]{1,0:T(8,128)(2,1)S(1)} %copy-done.9, bf16[2048,2048]{1,0:T(8,128)(2,1)} %bitcast.26), kind=kOutput, calls=%fused_computation.2 | convolution fusion | flops 3222011904 | bytes 11534336 | tf_op jit(solution)/shard_map/dot_general | solution.py:300
  260.6 5.6 %all-to-all-done.2.x_ref = bf16[16,128,384]{2,1,0:T(8,128)(2,1)S(1)} async-done(((bf16[16,128,384]{2,1,0:T(8,128)(2,1)}), bf16[16,128,384]{2,1,0:T(8,128)(2,1)S(1)}, u32[]{:S(2)}, u32[]{:S(2)}) %all-to-all-start.2) | async-done | bytes 1572896 | tf_op jit(solution)/shard_map/all_to_all | solution.py:297
  273.1 4.4 %collective-permute-done.31 = f32[6,6]{0,1:T(8,128)S(1)} collective-permute-done((f32[6,6]{0,1:T(8,128)S(1)}, f32[6,6]{0,1:T(8,128)S(1)}, u32[]{:S(2)}, u32[]{:S(2)}) %collective-permute-start.31) | collective-permute-done | bytes 176 | tf_op jit(solution)/shard_map/ppermute | solution.py:36
  277.9 3.2 %collective-permute-done.32 = f32[6,6]{0,1:T(8,128)S(1)} collective-permute-done((f32[6,6]{0,1:T(8,128)S(1)}, f32[6,6]{0,1:T(8,128)S(1)}, u32[]{:S(2)}, u32[]{:S(2)}) %collective-permute-start.32) | collective-permute-done | bytes 176 | tf_op jit(solution)/shard_map/ppermute | solution.py:36
  282.3 4.0 %collective-permute-done.33 = f32[6,6]{0,1:T(8,128)S(1)} collective-permute-done((f32[6,6]{0,1:T(8,128)S(1)}, f32[6,6]{0,1:T(8,128)S(1)}, u32[]{:S(2)}, u32[]{:S(2)}) %collective-permute-start.33) | collective-permute-done | bytes 176 | tf_op jit(solution)/shard_map/ppermute | solution.py:36
  (118 shorter events, 67.8 us)
Async XLA Ops:
  0.0 17.2 %collective-permute-start = (bf16[1,16,2048]{2,1,0:T(8,128)(2,1)}, bf16[1,16,2048]{2,1,0:T(8,128)(2,1)S(1)}, u32[]{:S(2)}, u32[]{:S(2)}) collective-permute-start(bf16[1,16,2048]{2,1,0:T(8,128)(2,1)} %bitcast.30), channel_id=1, source_target_pairs={{0,4},{1,5},{2,6},{3,7},{4,8},{5,9},{6,10},{7,11},{8,12},{9,13},{1... | collective-permute-start | bytes 196616 | tf_op jit(solution)/shard_map/ppermute | solution.py:36
  1.6 15.7 %collective-permute-start.1 = (bf16[1,16,2048]{2,1,0:T(8,128)(2,1)}, bf16[1,16,2048]{2,1,0:T(8,128)(2,1)S(1)}, u32[]{:S(2)}, u32[]{:S(2)}) collective-permute-start(bf16[1,16,2048]{2,1,0:T(8,128)(2,1)} %bitcast.31), channel_id=1, source_target_pairs={{0,12},{1,13},{2,14},{3,15},{4,0},{5,1},{6,2},{7,3},{8,4},{9,5},{1... | collective-permute-start | bytes 196616 | tf_op jit(solution)/shard_map/ppermute | solution.py:36
  3.2 14.0 %collective-permute-start.2 = (bf16[1,16,2048]{2,1,0:T(8,128)(2,1)}, bf16[1,16,2048]{2,1,0:T(8,128)(2,1)S(1)}, u32[]{:S(2)}, u32[]{:S(2)}) collective-permute-start(bf16[1,16,2048]{2,1,0:T(8,128)(2,1)} %bitcast.32), channel_id=1, source_target_pairs={{0,8},{1,9},{2,10},{3,11},{4,12},{5,13},{6,14},{7,15},{8,0},{9,1},... | collective-permute-start | bytes 196616 | tf_op jit(solution)/shard_map/ppermute | solution.py:36
  12.4 177.4 %all-to-all-start = ((bf16[16,1552,128]{2,1,0:T(8,128)(2,1)}), bf16[16,1552,128]{2,1,0:T(8,128)(2,1)}, u32[]{:S(2)}, u32[]{:S(2)}) async-start(bf16[16,1552,128]{2,1,0:T(8,128)(2,1)} %copy-done), calls=%async_computation | async-start | bytes 12713984 | tf_op jit(solution)/shard_map/all_to_all | solution.py:288
  17.3 78.0 %collective-permute-start.3 = (bf16[4,16,2048]{2,1,0:T(8,128)(2,1)S(1)}, bf16[4,16,2048]{2,1,0:T(8,128)(2,1)S(1)}, u32[]{:S(2)}, u32[]{:S(2)}) collective-permute-start(bf16[4,16,2048]{2,1,0:T(8,128)(2,1)S(1)} %pad_maximum_fusion), channel_id=1, source_target_pairs={{0,16},{1,17},{2,18},{3,19},{4,20},{5,21},{6,22},{7,23},{8,24},{9,... | collective-permute-start | bytes 786440 | tf_op jit(solution)/shard_map/ppermute | solution.py:189
  20.0 75.4 %collective-permute-start.4 = (bf16[4,16,2048]{2,1,0:T(8,128)(2,1)S(1)}, bf16[4,16,2048]{2,1,0:T(8,128)(2,1)S(1)}, u32[]{:S(2)}, u32[]{:S(2)}) collective-permute-start(bf16[4,16,2048]{2,1,0:T(8,128)(2,1)S(1)} %pad_maximum_fusion), channel_id=1, source_target_pairs={{0,18},{1,19},{2,16},{3,17},{4,22},{5,23},{6,20},{7,21},{8,26},{9,... | collective-permute-start | bytes 786440 | tf_op jit(solution)/shard_map/ppermute | solution.py:189
  20.0 82.1 %collective-permute-start.5 = (bf16[4,16,2048]{2,1,0:T(8,128)(2,1)S(1)}, bf16[4,16,2048]{2,1,0:T(8,128)(2,1)S(1)}, u32[]{:S(2)}, u32[]{:S(2)}) collective-permute-start(bf16[4,16,2048]{2,1,0:T(8,128)(2,1)S(1)} %pad_maximum_fusion), channel_id=1, source_target_pairs={{0,2},{1,3},{2,0},{3,1},{4,6},{5,7},{6,4},{7,5},{8,10},{9,11},{10,... | collective-permute-start | bytes 786440 | tf_op jit(solution)/shard_map/ppermute | solution.py:189
  102.2 27.1 %collective-permute-start.6 = (bf16[16,16,2048]{2,1,0:T(8,128)(2,1)S(1)}, bf16[16,16,2048]{2,1,0:T(8,128)(2,1)S(1)}, u32[]{:S(2)}, u32[]{:S(2)}) collective-permute-start(bf16[16,16,2048]{2,1,0:T(8,128)(2,1)S(1)} %constant_dynamic-update-slice_fusion.refs_0_), channel_id=1, source_target_pairs={{0,32},{1,33},{2,34},{3,35},{4,36},{5,37},{6,38},{7,39},{8,40},{9,... | collective-permute-start | bytes 3145736 | tf_op jit(solution)/shard_map/ppermute | solution.py:36
  104.1 25.1 %collective-permute-start.7 = (bf16[16,16,2048]{2,1,0:T(8,128)(2,1)S(1)}, bf16[16,16,2048]{2,1,0:T(8,128)(2,1)S(1)}, u32[]{:S(2)}, u32[]{:S(2)}) collective-permute-start(bf16[16,16,2048]{2,1,0:T(8,128)(2,1)S(1)} %constant_dynamic-update-slice_fusion.refs_0_), channel_id=1, source_target_pairs={{0,96},{1,97},{2,98},{3,99},{4,100},{5,101},{6,102},{7,103},{8,104... | collective-permute-start | bytes 3145736 | tf_op jit(solution)/shard_map/ppermute | solution.py:36
  106.4 53.3 %collective-permute-start.16 = (bf16[16,16,2048]{2,1,0:T(8,128)(2,1)S(1)}, bf16[16,16,2048]{2,1,0:T(8,128)(2,1)S(1)}, u32[]{:S(2)}, u32[]{:S(2)}) collective-permute-start(bf16[16,16,2048]{2,1,0:T(8,128)(2,1)S(1)} %constant_dynamic-update-slice_fusion.refs_0_), channel_id=1, source_target_pairs={{0,1},{1,0},{2,3},{3,2},{4,5},{5,4},{6,7},{7,6},{8,9},{9,8},{10,11... | collective-permute-start | bytes 3145736 | tf_op jit(solution)/shard_map/ppermute | solution.py:36
  133.4 26.2 %collective-permute-start.17 = (bf16[16,16,2048]{2,1,0:T(8,128)(2,1)S(1)}, bf16[16,16,2048]{2,1,0:T(8,128)(2,1)S(1)}, u32[]{:S(2)}, u32[]{:S(2)}) collective-permute-start(bf16[16,16,2048]{2,1,0:T(8,128)(2,1)S(1)} %collective-permute-done.6.refs_1_), channel_id=1, source_target_pairs={{0,1},{1,0},{2,3},{3,2},{4,5},{5,4},{6,7},{7,6},{8,9},{9,8},{10,11... | collective-permute-start | bytes 3145736 | tf_op jit(solution)/shard_map/ppermute | solution.py:36
  133.8 22.5 %collective-permute-start.8 = (bf16[8,16,2048]{2,1,0:T(8,128)(2,1)S(1)}, bf16[8,16,2048]{2,1,0:T(8,128)(2,1)S(1)}, u32[]{:S(2)}, u32[]{:S(2)}) collective-permute-start(bf16[8,16,2048]{2,1,0:T(8,128)(2,1)S(1)} %slice.15), channel_id=1, source_target_pairs={{0,32},{1,33},{2,34},{3,35},{4,36},{5,37},{6,38},{7,39},{8,40},{9,... | collective-permute-start | bytes 1572872 | tf_op jit(solution)/shard_map/ppermute | solution.py:36
  137.6 10.1 %collective-permute-start.14 = (bf16[4,16,2048]{2,1,0:T(8,128)(2,1)S(1)}, bf16[4,16,2048]{2,1,0:T(8,128)(2,1)S(1)}, u32[]{:S(2)}, u32[]{:S(2)}) collective-permute-start(bf16[4,16,2048]{2,1,0:T(8,128)(2,1)S(1)} %pad_maximum_fusion.1), channel_id=1, source_target_pairs={{0,12},{1,13},{2,14},{3,15},{4,0},{5,1},{6,2},{7,3},{8,4},{9,5},{1... | collective-permute-start | bytes 786440 | tf_op jit(solution)/shard_map/ppermute | solution.py:36
  144.7 11.6 %collective-permute-start.9 = (bf16[8,16,2048]{2,1,0:T(8,128)(2,1)S(1)}, bf16[8,16,2048]{2,1,0:T(8,128)(2,1)S(1)}, u32[]{:S(2)}, u32[]{:S(2)}) collective-permute-start(bf16[8,16,2048]{2,1,0:T(8,128)(2,1)S(1)} %slice.16), channel_id=1, source_target_pairs={{0,96},{1,97},{2,98},{3,99},{4,100},{5,101},{6,102},{7,103},{8,104... | collective-permute-start | bytes 1572872 | tf_op jit(solution)/shard_map/ppermute | solution.py:36
  147.8 7.9 %collective-permute-start.15 = (bf16[4,16,2048]{2,1,0:T(8,128)(2,1)S(1)}, bf16[4,16,2048]{2,1,0:T(8,128)(2,1)S(1)}, u32[]{:S(2)}, u32[]{:S(2)}) collective-permute-start(bf16[4,16,2048]{2,1,0:T(8,128)(2,1)S(1)} %pad_maximum_fusion.1), channel_id=1, source_target_pairs={{0,8},{1,9},{2,10},{3,11},{4,12},{5,13},{6,14},{7,15},{8,0},{9,1},... | collective-permute-start | bytes 786440 | tf_op jit(solution)/shard_map/ppermute | solution.py:36
  156.4 27.0 %collective-permute-start.21 = (bf16[16,16,2048]{2,1,0:T(8,128)(2,1)}, bf16[16,16,2048]{2,1,0:T(8,128)(2,1)S(1)}, u32[]{:S(2)}, u32[]{:S(2)}) collective-permute-start(bf16[16,16,2048]{2,1,0:T(8,128)(2,1)} %constant_dynamic-update-slice_fusion.7.refs_0_), channel_id=1, source_target_pairs={{0,32},{1,33},{2,34},{3,35},{4,36},{5,37},{6,38},{7,39},{8,40},{9,... | collective-permute-start | bytes 3145736 | tf_op jit(solution)/shard_map/ppermute | solution.py:36
  157.6 26.6 %collective-permute-start.22 = (bf16[16,16,2048]{2,1,0:T(8,128)(2,1)}, bf16[16,16,2048]{2,1,0:T(8,128)(2,1)}, u32[]{:S(2)}, u32[]{:S(2)}) collective-permute-start(bf16[16,16,2048]{2,1,0:T(8,128)(2,1)} %constant_dynamic-update-slice_fusion.7.refs_0_), channel_id=1, source_target_pairs={{0,96},{1,97},{2,98},{3,99},{4,100},{5,101},{6,102},{7,103},{8,104... | collective-permute-start | bytes 3145736 | tf_op jit(solution)/shard_map/ppermute | solution.py:36
  160.1 50.0 %collective-permute-start.25 = (bf16[16,16,2048]{2,1,0:T(8,128)(2,1)}, bf16[16,16,2048]{2,1,0:T(8,128)(2,1)}, u32[]{:S(2)}, u32[]{:S(2)}) collective-permute-start(bf16[16,16,2048]{2,1,0:T(8,128)(2,1)} %constant_dynamic-update-slice_fusion.7.refs_0_), channel_id=1, source_target_pairs={{0,1},{1,0},{2,3},{3,2},{4,5},{5,4},{6,7},{7,6},{8,9},{9,8},{10,11... | collective-permute-start | bytes 3145736 | tf_op jit(solution)/shard_map/ppermute | solution.py:36
  184.2 25.3 %collective-permute-start.23 = (bf16[8,16,2048]{2,1,0:T(8,128)(2,1)}, bf16[8,16,2048]{2,1,0:T(8,128)(2,1)S(1)}, u32[]{:S(2)}, u32[]{:S(2)}) collective-permute-start(bf16[8,16,2048]{2,1,0:T(8,128)(2,1)} %slice.21), channel_id=1, source_target_pairs={{0,32},{1,33},{2,34},{3,35},{4,36},{5,37},{6,38},{7,39},{8,40},{9,... | collective-permute-start | bytes 1572872 | tf_op jit(solution)/shard_map/ppermute | solution.py:36
  186.1 23.9 %collective-permute-start.24 = (bf16[8,16,2048]{2,1,0:T(8,128)(2,1)}, bf16[8,16,2048]{2,1,0:T(8,128)(2,1)}, u32[]{:S(2)}, u32[]{:S(2)}) collective-permute-start(bf16[8,16,2048]{2,1,0:T(8,128)(2,1)} %slice.22), channel_id=1, source_target_pairs={{0,96},{1,97},{2,98},{3,99},{4,100},{5,101},{6,102},{7,103},{8,104... | collective-permute-start | bytes 1572872 | tf_op jit(solution)/shard_map/ppermute | solution.py:36
  189.3 23.2 %collective-permute-start.26 = (bf16[16,16,2048]{2,1,0:T(8,128)(2,1)S(1)}, bf16[16,16,2048]{2,1,0:T(8,128)(2,1)}, u32[]{:S(2)}, u32[]{:S(2)}) collective-permute-start(bf16[16,16,2048]{2,1,0:T(8,128)(2,1)S(1)} %collective-permute-done.21.refs_1_), channel_id=1, source_target_pairs={{0,1},{1,0},{2,3},{3,2},{4,5},{5,4},{6,7},{7,6},{8,9},{9,8},{10,11... | collective-permute-start | bytes 3145736 | tf_op jit(solution)/shard_map/ppermute | solution.py:36
  189.3 23.2 %collective-permute-start.27 = (bf16[16,16,2048]{2,1,0:T(8,128)(2,1)}, bf16[16,16,2048]{2,1,0:T(8,128)(2,1)}, u32[]{:S(2)}, u32[]{:S(2)}) collective-permute-start(bf16[16,16,2048]{2,1,0:T(8,128)(2,1)} %collective-permute-done.22.refs_2_), channel_id=1, source_target_pairs={{0,1},{1,0},{2,3},{3,2},{4,5},{5,4},{6,7},{7,6},{8,9},{9,8},{10,11... | collective-permute-start | bytes 3145736 | tf_op jit(solution)/shard_map/ppermute | solution.py:36
  205.0 30.1 %all-to-all-start.1 = ((bf16[16,128,384]{2,1,0:T(8,128)(2,1)}), bf16[16,128,384]{2,1,0:T(8,128)(2,1)S(1)}, u32[]{:S(2)}, u32[]{:S(2)}) async-start(bf16[16,128,384]{2,1,0:T(8,128)(2,1)} %bitcast.28), calls=%async_computation.1 | async-start | bytes 3145728 | tf_op jit(solution)/shard_map/all_to_all | solution.py:297
  235.1 31.0 %all-to-all-start.2 = ((bf16[16,128,384]{2,1,0:T(8,128)(2,1)}), bf16[16,128,384]{2,1,0:T(8,128)(2,1)S(1)}, u32[]{:S(2)}, u32[]{:S(2)}) async-start(bf16[16,128,384]{2,1,0:T(8,128)(2,1)} %bitcast.29), calls=%async_computation.2 | async-start | bytes 3145728 | tf_op jit(solution)/shard_map/all_to_all | solution.py:297
  (25 other events, 210.1 us)

commit v4 on v3

--- a/solution.py
+++ b/solution.py
@@ -9,7 +9,7 @@
 from jax.sharding import PartitionSpec as P
 
 CAP = 2
-CHUNKS = 2
+CHUNKS = (2, 4)
 NOTE = 16
 AXES = ("z", "xl", "y", "xh", "core")
 SIZES = (4, 2, 4, 2, 2)
@@ -137,19 +137,37 @@
     )(first, *[recv] * CAP)
 
 
+FROM = (0, -1, 1, 2)
+
+
+def hop(x, by, first):
+    pairs = []
+    for device in range(128):
+        xl, y, xh, core = device // 16 % 2, device // 4 % 4, device // 2 % 2, device % 2
+        if (core == 0) == first:
+            to = device + ((y + by) % 4 - y) * 4
+        else:
+            to_x = (2 * xh + xl + by) % 4
+            to = device + (to_x % 2 - xl) * 16 + (to_x // 2 - xh) * 2
+        pairs.append((device, to))
+    return lax.ppermute(x, AXES, pairs)
+
+
+def ring(x, first):
+    return jnp.concatenate([x] + [hop(x, by, first) for by in (1, -1, 2)], axis=0)
+
+
 def lay_kernel(spots, *refs):
-    pieces, out_ref, sem = refs[:-2], refs[-2], refs[-1]
+    pieces, out_ref = refs[:-1], refs[-1]
     z, y, core = lax.axis_index("z"), lax.axis_index("y"), lax.axis_index("core")
     x = 2 * lax.axis_index("xh") + lax.axis_index("xl")
-    for piece, (side, dz, chips) in zip(pieces, spots, strict=True):
-        for i, (dx, dy) in enumerate(chips):
-            to_x = (x + dx) % 4
-            pltpu.make_async_copy(
-                piece.at[i],
-                out_ref.at[(z + dz) % 4, to_x % 2, (y + dy) % 4, to_x // 2, (core + side) % 2],
-                sem,
-            ).start()
-    pltpu.make_async_copy(out_ref, out_ref, sem).wait()
+    for piece, (side, dz, start) in zip(pieces, spots, strict=True):
+        source = (core + side) % 2
+        for i in range(piece.shape[0]):
+            late, early = FROM[(start + i) // 4], FROM[(start + i) % 4]
+            to_x = (x + 4 + late + (early - late) * source) % 4
+            to_y = (y + 4 + early + (late - early) * source) % 4
+            out_ref[(z + 4 + dz) % 4, to_x % 2, to_y, to_x // 2, source] = piece[i]
 
 
 def lay(spots, pieces):
@@ -157,10 +175,9 @@
     out = pl.pallas_call(
         functools.partial(lay_kernel, spots),
         out_shape=jax.ShapeDtypeStruct((*SIZES, rows, columns), pieces[0].dtype),
-        in_specs=[pl.BlockSpec(memory_space=pl.ANY)] * len(pieces),
+        in_specs=[pl.BlockSpec(memory_space=pltpu.VMEM)] * len(pieces),
         out_specs=pl.BlockSpec(memory_space=pltpu.VMEM),
-        scratch_shapes=[pltpu.SemaphoreType.DMA],
-        compiler_params=pltpu.CompilerParams(vmem_limit_bytes=12 * 1024 * 1024),
+        compiler_params=pltpu.CompilerParams(vmem_limit_bytes=20 * 1024 * 1024),
         cost_estimate=pl.CostEstimate(
             flops=0, bytes_accessed=512 * rows * columns, transcendentals=0
         ),
@@ -169,30 +186,6 @@
     return out.reshape(-1, columns)
 
 
-def ring(x, move):
-    return jnp.concatenate([x, move(x, 1), move(x, -1), move(x, 2)], axis=0)
-
-
-FROM = (0, -1, 1, 2)
-
-
-def y_move(x, by):
-    return permute(x, "y", lambda k: (k + by) % 4)
-
-
-def x_move(x, by):
-    pairs = []
-    for device in range(128):
-        xl, xh = device // 16 % 2, device // 2 % 2
-        to = (2 * xh + xl + by) % 4
-        pairs.append((device, device + (to % 2 - xl) * 16 + (to // 2 - xh) * 2))
-    return lax.ppermute(x, AXES, pairs)
-
-
-def plane_gather(shard, first, second):
-    return ring(ring(shard[None], first), second)
-
-
 def z_near(mine):
     return up(mine), down(mine)
 
@@ -202,11 +195,10 @@
     return up(near[0][:half]), down(near[1][half:])
 
 
-def assemble(mine, near, far, chips):
-    half = mine.shape[0] // 2
+def assemble(mine, near, far):
     pieces = [mine, *near, *far]
-    spots = [(0, chips), (-1, chips), (1, chips), (2, chips[:half]), (2, chips[half:])]
-    spots = [(side, dz, those) for side in range(2) for dz, those in spots]
+    spots = [(0, 0), (-1, 0), (1, 0), (2, 0), (2, mine.shape[0] // 2)]
+    spots = [(side, dz, start) for side in range(2) for dz, start in spots]
     return lay(spots, pieces + [other_core(p) for p in pieces])
 
 
@@ -268,33 +260,33 @@
     col_count = lax.axis_size(COL)
     blocks = tensor_blocks[0]
     aux, width = blocks.shape[1], blocks.shape[-1]
-    depth = aux // CHUNKS
     basis_total = occ_green.shape[1]
-
-    by_xy = tuple((dx, dy) for dx in FROM for dy in FROM)
-    by_yx = tuple((dx, dy) for dy in FROM for dx in FROM)
-    occ_plane = plane_gather(occ_green, y_move, x_move)
+    shard_rows = occ_green.shape[0]
+
+    picked = pick(block_list[0], blocks, col_count)
+    line = ring(jnp.concatenate([occ_green, virt_green.T], axis=0)[None], True)
+    plane = ring(line, False)
+    picked, plane = lax.optimization_barrier((picked, plane))
+    recv = lax.all_to_all(picked, COL, split_axis=0, concat_axis=0, tiled=True)
+    notes = CAP * aux * width
+    recv_first = recv[:, notes : notes + CAP, 0].astype(jnp.int32).reshape(-1) - 1
+
+    occ_plane, virt_plane = plane[:, :shard_rows], plane[:, shard_rows:]
     occ_near = z_near(occ_plane)
-    occ_near, virt_shard = lax.optimization_barrier((occ_near, virt_green.T))
     occ_far = z_far(occ_plane, occ_near)
-    virt_plane = plane_gather(virt_shard, x_move, y_move)
     occ_far, virt_plane = lax.optimization_barrier((occ_far, virt_plane))
     virt_near = z_near(virt_plane)
     virt_far = z_far(virt_plane, virt_near)
-    occ = assemble(occ_plane, occ_near, occ_far, by_xy)
-    virt_t = assemble(virt_plane, virt_near, virt_far, by_yx)
-
-    picked = pick(block_list[0], blocks, col_count)
-    recv = lax.all_to_all(picked, COL, split_axis=0, concat_axis=0, tiled=True)
-    notes = CAP * aux * width
-    recv_first = recv[:, notes : notes + CAP, 0].astype(jnp.int32).reshape(-1) - 1
-
-    dense, turned = [], []
-    for c in range(CHUNKS):
-        dense.append(place(recv_first, recv, c * depth, depth, aux, basis_total))
+    occ = assemble(occ_plane, occ_near, occ_far)
+    virt_t = assemble(virt_plane, virt_near, virt_far)
+
+    dense, turned, start = [], [], 0
+    for depth in CHUNKS:
+        dense.append(place(recv_first, recv, start, depth, aux, basis_total))
         half = jnp.dot(occ, dense[-1], preferred_element_type=jnp.float32).astype(jnp.bfloat16)
         half = half.reshape(col_count, width, -1)
         turned.append(lax.all_to_all(half, COL, split_axis=0, concat_axis=0, tiled=True))
+        start += depth
 
     virt_half = [
         lax.dot_general(

time: 290 us -> 220 us (0.76)
  waiting for transfers between devices: 139 us -> 113 us
  Pallas kernels: 32 us -> 14.5 us
  starting transfers between devices: 54.6 us -> 41.9 us
  matrix products: 34 us -> 27.1 us
  local copies, waits for them, and re-layouts: 24.8 us -> 19.6 us
    ppermute x6, waiting for transfers between devices: 81.4 us -> 12.2 us  [hop(): return lax.ppermute(x, AXES, pairs)]
    ppermute x28 -> x22, waiting for transfers between devices: 52.5 us -> 85.6 us  [permute(): return lax.ppermute(x, AXES, moved(axis, to))]
    pallas_call x2, Pallas kernels: 17.4 us -> 1.65 us  [lay(): pl.pallas_call(functools.partial(lay_kernel, spots), out_shape=jax.ShapeD...]
    ppermute x28 -> x22, starting transfers between devices: 29.2 us -> 15.9 us  [permute(): return lax.ppermute(x, AXES, moved(axis, to))]
    all_to_all x2, waiting for transfers between devices: 5.56 us -> 14.9 us  [shards(): lax.all_to_all(half, COL, split_axis=0, concat_axis=0, tiled=True)]
    dot_general x2, matrix products: 19.1 us -> 12.6 us  [shards(): jnp.dot(occ, dense[-1], preferred_element_type=jnp.float32)]
    unnamed x36 -> x33, local copies, waits for them, and re-layouts: 19.6 us -> 17.5 us
  transfers between devices with their start and end apart: 37 -> 31, of which waited for: 18 -> 14; matrix products, arithmetic and copies ran while one was open for 15% -> 11% of each run, Pallas kernels for 11% -> 4%
where the time goes in v4:
time: 220 us; the launch traced here: 219 us
  waiting for transfers between devices  113 us (51%)
  starting transfers between devices  41.9 us (19%)
  matrix products  27.1 us (12%)
  local copies, waits for them, and re-layouts  19.6 us (9%)
  Pallas kernels  14.5 us (7%)
  other arithmetic  2.65 us (1%)
    ppermute x22, waiting for transfers between devices, permute(): return lax.ppermute(x, AXES, moved(axis, to))  85.6 us
    unnamed x33, local copies, waits for them, and re-layouts  17.5 us
    ppermute x22, starting transfers between devices, permute(): return lax.ppermute(x, AXES, moved(axis, to))  15.9 us
    all_to_all x2, waiting for transfers between devices, shards(): lax.all_to_all(half, COL, split_axis=0, concat_axis=0, tiled=True)  14.9 us
    dot_general x2, matrix products, shards(): lax.dot_general(d, virt_t, (((0,), (0,)), ((), ())), preferred_element_ty...  14.4 us
    dot_general x2, matrix products, shards(): jnp.dot(occ, dense[-1], preferred_element_type=jnp.float32)  12.6 us
    ppermute x6, waiting for transfers between devices, hop(): return lax.ppermute(x, AXES, pairs)  12.2 us
    all_to_all x2, starting transfers between devices, shards(): lax.all_to_all(half, COL, split_axis=0, concat_axis=0, tiled=True)  11.3 us
  transfers between devices with their start and end apart: 31, of which 14 were waited for; matrix products, arithmetic and copies ran while one was open for 11% of the time, Pallas kernels for 4%

profile of v4, /device:TPU:2, one launch (start us, length us, event | category | flops | bytes accessed | tf_op | source)
XLA Modules:
  0.0 218.6 jit_solution(17588616144497376970)
XLA Ops:
  0.9 3.3 %collective-permute-start.2 = (bf16[1,32,2048]{2,1,0:T(8,128)(2,1)S(1)}, bf16[1,32,2048]{2,1,0:T(8,128)(2,1)S(1)}, u32[]{:S(2)}, u32[]{:S(2)}) collective-permute-start(bf16[1,32,2048]{2,1,0:T(8,128)(2,1)S(1)} %maximum_bitcast_fusion), channel_id=1, source_target_pairs={{0,8},{1,3},{2,10},{3,1},{4,12},{5,7},{6,14},{7,5},{8,0},{9,11},{1... | collective-permute-start | bytes 393224 | tf_op jit(solution)/shard_map/ppermute | solution.py:153
  17.8 12.2 %collective-permute-done.3 = bf16[4,32,2048]{2,1,0:T(8,128)(2,1)S(1)} collective-permute-done((bf16[4,32,2048]{2,1,0:T(8,128)(2,1)S(1)}, bf16[4,32,2048]{2,1,0:T(8,128)(2,1)S(1)}, u32[]{:S(2)}, u32[]{:S(2)}) %collective-permute-start.3) | collective-permute-done | bytes 524320 | tf_op jit(solution)/shard_map/ppermute | solution.py:153
  30.1 5.1 %all-to-all-start = ((bf16[16,1552,128]{2,1,0:T(8,128)(2,1)}), bf16[16,1552,128]{2,1,0:T(8,128)(2,1)}, u32[]{:S(2)}, u32[]{:S(2)}) async-start(bf16[16,1552,128]{2,1,0:T(8,128)(2,1)} %copy-done.1), calls=%async_computation | async-start | bytes 12713984 | tf_op jit(solution)/shard_map/all_to_all | solution.py:270
  35.4 4.1 %collective-permute-start.7 = (bf16[16,16,2048]{2,1,0:T(8,128)(2,1)S(1)}, bf16[16,16,2048]{2,1,0:T(8,128)(2,1)S(1)}, u32[]{:S(2)}, u32[]{:S(2)}) collective-permute-start(bf16[16,16,2048]{2,1,0:T(8,128)(2,1)S(1)} %get-tuple-element.16.refs_0_), channel_id=1, source_target_pairs={{0,96},{1,97},{2,98},{3,99},{4,100},{5,101},{6,102},{7,103},{8,104... | collective-permute-start | bytes 3145736 | tf_op jit(solution)/shard_map/ppermute | solution.py:36
  39.5 22.9 %collective-permute-done.7.refs_2_ = bf16[16,16,2048]{2,1,0:T(8,128)(2,1)S(1)} collective-permute-done((bf16[16,16,2048]{2,1,0:T(8,128)(2,1)S(1)}, bf16[16,16,2048]{2,1,0:T(8,128)(2,1)S(1)}, u32[]{:S(2)}, u32[]{:S(2)}) %collective-permute-start.7) | collective-permute-done | bytes 1048608 | tf_op jit(solution)/shard_map/ppermute | solution.py:36
  62.5 3.8 %collective-permute-start.9 = (bf16[8,16,2048]{2,1,0:T(8,128)(2,1)S(1)}, bf16[8,16,2048]{2,1,0:T(8,128)(2,1)S(1)}, u32[]{:S(2)}, u32[]{:S(2)}) collective-permute-start(bf16[8,16,2048]{2,1,0:T(8,128)(2,1)S(1)} %slice.29), channel_id=1, source_target_pairs={{0,96},{1,97},{2,98},{3,99},{4,100},{5,101},{6,102},{7,103},{8,104... | collective-permute-start | bytes 1572872 | tf_op jit(solution)/shard_map/ppermute | solution.py:36
  66.4 10.9 %collective-permute-done.9.refs_4_ = bf16[8,16,2048]{2,1,0:T(8,128)(2,1)S(1)} collective-permute-done((bf16[8,16,2048]{2,1,0:T(8,128)(2,1)S(1)}, bf16[8,16,2048]{2,1,0:T(8,128)(2,1)S(1)}, u32[]{:S(2)}, u32[]{:S(2)}) %collective-permute-start.9) | collective-permute-done | bytes 524320 | tf_op jit(solution)/shard_map/ppermute | solution.py:36
  77.2 3.5 %collective-permute-done.8.refs_3_ = bf16[8,16,2048]{2,1,0:T(8,128)(2,1)S(1)} collective-permute-done((bf16[8,16,2048]{2,1,0:T(8,128)(2,1)S(1)}, bf16[8,16,2048]{2,1,0:T(8,128)(2,1)S(1)}, u32[]{:S(2)}, u32[]{:S(2)}) %collective-permute-start.8) | collective-permute-done | bytes 524320 | tf_op jit(solution)/shard_map/ppermute | solution.py:36
  83.3 21.1 %collective-permute-done.16.refs_2_ = bf16[16,16,2048]{2,1,0:T(8,128)(2,1)S(1)} collective-permute-done((bf16[16,16,2048]{2,1,0:T(8,128)(2,1)S(1)}, bf16[16,16,2048]{2,1,0:T(8,128)(2,1)S(1)}, u32[]{:S(2)}, u32[]{:S(2)}) %collective-permute-start.16) | collective-permute-done | bytes 1048608 | tf_op jit(solution)/shard_map/ppermute | solution.py:36
  109.0 11.4 %collective-permute-done.18.refs_4_ = bf16[8,16,2048]{2,1,0:T(8,128)(2,1)S(1)} collective-permute-done((bf16[8,16,2048]{2,1,0:T(8,128)(2,1)S(1)}, bf16[8,16,2048]{2,1,0:T(8,128)(2,1)S(1)}, u32[]{:S(2)}, u32[]{:S(2)}) %collective-permute-start.18) | collective-permute-done | bytes 524320 | tf_op jit(solution)/shard_map/ppermute | solution.py:36
  122.8 3.2 %copy-done.2 = bf16[4,2,4,2,2,16,2048]{6,5,4,3,2,1,0:T(8,128)(2,1)} copy-done((bf16[4,2,4,2,2,16,2048]{6,5,4,3,2,1,0:T(8,128)(2,1)}, bf16[4,2,4,2,2,16,2048]{6,5,4,3,2,1,0:T(8,128)(2,1)S(1)}, u32[]{:S(2)}) %copy-start.2) | copy-done | bytes 8388632
  127.0 3.3 %copy-done = bf16[4,2,4,2,2,16,2048]{6,5,4,3,2,1,0:T(8,128)(2,1)} copy-done((bf16[4,2,4,2,2,16,2048]{6,5,4,3,2,1,0:T(8,128)(2,1)}, bf16[4,2,4,2,2,16,2048]{6,5,4,3,2,1,0:T(8,128)(2,1)S(1)}, u32[]{:S(2)}) %copy-start) | copy-done | bytes 8388632
  131.5 3.4 %place.2 = bf16[2048,256]{1,0:T(8,128)(2,1)S(1)} custom-call(s32[32]{0:T(128)S(1)} %sub.7.first_ref, bf16[16,1552,128]{2,1,0:T(8,128)(2,1)} %all-to-all-done.refs_0_.refs_1_, bf16[16,1552,128]{2,1,0:T(8,128)(2,1)} %all-to-all-done.refs_0_.refs_1_), custom_call_target="tpu_custom_call" | custom-call | flops 1048576 | bytes 4194304 | tf_op jit(solution)/shard_map/place/pallas_call | solution.py:124
  135.5 3.5 %convolution_convert_fusion.3 = bf16[2048,256]{1,0:T(8,128)(2,1)} fusion(bf16[2048,2048]{1,0:T(8,128)(2,1)S(1)} %bitcast.26, bf16[2048,256]{1,0:T(8,128)(2,1)S(1)} %place.2), kind=kOutput, calls=%fused_computation.3 | convolution fusion | flops 2148007936 | bytes 10485760 | tf_op jit(solution)/shard_map/dot_general | solution.py:286
  139.1 6.5 %all-to-all-start.1 = ((bf16[16,128,256]{2,1,0:T(8,128)(2,1)}), bf16[16,128,256]{2,1,0:T(8,128)(2,1)S(1)}, u32[]{:S(2)}, u32[]{:S(2)}) async-start(bf16[16,128,256]{2,1,0:T(8,128)(2,1)} %bitcast.5), calls=%async_computation.1 | async-start | bytes 2097152 | tf_op jit(solution)/shard_map/all_to_all | solution.py:288
  145.6 5.2 %place.3 = bf16[2048,512]{1,0:T(8,128)(2,1)S(1)} custom-call(s32[32]{0:T(128)S(1)} %sub.7.first_ref, bf16[16,1552,128]{2,1,0:T(8,128)(2,1)} %all-to-all-done.refs_0_.refs_1_, bf16[16,1552,128]{2,1,0:T(8,128)(2,1)} %all-to-all-done.refs_0_.refs_1_), custom_call_target="tpu_custom_call" | custom-call | flops 2097152 | bytes 8388608 | tf_op jit(solution)/shard_map/place/pallas_call | solution.py:124
  152.1 9.1 %convolution_convert_fusion = bf16[2048,512]{1,0:T(8,128)(2,1)} fusion(bf16[2048,2048]{1,0:T(8,128)(2,1)} %bitcast.25, bf16[2048,512]{1,0:T(8,128)(2,1)S(1)} %place.3), kind=kOutput, calls=%fused_computation | convolution fusion | flops 4296015872 | bytes 12582912 | tf_op jit(solution)/shard_map/dot_general | solution.py:286
  164.7 4.8 %all-to-all-start.2 = ((bf16[16,128,512]{2,1,0:T(8,128)(2,1)}), bf16[16,128,512]{2,1,0:T(8,128)(2,1)S(1)}, u32[]{:S(2)}, u32[]{:S(2)}) async-start(bf16[16,128,512]{2,1,0:T(8,128)(2,1)} %bitcast.28), calls=%async_computation.2 | async-start | bytes 4194304 | tf_op jit(solution)/shard_map/all_to_all | solution.py:288
  169.5 6.2 %convolution_convert_fusion.2.refs_0_ = bf16[256,2048]{1,0:T(8,128)(2,1)S(1)} fusion(bf16[2048,256]{1,0:T(8,128)(2,1)} %copy-done.6, bf16[2048,2048]{1,0:T(8,128)(2,1)} %bitcast.23), kind=kOutput, calls=%fused_computation.2 | convolution fusion | flops 2148007936 | bytes 10485760 | tf_op jit(solution)/shard_map/dot_general | solution.py:292
  175.7 8.2 %convolution_convert_fusion.1.refs_1_ = bf16[512,2048]{1,0:T(8,128)(2,1)S(1)} fusion(bf16[2048,512]{1,0:T(8,128)(2,1)S(1)} %copy-done.11, bf16[2048,2048]{1,0:T(8,128)(2,1)} %bitcast.24), kind=kOutput, calls=%fused_computation.1 | convolution fusion | flops 4296015872 | bytes 12582912 | tf_op jit(solution)/shard_map/dot_general | solution.py:292
  186.6 12.4 %all-to-all-done.2.x_ref = bf16[16,128,512]{2,1,0:T(8,128)(2,1)S(1)} async-done(((bf16[16,128,512]{2,1,0:T(8,128)(2,1)}), bf16[16,128,512]{2,1,0:T(8,128)(2,1)S(1)}, u32[]{:S(2)}, u32[]{:S(2)}) %all-to-all-start.2) | async-done | bytes 2097184 | tf_op jit(solution)/shard_map/all_to_all | solution.py:288
  204.6 4.6 %collective-permute-done.25 = f32[6,6]{0,1:T(8,128)S(1)} collective-permute-done((f32[6,6]{0,1:T(8,128)S(1)}, f32[6,6]{0,1:T(8,128)S(1)}, u32[]{:S(2)}, u32[]{:S(2)}) %collective-permute-start.25) | collective-permute-done | bytes 176 | tf_op jit(solution)/shard_map/ppermute | solution.py:36
  209.9 3.0 %collective-permute-done.26 = f32[6,6]{0,1:T(8,128)S(1)} collective-permute-done((f32[6,6]{0,1:T(8,128)S(1)}, f32[6,6]{0,1:T(8,128)S(1)}, u32[]{:S(2)}, u32[]{:S(2)}) %collective-permute-start.26) | collective-permute-done | bytes 176 | tf_op jit(solution)/shard_map/ppermute | solution.py:36
  214.0 4.0 %collective-permute-done.27 = f32[6,6]{0,1:T(8,128)S(1)} collective-permute-done((f32[6,6]{0,1:T(8,128)S(1)}, f32[6,6]{0,1:T(8,128)S(1)}, u32[]{:S(2)}, u32[]{:S(2)}) %collective-permute-start.27) | collective-permute-done | bytes 176 | tf_op jit(solution)/shard_map/ppermute | solution.py:36
  (104 shorter events, 42.5 us)
Async XLA Ops:
  0.9 12.5 %collective-permute-start.2 = (bf16[1,32,2048]{2,1,0:T(8,128)(2,1)S(1)}, bf16[1,32,2048]{2,1,0:T(8,128)(2,1)S(1)}, u32[]{:S(2)}, u32[]{:S(2)}) collective-permute-start(bf16[1,32,2048]{2,1,0:T(8,128)(2,1)S(1)} %maximum_bitcast_fusion), channel_id=1, source_target_pairs={{0,8},{1,3},{2,10},{3,1},{4,12},{5,7},{6,14},{7,5},{8,0},{9,11},{1... | collective-permute-start | bytes 393224 | tf_op jit(solution)/shard_map/ppermute | solution.py:153
  4.2 9.2 %collective-permute-start.1 = (bf16[1,32,2048]{2,1,0:T(8,128)(2,1)S(1)}, bf16[1,32,2048]{2,1,0:T(8,128)(2,1)S(1)}, u32[]{:S(2)}, u32[]{:S(2)}) collective-permute-start(bf16[1,32,2048]{2,1,0:T(8,128)(2,1)S(1)} %maximum_bitcast_fusion), channel_id=1, source_target_pairs={{0,12},{1,19},{2,14},{3,17},{4,0},{5,23},{6,2},{7,21},{8,4},{9,27}... | collective-permute-start | bytes 393224 | tf_op jit(solution)/shard_map/ppermute | solution.py:153
  5.2 8.2 %collective-permute-start = (bf16[1,32,2048]{2,1,0:T(8,128)(2,1)S(1)}, bf16[1,32,2048]{2,1,0:T(8,128)(2,1)S(1)}, u32[]{:S(2)}, u32[]{:S(2)}) collective-permute-start(bf16[1,32,2048]{2,1,0:T(8,128)(2,1)S(1)} %maximum_bitcast_fusion), channel_id=1, source_target_pairs={{0,4},{1,17},{2,6},{3,19},{4,8},{5,21},{6,10},{7,23},{8,12},{9,25}... | collective-permute-start | bytes 393224 | tf_op jit(solution)/shard_map/ppermute | solution.py:153
  13.5 16.6 %collective-permute-start.5 = (bf16[4,32,2048]{2,1,0:T(8,128)(2,1)S(1)}, bf16[4,32,2048]{2,1,0:T(8,128)(2,1)S(1)}, u32[]{:S(2)}, u32[]{:S(2)}) collective-permute-start(bf16[4,32,2048]{2,1,0:T(8,128)(2,1)S(1)} %pad_maximum_fusion), channel_id=1, source_target_pairs={{0,2},{1,9},{2,0},{3,11},{4,6},{5,13},{6,4},{7,15},{8,10},{9,1},{1... | collective-permute-start | bytes 1572872 | tf_op jit(solution)/shard_map/ppermute | solution.py:153
  15.7 14.3 %collective-permute-start.4 = (bf16[4,32,2048]{2,1,0:T(8,128)(2,1)S(1)}, bf16[4,32,2048]{2,1,0:T(8,128)(2,1)S(1)}, u32[]{:S(2)}, u32[]{:S(2)}) collective-permute-start(bf16[4,32,2048]{2,1,0:T(8,128)(2,1)S(1)} %pad_maximum_fusion), channel_id=1, source_target_pairs={{0,18},{1,13},{2,16},{3,15},{4,22},{5,1},{6,20},{7,3},{8,26},{9,5}... | collective-permute-start | bytes 1572872 | tf_op jit(solution)/shard_map/ppermute | solution.py:153
  17.1 12.8 %collective-permute-start.3 = (bf16[4,32,2048]{2,1,0:T(8,128)(2,1)S(1)}, bf16[4,32,2048]{2,1,0:T(8,128)(2,1)S(1)}, u32[]{:S(2)}, u32[]{:S(2)}) collective-permute-start(bf16[4,32,2048]{2,1,0:T(8,128)(2,1)S(1)} %pad_maximum_fusion), channel_id=1, source_target_pairs={{0,16},{1,5},{2,18},{3,7},{4,20},{5,9},{6,22},{7,11},{8,24},{9,13}... | collective-permute-start | bytes 1572872 | tf_op jit(solution)/shard_map/ppermute | solution.py:153
  30.1 100.2 %all-to-all-start = ((bf16[16,1552,128]{2,1,0:T(8,128)(2,1)}), bf16[16,1552,128]{2,1,0:T(8,128)(2,1)}, u32[]{:S(2)}, u32[]{:S(2)}) async-start(bf16[16,1552,128]{2,1,0:T(8,128)(2,1)} %copy-done.1), calls=%async_computation | async-start | bytes 12713984 | tf_op jit(solution)/shard_map/all_to_all | solution.py:270
  35.4 27.0 %collective-permute-start.7 = (bf16[16,16,2048]{2,1,0:T(8,128)(2,1)S(1)}, bf16[16,16,2048]{2,1,0:T(8,128)(2,1)S(1)}, u32[]{:S(2)}, u32[]{:S(2)}) collective-permute-start(bf16[16,16,2048]{2,1,0:T(8,128)(2,1)S(1)} %get-tuple-element.16.refs_0_), channel_id=1, source_target_pairs={{0,96},{1,97},{2,98},{3,99},{4,100},{5,101},{6,102},{7,103},{8,104... | collective-permute-start | bytes 3145736 | tf_op jit(solution)/shard_map/ppermute | solution.py:36
  39.5 26.7 %collective-permute-start.6 = (bf16[16,16,2048]{2,1,0:T(8,128)(2,1)S(1)}, bf16[16,16,2048]{2,1,0:T(8,128)(2,1)S(1)}, u32[]{:S(2)}, u32[]{:S(2)}) collective-permute-start(bf16[16,16,2048]{2,1,0:T(8,128)(2,1)S(1)} %get-tuple-element.16.refs_0_), channel_id=1, source_target_pairs={{0,32},{1,33},{2,34},{3,35},{4,36},{5,37},{6,38},{7,39},{8,40},{9,... | collective-permute-start | bytes 3145736 | tf_op jit(solution)/shard_map/ppermute | solution.py:36
  62.5 14.8 %collective-permute-start.9 = (bf16[8,16,2048]{2,1,0:T(8,128)(2,1)S(1)}, bf16[8,16,2048]{2,1,0:T(8,128)(2,1)S(1)}, u32[]{:S(2)}, u32[]{:S(2)}) collective-permute-start(bf16[8,16,2048]{2,1,0:T(8,128)(2,1)S(1)} %slice.29), channel_id=1, source_target_pairs={{0,96},{1,97},{2,98},{3,99},{4,100},{5,101},{6,102},{7,103},{8,104... | collective-permute-start | bytes 1572872 | tf_op jit(solution)/shard_map/ppermute | solution.py:36
  66.3 14.5 %collective-permute-start.8 = (bf16[8,16,2048]{2,1,0:T(8,128)(2,1)S(1)}, bf16[8,16,2048]{2,1,0:T(8,128)(2,1)S(1)}, u32[]{:S(2)}, u32[]{:S(2)}) collective-permute-start(bf16[8,16,2048]{2,1,0:T(8,128)(2,1)S(1)} %slice.28), channel_id=1, source_target_pairs={{0,32},{1,33},{2,34},{3,35},{4,36},{5,37},{6,38},{7,39},{8,40},{9,... | collective-permute-start | bytes 1572872 | tf_op jit(solution)/shard_map/ppermute | solution.py:36
  80.8 23.6 %collective-permute-start.16 = (bf16[16,16,2048]{2,1,0:T(8,128)(2,1)S(1)}, bf16[16,16,2048]{2,1,0:T(8,128)(2,1)S(1)}, u32[]{:S(2)}, u32[]{:S(2)}) collective-permute-start(bf16[16,16,2048]{2,1,0:T(8,128)(2,1)S(1)} %get-tuple-element.14.refs_0_), channel_id=1, source_target_pairs={{0,96},{1,97},{2,98},{3,99},{4,100},{5,101},{6,102},{7,103},{8,104... | collective-permute-start | bytes 3145736 | tf_op jit(solution)/shard_map/ppermute | solution.py:36
  80.9 24.8 %collective-permute-start.15 = (bf16[16,16,2048]{2,1,0:T(8,128)(2,1)S(1)}, bf16[16,16,2048]{2,1,0:T(8,128)(2,1)S(1)}, u32[]{:S(2)}, u32[]{:S(2)}) collective-permute-start(bf16[16,16,2048]{2,1,0:T(8,128)(2,1)S(1)} %get-tuple-element.14.refs_0_), channel_id=1, source_target_pairs={{0,32},{1,33},{2,34},{3,35},{4,36},{5,37},{6,38},{7,39},{8,40},{9,... | collective-permute-start | bytes 3145736 | tf_op jit(solution)/shard_map/ppermute | solution.py:36
  82.8 23.1 %collective-permute-start.10 = (bf16[16,16,2048]{2,1,0:T(8,128)(2,1)S(1)}, bf16[16,16,2048]{2,1,0:T(8,128)(2,1)S(1)}, u32[]{:S(2)}, u32[]{:S(2)}) collective-permute-start(bf16[16,16,2048]{2,1,0:T(8,128)(2,1)S(1)} %get-tuple-element.16.refs_0_), channel_id=1, source_target_pairs={{0,1},{1,0},{2,3},{3,2},{4,5},{5,4},{6,7},{7,6},{8,9},{9,8},{10,11... | collective-permute-start | bytes 3145736 | tf_op jit(solution)/shard_map/ppermute | solution.py:36
  82.8 23.7 %collective-permute-start.12 = (bf16[16,16,2048]{2,1,0:T(8,128)(2,1)S(1)}, bf16[16,16,2048]{2,1,0:T(8,128)(2,1)S(1)}, u32[]{:S(2)}, u32[]{:S(2)}) collective-permute-start(bf16[16,16,2048]{2,1,0:T(8,128)(2,1)S(1)} %collective-permute-done.7.refs_2_), channel_id=1, source_target_pairs={{0,1},{1,0},{2,3},{3,2},{4,5},{5,4},{6,7},{7,6},{8,9},{9,8},{10,11... | collective-permute-start | bytes 3145736 | tf_op jit(solution)/shard_map/ppermute | solution.py:36
  83.3 25.2 %collective-permute-start.11 = (bf16[16,16,2048]{2,1,0:T(8,128)(2,1)S(1)}, bf16[16,16,2048]{2,1,0:T(8,128)(2,1)S(1)}, u32[]{:S(2)}, u32[]{:S(2)}) collective-permute-start(bf16[16,16,2048]{2,1,0:T(8,128)(2,1)S(1)} %collective-permute-done.6.refs_1_), channel_id=1, source_target_pairs={{0,1},{1,0},{2,3},{3,2},{4,5},{5,4},{6,7},{7,6},{8,9},{9,8},{10,11... | collective-permute-start | bytes 3145736 | tf_op jit(solution)/shard_map/ppermute | solution.py:36
  105.9 20.2 %collective-permute-start.19 = (bf16[16,16,2048]{2,1,0:T(8,128)(2,1)S(1)}, bf16[16,16,2048]{2,1,0:T(8,128)(2,1)S(1)}, u32[]{:S(2)}, u32[]{:S(2)}) collective-permute-start(bf16[16,16,2048]{2,1,0:T(8,128)(2,1)S(1)} %get-tuple-element.14.refs_0_), channel_id=1, source_target_pairs={{0,1},{1,0},{2,3},{3,2},{4,5},{5,4},{6,7},{7,6},{8,9},{9,8},{10,11... | collective-permute-start | bytes 3145736 | tf_op jit(solution)/shard_map/ppermute | solution.py:36
  106.5 13.9 %collective-permute-start.18 = (bf16[8,16,2048]{2,1,0:T(8,128)(2,1)S(1)}, bf16[8,16,2048]{2,1,0:T(8,128)(2,1)S(1)}, u32[]{:S(2)}, u32[]{:S(2)}) collective-permute-start(bf16[8,16,2048]{2,1,0:T(8,128)(2,1)S(1)} %slice.32), channel_id=1, source_target_pairs={{0,96},{1,97},{2,98},{3,99},{4,100},{5,101},{6,102},{7,103},{8,104... | collective-permute-start | bytes 1572872 | tf_op jit(solution)/shard_map/ppermute | solution.py:36
  106.9 15.2 %collective-permute-start.17 = (bf16[8,16,2048]{2,1,0:T(8,128)(2,1)S(1)}, bf16[8,16,2048]{2,1,0:T(8,128)(2,1)S(1)}, u32[]{:S(2)}, u32[]{:S(2)}) collective-permute-start(bf16[8,16,2048]{2,1,0:T(8,128)(2,1)S(1)} %slice.31), channel_id=1, source_target_pairs={{0,32},{1,33},{2,34},{3,35},{4,36},{5,37},{6,38},{7,39},{8,40},{9,... | collective-permute-start | bytes 1572872 | tf_op jit(solution)/shard_map/ppermute | solution.py:36
  108.5 17.5 %collective-permute-start.21 = (bf16[16,16,2048]{2,1,0:T(8,128)(2,1)S(1)}, bf16[16,16,2048]{2,1,0:T(8,128)(2,1)S(1)}, u32[]{:S(2)}, u32[]{:S(2)}) collective-permute-start(bf16[16,16,2048]{2,1,0:T(8,128)(2,1)S(1)} %collective-permute-done.16.refs_2_), channel_id=1, source_target_pairs={{0,1},{1,0},{2,3},{3,2},{4,5},{5,4},{6,7},{7,6},{8,9},{9,8},{10,11... | collective-permute-start | bytes 3145736 | tf_op jit(solution)/shard_map/ppermute | solution.py:36
  108.5 17.6 %collective-permute-start.20 = (bf16[16,16,2048]{2,1,0:T(8,128)(2,1)S(1)}, bf16[16,16,2048]{2,1,0:T(8,128)(2,1)S(1)}, u32[]{:S(2)}, u32[]{:S(2)}) collective-permute-start(bf16[16,16,2048]{2,1,0:T(8,128)(2,1)S(1)} %collective-permute-done.15.refs_1_), channel_id=1, source_target_pairs={{0,1},{1,0},{2,3},{3,2},{4,5},{5,4},{6,7},{7,6},{8,9},{9,8},{10,11... | collective-permute-start | bytes 3145736 | tf_op jit(solution)/shard_map/ppermute | solution.py:36
  120.4 5.7 %collective-permute-start.23 = (bf16[8,16,2048]{2,1,0:T(8,128)(2,1)S(1)}, bf16[8,16,2048]{2,1,0:T(8,128)(2,1)S(1)}, u32[]{:S(2)}, u32[]{:S(2)}) collective-permute-start(bf16[8,16,2048]{2,1,0:T(8,128)(2,1)S(1)} %collective-permute-done.18.refs_4_), channel_id=1, source_target_pairs={{0,1},{1,0},{2,3},{3,2},{4,5},{5,4},{6,7},{7,6},{8,9},{9,8},{10,11... | collective-permute-start | bytes 1572872 | tf_op jit(solution)/shard_map/ppermute | solution.py:36
  139.1 24.6 %all-to-all-start.1 = ((bf16[16,128,256]{2,1,0:T(8,128)(2,1)}), bf16[16,128,256]{2,1,0:T(8,128)(2,1)S(1)}, u32[]{:S(2)}, u32[]{:S(2)}) async-start(bf16[16,128,256]{2,1,0:T(8,128)(2,1)} %bitcast.5), calls=%async_computation.1 | async-start | bytes 2097152 | tf_op jit(solution)/shard_map/all_to_all | solution.py:288
  164.7 34.4 %all-to-all-start.2 = ((bf16[16,128,512]{2,1,0:T(8,128)(2,1)}), bf16[16,128,512]{2,1,0:T(8,128)(2,1)S(1)}, u32[]{:S(2)}, u32[]{:S(2)}) async-start(bf16[16,128,512]{2,1,0:T(8,128)(2,1)} %bitcast.28), calls=%async_computation.2 | async-start | bytes 4194304 | tf_op jit(solution)/shard_map/all_to_all | solution.py:288
  (21 other events, 71.9 us)

commit v5 on v4

--- a/solution.py
+++ b/solution.py
@@ -9,7 +9,7 @@
 from jax.sharding import PartitionSpec as P
 
 CAP = 2
-CHUNKS = (2, 4)
+CHUNKS = (3, 3)
 NOTE = 16
 AXES = ("z", "xl", "y", "xh", "core")
 SIZES = (4, 2, 4, 2, 2)
@@ -36,8 +36,8 @@
     return lax.ppermute(x, AXES, moved(axis, to))
 
 
-def up(x):
-    return permute(x, "z", lambda k: (k + 1) % 4)
+def up(x, by=1):
+    return permute(x, "z", lambda k: (k + by) % 4)
 
 
 def down(x):
@@ -154,7 +154,7 @@
 
 
 def ring(x, first):
-    return jnp.concatenate([x] + [hop(x, by, first) for by in (1, -1, 2)], axis=0)
+    return [x] + [hop(x, by, first) for by in (1, -1, 2)]
 
 
 def lay_kernel(spots, *refs):
@@ -186,20 +186,23 @@
     return out.reshape(-1, columns)
 
 
-def z_near(mine):
-    return up(mine), down(mine)
-
-
-def z_far(mine, near):
+FORWARDED = ((0, 0), (-1, 0), (1, 0), (2, 0), (2, 8))
+DIRECT = ((0, 0), (-1, 0), (1, 0), (2, 0))
+
+
+def z_forwarded(mine):
     half = mine.shape[0] // 2
-    return up(near[0][:half]), down(near[1][half:])
-
-
-def assemble(mine, near, far):
-    pieces = [mine, *near, *far]
-    spots = [(0, 0), (-1, 0), (1, 0), (2, 0), (2, mine.shape[0] // 2)]
-    spots = [(side, dz, start) for side in range(2) for dz, start in spots]
-    return lay(spots, pieces + [other_core(p) for p in pieces])
+    below, above = up(mine), down(mine)
+    return [mine, below, above, up(below[:half]), down(above[half:])]
+
+
+def z_direct(mine):
+    return [mine, up(mine), down(mine), up(mine, 2)]
+
+
+def assemble(spots, pieces):
+    spots = [(side, *spot) for side in range(2) for spot in spots]
+    return lay(spots, pieces + [other_core(piece) for piece in pieces])
 
 
 def pair_kernel(x_ref, *refs):
@@ -265,29 +268,30 @@
 
     picked = pick(block_list[0], blocks, col_count)
     line = ring(jnp.concatenate([occ_green, virt_green.T], axis=0)[None], True)
-    plane = ring(line, False)
+    plane = ring(jnp.concatenate(line, axis=0), False)
     picked, plane = lax.optimization_barrier((picked, plane))
+    plane = jnp.concatenate(plane, axis=0)
     recv = lax.all_to_all(picked, COL, split_axis=0, concat_axis=0, tiled=True)
     notes = CAP * aux * width
     recv_first = recv[:, notes : notes + CAP, 0].astype(jnp.int32).reshape(-1) - 1
 
     occ_plane, virt_plane = plane[:, :shard_rows], plane[:, shard_rows:]
-    occ_near = z_near(occ_plane)
-    occ_far = z_far(occ_plane, occ_near)
-    occ_far, virt_plane = lax.optimization_barrier((occ_far, virt_plane))
-    virt_near = z_near(virt_plane)
-    virt_far = z_far(virt_plane, virt_near)
-    occ = assemble(occ_plane, occ_near, occ_far)
-    virt_t = assemble(virt_plane, virt_near, virt_far)
+    occ_pieces = z_forwarded(occ_plane)
+    occ_pieces, virt_plane = lax.optimization_barrier((occ_pieces, virt_plane))
+    virt_pieces = z_direct(virt_plane)
+    occ = assemble(FORWARDED, occ_pieces)
 
     dense, turned, start = [], [], 0
     for depth in CHUNKS:
         dense.append(place(recv_first, recv, start, depth, aux, basis_total))
         half = jnp.dot(occ, dense[-1], preferred_element_type=jnp.float32).astype(jnp.bfloat16)
+        if start == 0:
+            _, virt_pieces = lax.optimization_barrier((half, virt_pieces))
         half = half.reshape(col_count, width, -1)
         turned.append(lax.all_to_all(half, COL, split_axis=0, concat_axis=0, tiled=True))
         start += depth
 
+    virt_t = assemble(DIRECT, virt_pieces)
     virt_half = [
         lax.dot_general(
             d, virt_t, (((0,), (0,)), ((), ())), preferred_element_type=jnp.float32

time: 220 us -> 207 us (0.941)
  waiting for transfers between devices: 113 us -> 103 us
  Pallas kernels: 14.5 us -> 17.4 us
  starting transfers between devices: 41.9 us -> 39.2 us
    ppermute x22 -> x20, waiting for transfers between devices: 85.6 us -> 66.7 us  [permute(): return lax.ppermute(x, AXES, moved(axis, to))]
    all_to_all x1, waiting for transfers between devices: 0.01 us -> 16.3 us  [shards(): recv = lax.all_to_all(picked, COL, split_axis=0, concat_axis=0, tiled=True)]
    all_to_all x2, waiting for transfers between devices: 14.9 us -> 9.52 us  [shards(): lax.all_to_all(half, COL, split_axis=0, concat_axis=0, tiled=True)]
    dot_general x2, matrix products: 14.4 us -> 11 us  [shards(): lax.dot_general(d, virt_t, (((0,), (0,)), ((), ())), preferred_element_ty...]
    dot_general x2, matrix products: 12.6 us -> 15.2 us  [shards(): jnp.dot(occ, dense[-1], preferred_element_type=jnp.float32)]
    unnamed x33 -> x29, local copies, waits for them, and re-layouts: 17.5 us -> 15.6 us
    ppermute x22 -> x20, starting transfers between devices: 15.9 us -> 14.3 us  [permute(): return lax.ppermute(x, AXES, moved(axis, to))]
  transfers between devices with their start and end apart: 31 -> 29, of which waited for: 14 -> 18; matrix products, arithmetic and copies ran while one was open for 11% -> 14% of each run, Pallas kernels for 4% -> 8%
where the time goes in v5:
time: 207 us; the launch traced here: 206 us
  waiting for transfers between devices  103 us (50%)
  starting transfers between devices  39.2 us (19%)
  matrix products  26.2 us (13%)
  local copies, waits for them, and re-layouts  17.5 us (8%)
  Pallas kernels  17.4 us (8%)
  other arithmetic  2.64 us (1%)
    ppermute x20, waiting for transfers between devices, permute(): return lax.ppermute(x, AXES, moved(axis, to))  66.7 us
    all_to_all x1, waiting for transfers between devices, shards(): recv = lax.all_to_all(picked, COL, split_axis=0, concat_axis=0, tiled=True)  16.3 us
    unnamed x29, local copies, waits for them, and re-layouts  15.6 us
    dot_general x2, matrix products, shards(): jnp.dot(occ, dense[-1], preferred_element_type=jnp.float32)  15.2 us
    ppermute x20, starting transfers between devices, permute(): return lax.ppermute(x, AXES, moved(axis, to))  14.3 us
    dot_general x2, matrix products, shards(): lax.dot_general(d, virt_t, (((0,), (0,)), ((), ())), preferred_element_ty...  11 us
    all_to_all x2, starting transfers between devices, shards(): lax.all_to_all(half, COL, split_axis=0, concat_axis=0, tiled=True)  10.7 us
    ppermute x6, waiting for transfers between devices, hop(): return lax.ppermute(x, AXES, pairs)  10.3 us
  transfers between devices with their start and end apart: 29, of which 18 were waited for; matrix products, arithmetic and copies ran while one was open for 14% of the time, Pallas kernels for 8%

profile of v5, /device:TPU:2, one launch (start us, length us, event | category | flops | bytes accessed | tf_op | source)
XLA Modules:
  0.0 206.2 jit_solution(14702264997217614837)
XLA Ops:
  0.9 3.3 %collective-permute-start.2 = (bf16[1,32,2048]{2,1,0:T(8,128)(2,1)S(1)}, bf16[1,32,2048]{2,1,0:T(8,128)(2,1)S(1)}, u32[]{:S(2)}, u32[]{:S(2)}) collective-permute-start(bf16[1,32,2048]{2,1,0:T(8,128)(2,1)S(1)} %maximum_bitcast_fusion), channel_id=1, source_target_pairs={{0,8},{1,3},{2,10},{3,1},{4,12},{5,7},{6,14},{7,5},{8,0},{9,11},{1... | collective-permute-start | bytes 393224 | tf_op jit(solution)/shard_map/ppermute | solution.py:153
  22.8 5.1 %collective-permute-done.4 = bf16[4,32,2048]{2,1,0:T(8,128)(2,1)S(1)} collective-permute-done((bf16[4,32,2048]{2,1,0:T(8,128)(2,1)S(1)}, bf16[4,32,2048]{2,1,0:T(8,128)(2,1)S(1)}, u32[]{:S(2)}, u32[]{:S(2)}) %collective-permute-start.4) | collective-permute-done | bytes 524320 | tf_op jit(solution)/shard_map/ppermute | solution.py:153
  27.9 4.7 %all-to-all-start = ((bf16[16,1552,128]{2,1,0:T(8,128)(2,1)}), bf16[16,1552,128]{2,1,0:T(8,128)(2,1)}, u32[]{:S(2)}, u32[]{:S(2)}) async-start(bf16[16,1552,128]{2,1,0:T(8,128)(2,1)} %copy-done), calls=%async_computation | async-start | bytes 12713984 | tf_op jit(solution)/shard_map/all_to_all | solution.py:274
  32.9 4.1 %collective-permute-start.7 = (bf16[16,16,2048]{2,1,0:T(8,128)(2,1)S(1)}, bf16[16,16,2048]{2,1,0:T(8,128)(2,1)S(1)}, u32[]{:S(2)}, u32[]{:S(2)}) collective-permute-start(bf16[16,16,2048]{2,1,0:T(8,128)(2,1)S(1)} %get-tuple-element.24.refs_0_), channel_id=1, source_target_pairs={{0,96},{1,97},{2,98},{3,99},{4,100},{5,101},{6,102},{7,103},{8,104... | collective-permute-start | bytes 3145736 | tf_op jit(solution)/shard_map/ppermute | solution.py:36
  37.1 22.8 %collective-permute-done.7.refs_2_ = bf16[16,16,2048]{2,1,0:T(8,128)(2,1)S(1)} collective-permute-done((bf16[16,16,2048]{2,1,0:T(8,128)(2,1)S(1)}, bf16[16,16,2048]{2,1,0:T(8,128)(2,1)S(1)}, u32[]{:S(2)}, u32[]{:S(2)}) %collective-permute-start.7) | collective-permute-done | bytes 1048608 | tf_op jit(solution)/shard_map/ppermute | solution.py:36
  59.9 3.8 %collective-permute-start.9 = (bf16[8,16,2048]{2,1,0:T(8,128)(2,1)S(1)}, bf16[8,16,2048]{2,1,0:T(8,128)(2,1)S(1)}, u32[]{:S(2)}, u32[]{:S(2)}) collective-permute-start(bf16[8,16,2048]{2,1,0:T(8,128)(2,1)S(1)} %slice.22), channel_id=1, source_target_pairs={{0,96},{1,97},{2,98},{3,99},{4,100},{5,101},{6,102},{7,103},{8,104... | collective-permute-start | bytes 1572872 | tf_op jit(solution)/shard_map/ppermute | solution.py:36
  63.8 10.7 %collective-permute-done.9.refs_4_ = bf16[8,16,2048]{2,1,0:T(8,128)(2,1)S(1)} collective-permute-done((bf16[8,16,2048]{2,1,0:T(8,128)(2,1)S(1)}, bf16[8,16,2048]{2,1,0:T(8,128)(2,1)S(1)}, u32[]{:S(2)}, u32[]{:S(2)}) %collective-permute-start.9) | collective-permute-done | bytes 524320 | tf_op jit(solution)/shard_map/ppermute | solution.py:36
  74.5 3.5 %collective-permute-done.8.refs_3_ = bf16[8,16,2048]{2,1,0:T(8,128)(2,1)S(1)} collective-permute-done((bf16[8,16,2048]{2,1,0:T(8,128)(2,1)S(1)}, bf16[8,16,2048]{2,1,0:T(8,128)(2,1)S(1)}, u32[]{:S(2)}, u32[]{:S(2)}) %collective-permute-start.8) | collective-permute-done | bytes 524320 | tf_op jit(solution)/shard_map/ppermute | solution.py:36
  79.1 5.4 %collective-permute-done.13.refs_8_ = bf16[8,16,2048]{2,1,0:T(8,128)(2,1)S(1)} collective-permute-done((bf16[8,16,2048]{2,1,0:T(8,128)(2,1)S(1)}, bf16[8,16,2048]{2,1,0:T(8,128)(2,1)S(1)}, u32[]{:S(2)}, u32[]{:S(2)}) %collective-permute-start.13) | collective-permute-done | bytes 524320 | tf_op jit(solution)/shard_map/ppermute | solution.py:36
  88.0 3.3 %copy-done.1 = bf16[4,2,4,2,2,16,2048]{6,5,4,3,2,1,0:T(8,128)(2,1)} copy-done((bf16[4,2,4,2,2,16,2048]{6,5,4,3,2,1,0:T(8,128)(2,1)}, bf16[4,2,4,2,2,16,2048]{6,5,4,3,2,1,0:T(8,128)(2,1)S(1)}, u32[]{:S(2)}) %copy-start.1) | copy-done | bytes 8388632
  91.3 16.3 %all-to-all-done.refs_0_.refs_1_ = bf16[16,1552,128]{2,1,0:T(8,128)(2,1)} async-done(((bf16[16,1552,128]{2,1,0:T(8,128)(2,1)}), bf16[16,1552,128]{2,1,0:T(8,128)(2,1)}, u32[]{:S(2)}, u32[]{:S(2)}) %all-to-all-start) | async-done | bytes 6357024 | tf_op jit(solution)/shard_map/all_to_all | solution.py:274
  108.8 4.9 %place.2 = bf16[2048,384]{1,0:T(8,128)(2,1)S(1)} custom-call(s32[32]{0:T(128)S(1)} %sub.7.first_ref, bf16[16,1552,128]{2,1,0:T(8,128)(2,1)} %all-to-all-done.refs_0_.refs_1_, bf16[16,1552,128]{2,1,0:T(8,128)(2,1)} %all-to-all-done.refs_0_.refs_1_), custom_call_target="tpu_custom_call" | custom-call | flops 1572864 | bytes 6291456 | tf_op jit(solution)/shard_map/place/pallas_call | solution.py:124
  113.8 5.6 %convolution_convert_fusion.3 = bf16[2048,384]{1,0:T(8,128)(2,1)} fusion(bf16[2048,2048]{1,0:T(8,128)(2,1)S(1)} %bitcast.22, bf16[2048,384]{1,0:T(8,128)(2,1)S(1)} %place.2), kind=kOutput, calls=%fused_computation.3 | convolution fusion | flops 3222011904 | bytes 11534336 | tf_op jit(solution)/shard_map/dot_general | solution.py:287
  119.4 3.7 %all-to-all-start.1 = ((bf16[16,128,384]{2,1,0:T(8,128)(2,1)}), bf16[16,128,384]{2,1,0:T(8,128)(2,1)S(1)}, u32[]{:S(2)}, u32[]{:S(2)}) async-start(bf16[16,128,384]{2,1,0:T(8,128)(2,1)} %bitcast.26), calls=%async_computation.1 | async-start | bytes 3145728 | tf_op jit(solution)/shard_map/all_to_all | solution.py:291
  123.1 8.2 %collective-permute-done.16.refs_2_ = bf16[16,16,2048]{2,1,0:T(8,128)(2,1)} collective-permute-done((bf16[16,16,2048]{2,1,0:T(8,128)(2,1)S(1)}, bf16[16,16,2048]{2,1,0:T(8,128)(2,1)}, u32[]{:S(2)}, u32[]{:S(2)}) %collective-permute-start.16) | collective-permute-done | bytes 1048608 | tf_op jit(solution)/shard_map/ppermute | solution.py:36
  134.8 4.4 %place.3 = bf16[2048,384]{1,0:T(8,128)(2,1)S(1)} custom-call(s32[32]{0:T(128)S(1)} %sub.7.first_ref, bf16[16,1552,128]{2,1,0:T(8,128)(2,1)} %all-to-all-done.refs_0_.refs_1_, bf16[16,1552,128]{2,1,0:T(8,128)(2,1)} %all-to-all-done.refs_0_.refs_1_), custom_call_target="tpu_custom_call" | custom-call | flops 1572864 | bytes 6291456 | tf_op jit(solution)/shard_map/place/pallas_call | solution.py:124
  139.2 9.7 %convolution_convert_fusion = bf16[2048,384]{1,0:T(8,128)(2,1)} fusion(bf16[2048,2048]{1,0:T(8,128)(2,1)} %bitcast.21, bf16[2048,384]{1,0:T(8,128)(2,1)S(1)} %place.3), kind=kOutput, calls=%fused_computation | convolution fusion | flops 3222011904 | bytes 11534336 | tf_op jit(solution)/shard_map/dot_general | solution.py:287
  151.3 3.3 %copy-done.3 = bf16[4,2,4,2,2,16,2048]{6,5,4,3,2,1,0:T(8,128)(2,1)} copy-done((bf16[4,2,4,2,2,16,2048]{6,5,4,3,2,1,0:T(8,128)(2,1)}, bf16[4,2,4,2,2,16,2048]{6,5,4,3,2,1,0:T(8,128)(2,1)S(1)}, u32[]{:S(2)}) %copy-start.3) | copy-done | bytes 8388632
  154.6 7.0 %all-to-all-start.2 = ((bf16[16,128,384]{2,1,0:T(8,128)(2,1)}), bf16[16,128,384]{2,1,0:T(8,128)(2,1)S(1)}, u32[]{:S(2)}, u32[]{:S(2)}) async-start(bf16[16,128,384]{2,1,0:T(8,128)(2,1)} %bitcast.27), calls=%async_computation.2 | async-start | bytes 3145728 | tf_op jit(solution)/shard_map/all_to_all | solution.py:291
  161.6 7.5 %convolution_convert_fusion.1.refs_1_ = bf16[384,2048]{1,0:T(8,128)(2,1)S(1)} fusion(bf16[2048,384]{1,0:T(8,128)(2,1)} %copy-done.12, bf16[2048,2048]{1,0:T(8,128)(2,1)} %bitcast.23), kind=kOutput, calls=%fused_computation.1 | convolution fusion | flops 3222011904 | bytes 11534336 | tf_op jit(solution)/shard_map/dot_general | solution.py:296
  169.1 3.5 %convolution_convert_fusion.2.refs_0_ = bf16[384,2048]{1,0:T(8,128)(2,1)S(1)} fusion(bf16[2048,384]{1,0:T(8,128)(2,1)S(1)} %copy-done.11, bf16[2048,2048]{1,0:T(8,128)(2,1)S(1)} %bitcast.24), kind=kOutput, calls=%fused_computation.2 | convolution fusion | flops 3222011904 | bytes 11534336 | tf_op jit(solution)/shard_map/dot_general | solution.py:296
  175.8 9.5 %all-to-all-done.2.x_ref = bf16[16,128,384]{2,1,0:T(8,128)(2,1)S(1)} async-done(((bf16[16,128,384]{2,1,0:T(8,128)(2,1)}), bf16[16,128,384]{2,1,0:T(8,128)(2,1)S(1)}, u32[]{:S(2)}, u32[]{:S(2)}) %all-to-all-start.2) | async-done | bytes 1572896 | tf_op jit(solution)/shard_map/all_to_all | solution.py:291
  192.3 4.4 %collective-permute-done.23 = f32[6,6]{0,1:T(8,128)S(1)} collective-permute-done((f32[6,6]{0,1:T(8,128)S(1)}, f32[6,6]{0,1:T(8,128)S(1)}, u32[]{:S(2)}, u32[]{:S(2)}) %collective-permute-start.23) | collective-permute-done | bytes 176 | tf_op jit(solution)/shard_map/ppermute | solution.py:36
  201.5 4.0 %collective-permute-done.25 = f32[6,6]{0,1:T(8,128)S(1)} collective-permute-done((f32[6,6]{0,1:T(8,128)S(1)}, f32[6,6]{0,1:T(8,128)S(1)}, u32[]{:S(2)}, u32[]{:S(2)}) %collective-permute-start.25) | collective-permute-done | bytes 176 | tf_op jit(solution)/shard_map/ppermute | solution.py:36
  (93 shorter events, 47.4 us)
Async XLA Ops:
  0.9 6.6 %collective-permute-start.2 = (bf16[1,32,2048]{2,1,0:T(8,128)(2,1)S(1)}, bf16[1,32,2048]{2,1,0:T(8,128)(2,1)S(1)}, u32[]{:S(2)}, u32[]{:S(2)}) collective-permute-start(bf16[1,32,2048]{2,1,0:T(8,128)(2,1)S(1)} %maximum_bitcast_fusion), channel_id=1, source_target_pairs={{0,8},{1,3},{2,10},{3,1},{4,12},{5,7},{6,14},{7,5},{8,0},{9,11},{1... | collective-permute-start | bytes 393224 | tf_op jit(solution)/shard_map/ppermute | solution.py:153
  5.2 6.2 %collective-permute-start = (bf16[1,32,2048]{2,1,0:T(8,128)(2,1)S(1)}, bf16[1,32,2048]{2,1,0:T(8,128)(2,1)S(1)}, u32[]{:S(2)}, u32[]{:S(2)}) collective-permute-start(bf16[1,32,2048]{2,1,0:T(8,128)(2,1)S(1)} %maximum_bitcast_fusion), channel_id=1, source_target_pairs={{0,4},{1,17},{2,6},{3,19},{4,8},{5,21},{6,10},{7,23},{8,12},{9,25}... | collective-permute-start | bytes 393224 | tf_op jit(solution)/shard_map/ppermute | solution.py:153
  11.5 11.3 %collective-permute-start.5 = (bf16[4,32,2048]{2,1,0:T(8,128)(2,1)S(1)}, bf16[4,32,2048]{2,1,0:T(8,128)(2,1)S(1)}, u32[]{:S(2)}, u32[]{:S(2)}) collective-permute-start(bf16[4,32,2048]{2,1,0:T(8,128)(2,1)S(1)} %pad_maximum_fusion), channel_id=1, source_target_pairs={{0,2},{1,9},{2,0},{3,11},{4,6},{5,13},{6,4},{7,15},{8,10},{9,1},{1... | collective-permute-start | bytes 1572872 | tf_op jit(solution)/shard_map/ppermute | solution.py:153
  13.7 14.2 %collective-permute-start.4 = (bf16[4,32,2048]{2,1,0:T(8,128)(2,1)S(1)}, bf16[4,32,2048]{2,1,0:T(8,128)(2,1)S(1)}, u32[]{:S(2)}, u32[]{:S(2)}) collective-permute-start(bf16[4,32,2048]{2,1,0:T(8,128)(2,1)S(1)} %pad_maximum_fusion), channel_id=1, source_target_pairs={{0,18},{1,13},{2,16},{3,15},{4,22},{5,1},{6,20},{7,3},{8,26},{9,5}... | collective-permute-start | bytes 1572872 | tf_op jit(solution)/shard_map/ppermute | solution.py:153
  15.1 12.8 %collective-permute-start.3 = (bf16[4,32,2048]{2,1,0:T(8,128)(2,1)S(1)}, bf16[4,32,2048]{2,1,0:T(8,128)(2,1)S(1)}, u32[]{:S(2)}, u32[]{:S(2)}) collective-permute-start(bf16[4,32,2048]{2,1,0:T(8,128)(2,1)S(1)} %pad_maximum_fusion), channel_id=1, source_target_pairs={{0,16},{1,5},{2,18},{3,7},{4,20},{5,9},{6,22},{7,11},{8,24},{9,13}... | collective-permute-start | bytes 1572872 | tf_op jit(solution)/shard_map/ppermute | solution.py:153
  27.9 79.7 %all-to-all-start = ((bf16[16,1552,128]{2,1,0:T(8,128)(2,1)}), bf16[16,1552,128]{2,1,0:T(8,128)(2,1)}, u32[]{:S(2)}, u32[]{:S(2)}) async-start(bf16[16,1552,128]{2,1,0:T(8,128)(2,1)} %copy-done), calls=%async_computation | async-start | bytes 12713984 | tf_op jit(solution)/shard_map/all_to_all | solution.py:274
  32.9 26.9 %collective-permute-start.7 = (bf16[16,16,2048]{2,1,0:T(8,128)(2,1)S(1)}, bf16[16,16,2048]{2,1,0:T(8,128)(2,1)S(1)}, u32[]{:S(2)}, u32[]{:S(2)}) collective-permute-start(bf16[16,16,2048]{2,1,0:T(8,128)(2,1)S(1)} %get-tuple-element.24.refs_0_), channel_id=1, source_target_pairs={{0,96},{1,97},{2,98},{3,99},{4,100},{5,101},{6,102},{7,103},{8,104... | collective-permute-start | bytes 3145736 | tf_op jit(solution)/shard_map/ppermute | solution.py:36
  37.0 26.6 %collective-permute-start.6 = (bf16[16,16,2048]{2,1,0:T(8,128)(2,1)S(1)}, bf16[16,16,2048]{2,1,0:T(8,128)(2,1)S(1)}, u32[]{:S(2)}, u32[]{:S(2)}) collective-permute-start(bf16[16,16,2048]{2,1,0:T(8,128)(2,1)S(1)} %get-tuple-element.24.refs_0_), channel_id=1, source_target_pairs={{0,32},{1,33},{2,34},{3,35},{4,36},{5,37},{6,38},{7,39},{8,40},{9,... | collective-permute-start | bytes 3145736 | tf_op jit(solution)/shard_map/ppermute | solution.py:36
  59.9 14.6 %collective-permute-start.9 = (bf16[8,16,2048]{2,1,0:T(8,128)(2,1)S(1)}, bf16[8,16,2048]{2,1,0:T(8,128)(2,1)S(1)}, u32[]{:S(2)}, u32[]{:S(2)}) collective-permute-start(bf16[8,16,2048]{2,1,0:T(8,128)(2,1)S(1)} %slice.22), channel_id=1, source_target_pairs={{0,96},{1,97},{2,98},{3,99},{4,100},{5,101},{6,102},{7,103},{8,104... | collective-permute-start | bytes 1572872 | tf_op jit(solution)/shard_map/ppermute | solution.py:36
  63.7 14.3 %collective-permute-start.8 = (bf16[8,16,2048]{2,1,0:T(8,128)(2,1)S(1)}, bf16[8,16,2048]{2,1,0:T(8,128)(2,1)S(1)}, u32[]{:S(2)}, u32[]{:S(2)}) collective-permute-start(bf16[8,16,2048]{2,1,0:T(8,128)(2,1)S(1)} %slice.21), channel_id=1, source_target_pairs={{0,32},{1,33},{2,34},{3,35},{4,36},{5,37},{6,38},{7,39},{8,40},{9,... | collective-permute-start | bytes 1572872 | tf_op jit(solution)/shard_map/ppermute | solution.py:36
  78.1 8.2 %collective-permute-start.10 = (bf16[16,16,2048]{2,1,0:T(8,128)(2,1)S(1)}, bf16[16,16,2048]{2,1,0:T(8,128)(2,1)S(1)}, u32[]{:S(2)}, u32[]{:S(2)}) collective-permute-start(bf16[16,16,2048]{2,1,0:T(8,128)(2,1)S(1)} %get-tuple-element.24.refs_0_), channel_id=1, source_target_pairs={{0,1},{1,0},{2,3},{3,2},{4,5},{5,4},{6,7},{7,6},{8,9},{9,8},{10,11... | collective-permute-start | bytes 3145736 | tf_op jit(solution)/shard_map/ppermute | solution.py:36
  78.1 9.2 %collective-permute-start.11 = (bf16[16,16,2048]{2,1,0:T(8,128)(2,1)S(1)}, bf16[16,16,2048]{2,1,0:T(8,128)(2,1)S(1)}, u32[]{:S(2)}, u32[]{:S(2)}) collective-permute-start(bf16[16,16,2048]{2,1,0:T(8,128)(2,1)S(1)} %collective-permute-done.6.refs_1_), channel_id=1, source_target_pairs={{0,1},{1,0},{2,3},{3,2},{4,5},{5,4},{6,7},{7,6},{8,9},{9,8},{10,11... | collective-permute-start | bytes 3145736 | tf_op jit(solution)/shard_map/ppermute | solution.py:36
  78.6 8.7 %collective-permute-start.12 = (bf16[16,16,2048]{2,1,0:T(8,128)(2,1)S(1)}, bf16[16,16,2048]{2,1,0:T(8,128)(2,1)S(1)}, u32[]{:S(2)}, u32[]{:S(2)}) collective-permute-start(bf16[16,16,2048]{2,1,0:T(8,128)(2,1)S(1)} %collective-permute-done.7.refs_2_), channel_id=1, source_target_pairs={{0,1},{1,0},{2,3},{3,2},{4,5},{5,4},{6,7},{7,6},{8,9},{9,8},{10,11... | collective-permute-start | bytes 3145736 | tf_op jit(solution)/shard_map/ppermute | solution.py:36
  78.6 5.9 %collective-permute-start.13 = (bf16[8,16,2048]{2,1,0:T(8,128)(2,1)S(1)}, bf16[8,16,2048]{2,1,0:T(8,128)(2,1)S(1)}, u32[]{:S(2)}, u32[]{:S(2)}) collective-permute-start(bf16[8,16,2048]{2,1,0:T(8,128)(2,1)S(1)} %collective-permute-done.8.refs_3_), channel_id=1, source_target_pairs={{0,1},{1,0},{2,3},{3,2},{4,5},{5,4},{6,7},{7,6},{8,9},{9,8},{10,11... | collective-permute-start | bytes 1572872 | tf_op jit(solution)/shard_map/ppermute | solution.py:36
  79.1 6.1 %collective-permute-start.14 = (bf16[8,16,2048]{2,1,0:T(8,128)(2,1)S(1)}, bf16[8,16,2048]{2,1,0:T(8,128)(2,1)S(1)}, u32[]{:S(2)}, u32[]{:S(2)}) collective-permute-start(bf16[8,16,2048]{2,1,0:T(8,128)(2,1)S(1)} %collective-permute-done.9.refs_4_), channel_id=1, source_target_pairs={{0,1},{1,0},{2,3},{3,2},{4,5},{5,4},{6,7},{7,6},{8,9},{9,8},{10,11... | collective-permute-start | bytes 1572872 | tf_op jit(solution)/shard_map/ppermute | solution.py:36
  84.5 38.6 %collective-permute-start.17 = (bf16[16,16,2048]{2,1,0:T(8,128)(2,1)S(1)}, bf16[16,16,2048]{2,1,0:T(8,128)(2,1)}, u32[]{:S(2)}, u32[]{:S(2)}) collective-permute-start(bf16[16,16,2048]{2,1,0:T(8,128)(2,1)S(1)} %get-tuple-element.31.refs_0_), channel_id=1, source_target_pairs={{0,64},{1,65},{2,66},{3,67},{4,68},{5,69},{6,70},{7,71},{8,72},{9,... | collective-permute-start | bytes 3145736 | tf_op jit(solution)/shard_map/ppermute | solution.py:36
  85.2 46.1 %collective-permute-start.16 = (bf16[16,16,2048]{2,1,0:T(8,128)(2,1)S(1)}, bf16[16,16,2048]{2,1,0:T(8,128)(2,1)}, u32[]{:S(2)}, u32[]{:S(2)}) collective-permute-start(bf16[16,16,2048]{2,1,0:T(8,128)(2,1)S(1)} %get-tuple-element.31.refs_0_), channel_id=1, source_target_pairs={{0,96},{1,97},{2,98},{3,99},{4,100},{5,101},{6,102},{7,103},{8,104... | collective-permute-start | bytes 3145736 | tf_op jit(solution)/shard_map/ppermute | solution.py:36
  86.2 47.5 %collective-permute-start.15 = (bf16[16,16,2048]{2,1,0:T(8,128)(2,1)S(1)}, bf16[16,16,2048]{2,1,0:T(8,128)(2,1)}, u32[]{:S(2)}, u32[]{:S(2)}) collective-permute-start(bf16[16,16,2048]{2,1,0:T(8,128)(2,1)S(1)} %get-tuple-element.31.refs_0_), channel_id=1, source_target_pairs={{0,32},{1,33},{2,34},{3,35},{4,36},{5,37},{6,38},{7,39},{8,40},{9,... | collective-permute-start | bytes 3145736 | tf_op jit(solution)/shard_map/ppermute | solution.py:36
  119.4 35.2 %all-to-all-start.1 = ((bf16[16,128,384]{2,1,0:T(8,128)(2,1)}), bf16[16,128,384]{2,1,0:T(8,128)(2,1)S(1)}, u32[]{:S(2)}, u32[]{:S(2)}) async-start(bf16[16,128,384]{2,1,0:T(8,128)(2,1)} %bitcast.26), calls=%async_computation.1 | async-start | bytes 3145728 | tf_op jit(solution)/shard_map/all_to_all | solution.py:291
  133.8 15.1 %collective-permute-start.18 = (bf16[16,16,2048]{2,1,0:T(8,128)(2,1)S(1)}, bf16[16,16,2048]{2,1,0:T(8,128)(2,1)S(1)}, u32[]{:S(2)}, u32[]{:S(2)}) collective-permute-start(bf16[16,16,2048]{2,1,0:T(8,128)(2,1)S(1)} %get-tuple-element.31.refs_0_), channel_id=1, source_target_pairs={{0,1},{1,0},{2,3},{3,2},{4,5},{5,4},{6,7},{7,6},{8,9},{9,8},{10,11... | collective-permute-start | bytes 3145736 | tf_op jit(solution)/shard_map/ppermute | solution.py:36
  133.8 15.0 %collective-permute-start.19 = (bf16[16,16,2048]{2,1,0:T(8,128)(2,1)}, bf16[16,16,2048]{2,1,0:T(8,128)(2,1)S(1)}, u32[]{:S(2)}, u32[]{:S(2)}) collective-permute-start(bf16[16,16,2048]{2,1,0:T(8,128)(2,1)} %collective-permute-done.15.refs_1_), channel_id=1, source_target_pairs={{0,1},{1,0},{2,3},{3,2},{4,5},{5,4},{6,7},{7,6},{8,9},{9,8},{10,11... | collective-permute-start | bytes 3145736 | tf_op jit(solution)/shard_map/ppermute | solution.py:36
  134.3 14.6 %collective-permute-start.20 = (bf16[16,16,2048]{2,1,0:T(8,128)(2,1)}, bf16[16,16,2048]{2,1,0:T(8,128)(2,1)S(1)}, u32[]{:S(2)}, u32[]{:S(2)}) collective-permute-start(bf16[16,16,2048]{2,1,0:T(8,128)(2,1)} %collective-permute-done.16.refs_2_), channel_id=1, source_target_pairs={{0,1},{1,0},{2,3},{3,2},{4,5},{5,4},{6,7},{7,6},{8,9},{9,8},{10,11... | collective-permute-start | bytes 3145736 | tf_op jit(solution)/shard_map/ppermute | solution.py:36
  134.3 14.6 %collective-permute-start.21 = (bf16[16,16,2048]{2,1,0:T(8,128)(2,1)}, bf16[16,16,2048]{2,1,0:T(8,128)(2,1)S(1)}, u32[]{:S(2)}, u32[]{:S(2)}) collective-permute-start(bf16[16,16,2048]{2,1,0:T(8,128)(2,1)} %collective-permute-done.17.refs_3_), channel_id=1, source_target_pairs={{0,1},{1,0},{2,3},{3,2},{4,5},{5,4},{6,7},{7,6},{8,9},{9,8},{10,11... | collective-permute-start | bytes 3145736 | tf_op jit(solution)/shard_map/ppermute | solution.py:36
  154.6 30.7 %all-to-all-start.2 = ((bf16[16,128,384]{2,1,0:T(8,128)(2,1)}), bf16[16,128,384]{2,1,0:T(8,128)(2,1)S(1)}, u32[]{:S(2)}, u32[]{:S(2)}) async-start(bf16[16,128,384]{2,1,0:T(8,128)(2,1)} %bitcast.27), calls=%async_computation.2 | async-start | bytes 3145728 | tf_op jit(solution)/shard_map/all_to_all | solution.py:291
  (18 other events, 74.3 us)

commit v6 on v5

--- a/solution.py
+++ b/solution.py
@@ -200,9 +200,9 @@
     return [mine, up(mine), down(mine), up(mine, 2)]
 
 
-def assemble(spots, pieces):
+def assemble(spots, pieces, copies):
     spots = [(side, *spot) for side in range(2) for spot in spots]
-    return lay(spots, pieces + [other_core(piece) for piece in pieces])
+    return lay(spots, pieces + copies)
 
 
 def pair_kernel(x_ref, *refs):
@@ -279,19 +279,20 @@
     occ_pieces = z_forwarded(occ_plane)
     occ_pieces, virt_plane = lax.optimization_barrier((occ_pieces, virt_plane))
     virt_pieces = z_direct(virt_plane)
-    occ = assemble(FORWARDED, occ_pieces)
+    occ = assemble(FORWARDED, occ_pieces, [other_core(p) for p in occ_pieces])
 
     dense, turned, start = [], [], 0
     for depth in CHUNKS:
         dense.append(place(recv_first, recv, start, depth, aux, basis_total))
         half = jnp.dot(occ, dense[-1], preferred_element_type=jnp.float32).astype(jnp.bfloat16)
-        if start == 0:
-            _, virt_pieces = lax.optimization_barrier((half, virt_pieces))
-        half = half.reshape(col_count, width, -1)
-        turned.append(lax.all_to_all(half, COL, split_axis=0, concat_axis=0, tiled=True))
+        cut = half.reshape(col_count, width, -1)
+        turned.append(lax.all_to_all(cut, COL, split_axis=0, concat_axis=0, tiled=True))
         start += depth
 
-    virt_t = assemble(DIRECT, virt_pieces)
+    _, virt_pieces = lax.optimization_barrier((half, virt_pieces))
+    virt_copies = [other_core(p) for p in virt_pieces]
+    turned[0], virt_copies = lax.optimization_barrier((turned[0], virt_copies))
+    virt_t = assemble(DIRECT, virt_pieces, virt_copies)
     virt_half = [
         lax.dot_general(
             d, virt_t, (((0,), (0,)), ((), ())), preferred_element_type=jnp.float32

time: 207 us -> 196 us (0.947)
  matrix products: 26.2 us -> 22.2 us
  waiting for transfers between devices: 103 us -> 99.3 us
  starting transfers between devices: 39.2 us -> 35.8 us
  local copies, waits for them, and re-layouts: 17.5 us -> 15.4 us
    ppermute x20, waiting for transfers between devices: 66.7 us -> 56.2 us  [permute(): return lax.ppermute(x, AXES, moved(axis, to))]
    all_to_all x2, waiting for transfers between devices: 9.52 us -> 17.4 us  [shards(): lax.all_to_all(cut, COL, split_axis=0, concat_axis=0, tiled=True)]
    dot_general x2, matrix products: 11 us -> 6.96 us  [shards(): lax.dot_general(d, virt_t, (((0,), (0,)), ((), ())), preferred_element_ty...]
    unnamed x29 -> x27, local copies, waits for them, and re-layouts: 15.6 us -> 12.3 us
    all_to_all x2, starting transfers between devices: 10.7 us -> 7.6 us  [shards(): lax.all_to_all(cut, COL, split_axis=0, concat_axis=0, tiled=True)]
  transfers between devices with their start and end apart: 29 -> 29, of which waited for: 18 -> 17; matrix products, arithmetic and copies ran while one was open for 14% -> 13% of each run, Pallas kernels for 8% -> 9%
where the time goes in v6:
time: 196 us; the launch traced here: 195 us
  waiting for transfers between devices  99.3 us (51%)
  starting transfers between devices  35.8 us (18%)
  matrix products  22.2 us (11%)
  Pallas kernels  19.4 us (10%)
  local copies, waits for them, and re-layouts  15.4 us (8%)
  other arithmetic  2.64 us (1%)
    ppermute x20, waiting for transfers between devices, permute(): return lax.ppermute(x, AXES, moved(axis, to))  56.2 us
    all_to_all x2, waiting for transfers between devices, shards(): lax.all_to_all(cut, COL, split_axis=0, concat_axis=0, tiled=True)  17.4 us
    all_to_all x1, waiting for transfers between devices, shards(): recv = lax.all_to_all(picked, COL, split_axis=0, concat_axis=0, tiled=True)  15.3 us
    dot_general x2, matrix products, shards(): jnp.dot(occ, dense[-1], preferred_element_type=jnp.float32)  15.2 us
    ppermute x20, starting transfers between devices, permute(): return lax.ppermute(x, AXES, moved(axis, to))  14 us
    unnamed x27, local copies, waits for them, and re-layouts  12.3 us
    ppermute x6, waiting for transfers between devices, hop(): return lax.ppermute(x, AXES, pairs)  10.3 us
    ppermute x6, starting transfers between devices, hop(): return lax.ppermute(x, AXES, pairs)  9.53 us
  transfers between devices with their start and end apart: 29, of which 17 were waited for; matrix products, arithmetic and copies ran while one was open for 13% of the time, Pallas kernels for 9%

profile of v6, /device:TPU:2, one launch (start us, length us, event | category | flops | bytes accessed | tf_op | source)
XLA Modules:
  0.0 195.1 jit_solution(18276886249874401690)
XLA Ops:
  0.9 3.3 %collective-permute-start.2 = (bf16[1,32,2048]{2,1,0:T(8,128)(2,1)S(1)}, bf16[1,32,2048]{2,1,0:T(8,128)(2,1)S(1)}, u32[]{:S(2)}, u32[]{:S(2)}) collective-permute-start(bf16[1,32,2048]{2,1,0:T(8,128)(2,1)S(1)} %maximum_bitcast_fusion), channel_id=1, source_target_pairs={{0,8},{1,3},{2,10},{3,1},{4,12},{5,7},{6,14},{7,5},{8,0},{9,11},{1... | collective-permute-start | bytes 393224 | tf_op jit(solution)/shard_map/ppermute | solution.py:153
  22.8 5.1 %collective-permute-done.4 = bf16[4,32,2048]{2,1,0:T(8,128)(2,1)S(1)} collective-permute-done((bf16[4,32,2048]{2,1,0:T(8,128)(2,1)S(1)}, bf16[4,32,2048]{2,1,0:T(8,128)(2,1)S(1)}, u32[]{:S(2)}, u32[]{:S(2)}) %collective-permute-start.4) | collective-permute-done | bytes 524320 | tf_op jit(solution)/shard_map/ppermute | solution.py:153
  27.9 4.7 %all-to-all-start = ((bf16[16,1552,128]{2,1,0:T(8,128)(2,1)}), bf16[16,1552,128]{2,1,0:T(8,128)(2,1)}, u32[]{:S(2)}, u32[]{:S(2)}) async-start(bf16[16,1552,128]{2,1,0:T(8,128)(2,1)} %copy-done), calls=%async_computation | async-start | bytes 12713984 | tf_op jit(solution)/shard_map/all_to_all | solution.py:274
  34.0 4.0 %collective-permute-start.7 = (bf16[16,16,2048]{2,1,0:T(8,128)(2,1)S(1)}, bf16[16,16,2048]{2,1,0:T(8,128)(2,1)S(1)}, u32[]{:S(2)}, u32[]{:S(2)}) collective-permute-start(bf16[16,16,2048]{2,1,0:T(8,128)(2,1)S(1)} %get-tuple-element.29.refs_0_), channel_id=1, source_target_pairs={{0,96},{1,97},{2,98},{3,99},{4,100},{5,101},{6,102},{7,103},{8,104... | collective-permute-start | bytes 3145736 | tf_op jit(solution)/shard_map/ppermute | solution.py:36
  38.1 22.8 %collective-permute-done.7.refs_2_ = bf16[16,16,2048]{2,1,0:T(8,128)(2,1)S(1)} collective-permute-done((bf16[16,16,2048]{2,1,0:T(8,128)(2,1)S(1)}, bf16[16,16,2048]{2,1,0:T(8,128)(2,1)S(1)}, u32[]{:S(2)}, u32[]{:S(2)}) %collective-permute-start.7) | collective-permute-done | bytes 1048608 | tf_op jit(solution)/shard_map/ppermute | solution.py:36
  60.9 3.8 %collective-permute-start.9 = (bf16[8,16,2048]{2,1,0:T(8,128)(2,1)S(1)}, bf16[8,16,2048]{2,1,0:T(8,128)(2,1)S(1)}, u32[]{:S(2)}, u32[]{:S(2)}) collective-permute-start(bf16[8,16,2048]{2,1,0:T(8,128)(2,1)S(1)} %slice.22), channel_id=1, source_target_pairs={{0,96},{1,97},{2,98},{3,99},{4,100},{5,101},{6,102},{7,103},{8,104... | collective-permute-start | bytes 1572872 | tf_op jit(solution)/shard_map/ppermute | solution.py:36
  64.8 10.7 %collective-permute-done.9.refs_4_ = bf16[8,16,2048]{2,1,0:T(8,128)(2,1)S(1)} collective-permute-done((bf16[8,16,2048]{2,1,0:T(8,128)(2,1)S(1)}, bf16[8,16,2048]{2,1,0:T(8,128)(2,1)S(1)}, u32[]{:S(2)}, u32[]{:S(2)}) %collective-permute-start.9) | collective-permute-done | bytes 524320 | tf_op jit(solution)/shard_map/ppermute | solution.py:36
  75.6 3.5 %collective-permute-done.8.refs_3_ = bf16[8,16,2048]{2,1,0:T(8,128)(2,1)S(1)} collective-permute-done((bf16[8,16,2048]{2,1,0:T(8,128)(2,1)S(1)}, bf16[8,16,2048]{2,1,0:T(8,128)(2,1)S(1)}, u32[]{:S(2)}, u32[]{:S(2)}) %collective-permute-start.8) | collective-permute-done | bytes 524320 | tf_op jit(solution)/shard_map/ppermute | solution.py:36
  80.1 5.4 %collective-permute-done.13.refs_8_ = bf16[8,16,2048]{2,1,0:T(8,128)(2,1)S(1)} collective-permute-done((bf16[8,16,2048]{2,1,0:T(8,128)(2,1)S(1)}, bf16[8,16,2048]{2,1,0:T(8,128)(2,1)S(1)}, u32[]{:S(2)}, u32[]{:S(2)}) %collective-permute-start.13) | collective-permute-done | bytes 524320 | tf_op jit(solution)/shard_map/ppermute | solution.py:36
  92.3 15.3 %all-to-all-done.refs_0_.refs_1_ = bf16[16,1552,128]{2,1,0:T(8,128)(2,1)} async-done(((bf16[16,1552,128]{2,1,0:T(8,128)(2,1)}), bf16[16,1552,128]{2,1,0:T(8,128)(2,1)}, u32[]{:S(2)}, u32[]{:S(2)}) %all-to-all-start) | async-done | bytes 6357024 | tf_op jit(solution)/shard_map/all_to_all | solution.py:274
  108.8 4.9 %place.2 = bf16[2048,384]{1,0:T(8,128)(2,1)S(1)} custom-call(s32[32]{0:T(128)S(1)} %sub.7.first_ref, bf16[16,1552,128]{2,1,0:T(8,128)(2,1)} %all-to-all-done.refs_0_.refs_1_, bf16[16,1552,128]{2,1,0:T(8,128)(2,1)} %all-to-all-done.refs_0_.refs_1_), custom_call_target="tpu_custom_call" | custom-call | flops 1572864 | bytes 6291456 | tf_op jit(solution)/shard_map/place/pallas_call | solution.py:124
  113.8 5.6 %convolution_convert_fusion.3 = bf16[2048,384]{1,0:T(8,128)(2,1)} fusion(bf16[2048,2048]{1,0:T(8,128)(2,1)S(1)} %bitcast.22, bf16[2048,384]{1,0:T(8,128)(2,1)S(1)} %place.2), kind=kOutput, calls=%fused_computation.3 | convolution fusion | flops 3222011904 | bytes 11534336 | tf_op jit(solution)/shard_map/dot_general | solution.py:287
  119.3 3.9 %all-to-all-start.1 = ((bf16[16,128,384]{2,1,0:T(8,128)(2,1)}), bf16[16,128,384]{2,1,0:T(8,128)(2,1)S(1)}, u32[]{:S(2)}, u32[]{:S(2)}) async-start(bf16[16,128,384]{2,1,0:T(8,128)(2,1)} %bitcast.5), calls=%async_computation.1 | async-start | bytes 3145728 | tf_op jit(solution)/shard_map/all_to_all | solution.py:289
  123.2 4.4 %place.3 = bf16[2048,384]{1,0:T(8,128)(2,1)S(1)} custom-call(s32[32]{0:T(128)S(1)} %sub.7.first_ref, bf16[16,1552,128]{2,1,0:T(8,128)(2,1)} %all-to-all-done.refs_0_.refs_1_, bf16[16,1552,128]{2,1,0:T(8,128)(2,1)} %all-to-all-done.refs_0_.refs_1_), custom_call_target="tpu_custom_call" | custom-call | flops 1572864 | bytes 6291456 | tf_op jit(solution)/shard_map/place/pallas_call | solution.py:124
  127.7 9.6 %convolution_convert_fusion.2 = bf16[2048,384]{1,0:T(8,128)(2,1)} fusion(bf16[2048,2048]{1,0:T(8,128)(2,1)} %bitcast.21, bf16[2048,384]{1,0:T(8,128)(2,1)S(1)} %place.3), kind=kOutput, calls=%fused_computation.2 | convolution fusion | flops 3222011904 | bytes 11534336 | tf_op jit(solution)/shard_map/dot_general | solution.py:287
  138.4 8.4 %all-to-all-done.1.x_ref = bf16[16,128,384]{2,1,0:T(8,128)(2,1)S(1)} async-done(((bf16[16,128,384]{2,1,0:T(8,128)(2,1)}), bf16[16,128,384]{2,1,0:T(8,128)(2,1)S(1)}, u32[]{:S(2)}, u32[]{:S(2)}) %all-to-all-start.1) | async-done | bytes 1572896 | tf_op jit(solution)/shard_map/all_to_all | solution.py:289
  146.8 3.7 %all-to-all-start.2 = ((bf16[16,128,384]{2,1,0:T(8,128)(2,1)}), bf16[16,128,384]{2,1,0:T(8,128)(2,1)S(1)}, u32[]{:S(2)}, u32[]{:S(2)}) async-start(bf16[16,128,384]{2,1,0:T(8,128)(2,1)} %bitcast.26), calls=%async_computation.2 | async-start | bytes 3145728 | tf_op jit(solution)/shard_map/all_to_all | solution.py:289
  150.6 4.4 %lay.3 = bf16[4,2,4,2,2,16,2048]{6,5,4,3,2,1,0:T(8,128)(2,1)S(1)} custom-call(bf16[16,16,2048]{2,1,0:T(8,128)(2,1)} %get-tuple-element.36.refs_0_, bf16[16,16,2048]{2,1,0:T(8,128)(2,1)} %collective-permute-done.15.refs_1_, bf16[16,16,2048]{2,1,0:T(8,128)(2,1)} %collective-permute-done.16.refs_2_, bf16[16,16,2048]{2,1,0:T(8,128)(2,1)} %collective-permute-done.17.refs_3_, ...), custom_call_target="tpu_custom_call" | custom-call | bytes 16777216 | tf_op jit(solution)/shard_map/lay/pallas_call | solution.py:175
  155.0 3.5 %convolution_convert_fusion.refs_1_ = bf16[384,2048]{1,0:T(8,128)(2,1)S(1)} fusion(bf16[2048,384]{1,0:T(8,128)(2,1)S(1)} %copy-done.11, bf16[2048,2048]{1,0:T(8,128)(2,1)S(1)} %bitcast.23), kind=kOutput, calls=%fused_computation | convolution fusion | flops 3222011904 | bytes 11534336 | tf_op jit(solution)/shard_map/dot_general | solution.py:297
  158.5 3.5 %convolution_convert_fusion.1.refs_0_ = bf16[384,2048]{1,0:T(8,128)(2,1)S(1)} fusion(bf16[2048,384]{1,0:T(8,128)(2,1)S(1)} %copy-done.9, bf16[2048,2048]{1,0:T(8,128)(2,1)S(1)} %bitcast.24), kind=kOutput, calls=%fused_computation.1 | convolution fusion | flops 3222011904 | bytes 11534336 | tf_op jit(solution)/shard_map/dot_general | solution.py:297
  165.2 9.0 %all-to-all-done.2.x_ref = bf16[16,128,384]{2,1,0:T(8,128)(2,1)S(1)} async-done(((bf16[16,128,384]{2,1,0:T(8,128)(2,1)}), bf16[16,128,384]{2,1,0:T(8,128)(2,1)S(1)}, u32[]{:S(2)}, u32[]{:S(2)}) %all-to-all-start.2) | async-done | bytes 1572896 | tf_op jit(solution)/shard_map/all_to_all | solution.py:289
  181.2 4.5 %collective-permute-done.23 = f32[6,6]{0,1:T(8,128)S(1)} collective-permute-done((f32[6,6]{0,1:T(8,128)S(1)}, f32[6,6]{0,1:T(8,128)S(1)}, u32[]{:S(2)}, u32[]{:S(2)}) %collective-permute-start.23) | collective-permute-done | bytes 176 | tf_op jit(solution)/shard_map/ppermute | solution.py:36
  186.0 3.3 %collective-permute-done.24 = f32[6,6]{0,1:T(8,128)S(1)} collective-permute-done((f32[6,6]{0,1:T(8,128)S(1)}, f32[6,6]{0,1:T(8,128)S(1)}, u32[]{:S(2)}, u32[]{:S(2)}) %collective-permute-start.24) | collective-permute-done | bytes 176 | tf_op jit(solution)/shard_map/ppermute | solution.py:36
  190.3 4.1 %collective-permute-done.25 = f32[6,6]{0,1:T(8,128)S(1)} collective-permute-done((f32[6,6]{0,1:T(8,128)S(1)}, f32[6,6]{0,1:T(8,128)S(1)}, u32[]{:S(2)}, u32[]{:S(2)}) %collective-permute-start.25) | collective-permute-done | bytes 176 | tf_op jit(solution)/shard_map/ppermute | solution.py:36
  (91 shorter events, 43.4 us)
Async XLA Ops:
  0.9 6.6 %collective-permute-start.2 = (bf16[1,32,2048]{2,1,0:T(8,128)(2,1)S(1)}, bf16[1,32,2048]{2,1,0:T(8,128)(2,1)S(1)}, u32[]{:S(2)}, u32[]{:S(2)}) collective-permute-start(bf16[1,32,2048]{2,1,0:T(8,128)(2,1)S(1)} %maximum_bitcast_fusion), channel_id=1, source_target_pairs={{0,8},{1,3},{2,10},{3,1},{4,12},{5,7},{6,14},{7,5},{8,0},{9,11},{1... | collective-permute-start | bytes 393224 | tf_op jit(solution)/shard_map/ppermute | solution.py:153
  5.2 6.2 %collective-permute-start = (bf16[1,32,2048]{2,1,0:T(8,128)(2,1)S(1)}, bf16[1,32,2048]{2,1,0:T(8,128)(2,1)S(1)}, u32[]{:S(2)}, u32[]{:S(2)}) collective-permute-start(bf16[1,32,2048]{2,1,0:T(8,128)(2,1)S(1)} %maximum_bitcast_fusion), channel_id=1, source_target_pairs={{0,4},{1,17},{2,6},{3,19},{4,8},{5,21},{6,10},{7,23},{8,12},{9,25}... | collective-permute-start | bytes 393224 | tf_op jit(solution)/shard_map/ppermute | solution.py:153
  11.5 11.3 %collective-permute-start.5 = (bf16[4,32,2048]{2,1,0:T(8,128)(2,1)S(1)}, bf16[4,32,2048]{2,1,0:T(8,128)(2,1)S(1)}, u32[]{:S(2)}, u32[]{:S(2)}) collective-permute-start(bf16[4,32,2048]{2,1,0:T(8,128)(2,1)S(1)} %pad_maximum_fusion), channel_id=1, source_target_pairs={{0,2},{1,9},{2,0},{3,11},{4,6},{5,13},{6,4},{7,15},{8,10},{9,1},{1... | collective-permute-start | bytes 1572872 | tf_op jit(solution)/shard_map/ppermute | solution.py:153
  13.7 14.2 %collective-permute-start.4 = (bf16[4,32,2048]{2,1,0:T(8,128)(2,1)S(1)}, bf16[4,32,2048]{2,1,0:T(8,128)(2,1)S(1)}, u32[]{:S(2)}, u32[]{:S(2)}) collective-permute-start(bf16[4,32,2048]{2,1,0:T(8,128)(2,1)S(1)} %pad_maximum_fusion), channel_id=1, source_target_pairs={{0,18},{1,13},{2,16},{3,15},{4,22},{5,1},{6,20},{7,3},{8,26},{9,5}... | collective-permute-start | bytes 1572872 | tf_op jit(solution)/shard_map/ppermute | solution.py:153
  15.1 12.8 %collective-permute-start.3 = (bf16[4,32,2048]{2,1,0:T(8,128)(2,1)S(1)}, bf16[4,32,2048]{2,1,0:T(8,128)(2,1)S(1)}, u32[]{:S(2)}, u32[]{:S(2)}) collective-permute-start(bf16[4,32,2048]{2,1,0:T(8,128)(2,1)S(1)} %pad_maximum_fusion), channel_id=1, source_target_pairs={{0,16},{1,5},{2,18},{3,7},{4,20},{5,9},{6,22},{7,11},{8,24},{9,13}... | collective-permute-start | bytes 1572872 | tf_op jit(solution)/shard_map/ppermute | solution.py:153
  27.9 79.7 %all-to-all-start = ((bf16[16,1552,128]{2,1,0:T(8,128)(2,1)}), bf16[16,1552,128]{2,1,0:T(8,128)(2,1)}, u32[]{:S(2)}, u32[]{:S(2)}) async-start(bf16[16,1552,128]{2,1,0:T(8,128)(2,1)} %copy-done), calls=%async_computation | async-start | bytes 12713984 | tf_op jit(solution)/shard_map/all_to_all | solution.py:274
  34.0 26.9 %collective-permute-start.7 = (bf16[16,16,2048]{2,1,0:T(8,128)(2,1)S(1)}, bf16[16,16,2048]{2,1,0:T(8,128)(2,1)S(1)}, u32[]{:S(2)}, u32[]{:S(2)}) collective-permute-start(bf16[16,16,2048]{2,1,0:T(8,128)(2,1)S(1)} %get-tuple-element.29.refs_0_), channel_id=1, source_target_pairs={{0,96},{1,97},{2,98},{3,99},{4,100},{5,101},{6,102},{7,103},{8,104... | collective-permute-start | bytes 3145736 | tf_op jit(solution)/shard_map/ppermute | solution.py:36
  38.1 26.6 %collective-permute-start.6 = (bf16[16,16,2048]{2,1,0:T(8,128)(2,1)S(1)}, bf16[16,16,2048]{2,1,0:T(8,128)(2,1)S(1)}, u32[]{:S(2)}, u32[]{:S(2)}) collective-permute-start(bf16[16,16,2048]{2,1,0:T(8,128)(2,1)S(1)} %get-tuple-element.29.refs_0_), channel_id=1, source_target_pairs={{0,32},{1,33},{2,34},{3,35},{4,36},{5,37},{6,38},{7,39},{8,40},{9,... | collective-permute-start | bytes 3145736 | tf_op jit(solution)/shard_map/ppermute | solution.py:36
  60.9 14.6 %collective-permute-start.9 = (bf16[8,16,2048]{2,1,0:T(8,128)(2,1)S(1)}, bf16[8,16,2048]{2,1,0:T(8,128)(2,1)S(1)}, u32[]{:S(2)}, u32[]{:S(2)}) collective-permute-start(bf16[8,16,2048]{2,1,0:T(8,128)(2,1)S(1)} %slice.22), channel_id=1, source_target_pairs={{0,96},{1,97},{2,98},{3,99},{4,100},{5,101},{6,102},{7,103},{8,104... | collective-permute-start | bytes 1572872 | tf_op jit(solution)/shard_map/ppermute | solution.py:36
  64.7 14.3 %collective-permute-start.8 = (bf16[8,16,2048]{2,1,0:T(8,128)(2,1)S(1)}, bf16[8,16,2048]{2,1,0:T(8,128)(2,1)S(1)}, u32[]{:S(2)}, u32[]{:S(2)}) collective-permute-start(bf16[8,16,2048]{2,1,0:T(8,128)(2,1)S(1)} %slice.21), channel_id=1, source_target_pairs={{0,32},{1,33},{2,34},{3,35},{4,36},{5,37},{6,38},{7,39},{8,40},{9,... | collective-permute-start | bytes 1572872 | tf_op jit(solution)/shard_map/ppermute | solution.py:36
  79.1 8.2 %collective-permute-start.10 = (bf16[16,16,2048]{2,1,0:T(8,128)(2,1)S(1)}, bf16[16,16,2048]{2,1,0:T(8,128)(2,1)S(1)}, u32[]{:S(2)}, u32[]{:S(2)}) collective-permute-start(bf16[16,16,2048]{2,1,0:T(8,128)(2,1)S(1)} %get-tuple-element.29.refs_0_), channel_id=1, source_target_pairs={{0,1},{1,0},{2,3},{3,2},{4,5},{5,4},{6,7},{7,6},{8,9},{9,8},{10,11... | collective-permute-start | bytes 3145736 | tf_op jit(solution)/shard_map/ppermute | solution.py:36
  79.1 9.2 %collective-permute-start.11 = (bf16[16,16,2048]{2,1,0:T(8,128)(2,1)S(1)}, bf16[16,16,2048]{2,1,0:T(8,128)(2,1)S(1)}, u32[]{:S(2)}, u32[]{:S(2)}) collective-permute-start(bf16[16,16,2048]{2,1,0:T(8,128)(2,1)S(1)} %collective-permute-done.6.refs_1_), channel_id=1, source_target_pairs={{0,1},{1,0},{2,3},{3,2},{4,5},{5,4},{6,7},{7,6},{8,9},{9,8},{10,11... | collective-permute-start | bytes 3145736 | tf_op jit(solution)/shard_map/ppermute | solution.py:36
  79.6 8.7 %collective-permute-start.12 = (bf16[16,16,2048]{2,1,0:T(8,128)(2,1)S(1)}, bf16[16,16,2048]{2,1,0:T(8,128)(2,1)S(1)}, u32[]{:S(2)}, u32[]{:S(2)}) collective-permute-start(bf16[16,16,2048]{2,1,0:T(8,128)(2,1)S(1)} %collective-permute-done.7.refs_2_), channel_id=1, source_target_pairs={{0,1},{1,0},{2,3},{3,2},{4,5},{5,4},{6,7},{7,6},{8,9},{9,8},{10,11... | collective-permute-start | bytes 3145736 | tf_op jit(solution)/shard_map/ppermute | solution.py:36
  79.6 5.9 %collective-permute-start.13 = (bf16[8,16,2048]{2,1,0:T(8,128)(2,1)S(1)}, bf16[8,16,2048]{2,1,0:T(8,128)(2,1)S(1)}, u32[]{:S(2)}, u32[]{:S(2)}) collective-permute-start(bf16[8,16,2048]{2,1,0:T(8,128)(2,1)S(1)} %collective-permute-done.8.refs_3_), channel_id=1, source_target_pairs={{0,1},{1,0},{2,3},{3,2},{4,5},{5,4},{6,7},{7,6},{8,9},{9,8},{10,11... | collective-permute-start | bytes 1572872 | tf_op jit(solution)/shard_map/ppermute | solution.py:36
  80.1 6.1 %collective-permute-start.14 = (bf16[8,16,2048]{2,1,0:T(8,128)(2,1)S(1)}, bf16[8,16,2048]{2,1,0:T(8,128)(2,1)S(1)}, u32[]{:S(2)}, u32[]{:S(2)}) collective-permute-start(bf16[8,16,2048]{2,1,0:T(8,128)(2,1)S(1)} %collective-permute-done.9.refs_4_), channel_id=1, source_target_pairs={{0,1},{1,0},{2,3},{3,2},{4,5},{5,4},{6,7},{7,6},{8,9},{9,8},{10,11... | collective-permute-start | bytes 1572872 | tf_op jit(solution)/shard_map/ppermute | solution.py:36
  85.5 51.8 %collective-permute-start.17 = (bf16[16,16,2048]{2,1,0:T(8,128)(2,1)}, bf16[16,16,2048]{2,1,0:T(8,128)(2,1)}, u32[]{:S(2)}, u32[]{:S(2)}) collective-permute-start(bf16[16,16,2048]{2,1,0:T(8,128)(2,1)} %get-tuple-element.36.refs_0_), channel_id=1, source_target_pairs={{0,64},{1,65},{2,66},{3,67},{4,68},{5,69},{6,70},{7,71},{8,72},{9,... | collective-permute-start | bytes 3145736 | tf_op jit(solution)/shard_map/ppermute | solution.py:36
  86.2 51.0 %collective-permute-start.16 = (bf16[16,16,2048]{2,1,0:T(8,128)(2,1)}, bf16[16,16,2048]{2,1,0:T(8,128)(2,1)}, u32[]{:S(2)}, u32[]{:S(2)}) collective-permute-start(bf16[16,16,2048]{2,1,0:T(8,128)(2,1)} %get-tuple-element.36.refs_0_), channel_id=1, source_target_pairs={{0,96},{1,97},{2,98},{3,99},{4,100},{5,101},{6,102},{7,103},{8,104... | collective-permute-start | bytes 3145736 | tf_op jit(solution)/shard_map/ppermute | solution.py:36
  87.2 50.0 %collective-permute-start.15 = (bf16[16,16,2048]{2,1,0:T(8,128)(2,1)}, bf16[16,16,2048]{2,1,0:T(8,128)(2,1)}, u32[]{:S(2)}, u32[]{:S(2)}) collective-permute-start(bf16[16,16,2048]{2,1,0:T(8,128)(2,1)} %get-tuple-element.36.refs_0_), channel_id=1, source_target_pairs={{0,32},{1,33},{2,34},{3,35},{4,36},{5,37},{6,38},{7,39},{8,40},{9,... | collective-permute-start | bytes 3145736 | tf_op jit(solution)/shard_map/ppermute | solution.py:36
  119.3 27.4 %all-to-all-start.1 = ((bf16[16,128,384]{2,1,0:T(8,128)(2,1)}), bf16[16,128,384]{2,1,0:T(8,128)(2,1)S(1)}, u32[]{:S(2)}, u32[]{:S(2)}) async-start(bf16[16,128,384]{2,1,0:T(8,128)(2,1)} %bitcast.5), calls=%async_computation.1 | async-start | bytes 3145728 | tf_op jit(solution)/shard_map/all_to_all | solution.py:289
  137.3 13.2 %collective-permute-start.18 = (bf16[16,16,2048]{2,1,0:T(8,128)(2,1)}, bf16[16,16,2048]{2,1,0:T(8,128)(2,1)}, u32[]{:S(2)}, u32[]{:S(2)}) collective-permute-start(bf16[16,16,2048]{2,1,0:T(8,128)(2,1)} %get-tuple-element.36.refs_0_), channel_id=1, source_target_pairs={{0,1},{1,0},{2,3},{3,2},{4,5},{5,4},{6,7},{7,6},{8,9},{9,8},{10,11... | collective-permute-start | bytes 3145736 | tf_op jit(solution)/shard_map/ppermute | solution.py:36
  137.5 13.1 %collective-permute-start.19 = (bf16[16,16,2048]{2,1,0:T(8,128)(2,1)}, bf16[16,16,2048]{2,1,0:T(8,128)(2,1)}, u32[]{:S(2)}, u32[]{:S(2)}) collective-permute-start(bf16[16,16,2048]{2,1,0:T(8,128)(2,1)} %collective-permute-done.15.refs_1_), channel_id=1, source_target_pairs={{0,1},{1,0},{2,3},{3,2},{4,5},{5,4},{6,7},{7,6},{8,9},{9,8},{10,11... | collective-permute-start | bytes 3145736 | tf_op jit(solution)/shard_map/ppermute | solution.py:36
  137.9 12.6 %collective-permute-start.20 = (bf16[16,16,2048]{2,1,0:T(8,128)(2,1)}, bf16[16,16,2048]{2,1,0:T(8,128)(2,1)}, u32[]{:S(2)}, u32[]{:S(2)}) collective-permute-start(bf16[16,16,2048]{2,1,0:T(8,128)(2,1)} %collective-permute-done.16.refs_2_), channel_id=1, source_target_pairs={{0,1},{1,0},{2,3},{3,2},{4,5},{5,4},{6,7},{7,6},{8,9},{9,8},{10,11... | collective-permute-start | bytes 3145736 | tf_op jit(solution)/shard_map/ppermute | solution.py:36
  138.0 12.6 %collective-permute-start.21 = (bf16[16,16,2048]{2,1,0:T(8,128)(2,1)}, bf16[16,16,2048]{2,1,0:T(8,128)(2,1)}, u32[]{:S(2)}, u32[]{:S(2)}) collective-permute-start(bf16[16,16,2048]{2,1,0:T(8,128)(2,1)} %collective-permute-done.17.refs_3_), channel_id=1, source_target_pairs={{0,1},{1,0},{2,3},{3,2},{4,5},{5,4},{6,7},{7,6},{8,9},{9,8},{10,11... | collective-permute-start | bytes 3145736 | tf_op jit(solution)/shard_map/ppermute | solution.py:36
  146.8 27.4 %all-to-all-start.2 = ((bf16[16,128,384]{2,1,0:T(8,128)(2,1)}), bf16[16,128,384]{2,1,0:T(8,128)(2,1)S(1)}, u32[]{:S(2)}, u32[]{:S(2)}) async-start(bf16[16,128,384]{2,1,0:T(8,128)(2,1)} %bitcast.26), calls=%async_computation.2 | async-start | bytes 3145728 | tf_op jit(solution)/shard_map/all_to_all | solution.py:289
  (17 other events, 63.9 us)

commit v7 on v6

--- a/solution.py
+++ b/solution.py
@@ -206,12 +206,11 @@
 
 
 def pair_kernel(x_ref, *refs):
-    y_refs, out_ref = refs[:-1], refs[-1]
+    count = (len(refs) - 1) // 2
+    y_refs, out_ref, totals = refs[:count], refs[count], refs[count + 1 :]
     blocks, width, _ = x_ref.shape
     aux_x = x_ref.shape[2] // width
-    same = lax.broadcasted_iota(jnp.int32, (width, width), 0) == lax.broadcasted_iota(
-        jnp.int32, (width, width), 1
-    )
+    step = pl.program_id(0)
     x = jnp.concatenate(
         [
             jnp.concatenate(
@@ -221,29 +220,48 @@
         ],
         axis=0,
     )
-    done = 0
-    for y_ref in y_refs:
+    for y_ref, total in zip(y_refs, totals, strict=True):
         products = lax.dot_general(
             x, y_ref[...], (((1,), (1,)), ((), ())), preferred_element_type=jnp.float32
         )
-        aux_y = y_ref.shape[0] // width
-        for q in range(aux_y):
-            for p in range(aux_x):
-                tile = products[p * width : (p + 1) * width, q * width : (q + 1) * width]
-                tile = jnp.where(same, tile, 0.0).reshape(width // 8, 8, width)
-                out_ref[(done + q) * aux_x + p] = tile.sum(axis=0)
-        done += aux_y
+
+        @pl.when(step == 0)
+        def _():
+            total[...] = products
+
+        @pl.when(step > 0)
+        def _():
+            total[...] += products
+
+    @pl.when(step == pl.num_programs(0) - 1)
+    def _():
+        same = lax.broadcasted_iota(jnp.int32, (width, width), 0) == lax.broadcasted_iota(
+            jnp.int32, (width, width), 1
+        )
+        done = 0
+        for total in totals:
+            aux_y = total.shape[1] // width
+            for q in range(aux_y):
+                for p in range(aux_x):
+                    tile = total[p * width : (p + 1) * width, q * width : (q + 1) * width]
+                    tile = jnp.where(same, tile, 0.0).reshape(width // 8, 8, width)
+                    out_ref[(done + q) * aux_x + p] = tile.sum(axis=0)
+            done += aux_y
 
 
 def pair_sums(x, ys):
-    _, width, _ = x.shape
-    aux_x, aux_y = x.shape[2] // width, sum(y.shape[0] for y in ys) // width
+    blocks, width, columns = x.shape
+    aux_x, aux_y = columns // width, sum(y.shape[0] for y in ys) // width
+    group = blocks // 4
     sums = pl.pallas_call(
         pair_kernel,
         out_shape=jax.ShapeDtypeStruct((aux_y * aux_x, 8, width), jnp.float32),
-        in_specs=[pl.BlockSpec(memory_space=pltpu.VMEM)] * (1 + len(ys)),
-        out_specs=pl.BlockSpec(memory_space=pltpu.VMEM),
-        compiler_params=pltpu.CompilerParams(vmem_limit_bytes=16 * 1024 * 1024),
+        grid=(4,),
+        in_specs=[pl.BlockSpec((group, width, columns), lambda k: (k, 0, 0))]
+        + [pl.BlockSpec((y.shape[0], group * width), lambda k: (0, k)) for y in ys],
+        out_specs=pl.BlockSpec((aux_y * aux_x, 8, width), lambda k: (0, 0, 0)),
+        scratch_shapes=[pltpu.VMEM((columns, y.shape[0]), jnp.float32) for y in ys],
+        compiler_params=pltpu.CompilerParams(vmem_limit_bytes=60 * 1024 * 1024),
         cost_estimate=pl.CostEstimate(
             flops=2 * x.size * aux_y, bytes_accessed=6 * x.size, transcendentals=0
         ),
@@ -256,7 +274,7 @@
     x = x + other_core(x)
     x = x + permute(x, "xh", lambda k: 1 - k)
     x = x + permute(x, "y", lambda k: k ^ 1)
-    return x + permute(x, "y", lambda k: k ^ 2)
+    return x + permute(x, "y", lambda k: 3 - k)
 
 
 def shards(tensor_blocks, block_list, occ_green, virt_green):
@@ -287,6 +305,7 @@
         half = jnp.dot(occ, dense[-1], preferred_element_type=jnp.float32).astype(jnp.bfloat16)
         cut = half.reshape(col_count, width, -1)
         turned.append(lax.all_to_all(cut, COL, split_axis=0, concat_axis=0, tiled=True))
+        recv_first, _ = lax.optimization_barrier((recv_first, half))
         start += depth
 
     _, virt_pieces = lax.optimization_barrier((half, virt_pieces))

time: 196 us -> 199 us (1.015)
  Pallas kernels: 19.4 us -> 27.1 us
  waiting for transfers between devices: 99.3 us -> 92.6 us
  local copies, waits for them, and re-layouts: 15.4 us -> 10.3 us
  starting transfers between devices: 35.8 us -> 39.2 us
  matrix products: 22.2 us -> 24.4 us
    pallas_call x2, Pallas kernels: 3.59 us -> 11.9 us  [pair_sums(): pl.pallas_call(pair_kernel, out_shape=jax.ShapeDtypeStruct((aux_y * aux_x...]
    all_to_all x2, waiting for transfers between devices: 17.4 us -> 12.1 us  [shards(): lax.all_to_all(cut, COL, split_axis=0, concat_axis=0, tiled=True)]
    unnamed x27 -> x15, local copies, waits for them, and re-layouts: 12.3 us -> 8.34 us
    ppermute x20, waiting for transfers between devices: 56.2 us -> 53.4 us  [permute(): return lax.ppermute(x, AXES, moved(axis, to))]
    dot_general x2, matrix products: 6.96 us -> 9.1 us  [shards(): lax.dot_general(d, virt_t, (((0,), (0,)), ((), ())), preferred_element_ty...]
  transfers between devices with their start and end apart: 29 -> 29, of which waited for: 17 -> 15; matrix products, arithmetic and copies ran while one was open for 13% -> 14% of each run, Pallas kernels for 9% -> 11%
where the time goes in v7:
time: 199 us; the launch traced here: 198 us
  waiting for transfers between devices  92.6 us (47%)
  starting transfers between devices  39.2 us (20%)
  Pallas kernels  27.1 us (14%)
  matrix products  24.4 us (12%)
  local copies, waits for them, and re-layouts  10.3 us (5%)
  other arithmetic  4.41 us (2%)
    ppermute x20, waiting for transfers between devices, permute(): return lax.ppermute(x, AXES, moved(axis, to))  53.4 us
    all_to_all x1, waiting for transfers between devices, shards(): recv = lax.all_to_all(picked, COL, split_axis=0, concat_axis=0, tiled=True)  16.9 us
    ppermute x20, starting transfers between devices, permute(): return lax.ppermute(x, AXES, moved(axis, to))  16 us
    dot_general x2, matrix products, shards(): jnp.dot(occ, dense[-1], preferred_element_type=jnp.float32)  15.2 us
    all_to_all x2, waiting for transfers between devices, shards(): lax.all_to_all(cut, COL, split_axis=0, concat_axis=0, tiled=True)  12.1 us
    pallas_call x2, Pallas kernels, pair_sums(): pl.pallas_call(pair_kernel, out_shape=jax.ShapeDtypeStruct((aux_y * aux_x...  11.9 us
    ppermute x6, waiting for transfers between devices, hop(): return lax.ppermute(x, AXES, pairs)  10.2 us
    ppermute x6, starting transfers between devices, hop(): return lax.ppermute(x, AXES, pairs)  9.51 us
  transfers between devices with their start and end apart: 29, of which 15 were waited for; matrix products, arithmetic and copies ran while one was open for 14% of the time, Pallas kernels for 11%

profile of v7, /device:TPU:2, one launch (start us, length us, event | category | flops | bytes accessed | tf_op | source)
XLA Modules:
  0.0 198.2 jit_solution(2193849516181945982)
XLA Ops:
  22.0 5.7 %collective-permute-done.5 = bf16[4,32,2048]{2,1,0:T(8,128)(2,1)S(1)} collective-permute-done((bf16[4,32,2048]{2,1,0:T(8,128)(2,1)S(1)}, bf16[4,32,2048]{2,1,0:T(8,128)(2,1)S(1)}, u32[]{:S(2)}, u32[]{:S(2)}) %collective-permute-start.5) | collective-permute-done | bytes 524320 | tf_op jit(solution)/shard_map/ppermute | solution.py:153
  27.7 4.7 %all-to-all-start = ((bf16[16,1552,128]{2,1,0:T(8,128)(2,1)}), bf16[16,1552,128]{2,1,0:T(8,128)(2,1)}, u32[]{:S(2)}, u32[]{:S(2)}) async-start(bf16[16,1552,128]{2,1,0:T(8,128)(2,1)} %copy-done), calls=%async_computation | async-start | bytes 12713984 | tf_op jit(solution)/shard_map/all_to_all | solution.py:292
  37.0 23.5 %collective-permute-done.6.refs_1_ = bf16[16,16,2048]{2,1,0:T(8,128)(2,1)S(1)} collective-permute-done((bf16[16,16,2048]{2,1,0:T(8,128)(2,1)S(1)}, bf16[16,16,2048]{2,1,0:T(8,128)(2,1)S(1)}, u32[]{:S(2)}, u32[]{:S(2)}) %collective-permute-start.6) | collective-permute-done | bytes 1048608 | tf_op jit(solution)/shard_map/ppermute | solution.py:36
  60.7 3.3 %collective-permute-start.9 = (bf16[8,16,2048]{2,1,0:T(8,128)(2,1)S(1)}, bf16[8,16,2048]{2,1,0:T(8,128)(2,1)S(1)}, u32[]{:S(2)}, u32[]{:S(2)}) collective-permute-start(bf16[8,16,2048]{2,1,0:T(8,128)(2,1)S(1)} %slice.22), channel_id=1, source_target_pairs={{0,96},{1,97},{2,98},{3,99},{4,100},{5,101},{6,102},{7,103},{8,104... | collective-permute-start | bytes 1572872 | tf_op jit(solution)/shard_map/ppermute | solution.py:36
  63.9 11.5 %collective-permute-done.8.refs_3_ = bf16[8,16,2048]{2,1,0:T(8,128)(2,1)S(1)} collective-permute-done((bf16[8,16,2048]{2,1,0:T(8,128)(2,1)S(1)}, bf16[8,16,2048]{2,1,0:T(8,128)(2,1)S(1)}, u32[]{:S(2)}, u32[]{:S(2)}) %collective-permute-start.8) | collective-permute-done | bytes 524320 | tf_op jit(solution)/shard_map/ppermute | solution.py:36
  76.5 5.4 %collective-permute-done.13.refs_8_ = bf16[8,16,2048]{2,1,0:T(8,128)(2,1)S(1)} collective-permute-done((bf16[8,16,2048]{2,1,0:T(8,128)(2,1)S(1)}, bf16[8,16,2048]{2,1,0:T(8,128)(2,1)S(1)}, u32[]{:S(2)}, u32[]{:S(2)}) %collective-permute-start.13) | collective-permute-done | bytes 524320 | tf_op jit(solution)/shard_map/ppermute | solution.py:36
  87.3 3.3 %copy-done.1 = bf16[4,2,4,2,2,16,2048]{6,5,4,3,2,1,0:T(8,128)(2,1)} copy-done((bf16[4,2,4,2,2,16,2048]{6,5,4,3,2,1,0:T(8,128)(2,1)}, bf16[4,2,4,2,2,16,2048]{6,5,4,3,2,1,0:T(8,128)(2,1)S(1)}, u32[]{:S(2)}) %copy-start.1) | copy-done | bytes 8388632
  90.5 16.9 %all-to-all-done.refs_0_.refs_1_ = bf16[16,1552,128]{2,1,0:T(8,128)(2,1)} async-done(((bf16[16,1552,128]{2,1,0:T(8,128)(2,1)}), bf16[16,1552,128]{2,1,0:T(8,128)(2,1)}, u32[]{:S(2)}, u32[]{:S(2)}) %all-to-all-start) | async-done | bytes 6357024 | tf_op jit(solution)/shard_map/all_to_all | solution.py:292
  108.7 4.9 %place.2 = bf16[2048,384]{1,0:T(8,128)(2,1)S(1)} custom-call(s32[32]{0:T(128)S(1)} %sub.7.first_ref, bf16[16,1552,128]{2,1,0:T(8,128)(2,1)} %all-to-all-done.refs_0_.refs_1_, bf16[16,1552,128]{2,1,0:T(8,128)(2,1)} %all-to-all-done.refs_0_.refs_1_), custom_call_target="tpu_custom_call" | custom-call | flops 1572864 | bytes 6291456 | tf_op jit(solution)/shard_map/place/pallas_call | solution.py:124
  113.6 5.6 %convolution_convert_fusion.3 = bf16[2048,384]{1,0:T(8,128)(2,1)} fusion(bf16[2048,2048]{1,0:T(8,128)(2,1)S(1)} %bitcast.22, bf16[2048,384]{1,0:T(8,128)(2,1)S(1)} %place.2), kind=kOutput, calls=%fused_computation.3 | convolution fusion | flops 3222011904 | bytes 11534336 | tf_op jit(solution)/shard_map/dot_general | solution.py:305
  119.2 4.6 %all-to-all-start.1 = ((bf16[16,128,384]{2,1,0:T(8,128)(2,1)}), bf16[16,128,384]{2,1,0:T(8,128)(2,1)}, u32[]{:S(2)}, u32[]{:S(2)}) async-start(bf16[16,128,384]{2,1,0:T(8,128)(2,1)} %bitcast.27), calls=%async_computation.1 | async-start | bytes 3145728 | tf_op jit(solution)/shard_map/all_to_all | solution.py:307
  123.8 4.4 %place.3 = bf16[2048,384]{1,0:T(8,128)(2,1)S(1)} custom-call(s32[32]{0:T(128)S(1)} %sub.7.first_ref, bf16[16,1552,128]{2,1,0:T(8,128)(2,1)} %all-to-all-done.refs_0_.refs_1_, bf16[16,1552,128]{2,1,0:T(8,128)(2,1)} %all-to-all-done.refs_0_.refs_1_), custom_call_target="tpu_custom_call" | custom-call | flops 1572864 | bytes 6291456 | tf_op jit(solution)/shard_map/place/pallas_call | solution.py:124
  128.2 9.7 %convolution_convert_fusion.2 = bf16[2048,384]{1,0:T(8,128)(2,1)} fusion(bf16[2048,2048]{1,0:T(8,128)(2,1)} %bitcast.21, bf16[2048,384]{1,0:T(8,128)(2,1)S(1)} %place.3), kind=kOutput, calls=%fused_computation.2 | convolution fusion | flops 3222011904 | bytes 11534336 | tf_op jit(solution)/shard_map/dot_general | solution.py:305
  139.0 8.4 %all-to-all-done.1.x_ref = bf16[16,128,384]{2,1,0:T(8,128)(2,1)} async-done(((bf16[16,128,384]{2,1,0:T(8,128)(2,1)}), bf16[16,128,384]{2,1,0:T(8,128)(2,1)}, u32[]{:S(2)}, u32[]{:S(2)}) %all-to-all-start.1) | async-done | bytes 1572896 | tf_op jit(solution)/shard_map/all_to_all | solution.py:307
  147.4 4.4 %all-to-all-start.2 = ((bf16[16,128,384]{2,1,0:T(8,128)(2,1)}), bf16[16,128,384]{2,1,0:T(8,128)(2,1)}, u32[]{:S(2)}, u32[]{:S(2)}) async-start(bf16[16,128,384]{2,1,0:T(8,128)(2,1)} %bitcast.26), calls=%async_computation.2 | async-start | bytes 3145728 | tf_op jit(solution)/shard_map/all_to_all | solution.py:307
  151.8 3.8 %lay.3 = bf16[4,2,4,2,2,16,2048]{6,5,4,3,2,1,0:T(8,128)(2,1)S(1)} custom-call(bf16[16,16,2048]{2,1,0:T(8,128)(2,1)S(1)} %get-tuple-element.38.refs_0_, bf16[16,16,2048]{2,1,0:T(8,128)(2,1)} %collective-permute-done.15.refs_1_, bf16[16,16,2048]{2,1,0:T(8,128)(2,1)} %collective-permute-done.16.refs_2_, bf16[16,16,2048]{2,1,0:T(8,128)(2,1)} %collective-permute-done.17.refs_3_, ...), custom_call_target="tpu_custom_call" | custom-call | bytes 16777216 | tf_op jit(solution)/shard_map/lay/pallas_call | solution.py:175
  155.6 4.5 %convolution_convert_fusion.refs_1_ = bf16[384,2048]{1,0:T(8,128)(2,1)} fusion(bf16[2048,384]{1,0:T(8,128)(2,1)S(1)} %copy-done.5, bf16[2048,2048]{1,0:T(8,128)(2,1)S(1)} %bitcast.23), kind=kOutput, calls=%fused_computation | convolution fusion | flops 3222011904 | bytes 11534336 | tf_op jit(solution)/shard_map/dot_general | solution.py:316
  160.2 4.6 %convolution_convert_fusion.1.refs_0_ = bf16[384,2048]{1,0:T(8,128)(2,1)} fusion(bf16[2048,384]{1,0:T(8,128)(2,1)S(1)} %place.2, bf16[2048,2048]{1,0:T(8,128)(2,1)S(1)} %bitcast.24), kind=kOutput, calls=%fused_computation.1 | convolution fusion | flops 3222011904 | bytes 11534336 | tf_op jit(solution)/shard_map/dot_general | solution.py:316
  164.7 5.9 %pair.2 = f32[18,8,128]{2,1,0:T(8,128)} custom-call(bf16[16,128,384]{2,1,0:T(8,128)(2,1)} %all-to-all-done.1.x_ref, bf16[384,2048]{1,0:T(8,128)(2,1)} %convolution_convert_fusion.1.refs_0_, bf16[384,2048]{1,0:T(8,128)(2,1)} %convolution_convert_fusion.refs_1_), custom_call_target="tpu_custom_call" | custom-call | flops 9437184 | bytes 4718592 | tf_op jit(solution)/shard_map/pair/pallas_call | solution.py:256
  171.9 3.7 %all-to-all-done.2.x_ref = bf16[16,128,384]{2,1,0:T(8,128)(2,1)} async-done(((bf16[16,128,384]{2,1,0:T(8,128)(2,1)}), bf16[16,128,384]{2,1,0:T(8,128)(2,1)}, u32[]{:S(2)}, u32[]{:S(2)}) %all-to-all-start.2) | async-done | bytes 1572896 | tf_op jit(solution)/shard_map/all_to_all | solution.py:307
  175.6 5.9 %pair.3 = f32[18,8,128]{2,1,0:T(8,128)} custom-call(bf16[16,128,384]{2,1,0:T(8,128)(2,1)} %all-to-all-done.2.x_ref, bf16[384,2048]{1,0:T(8,128)(2,1)} %convolution_convert_fusion.1.refs_0_, bf16[384,2048]{1,0:T(8,128)(2,1)} %convolution_convert_fusion.refs_1_), custom_call_target="tpu_custom_call" | custom-call | flops 9437184 | bytes 4718592 | tf_op jit(solution)/shard_map/pair/pallas_call | solution.py:256
  184.7 4.5 %collective-permute-done.23 = f32[6,6]{0,1:T(8,128)S(1)} collective-permute-done((f32[6,6]{0,1:T(8,128)S(1)}, f32[6,6]{0,1:T(8,128)S(1)}, u32[]{:S(2)}, u32[]{:S(2)}) %collective-permute-start.23) | collective-permute-done | bytes 176 | tf_op jit(solution)/shard_map/ppermute | solution.py:36
  189.4 3.3 %collective-permute-done.24 = f32[6,6]{0,1:T(8,128)S(1)} collective-permute-done((f32[6,6]{0,1:T(8,128)S(1)}, f32[6,6]{0,1:T(8,128)S(1)}, u32[]{:S(2)}, u32[]{:S(2)}) %collective-permute-start.24) | collective-permute-done | bytes 176 | tf_op jit(solution)/shard_map/ppermute | solution.py:36
  194.2 3.3 %collective-permute-done.25 = f32[6,6]{0,1:T(8,128)S(1)} collective-permute-done((f32[6,6]{0,1:T(8,128)S(1)}, f32[6,6]{0,1:T(8,128)S(1)}, u32[]{:S(2)}, u32[]{:S(2)}) %collective-permute-start.25) | collective-permute-done | bytes 176 | tf_op jit(solution)/shard_map/ppermute | solution.py:36
  (79 shorter events, 42.2 us)
Async XLA Ops:
  0.9 6.2 %collective-permute-start = (bf16[1,32,2048]{2,1,0:T(8,128)(2,1)S(1)}, bf16[1,32,2048]{2,1,0:T(8,128)(2,1)S(1)}, u32[]{:S(2)}, u32[]{:S(2)}) collective-permute-start(bf16[1,32,2048]{2,1,0:T(8,128)(2,1)S(1)} %maximum_bitcast_fusion), channel_id=1, source_target_pairs={{0,4},{1,17},{2,6},{3,19},{4,8},{5,21},{6,10},{7,23},{8,12},{9,25}... | collective-permute-start | bytes 393224 | tf_op jit(solution)/shard_map/ppermute | solution.py:153
  4.2 6.5 %collective-permute-start.2 = (bf16[1,32,2048]{2,1,0:T(8,128)(2,1)S(1)}, bf16[1,32,2048]{2,1,0:T(8,128)(2,1)S(1)}, u32[]{:S(2)}, u32[]{:S(2)}) collective-permute-start(bf16[1,32,2048]{2,1,0:T(8,128)(2,1)S(1)} %maximum_bitcast_fusion), channel_id=1, source_target_pairs={{0,8},{1,3},{2,10},{3,1},{4,12},{5,7},{6,14},{7,5},{8,0},{9,11},{1... | collective-permute-start | bytes 393224 | tf_op jit(solution)/shard_map/ppermute | solution.py:153
  10.7 11.3 %collective-permute-start.3 = (bf16[4,32,2048]{2,1,0:T(8,128)(2,1)S(1)}, bf16[4,32,2048]{2,1,0:T(8,128)(2,1)S(1)}, u32[]{:S(2)}, u32[]{:S(2)}) collective-permute-start(bf16[4,32,2048]{2,1,0:T(8,128)(2,1)S(1)} %pad_maximum_fusion), channel_id=1, source_target_pairs={{0,16},{1,5},{2,18},{3,7},{4,20},{5,9},{6,22},{7,11},{8,24},{9,13}... | collective-permute-start | bytes 1572872 | tf_op jit(solution)/shard_map/ppermute | solution.py:153
  12.3 9.7 %collective-permute-start.4 = (bf16[4,32,2048]{2,1,0:T(8,128)(2,1)S(1)}, bf16[4,32,2048]{2,1,0:T(8,128)(2,1)S(1)}, u32[]{:S(2)}, u32[]{:S(2)}) collective-permute-start(bf16[4,32,2048]{2,1,0:T(8,128)(2,1)S(1)} %pad_maximum_fusion), channel_id=1, source_target_pairs={{0,18},{1,13},{2,16},{3,15},{4,22},{5,1},{6,20},{7,3},{8,26},{9,5}... | collective-permute-start | bytes 1572872 | tf_op jit(solution)/shard_map/ppermute | solution.py:153
  12.8 14.9 %collective-permute-start.5 = (bf16[4,32,2048]{2,1,0:T(8,128)(2,1)S(1)}, bf16[4,32,2048]{2,1,0:T(8,128)(2,1)S(1)}, u32[]{:S(2)}, u32[]{:S(2)}) collective-permute-start(bf16[4,32,2048]{2,1,0:T(8,128)(2,1)S(1)} %pad_maximum_fusion), channel_id=1, source_target_pairs={{0,2},{1,9},{2,0},{3,11},{4,6},{5,13},{6,4},{7,15},{8,10},{9,1},{1... | collective-permute-start | bytes 1572872 | tf_op jit(solution)/shard_map/ppermute | solution.py:153
  27.7 79.7 %all-to-all-start = ((bf16[16,1552,128]{2,1,0:T(8,128)(2,1)}), bf16[16,1552,128]{2,1,0:T(8,128)(2,1)}, u32[]{:S(2)}, u32[]{:S(2)}) async-start(bf16[16,1552,128]{2,1,0:T(8,128)(2,1)} %copy-done), calls=%async_computation | async-start | bytes 12713984 | tf_op jit(solution)/shard_map/all_to_all | solution.py:292
  32.8 27.7 %collective-permute-start.6 = (bf16[16,16,2048]{2,1,0:T(8,128)(2,1)S(1)}, bf16[16,16,2048]{2,1,0:T(8,128)(2,1)S(1)}, u32[]{:S(2)}, u32[]{:S(2)}) collective-permute-start(bf16[16,16,2048]{2,1,0:T(8,128)(2,1)S(1)} %get-tuple-element.30.refs_0_), channel_id=1, source_target_pairs={{0,32},{1,33},{2,34},{3,35},{4,36},{5,37},{6,38},{7,39},{8,40},{9,... | collective-permute-start | bytes 3145736 | tf_op jit(solution)/shard_map/ppermute | solution.py:36
  34.8 25.8 %collective-permute-start.7 = (bf16[16,16,2048]{2,1,0:T(8,128)(2,1)S(1)}, bf16[16,16,2048]{2,1,0:T(8,128)(2,1)S(1)}, u32[]{:S(2)}, u32[]{:S(2)}) collective-permute-start(bf16[16,16,2048]{2,1,0:T(8,128)(2,1)S(1)} %get-tuple-element.30.refs_0_), channel_id=1, source_target_pairs={{0,96},{1,97},{2,98},{3,99},{4,100},{5,101},{6,102},{7,103},{8,104... | collective-permute-start | bytes 3145736 | tf_op jit(solution)/shard_map/ppermute | solution.py:36
  60.5 14.9 %collective-permute-start.8 = (bf16[8,16,2048]{2,1,0:T(8,128)(2,1)S(1)}, bf16[8,16,2048]{2,1,0:T(8,128)(2,1)S(1)}, u32[]{:S(2)}, u32[]{:S(2)}) collective-permute-start(bf16[8,16,2048]{2,1,0:T(8,128)(2,1)S(1)} %slice.21), channel_id=1, source_target_pairs={{0,32},{1,33},{2,34},{3,35},{4,36},{5,37},{6,38},{7,39},{8,40},{9,... | collective-permute-start | bytes 1572872 | tf_op jit(solution)/shard_map/ppermute | solution.py:36
  60.7 14.8 %collective-permute-start.9 = (bf16[8,16,2048]{2,1,0:T(8,128)(2,1)S(1)}, bf16[8,16,2048]{2,1,0:T(8,128)(2,1)S(1)}, u32[]{:S(2)}, u32[]{:S(2)}) collective-permute-start(bf16[8,16,2048]{2,1,0:T(8,128)(2,1)S(1)} %slice.22), channel_id=1, source_target_pairs={{0,96},{1,97},{2,98},{3,99},{4,100},{5,101},{6,102},{7,103},{8,104... | collective-permute-start | bytes 1572872 | tf_op jit(solution)/shard_map/ppermute | solution.py:36
  75.5 10.2 %collective-permute-start.10 = (bf16[16,16,2048]{2,1,0:T(8,128)(2,1)S(1)}, bf16[16,16,2048]{2,1,0:T(8,128)(2,1)S(1)}, u32[]{:S(2)}, u32[]{:S(2)}) collective-permute-start(bf16[16,16,2048]{2,1,0:T(8,128)(2,1)S(1)} %get-tuple-element.30.refs_0_), channel_id=1, source_target_pairs={{0,1},{1,0},{2,3},{3,2},{4,5},{5,4},{6,7},{7,6},{8,9},{9,8},{10,11... | collective-permute-start | bytes 3145736 | tf_op jit(solution)/shard_map/ppermute | solution.py:36
  75.5 11.0 %collective-permute-start.11 = (bf16[16,16,2048]{2,1,0:T(8,128)(2,1)S(1)}, bf16[16,16,2048]{2,1,0:T(8,128)(2,1)S(1)}, u32[]{:S(2)}, u32[]{:S(2)}) collective-permute-start(bf16[16,16,2048]{2,1,0:T(8,128)(2,1)S(1)} %collective-permute-done.6.refs_1_), channel_id=1, source_target_pairs={{0,1},{1,0},{2,3},{3,2},{4,5},{5,4},{6,7},{7,6},{8,9},{9,8},{10,11... | collective-permute-start | bytes 3145736 | tf_op jit(solution)/shard_map/ppermute | solution.py:36
  76.0 10.5 %collective-permute-start.12 = (bf16[16,16,2048]{2,1,0:T(8,128)(2,1)S(1)}, bf16[16,16,2048]{2,1,0:T(8,128)(2,1)S(1)}, u32[]{:S(2)}, u32[]{:S(2)}) collective-permute-start(bf16[16,16,2048]{2,1,0:T(8,128)(2,1)S(1)} %collective-permute-done.7.refs_2_), channel_id=1, source_target_pairs={{0,1},{1,0},{2,3},{3,2},{4,5},{5,4},{6,7},{7,6},{8,9},{9,8},{10,11... | collective-permute-start | bytes 3145736 | tf_op jit(solution)/shard_map/ppermute | solution.py:36
  76.0 5.9 %collective-permute-start.13 = (bf16[8,16,2048]{2,1,0:T(8,128)(2,1)S(1)}, bf16[8,16,2048]{2,1,0:T(8,128)(2,1)S(1)}, u32[]{:S(2)}, u32[]{:S(2)}) collective-permute-start(bf16[8,16,2048]{2,1,0:T(8,128)(2,1)S(1)} %collective-permute-done.8.refs_3_), channel_id=1, source_target_pairs={{0,1},{1,0},{2,3},{3,2},{4,5},{5,4},{6,7},{7,6},{8,9},{9,8},{10,11... | collective-permute-start | bytes 1572872 | tf_op jit(solution)/shard_map/ppermute | solution.py:36
  76.5 6.1 %collective-permute-start.14 = (bf16[8,16,2048]{2,1,0:T(8,128)(2,1)S(1)}, bf16[8,16,2048]{2,1,0:T(8,128)(2,1)S(1)}, u32[]{:S(2)}, u32[]{:S(2)}) collective-permute-start(bf16[8,16,2048]{2,1,0:T(8,128)(2,1)S(1)} %collective-permute-done.9.refs_4_), channel_id=1, source_target_pairs={{0,1},{1,0},{2,3},{3,2},{4,5},{5,4},{6,7},{7,6},{8,9},{9,8},{10,11... | collective-permute-start | bytes 1572872 | tf_op jit(solution)/shard_map/ppermute | solution.py:36
  81.9 56.0 %collective-permute-start.15 = (bf16[16,16,2048]{2,1,0:T(8,128)(2,1)S(1)}, bf16[16,16,2048]{2,1,0:T(8,128)(2,1)}, u32[]{:S(2)}, u32[]{:S(2)}) collective-permute-start(bf16[16,16,2048]{2,1,0:T(8,128)(2,1)S(1)} %get-tuple-element.38.refs_0_), channel_id=1, source_target_pairs={{0,32},{1,33},{2,34},{3,35},{4,36},{5,37},{6,38},{7,39},{8,40},{9,... | collective-permute-start | bytes 3145736 | tf_op jit(solution)/shard_map/ppermute | solution.py:36
  82.6 55.2 %collective-permute-start.16 = (bf16[16,16,2048]{2,1,0:T(8,128)(2,1)S(1)}, bf16[16,16,2048]{2,1,0:T(8,128)(2,1)}, u32[]{:S(2)}, u32[]{:S(2)}) collective-permute-start(bf16[16,16,2048]{2,1,0:T(8,128)(2,1)S(1)} %get-tuple-element.38.refs_0_), channel_id=1, source_target_pairs={{0,96},{1,97},{2,98},{3,99},{4,100},{5,101},{6,102},{7,103},{8,104... | collective-permute-start | bytes 3145736 | tf_op jit(solution)/shard_map/ppermute | solution.py:36
  85.7 52.2 %collective-permute-start.17 = (bf16[16,16,2048]{2,1,0:T(8,128)(2,1)S(1)}, bf16[16,16,2048]{2,1,0:T(8,128)(2,1)}, u32[]{:S(2)}, u32[]{:S(2)}) collective-permute-start(bf16[16,16,2048]{2,1,0:T(8,128)(2,1)S(1)} %get-tuple-element.38.refs_0_), channel_id=1, source_target_pairs={{0,64},{1,65},{2,66},{3,67},{4,68},{5,69},{6,70},{7,71},{8,72},{9,... | collective-permute-start | bytes 3145736 | tf_op jit(solution)/shard_map/ppermute | solution.py:36
  119.2 28.2 %all-to-all-start.1 = ((bf16[16,128,384]{2,1,0:T(8,128)(2,1)}), bf16[16,128,384]{2,1,0:T(8,128)(2,1)}, u32[]{:S(2)}, u32[]{:S(2)}) async-start(bf16[16,128,384]{2,1,0:T(8,128)(2,1)} %bitcast.27), calls=%async_computation.1 | async-start | bytes 3145728 | tf_op jit(solution)/shard_map/all_to_all | solution.py:307
  137.9 13.9 %collective-permute-start.18 = (bf16[16,16,2048]{2,1,0:T(8,128)(2,1)S(1)}, bf16[16,16,2048]{2,1,0:T(8,128)(2,1)}, u32[]{:S(2)}, u32[]{:S(2)}) collective-permute-start(bf16[16,16,2048]{2,1,0:T(8,128)(2,1)S(1)} %get-tuple-element.38.refs_0_), channel_id=1, source_target_pairs={{0,1},{1,0},{2,3},{3,2},{4,5},{5,4},{6,7},{7,6},{8,9},{9,8},{10,11... | collective-permute-start | bytes 3145736 | tf_op jit(solution)/shard_map/ppermute | solution.py:36
  138.0 13.8 %collective-permute-start.19 = (bf16[16,16,2048]{2,1,0:T(8,128)(2,1)}, bf16[16,16,2048]{2,1,0:T(8,128)(2,1)}, u32[]{:S(2)}, u32[]{:S(2)}) collective-permute-start(bf16[16,16,2048]{2,1,0:T(8,128)(2,1)} %collective-permute-done.15.refs_1_), channel_id=1, source_target_pairs={{0,1},{1,0},{2,3},{3,2},{4,5},{5,4},{6,7},{7,6},{8,9},{9,8},{10,11... | collective-permute-start | bytes 3145736 | tf_op jit(solution)/shard_map/ppermute | solution.py:36
  138.5 13.4 %collective-permute-start.20 = (bf16[16,16,2048]{2,1,0:T(8,128)(2,1)}, bf16[16,16,2048]{2,1,0:T(8,128)(2,1)}, u32[]{:S(2)}, u32[]{:S(2)}) collective-permute-start(bf16[16,16,2048]{2,1,0:T(8,128)(2,1)} %collective-permute-done.16.refs_2_), channel_id=1, source_target_pairs={{0,1},{1,0},{2,3},{3,2},{4,5},{5,4},{6,7},{7,6},{8,9},{9,8},{10,11... | collective-permute-start | bytes 3145736 | tf_op jit(solution)/shard_map/ppermute | solution.py:36
  138.6 13.3 %collective-permute-start.21 = (bf16[16,16,2048]{2,1,0:T(8,128)(2,1)}, bf16[16,16,2048]{2,1,0:T(8,128)(2,1)}, u32[]{:S(2)}, u32[]{:S(2)}) collective-permute-start(bf16[16,16,2048]{2,1,0:T(8,128)(2,1)} %collective-permute-done.17.refs_3_), channel_id=1, source_target_pairs={{0,1},{1,0},{2,3},{3,2},{4,5},{5,4},{6,7},{7,6},{8,9},{9,8},{10,11... | collective-permute-start | bytes 3145736 | tf_op jit(solution)/shard_map/ppermute | solution.py:36
  147.4 28.2 %all-to-all-start.2 = ((bf16[16,128,384]{2,1,0:T(8,128)(2,1)}), bf16[16,128,384]{2,1,0:T(8,128)(2,1)}, u32[]{:S(2)}, u32[]{:S(2)}) async-start(bf16[16,128,384]{2,1,0:T(8,128)(2,1)} %bitcast.26), calls=%async_computation.2 | async-start | bytes 3145728 | tf_op jit(solution)/shard_map/all_to_all | solution.py:307
  (11 other events, 46.4 us)

commit v8 on v6

--- a/solution.py
+++ b/solution.py
@@ -9,7 +9,7 @@
 from jax.sharding import PartitionSpec as P
 
 CAP = 2
-CHUNKS = (3, 3)
+CHUNKS = (2, 4)
 NOTE = 16
 AXES = ("z", "xl", "y", "xh", "core")
 SIZES = (4, 2, 4, 2, 2)
@@ -110,7 +110,7 @@
 
         return carry
 
-    lax.fori_loop(0, slot_refs[0].shape[0], body, 0)
+    lax.fori_loop(0, slot_refs[0].shape[0], body, 0, unroll=4)
     out_ref[...] = total[...].astype(out_ref.dtype)
 
 
@@ -161,28 +161,52 @@
     pieces, out_ref = refs[:-1], refs[-1]
     z, y, core = lax.axis_index("z"), lax.axis_index("y"), lax.axis_index("core")
     x = 2 * lax.axis_index("xh") + lax.axis_index("xl")
-    for piece, (side, dz, start) in zip(pieces, spots, strict=True):
-        source = (core + side) % 2
+    for piece, (dz, start) in zip(pieces, spots, strict=True):
         for i in range(piece.shape[0]):
             late, early = FROM[(start + i) // 4], FROM[(start + i) % 4]
-            to_x = (x + 4 + late + (early - late) * source) % 4
-            to_y = (y + 4 + early + (late - early) * source) % 4
-            out_ref[(z + 4 + dz) % 4, to_x % 2, to_y, to_x // 2, source] = piece[i]
+            to_x = (x + 4 + late + (early - late) * core) % 4
+            to_y = (y + 4 + early + (late - early) * core) % 4
+            out_ref[(z + 4 + dz) % 4, to_x % 2, to_y, to_x // 2] = piece[i]
 
 
 def lay(spots, pieces):
     _, rows, columns = pieces[0].shape
     out = pl.pallas_call(
         functools.partial(lay_kernel, spots),
-        out_shape=jax.ShapeDtypeStruct((*SIZES, rows, columns), pieces[0].dtype),
+        out_shape=jax.ShapeDtypeStruct((*SIZES[:-1], rows, columns), pieces[0].dtype),
         in_specs=[pl.BlockSpec(memory_space=pltpu.VMEM)] * len(pieces),
         out_specs=pl.BlockSpec(memory_space=pltpu.VMEM),
-        compiler_params=pltpu.CompilerParams(vmem_limit_bytes=20 * 1024 * 1024),
+        compiler_params=pltpu.CompilerParams(vmem_limit_bytes=10 * 1024 * 1024),
         cost_estimate=pl.CostEstimate(
-            flops=0, bytes_accessed=512 * rows * columns, transcendentals=0
+            flops=0, bytes_accessed=256 * rows * columns, transcendentals=0
         ),
         name="lay",
     )(*pieces)
+    return out.reshape(-1, rows, columns)
+
+
+def merge_kernel(mine_ref, other_ref, out_ref):
+    core = lax.axis_index("core")
+
+    def body(i, carry):
+        out_ref[i, core] = mine_ref[i]
+        out_ref[i, 1 - core] = other_ref[i]
+        return carry
+
+    lax.fori_loop(0, mine_ref.shape[0], body, 0, unroll=2)
+
+
+def merge(mine, other):
+    chips, rows, columns = mine.shape
+    out = pl.pallas_call(
+        merge_kernel,
+        out_shape=jax.ShapeDtypeStruct((chips, 2, rows, columns), mine.dtype),
+        in_specs=[pl.BlockSpec(memory_space=pltpu.VMEM)] * 2,
+        out_specs=pl.BlockSpec(memory_space=pltpu.VMEM),
+        compiler_params=pltpu.CompilerParams(vmem_limit_bytes=20 * 1024 * 1024),
+        cost_estimate=pl.CostEstimate(flops=0, bytes_accessed=8 * mine.size, transcendentals=0),
+        name="merge",
+    )(mine, other)
     return out.reshape(-1, columns)
 
 
@@ -198,11 +222,6 @@
 
 def z_direct(mine):
     return [mine, up(mine), down(mine), up(mine, 2)]
-
-
-def assemble(spots, pieces, copies):
-    spots = [(side, *spot) for side in range(2) for spot in spots]
-    return lay(spots, pieces + copies)
 
 
 def pair_kernel(x_ref, *refs):
@@ -256,7 +275,7 @@
     x = x + other_core(x)
     x = x + permute(x, "xh", lambda k: 1 - k)
     x = x + permute(x, "y", lambda k: k ^ 1)
-    return x + permute(x, "y", lambda k: k ^ 2)
+    return x + permute(x, "y", lambda k: 3 - k)
 
 
 def shards(tensor_blocks, block_list, occ_green, virt_green):
@@ -279,7 +298,8 @@
     occ_pieces = z_forwarded(occ_plane)
     occ_pieces, virt_plane = lax.optimization_barrier((occ_pieces, virt_plane))
     virt_pieces = z_direct(virt_plane)
-    occ = assemble(FORWARDED, occ_pieces, [other_core(p) for p in occ_pieces])
+    occ_mine = lay(FORWARDED, occ_pieces)
+    occ = merge(occ_mine, other_core(occ_mine))
 
     dense, turned, start = [], [], 0
     for depth in CHUNKS:
@@ -287,12 +307,13 @@
         half = jnp.dot(occ, dense[-1], preferred_element_type=jnp.float32).astype(jnp.bfloat16)
         cut = half.reshape(col_count, width, -1)
         turned.append(lax.all_to_all(cut, COL, split_axis=0, concat_axis=0, tiled=True))
+        recv_first, _ = lax.optimization_barrier((recv_first, half))
         start += depth
 
     _, virt_pieces = lax.optimization_barrier((half, virt_pieces))
-    virt_copies = [other_core(p) for p in virt_pieces]
-    turned[0], virt_copies = lax.optimization_barrier((turned[0], virt_copies))
-    virt_t = assemble(DIRECT, virt_pieces, virt_copies)
+    virt_mine = lay(DIRECT, virt_pieces)
+    turned[0], virt_mine = lax.optimization_barrier((turned[0], virt_mine))
+    virt_t = merge(virt_mine, other_core(virt_mine))
     virt_half = [
         lax.dot_general(
             d, virt_t, (((0,), (0,)), ((), ())), preferred_element_type=jnp.float32

time: 196 us -> 197 us (level)
  local copies, waits for them, and re-layouts: 15.4 us -> 23.8 us
  waiting for transfers between devices: 99.3 us -> 91.1 us
  starting transfers between devices: 35.8 us -> 39.9 us
    unnamed x27 -> x31, local copies, waits for them, and re-layouts: 12.3 us -> 19.5 us
    ppermute x20 -> x13, waiting for transfers between devices: 56.2 us -> 49.7 us  [permute(): return lax.ppermute(x, AXES, moved(axis, to))]
    pallas_call x0 -> x2, Pallas kernels: none -> 3.51 us  [merge(): pl.pallas_call(merge_kernel, out_shape=jax.ShapeDtypeStruct((chips, 2, ro...]
    all_to_all x2, starting transfers between devices: 7.6 us -> 10.8 us  [shards(): lax.all_to_all(cut, COL, split_axis=0, concat_axis=0, tiled=True)]
    pallas_call x2, Pallas kernels: 5.14 us -> 2.25 us  [lay(): pl.pallas_call(functools.partial(lay_kernel, spots), out_shape=jax.ShapeD...]
    all_to_all x2, waiting for transfers between devices: 17.4 us -> 14.7 us  [shards(): lax.all_to_all(cut, COL, split_axis=0, concat_axis=0, tiled=True)]
    ppermute x20 -> x13, starting transfers between devices: 14 us -> 14.9 us  [permute(): return lax.ppermute(x, AXES, moved(axis, to))]
  transfers between devices with their start and end apart: 29 -> 22, of which waited for: 17 -> 13; matrix products, arithmetic and copies ran while one was open for 13% -> 14% of each run, Pallas kernels for 9% -> 8%
where the time goes in v8:
time: 197 us; the launch traced here: 196 us
  waiting for transfers between devices  91.1 us (46%)
  starting transfers between devices  39.9 us (20%)
  local copies, waits for them, and re-layouts  23.8 us (12%)
  matrix products  20.5 us (10%)
  Pallas kernels  18.2 us (9%)
  other arithmetic  2.64 us (1%)
    ppermute x13, waiting for transfers between devices, permute(): return lax.ppermute(x, AXES, moved(axis, to))  49.7 us
    unnamed x31, local copies, waits for them, and re-layouts  19.5 us
    all_to_all x1, waiting for transfers between devices, shards(): recv = lax.all_to_all(picked, COL, split_axis=0, concat_axis=0, tiled=True)  16.6 us
    ppermute x13, starting transfers between devices, permute(): return lax.ppermute(x, AXES, moved(axis, to))  14.9 us
    all_to_all x2, waiting for transfers between devices, shards(): lax.all_to_all(cut, COL, split_axis=0, concat_axis=0, tiled=True)  14.7 us
    dot_general x2, matrix products, shards(): jnp.dot(occ, dense[-1], preferred_element_type=jnp.float32)  13.4 us
    all_to_all x2, starting transfers between devices, shards(): lax.all_to_all(cut, COL, split_axis=0, concat_axis=0, tiled=True)  10.8 us
    ppermute x6, waiting for transfers between devices, hop(): return lax.ppermute(x, AXES, pairs)  10.2 us
  transfers between devices with their start and end apart: 22, of which 13 were waited for; matrix products, arithmetic and copies ran while one was open for 14% of the time, Pallas kernels for 8%

profile of v8, /device:TPU:2, one launch (start us, length us, event | category | flops | bytes accessed | tf_op | source)
XLA Modules:
  0.0 196.5 jit_solution(157605608155801622)
XLA Ops:
  7.5 3.2 %collective-permute-done.2 = bf16[1,32,2048]{2,1,0:T(8,128)(2,1)S(1)} collective-permute-done((bf16[1,32,2048]{2,1,0:T(8,128)(2,1)S(1)}, bf16[1,32,2048]{2,1,0:T(8,128)(2,1)S(1)}, u32[]{:S(2)}, u32[]{:S(2)}) %collective-permute-start.2) | collective-permute-done | bytes 131104 | tf_op jit(solution)/shard_map/ppermute | solution.py:153
  19.4 2.6 %copy-done = bf16[16,1552,128]{2,1,0:T(8,128)(2,1)} copy-done((bf16[16,1552,128]{2,1,0:T(8,128)(2,1)}, bf16[16,1552,128]{2,1,0:T(8,128)(2,1)S(1)}, u32[]{:S(2)}) %copy-start) | copy-done | bytes 6357016
  22.1 5.7 %collective-permute-done.5 = bf16[4,32,2048]{2,1,0:T(8,128)(2,1)S(1)} collective-permute-done((bf16[4,32,2048]{2,1,0:T(8,128)(2,1)S(1)}, bf16[4,32,2048]{2,1,0:T(8,128)(2,1)S(1)}, u32[]{:S(2)}, u32[]{:S(2)}) %collective-permute-start.5) | collective-permute-done | bytes 524320 | tf_op jit(solution)/shard_map/ppermute | solution.py:153
  28.6 4.7 %all-to-all-start = ((bf16[16,1552,128]{2,1,0:T(8,128)(2,1)}), bf16[16,1552,128]{2,1,0:T(8,128)(2,1)}, u32[]{:S(2)}, u32[]{:S(2)}) async-start(bf16[16,1552,128]{2,1,0:T(8,128)(2,1)} %copy-done), calls=%async_computation | async-start | bytes 12713984 | tf_op jit(solution)/shard_map/all_to_all | solution.py:293
  41.7 23.5 %collective-permute-done.6.refs_1_ = bf16[16,16,2048]{2,1,0:T(8,128)(2,1)S(1)} collective-permute-done((bf16[16,16,2048]{2,1,0:T(8,128)(2,1)S(1)}, bf16[16,16,2048]{2,1,0:T(8,128)(2,1)S(1)}, u32[]{:S(2)}, u32[]{:S(2)}) %collective-permute-start.6) | collective-permute-done | bytes 1048608 | tf_op jit(solution)/shard_map/ppermute | solution.py:36
  65.4 3.3 %collective-permute-start.9 = (bf16[8,16,2048]{2,1,0:T(8,128)(2,1)S(1)}, bf16[8,16,2048]{2,1,0:T(8,128)(2,1)S(1)}, u32[]{:S(2)}, u32[]{:S(2)}) collective-permute-start(bf16[8,16,2048]{2,1,0:T(8,128)(2,1)S(1)} %slice.22), channel_id=1, source_target_pairs={{0,96},{1,97},{2,98},{3,99},{4,100},{5,101},{6,102},{7,103},{8,104... | collective-permute-start | bytes 1572872 | tf_op jit(solution)/shard_map/ppermute | solution.py:36
  68.7 11.5 %collective-permute-done.8.refs_3_ = bf16[8,16,2048]{2,1,0:T(8,128)(2,1)S(1)} collective-permute-done((bf16[8,16,2048]{2,1,0:T(8,128)(2,1)S(1)}, bf16[8,16,2048]{2,1,0:T(8,128)(2,1)S(1)}, u32[]{:S(2)}, u32[]{:S(2)}) %collective-permute-start.8) | collective-permute-done | bytes 524320 | tf_op jit(solution)/shard_map/ppermute | solution.py:36
  80.8 3.2 %collective-permute-start.12 = (bf16[16,16,2048]{2,1,0:T(8,128)(2,1)S(1)}, bf16[16,16,2048]{2,1,0:T(8,128)(2,1)}, u32[]{:S(2)}, u32[]{:S(2)}) collective-permute-start(bf16[16,16,2048]{2,1,0:T(8,128)(2,1)S(1)} %get-tuple-element.35.refs_0_), channel_id=1, source_target_pairs={{0,96},{1,97},{2,98},{3,99},{4,100},{5,101},{6,102},{7,103},{8,104... | collective-permute-start | bytes 3145736 | tf_op jit(solution)/shard_map/ppermute | solution.py:36
  85.2 2.6 %collective-permute-done.10.other_ref = bf16[64,16,2048]{2,1,0:T(8,128)(2,1)S(1)} collective-permute-done((bf16[64,16,2048]{2,1,0:T(8,128)(2,1)S(1)}, bf16[64,16,2048]{2,1,0:T(8,128)(2,1)S(1)}, u32[]{:S(2)}, u32[]{:S(2)}) %collective-permute-start.10) | collective-permute-done | bytes 4194336 | tf_op jit(solution)/shard_map/ppermute | solution.py:36
  88.5 3.3 %copy-done.3 = bf16[64,2,16,2048]{3,2,1,0:T(8,128)(2,1)} copy-done((bf16[64,2,16,2048]{3,2,1,0:T(8,128)(2,1)}, bf16[64,2,16,2048]{3,2,1,0:T(8,128)(2,1)S(1)}, u32[]{:S(2)}) %copy-start.3) | copy-done | bytes 8388632
  91.7 16.6 %all-to-all-done.refs_0_.refs_1_ = bf16[16,1552,128]{2,1,0:T(8,128)(2,1)} async-done(((bf16[16,1552,128]{2,1,0:T(8,128)(2,1)}), bf16[16,1552,128]{2,1,0:T(8,128)(2,1)}, u32[]{:S(2)}, u32[]{:S(2)}) %all-to-all-start) | async-done | bytes 6357024 | tf_op jit(solution)/shard_map/all_to_all | solution.py:293
  109.5 3.3 %place.2 = bf16[2048,256]{1,0:T(8,128)(2,1)S(1)} custom-call(s32[32]{0:T(128)S(1)} %sub.7.first_ref, bf16[16,1552,128]{2,1,0:T(8,128)(2,1)} %all-to-all-done.refs_0_.refs_1_, bf16[16,1552,128]{2,1,0:T(8,128)(2,1)} %all-to-all-done.refs_0_.refs_1_), custom_call_target="tpu_custom_call" | custom-call | flops 1048576 | bytes 4194304 | tf_op jit(solution)/shard_map/place/pallas_call | solution.py:124
  113.5 3.5 %convolution_convert_fusion.3 = bf16[2048,256]{1,0:T(8,128)(2,1)} fusion(bf16[2048,2048]{1,0:T(8,128)(2,1)S(1)} %bitcast.30, bf16[2048,256]{1,0:T(8,128)(2,1)S(1)} %place.2), kind=kOutput, calls=%fused_computation.3 | convolution fusion | flops 2148007936 | bytes 10485760 | tf_op jit(solution)/shard_map/dot_general | solution.py:307
  117.0 3.8 %all-to-all-start.1 = ((bf16[16,128,256]{2,1,0:T(8,128)(2,1)}), bf16[16,128,256]{2,1,0:T(8,128)(2,1)S(1)}, u32[]{:S(2)}, u32[]{:S(2)}) async-start(bf16[16,128,256]{2,1,0:T(8,128)(2,1)} %bitcast.33), calls=%async_computation.1 | async-start | bytes 2097152 | tf_op jit(solution)/shard_map/all_to_all | solution.py:309
  120.8 5.0 %place.3 = bf16[2048,512]{1,0:T(8,128)(2,1)S(1)} custom-call(s32[32]{0:T(128)S(1)} %sub.7.first_ref, bf16[16,1552,128]{2,1,0:T(8,128)(2,1)} %all-to-all-done.refs_0_.refs_1_, bf16[16,1552,128]{2,1,0:T(8,128)(2,1)} %all-to-all-done.refs_0_.refs_1_), custom_call_target="tpu_custom_call" | custom-call | flops 2097152 | bytes 8388608 | tf_op jit(solution)/shard_map/place/pallas_call | solution.py:124
  125.8 9.9 %convolution_convert_fusion.1 = bf16[2048,512]{1,0:T(8,128)(2,1)} fusion(bf16[2048,2048]{1,0:T(8,128)(2,1)} %bitcast.29, bf16[2048,512]{1,0:T(8,128)(2,1)S(1)} %place.3), kind=kOutput, calls=%fused_computation.1 | convolution fusion | flops 4296015872 | bytes 12582912 | tf_op jit(solution)/shard_map/dot_general | solution.py:307
  140.6 7.0 %all-to-all-start.2 = ((bf16[16,128,512]{2,1,0:T(8,128)(2,1)}), bf16[16,128,512]{2,1,0:T(8,128)(2,1)S(1)}, u32[]{:S(2)}, u32[]{:S(2)}) async-start(bf16[16,128,512]{2,1,0:T(8,128)(2,1)} %bitcast.32), calls=%async_computation.2 | async-start | bytes 4194304 | tf_op jit(solution)/shard_map/all_to_all | solution.py:309
  149.8 2.9 %merge.3 = bf16[64,2,16,2048]{3,2,1,0:T(8,128)(2,1)S(1)} custom-call(bf16[64,16,2048]{2,1,0:T(8,128)(2,1)S(1)} %bitcast.28, bf16[64,16,2048]{2,1,0:T(8,128)(2,1)} %collective-permute-done.14.other_ref), custom_call_target="tpu_custom_call" | custom-call | bytes 16777216 | tf_op jit(solution)/shard_map/merge/pallas_call | solution.py:201
  152.7 2.4 %convolution_convert_fusion.2.refs_0_ = bf16[256,2048]{1,0:T(8,128)(2,1)S(1)} fusion(bf16[2048,256]{1,0:T(8,128)(2,1)S(1)} %copy-done.8, bf16[2048,2048]{1,0:T(8,128)(2,1)S(1)} %bitcast.23), kind=kOutput, calls=%fused_computation.2 | convolution fusion | flops 2148007936 | bytes 10485760 | tf_op jit(solution)/shard_map/dot_general | solution.py:318
  155.1 4.8 %convolution_convert_fusion.refs_1_ = bf16[512,2048]{1,0:T(8,128)(2,1)S(1)} fusion(bf16[2048,512]{1,0:T(8,128)(2,1)S(1)} %copy-done.13, bf16[2048,2048]{1,0:T(8,128)(2,1)S(1)} %bitcast.24), kind=kOutput, calls=%fused_computation | convolution fusion | flops 4296015872 | bytes 12582912 | tf_op jit(solution)/shard_map/dot_general | solution.py:318
  162.5 14.7 %all-to-all-done.2.x_ref = bf16[16,128,512]{2,1,0:T(8,128)(2,1)S(1)} async-done(((bf16[16,128,512]{2,1,0:T(8,128)(2,1)}), bf16[16,128,512]{2,1,0:T(8,128)(2,1)S(1)}, u32[]{:S(2)}, u32[]{:S(2)}) %all-to-all-start.2) | async-done | bytes 2097184 | tf_op jit(solution)/shard_map/all_to_all | solution.py:309
  182.8 4.6 %collective-permute-done.16 = f32[6,6]{0,1:T(8,128)S(1)} collective-permute-done((f32[6,6]{0,1:T(8,128)S(1)}, f32[6,6]{0,1:T(8,128)S(1)}, u32[]{:S(2)}, u32[]{:S(2)}) %collective-permute-start.16) | collective-permute-done | bytes 176 | tf_op jit(solution)/shard_map/ppermute | solution.py:36
  188.0 3.0 %collective-permute-done.17 = f32[6,6]{0,1:T(8,128)S(1)} collective-permute-done((f32[6,6]{0,1:T(8,128)S(1)}, f32[6,6]{0,1:T(8,128)S(1)}, u32[]{:S(2)}, u32[]{:S(2)}) %collective-permute-start.17) | collective-permute-done | bytes 176 | tf_op jit(solution)/shard_map/ppermute | solution.py:36
  192.5 3.3 %collective-permute-done.18 = f32[6,6]{0,1:T(8,128)S(1)} collective-permute-done((f32[6,6]{0,1:T(8,128)S(1)}, f32[6,6]{0,1:T(8,128)S(1)}, u32[]{:S(2)}, u32[]{:S(2)}) %collective-permute-start.18) | collective-permute-done | bytes 176 | tf_op jit(solution)/shard_map/ppermute | solution.py:36
  (83 shorter events, 48.0 us)
Async XLA Ops:
  0.9 6.2 %collective-permute-start = (bf16[1,32,2048]{2,1,0:T(8,128)(2,1)S(1)}, bf16[1,32,2048]{2,1,0:T(8,128)(2,1)S(1)}, u32[]{:S(2)}, u32[]{:S(2)}) collective-permute-start(bf16[1,32,2048]{2,1,0:T(8,128)(2,1)S(1)} %maximum_bitcast_fusion), channel_id=1, source_target_pairs={{0,4},{1,17},{2,6},{3,19},{4,8},{5,21},{6,10},{7,23},{8,12},{9,25}... | collective-permute-start | bytes 393224 | tf_op jit(solution)/shard_map/ppermute | solution.py:153
  2.5 5.0 %collective-permute-start.1 = (bf16[1,32,2048]{2,1,0:T(8,128)(2,1)S(1)}, bf16[1,32,2048]{2,1,0:T(8,128)(2,1)S(1)}, u32[]{:S(2)}, u32[]{:S(2)}) collective-permute-start(bf16[1,32,2048]{2,1,0:T(8,128)(2,1)S(1)} %maximum_bitcast_fusion), channel_id=1, source_target_pairs={{0,12},{1,19},{2,14},{3,17},{4,0},{5,23},{6,2},{7,21},{8,4},{9,27}... | collective-permute-start | bytes 393224 | tf_op jit(solution)/shard_map/ppermute | solution.py:153
  4.2 6.5 %collective-permute-start.2 = (bf16[1,32,2048]{2,1,0:T(8,128)(2,1)S(1)}, bf16[1,32,2048]{2,1,0:T(8,128)(2,1)S(1)}, u32[]{:S(2)}, u32[]{:S(2)}) collective-permute-start(bf16[1,32,2048]{2,1,0:T(8,128)(2,1)S(1)} %maximum_bitcast_fusion), channel_id=1, source_target_pairs={{0,8},{1,3},{2,10},{3,1},{4,12},{5,7},{6,14},{7,5},{8,0},{9,11},{1... | collective-permute-start | bytes 393224 | tf_op jit(solution)/shard_map/ppermute | solution.py:153
  10.7 11.3 %collective-permute-start.3 = (bf16[4,32,2048]{2,1,0:T(8,128)(2,1)S(1)}, bf16[4,32,2048]{2,1,0:T(8,128)(2,1)S(1)}, u32[]{:S(2)}, u32[]{:S(2)}) collective-permute-start(bf16[4,32,2048]{2,1,0:T(8,128)(2,1)S(1)} %pad_maximum_fusion), channel_id=1, source_target_pairs={{0,16},{1,5},{2,18},{3,7},{4,20},{5,9},{6,22},{7,11},{8,24},{9,13}... | collective-permute-start | bytes 1572872 | tf_op jit(solution)/shard_map/ppermute | solution.py:153
  12.3 9.8 %collective-permute-start.4 = (bf16[4,32,2048]{2,1,0:T(8,128)(2,1)S(1)}, bf16[4,32,2048]{2,1,0:T(8,128)(2,1)S(1)}, u32[]{:S(2)}, u32[]{:S(2)}) collective-permute-start(bf16[4,32,2048]{2,1,0:T(8,128)(2,1)S(1)} %pad_maximum_fusion), channel_id=1, source_target_pairs={{0,18},{1,13},{2,16},{3,15},{4,22},{5,1},{6,20},{7,3},{8,26},{9,5}... | collective-permute-start | bytes 1572872 | tf_op jit(solution)/shard_map/ppermute | solution.py:153
  12.8 14.9 %collective-permute-start.5 = (bf16[4,32,2048]{2,1,0:T(8,128)(2,1)S(1)}, bf16[4,32,2048]{2,1,0:T(8,128)(2,1)S(1)}, u32[]{:S(2)}, u32[]{:S(2)}) collective-permute-start(bf16[4,32,2048]{2,1,0:T(8,128)(2,1)S(1)} %pad_maximum_fusion), channel_id=1, source_target_pairs={{0,2},{1,9},{2,0},{3,11},{4,6},{5,13},{6,4},{7,15},{8,10},{9,1},{1... | collective-permute-start | bytes 1572872 | tf_op jit(solution)/shard_map/ppermute | solution.py:153
  28.6 79.7 %all-to-all-start = ((bf16[16,1552,128]{2,1,0:T(8,128)(2,1)}), bf16[16,1552,128]{2,1,0:T(8,128)(2,1)}, u32[]{:S(2)}, u32[]{:S(2)}) async-start(bf16[16,1552,128]{2,1,0:T(8,128)(2,1)} %copy-done), calls=%async_computation | async-start | bytes 12713984 | tf_op jit(solution)/shard_map/all_to_all | solution.py:293
  37.5 27.7 %collective-permute-start.6 = (bf16[16,16,2048]{2,1,0:T(8,128)(2,1)S(1)}, bf16[16,16,2048]{2,1,0:T(8,128)(2,1)S(1)}, u32[]{:S(2)}, u32[]{:S(2)}) collective-permute-start(bf16[16,16,2048]{2,1,0:T(8,128)(2,1)S(1)} %get-tuple-element.27.refs_0_), channel_id=1, source_target_pairs={{0,32},{1,33},{2,34},{3,35},{4,36},{5,37},{6,38},{7,39},{8,40},{9,... | collective-permute-start | bytes 3145736 | tf_op jit(solution)/shard_map/ppermute | solution.py:36
  39.5 25.8 %collective-permute-start.7 = (bf16[16,16,2048]{2,1,0:T(8,128)(2,1)S(1)}, bf16[16,16,2048]{2,1,0:T(8,128)(2,1)S(1)}, u32[]{:S(2)}, u32[]{:S(2)}) collective-permute-start(bf16[16,16,2048]{2,1,0:T(8,128)(2,1)S(1)} %get-tuple-element.27.refs_0_), channel_id=1, source_target_pairs={{0,96},{1,97},{2,98},{3,99},{4,100},{5,101},{6,102},{7,103},{8,104... | collective-permute-start | bytes 3145736 | tf_op jit(solution)/shard_map/ppermute | solution.py:36
  65.2 14.9 %collective-permute-start.8 = (bf16[8,16,2048]{2,1,0:T(8,128)(2,1)S(1)}, bf16[8,16,2048]{2,1,0:T(8,128)(2,1)S(1)}, u32[]{:S(2)}, u32[]{:S(2)}) collective-permute-start(bf16[8,16,2048]{2,1,0:T(8,128)(2,1)S(1)} %slice.21), channel_id=1, source_target_pairs={{0,32},{1,33},{2,34},{3,35},{4,36},{5,37},{6,38},{7,39},{8,40},{9,... | collective-permute-start | bytes 1572872 | tf_op jit(solution)/shard_map/ppermute | solution.py:36
  65.4 14.8 %collective-permute-start.9 = (bf16[8,16,2048]{2,1,0:T(8,128)(2,1)S(1)}, bf16[8,16,2048]{2,1,0:T(8,128)(2,1)S(1)}, u32[]{:S(2)}, u32[]{:S(2)}) collective-permute-start(bf16[8,16,2048]{2,1,0:T(8,128)(2,1)S(1)} %slice.22), channel_id=1, source_target_pairs={{0,96},{1,97},{2,98},{3,99},{4,100},{5,101},{6,102},{7,103},{8,104... | collective-permute-start | bytes 1572872 | tf_op jit(solution)/shard_map/ppermute | solution.py:36
  80.6 7.2 %collective-permute-start.10 = (bf16[64,16,2048]{2,1,0:T(8,128)(2,1)S(1)}, bf16[64,16,2048]{2,1,0:T(8,128)(2,1)S(1)}, u32[]{:S(2)}, u32[]{:S(2)}) collective-permute-start(bf16[64,16,2048]{2,1,0:T(8,128)(2,1)S(1)} %bitcast.25), channel_id=1, source_target_pairs={{0,1},{1,0},{2,3},{3,2},{4,5},{5,4},{6,7},{7,6},{8,9},{9,8},{10,11... | collective-permute-start | bytes 12582920 | tf_op jit(solution)/shard_map/ppermute | solution.py:36
  80.7 55.0 %collective-permute-start.11 = (bf16[16,16,2048]{2,1,0:T(8,128)(2,1)S(1)}, bf16[16,16,2048]{2,1,0:T(8,128)(2,1)S(1)}, u32[]{:S(2)}, u32[]{:S(2)}) collective-permute-start(bf16[16,16,2048]{2,1,0:T(8,128)(2,1)S(1)} %get-tuple-element.35.refs_0_), channel_id=1, source_target_pairs={{0,32},{1,33},{2,34},{3,35},{4,36},{5,37},{6,38},{7,39},{8,40},{9,... | collective-permute-start | bytes 3145736 | tf_op jit(solution)/shard_map/ppermute | solution.py:36
  80.8 55.0 %collective-permute-start.12 = (bf16[16,16,2048]{2,1,0:T(8,128)(2,1)S(1)}, bf16[16,16,2048]{2,1,0:T(8,128)(2,1)}, u32[]{:S(2)}, u32[]{:S(2)}) collective-permute-start(bf16[16,16,2048]{2,1,0:T(8,128)(2,1)S(1)} %get-tuple-element.35.refs_0_), channel_id=1, source_target_pairs={{0,96},{1,97},{2,98},{3,99},{4,100},{5,101},{6,102},{7,103},{8,104... | collective-permute-start | bytes 3145736 | tf_op jit(solution)/shard_map/ppermute | solution.py:36
  84.0 51.7 %collective-permute-start.13 = (bf16[16,16,2048]{2,1,0:T(8,128)(2,1)S(1)}, bf16[16,16,2048]{2,1,0:T(8,128)(2,1)}, u32[]{:S(2)}, u32[]{:S(2)}) collective-permute-start(bf16[16,16,2048]{2,1,0:T(8,128)(2,1)S(1)} %get-tuple-element.35.refs_0_), channel_id=1, source_target_pairs={{0,64},{1,65},{2,66},{3,67},{4,68},{5,69},{6,70},{7,71},{8,72},{9,... | collective-permute-start | bytes 3145736 | tf_op jit(solution)/shard_map/ppermute | solution.py:36
  117.0 22.6 %all-to-all-start.1 = ((bf16[16,128,256]{2,1,0:T(8,128)(2,1)}), bf16[16,128,256]{2,1,0:T(8,128)(2,1)S(1)}, u32[]{:S(2)}, u32[]{:S(2)}) async-start(bf16[16,128,256]{2,1,0:T(8,128)(2,1)} %bitcast.33), calls=%async_computation.1 | async-start | bytes 2097152 | tf_op jit(solution)/shard_map/all_to_all | solution.py:309
  125.8 9.9 %copy-start.12 = (bf16[2048,512]{1,0:T(8,128)(2,1)}, bf16[2048,512]{1,0:T(8,128)(2,1)S(1)}, u32[]{:S(2)}) copy-start(bf16[2048,512]{1,0:T(8,128)(2,1)S(1)} %place.3) | copy-start | bytes 6291460
  139.6 8.0 %collective-permute-start.14 = (bf16[64,16,2048]{2,1,0:T(8,128)(2,1)}, bf16[64,16,2048]{2,1,0:T(8,128)(2,1)}, u32[]{:S(2)}, u32[]{:S(2)}) collective-permute-start(bf16[64,16,2048]{2,1,0:T(8,128)(2,1)} %bitcast.27), channel_id=1, source_target_pairs={{0,1},{1,0},{2,3},{3,2},{4,5},{5,4},{6,7},{7,6},{8,9},{9,8},{10,11... | collective-permute-start | bytes 12582920 | tf_op jit(solution)/shard_map/ppermute | solution.py:36
  140.6 36.6 %all-to-all-start.2 = ((bf16[16,128,512]{2,1,0:T(8,128)(2,1)}), bf16[16,128,512]{2,1,0:T(8,128)(2,1)S(1)}, u32[]{:S(2)}, u32[]{:S(2)}) async-start(bf16[16,128,512]{2,1,0:T(8,128)(2,1)} %bitcast.32), calls=%async_computation.2 | async-start | bytes 4194304 | tf_op jit(solution)/shard_map/all_to_all | solution.py:309
  155.1 4.8 %copy-start.11 = (bf16[16,128,256]{2,1,0:T(8,128)(2,1)S(1)}, bf16[16,128,256]{2,1,0:T(8,128)(2,1)}, u32[]{:S(2)}) copy-start(bf16[16,128,256]{2,1,0:T(8,128)(2,1)} %copy-done.10) | copy-start | bytes 3145732
  181.0 1.2 collective-permute-start.15
  182.2 5.1 %collective-permute-start.16 = (f32[6,6]{0,1:T(8,128)S(1)}, f32[6,6]{0,1:T(8,128)S(1)}, u32[]{:S(2)}, u32[]{:S(2)}) collective-permute-start(f32[6,6]{0,1:T(8,128)S(1)} %fusion.9), channel_id=1, source_target_pairs={{0,2},{1,3},{2,0},{3,1},{4,6},{5,7},{6,4},{7,5},{8,10},{9,11},{10,... | collective-permute-start | bytes 440 | tf_op jit(solution)/shard_map/ppermute | solution.py:36
  187.4 3.6 %collective-permute-start.17 = (f32[6,6]{0,1:T(8,128)S(1)}, f32[6,6]{0,1:T(8,128)S(1)}, u32[]{:S(2)}, u32[]{:S(2)}) collective-permute-start(f32[6,6]{0,1:T(8,128)S(1)} %add.15), channel_id=1, source_target_pairs={{0,4},{1,5},{2,6},{3,7},{4,0},{5,1},{6,2},{7,3},{8,12},{9,13},{10,... | collective-permute-start | bytes 440 | tf_op jit(solution)/shard_map/ppermute | solution.py:36
  191.0 4.8 %collective-permute-start.18 = (f32[6,6]{0,1:T(8,128)S(1)}, f32[6,6]{0,1:T(8,128)S(1)}, u32[]{:S(2)}, u32[]{:S(2)}) collective-permute-start(f32[6,6]{0,1:T(8,128)S(1)} %add.16), channel_id=1, source_target_pairs={{0,12},{1,13},{2,14},{3,15},{4,8},{5,9},{6,10},{7,11},{8,4},{9,5},... | collective-permute-start | bytes 440 | tf_op jit(solution)/shard_map/ppermute | solution.py:36
  (12 other events, 29.8 us)

commit v9 on v8

--- a/solution.py
+++ b/solution.py
@@ -287,8 +287,9 @@
 
     picked = pick(block_list[0], blocks, col_count)
     line = ring(jnp.concatenate([occ_green, virt_green.T], axis=0)[None], True)
-    plane = ring(jnp.concatenate(line, axis=0), False)
-    picked, plane = lax.optimization_barrier((picked, plane))
+    line = jnp.concatenate(line, axis=0)
+    picked, line = lax.optimization_barrier((picked, line))
+    plane = ring(line, False)
     plane = jnp.concatenate(plane, axis=0)
     recv = lax.all_to_all(picked, COL, split_axis=0, concat_axis=0, tiled=True)
     notes = CAP * aux * width
@@ -310,9 +311,8 @@
         recv_first, _ = lax.optimization_barrier((recv_first, half))
         start += depth
 
-    _, virt_pieces = lax.optimization_barrier((half, virt_pieces))
+    turned[0], _, virt_pieces = lax.optimization_barrier((turned[0], half, virt_pieces))
     virt_mine = lay(DIRECT, virt_pieces)
-    turned[0], virt_mine = lax.optimization_barrier((turned[0], virt_mine))
     virt_t = merge(virt_mine, other_core(virt_mine))
     virt_half = [
         lax.dot_general(

time: 197 us -> 240 us (1.22)
  starting transfers between devices: 39.9 us -> 96.3 us
  waiting for transfers between devices: 91.1 us -> 81.1 us
  Pallas kernels: 18.2 us -> 28 us
  local copies, waits for them, and re-layouts: 23.8 us -> 14.7 us
  matrix products: 20.5 us -> 16.3 us
    all_to_all x2, starting transfers between devices: 10.8 us -> 56.6 us  [shards(): lax.all_to_all(cut, COL, split_axis=0, concat_axis=0, tiled=True)]
    ppermute x13, waiting for transfers between devices: 49.7 us -> 37.5 us  [permute(): return lax.ppermute(x, AXES, moved(axis, to))]
    ppermute x13, starting transfers between devices: 14.9 us -> 25.5 us  [permute(): return lax.ppermute(x, AXES, moved(axis, to))]
    unnamed x31 -> x27, local copies, waits for them, and re-layouts: 19.5 us -> 10.4 us
    all_to_all x2, waiting for transfers between devices: 14.7 us -> 22.5 us  [shards(): lax.all_to_all(cut, COL, split_axis=0, concat_axis=0, tiled=True)]
    pallas_call x2, Pallas kernels: 3.51 us -> 8.6 us  [merge(): pl.pallas_call(merge_kernel, out_shape=jax.ShapeDtypeStruct((chips, 2, ro...]
    pallas_call x2, Pallas kernels: 2.25 us -> 6.65 us  [lay(): pl.pallas_call(functools.partial(lay_kernel, spots), out_shape=jax.ShapeD...]
    dot_general x2, matrix products: 13.4 us -> 9.2 us  [shards(): jnp.dot(occ, dense[-1], preferred_element_type=jnp.float32)]
  transfers between devices with their start and end apart: 22 -> 22, of which waited for: 13 -> 11; matrix products, arithmetic and copies ran while one was open for 14% -> 10% of each run, Pallas kernels for 8% -> 9%
where the time goes in v9:
time: 240 us; the launch traced here: 239 us
  starting transfers between devices  96.3 us (40%)
  waiting for transfers between devices  81.1 us (34%)
  Pallas kernels  28 us (12%)
  matrix products  16.3 us (7%)
  local copies, waits for them, and re-layouts  14.7 us (6%)
  other arithmetic  2.64 us (1%)
    all_to_all x2, starting transfers between devices, shards(): lax.all_to_all(cut, COL, split_axis=0, concat_axis=0, tiled=True)  56.6 us
    ppermute x13, waiting for transfers between devices, permute(): return lax.ppermute(x, AXES, moved(axis, to))  37.5 us
    ppermute x13, starting transfers between devices, permute(): return lax.ppermute(x, AXES, moved(axis, to))  25.5 us
    all_to_all x2, waiting for transfers between devices, shards(): lax.all_to_all(cut, COL, split_axis=0, concat_axis=0, tiled=True)  22.5 us
    all_to_all x1, waiting for transfers between devices, shards(): recv = lax.all_to_all(picked, COL, split_axis=0, concat_axis=0, tiled=True)  12.8 us
    unnamed x27, local copies, waits for them, and re-layouts  10.4 us
    ppermute x6, starting transfers between devices, hop(): return lax.ppermute(x, AXES, pairs)  9.51 us
    dot_general x2, matrix products, shards(): jnp.dot(occ, dense[-1], preferred_element_type=jnp.float32)  9.2 us
  transfers between devices with their start and end apart: 22, of which 11 were waited for; matrix products, arithmetic and copies ran while one was open for 10% of the time, Pallas kernels for 9%

profile of v9, /device:TPU:2, one launch (start us, length us, event | category | flops | bytes accessed | tf_op | source)
XLA Modules:
  0.0 239.4 jit_solution(7679611279100927906)
XLA Ops:
  10.7 2.6 %copy-done = bf16[16,1552,128]{2,1,0:T(8,128)(2,1)} copy-done((bf16[16,1552,128]{2,1,0:T(8,128)(2,1)}, bf16[16,1552,128]{2,1,0:T(8,128)(2,1)S(1)}, u32[]{:S(2)}) %copy-start) | copy-done | bytes 6357016
  18.4 4.7 %all-to-all-start = ((bf16[16,1552,128]{2,1,0:T(8,128)(2,1)}), bf16[16,1552,128]{2,1,0:T(8,128)(2,1)}, u32[]{:S(2)}, u32[]{:S(2)}) async-start(bf16[16,1552,128]{2,1,0:T(8,128)(2,1)} %copy-done), calls=%async_computation | async-start | bytes 12713984 | tf_op jit(solution)/shard_map/all_to_all | solution.py:294
  25.0 8.1 %collective-permute-done.5 = bf16[4,32,2048]{2,1,0:T(8,128)(2,1)S(1)} collective-permute-done((bf16[4,32,2048]{2,1,0:T(8,128)(2,1)S(1)}, bf16[4,32,2048]{2,1,0:T(8,128)(2,1)S(1)}, u32[]{:S(2)}, u32[]{:S(2)}) %collective-permute-start.5) | collective-permute-done | bytes 524320 | tf_op jit(solution)/shard_map/ppermute | solution.py:153
  39.9 12.7 %collective-permute-done.6.refs_1_ = bf16[16,16,2048]{2,1,0:T(8,128)(2,1)S(1)} collective-permute-done((bf16[16,16,2048]{2,1,0:T(8,128)(2,1)S(1)}, bf16[16,16,2048]{2,1,0:T(8,128)(2,1)S(1)}, u32[]{:S(2)}, u32[]{:S(2)}) %collective-permute-start.6) | collective-permute-done | bytes 1048608 | tf_op jit(solution)/shard_map/ppermute | solution.py:36
  52.7 3.3 %collective-permute-start.9 = (bf16[8,16,2048]{2,1,0:T(8,128)(2,1)S(1)}, bf16[8,16,2048]{2,1,0:T(8,128)(2,1)S(1)}, u32[]{:S(2)}, u32[]{:S(2)}) collective-permute-start(bf16[8,16,2048]{2,1,0:T(8,128)(2,1)S(1)} %slice.22), channel_id=1, source_target_pairs={{0,96},{1,97},{2,98},{3,99},{4,100},{5,101},{6,102},{7,103},{8,104... | collective-permute-start | bytes 1572872 | tf_op jit(solution)/shard_map/ppermute | solution.py:36
  56.0 12.7 %collective-permute-done.8.refs_3_ = bf16[8,16,2048]{2,1,0:T(8,128)(2,1)S(1)} collective-permute-done((bf16[8,16,2048]{2,1,0:T(8,128)(2,1)S(1)}, bf16[8,16,2048]{2,1,0:T(8,128)(2,1)S(1)}, u32[]{:S(2)}, u32[]{:S(2)}) %collective-permute-start.8) | collective-permute-done | bytes 524320 | tf_op jit(solution)/shard_map/ppermute | solution.py:36
  71.1 10.9 %collective-permute-start.10 = (bf16[64,16,2048]{2,1,0:T(8,128)(2,1)}, bf16[64,16,2048]{2,1,0:T(8,128)(2,1)}, u32[]{:S(2)}, u32[]{:S(2)}) collective-permute-start(bf16[64,16,2048]{2,1,0:T(8,128)(2,1)} %bitcast.4.mine_ref), channel_id=1, source_target_pairs={{0,1},{1,0},{2,3},{3,2},{4,5},{5,4},{6,7},{7,6},{8,9},{9,8},{10,11... | collective-permute-start | bytes 12582920 | tf_op jit(solution)/shard_map/ppermute | solution.py:36
  82.3 3.0 %collective-permute-start.12 = (bf16[16,16,2048]{2,1,0:T(8,128)(2,1)S(1)}, bf16[16,16,2048]{2,1,0:T(8,128)(2,1)}, u32[]{:S(2)}, u32[]{:S(2)}) collective-permute-start(bf16[16,16,2048]{2,1,0:T(8,128)(2,1)S(1)} %get-tuple-element.29.refs_0_), channel_id=1, source_target_pairs={{0,96},{1,97},{2,98},{3,99},{4,100},{5,101},{6,102},{7,103},{8,104... | collective-permute-start | bytes 3145736 | tf_op jit(solution)/shard_map/ppermute | solution.py:36
  86.5 12.8 %all-to-all-done.refs_0_.refs_1_ = bf16[16,1552,128]{2,1,0:T(8,128)(2,1)} async-done(((bf16[16,1552,128]{2,1,0:T(8,128)(2,1)}), bf16[16,1552,128]{2,1,0:T(8,128)(2,1)}, u32[]{:S(2)}, u32[]{:S(2)}) %all-to-all-start) | async-done | bytes 6357024 | tf_op jit(solution)/shard_map/all_to_all | solution.py:294
  100.4 3.0 %place.2 = bf16[2048,256]{1,0:T(8,128)(2,1)S(1)} custom-call(s32[32]{0:T(128)S(1)} %sub.7.first_ref, bf16[16,1552,128]{2,1,0:T(8,128)(2,1)} %all-to-all-done.refs_0_.refs_1_, bf16[16,1552,128]{2,1,0:T(8,128)(2,1)} %all-to-all-done.refs_0_.refs_1_), custom_call_target="tpu_custom_call" | custom-call | flops 1048576 | bytes 4194304 | tf_op jit(solution)/shard_map/place/pallas_call | solution.py:124
  103.5 4.4 %merge.2 = bf16[64,2,16,2048]{3,2,1,0:T(8,128)(2,1)S(1)} custom-call(bf16[64,16,2048]{2,1,0:T(8,128)(2,1)} %bitcast.4.mine_ref, bf16[64,16,2048]{2,1,0:T(8,128)(2,1)} %collective-permute-done.10.other_ref), custom_call_target="tpu_custom_call" | custom-call | bytes 16777216 | tf_op jit(solution)/shard_map/merge/pallas_call | solution.py:201
  108.0 3.6 %convolution_convert_fusion.3 = bf16[2048,256]{1,0:T(8,128)(2,1)} fusion(bf16[2048,2048]{1,0:T(8,128)(2,1)S(1)} %bitcast.25, bf16[2048,256]{1,0:T(8,128)(2,1)S(1)} %place.2), kind=kOutput, calls=%fused_computation.3 | convolution fusion | flops 2148007936 | bytes 10485760 | tf_op jit(solution)/shard_map/dot_general | solution.py:308
  111.6 40.7 %all-to-all-start.1 = ((bf16[16,128,256]{2,1,0:T(8,128)(2,1)}), bf16[16,128,256]{2,1,0:T(8,128)(2,1)S(1)}, u32[]{:S(2)}, u32[]{:S(2)}) async-start(bf16[16,128,256]{2,1,0:T(8,128)(2,1)} %bitcast.29), calls=%async_computation.1 | async-start | bytes 2097152 | tf_op jit(solution)/shard_map/all_to_all | solution.py:310
  152.3 5.5 %place.3 = bf16[2048,512]{1,0:T(8,128)(2,1)S(1)} custom-call(s32[32]{0:T(128)S(1)} %sub.7.first_ref, bf16[16,1552,128]{2,1,0:T(8,128)(2,1)} %all-to-all-done.refs_0_.refs_1_, bf16[16,1552,128]{2,1,0:T(8,128)(2,1)} %all-to-all-done.refs_0_.refs_1_), custom_call_target="tpu_custom_call" | custom-call | flops 2097152 | bytes 8388608 | tf_op jit(solution)/shard_map/place/pallas_call | solution.py:124
  157.8 5.6 %convolution_convert_fusion.1 = bf16[2048,512]{1,0:T(8,128)(2,1)} fusion(bf16[2048,2048]{1,0:T(8,128)(2,1)S(1)} %bitcast.26, bf16[2048,512]{1,0:T(8,128)(2,1)S(1)} %place.3), kind=kOutput, calls=%fused_computation.1 | convolution fusion | flops 4296015872 | bytes 12582912 | tf_op jit(solution)/shard_map/dot_general | solution.py:308
  163.5 6.9 %all-to-all-done.1.x_ref = bf16[16,128,256]{2,1,0:T(8,128)(2,1)S(1)} async-done(((bf16[16,128,256]{2,1,0:T(8,128)(2,1)}), bf16[16,128,256]{2,1,0:T(8,128)(2,1)S(1)}, u32[]{:S(2)}, u32[]{:S(2)}) %all-to-all-start.1) | async-done | bytes 1048608 | tf_op jit(solution)/shard_map/all_to_all | solution.py:310
  170.4 4.3 %lay.3 = bf16[4,2,4,2,16,2048]{5,4,3,2,1,0:T(8,128)(2,1)} custom-call(bf16[16,16,2048]{2,1,0:T(8,128)(2,1)S(1)} %get-tuple-element.29.refs_0_, bf16[16,16,2048]{2,1,0:T(8,128)(2,1)S(1)} %collective-permute-done.11.refs_1_, bf16[16,16,2048]{2,1,0:T(8,128)(2,1)} %collective-permute-done.12.refs_2_, bf16[16,16,2048]{2,1,0:T(8,128)(2,1)} %collective-permute-done.13.refs_3_), custom_call_target="tpu_custom_call" | custom-call | bytes 8388608 | tf_op jit(solution)/shard_map/lay/pallas_call | solution.py:174
  174.7 15.8 %all-to-all-start.2 = ((bf16[16,128,512]{2,1,0:T(8,128)(2,1)}), bf16[16,128,512]{2,1,0:T(8,128)(2,1)S(1)}, u32[]{:S(2)}, u32[]{:S(2)}) async-start(bf16[16,128,512]{2,1,0:T(8,128)(2,1)} %bitcast.28), calls=%async_computation.2 | async-start | bytes 4194304 | tf_op jit(solution)/shard_map/all_to_all | solution.py:310
  190.5 4.2 %merge.3 = bf16[64,2,16,2048]{3,2,1,0:T(8,128)(2,1)S(1)} custom-call(bf16[64,16,2048]{2,1,0:T(8,128)(2,1)} %bitcast.7.mine_ref, bf16[64,16,2048]{2,1,0:T(8,128)(2,1)} %collective-permute-done.14.other_ref), custom_call_target="tpu_custom_call" | custom-call | bytes 16777216 | tf_op jit(solution)/shard_map/merge/pallas_call | solution.py:201
  197.1 4.8 %convolution_convert_fusion.refs_1_ = bf16[512,2048]{1,0:T(8,128)(2,1)S(1)} fusion(bf16[2048,512]{1,0:T(8,128)(2,1)S(1)} %copy-done.11, bf16[2048,2048]{1,0:T(8,128)(2,1)S(1)} %bitcast.24), kind=kOutput, calls=%fused_computation | convolution fusion | flops 4296015872 | bytes 12582912 | tf_op jit(solution)/shard_map/dot_general | solution.py:318
  204.5 15.6 %all-to-all-done.2.x_ref = bf16[16,128,512]{2,1,0:T(8,128)(2,1)S(1)} async-done(((bf16[16,128,512]{2,1,0:T(8,128)(2,1)}), bf16[16,128,512]{2,1,0:T(8,128)(2,1)S(1)}, u32[]{:S(2)}, u32[]{:S(2)}) %all-to-all-start.2) | async-done | bytes 2097184 | tf_op jit(solution)/shard_map/all_to_all | solution.py:310
  225.7 4.6 %collective-permute-done.16 = f32[6,6]{0,1:T(8,128)S(1)} collective-permute-done((f32[6,6]{0,1:T(8,128)S(1)}, f32[6,6]{0,1:T(8,128)S(1)}, u32[]{:S(2)}, u32[]{:S(2)}) %collective-permute-start.16) | collective-permute-done | bytes 176 | tf_op jit(solution)/shard_map/ppermute | solution.py:36
  230.9 3.0 %collective-permute-done.17 = f32[6,6]{0,1:T(8,128)S(1)} collective-permute-done((f32[6,6]{0,1:T(8,128)S(1)}, f32[6,6]{0,1:T(8,128)S(1)}, u32[]{:S(2)}, u32[]{:S(2)}) %collective-permute-start.17) | collective-permute-done | bytes 176 | tf_op jit(solution)/shard_map/ppermute | solution.py:36
  235.4 3.3 %collective-permute-done.18 = f32[6,6]{0,1:T(8,128)S(1)} collective-permute-done((f32[6,6]{0,1:T(8,128)S(1)}, f32[6,6]{0,1:T(8,128)S(1)}, u32[]{:S(2)}, u32[]{:S(2)}) %collective-permute-start.18) | collective-permute-done | bytes 176 | tf_op jit(solution)/shard_map/ppermute | solution.py:36
  (79 shorter events, 42.9 us)
Async XLA Ops:
  0.9 12.4 %collective-permute-start = (bf16[1,32,2048]{2,1,0:T(8,128)(2,1)S(1)}, bf16[1,32,2048]{2,1,0:T(8,128)(2,1)S(1)}, u32[]{:S(2)}, u32[]{:S(2)}) collective-permute-start(bf16[1,32,2048]{2,1,0:T(8,128)(2,1)S(1)} %maximum_bitcast_fusion), channel_id=1, source_target_pairs={{0,4},{1,17},{2,6},{3,19},{4,8},{5,21},{6,10},{7,23},{8,12},{9,25}... | collective-permute-start | bytes 393224 | tf_op jit(solution)/shard_map/ppermute | solution.py:153
  2.5 10.8 %collective-permute-start.1 = (bf16[1,32,2048]{2,1,0:T(8,128)(2,1)S(1)}, bf16[1,32,2048]{2,1,0:T(8,128)(2,1)S(1)}, u32[]{:S(2)}, u32[]{:S(2)}) collective-permute-start(bf16[1,32,2048]{2,1,0:T(8,128)(2,1)S(1)} %maximum_bitcast_fusion), channel_id=1, source_target_pairs={{0,12},{1,19},{2,14},{3,17},{4,0},{5,23},{6,2},{7,21},{8,4},{9,27}... | collective-permute-start | bytes 393224 | tf_op jit(solution)/shard_map/ppermute | solution.py:153
  4.2 9.1 %collective-permute-start.2 = (bf16[1,32,2048]{2,1,0:T(8,128)(2,1)S(1)}, bf16[1,32,2048]{2,1,0:T(8,128)(2,1)S(1)}, u32[]{:S(2)}, u32[]{:S(2)}) collective-permute-start(bf16[1,32,2048]{2,1,0:T(8,128)(2,1)S(1)} %maximum_bitcast_fusion), channel_id=1, source_target_pairs={{0,8},{1,3},{2,10},{3,1},{4,12},{5,7},{6,14},{7,5},{8,0},{9,11},{1... | collective-permute-start | bytes 393224 | tf_op jit(solution)/shard_map/ppermute | solution.py:153
  13.4 9.7 %collective-permute-start.3 = (bf16[4,32,2048]{2,1,0:T(8,128)(2,1)S(1)}, bf16[4,32,2048]{2,1,0:T(8,128)(2,1)S(1)}, u32[]{:S(2)}, u32[]{:S(2)}) collective-permute-start(bf16[4,32,2048]{2,1,0:T(8,128)(2,1)S(1)} %pad_maximum_fusion), channel_id=1, source_target_pairs={{0,16},{1,5},{2,18},{3,7},{4,20},{5,9},{6,22},{7,11},{8,24},{9,13}... | collective-permute-start | bytes 1572872 | tf_op jit(solution)/shard_map/ppermute | solution.py:153
  14.9 9.2 %collective-permute-start.4 = (bf16[4,32,2048]{2,1,0:T(8,128)(2,1)S(1)}, bf16[4,32,2048]{2,1,0:T(8,128)(2,1)S(1)}, u32[]{:S(2)}, u32[]{:S(2)}) collective-permute-start(bf16[4,32,2048]{2,1,0:T(8,128)(2,1)S(1)} %pad_maximum_fusion), channel_id=1, source_target_pairs={{0,18},{1,13},{2,16},{3,15},{4,22},{5,1},{6,20},{7,3},{8,26},{9,5}... | collective-permute-start | bytes 1572872 | tf_op jit(solution)/shard_map/ppermute | solution.py:153
  15.5 17.6 %collective-permute-start.5 = (bf16[4,32,2048]{2,1,0:T(8,128)(2,1)S(1)}, bf16[4,32,2048]{2,1,0:T(8,128)(2,1)S(1)}, u32[]{:S(2)}, u32[]{:S(2)}) collective-permute-start(bf16[4,32,2048]{2,1,0:T(8,128)(2,1)S(1)} %pad_maximum_fusion), channel_id=1, source_target_pairs={{0,2},{1,9},{2,0},{3,11},{4,6},{5,13},{6,4},{7,15},{8,10},{9,1},{1... | collective-permute-start | bytes 1572872 | tf_op jit(solution)/shard_map/ppermute | solution.py:153
  18.4 80.8 %all-to-all-start = ((bf16[16,1552,128]{2,1,0:T(8,128)(2,1)}), bf16[16,1552,128]{2,1,0:T(8,128)(2,1)}, u32[]{:S(2)}, u32[]{:S(2)}) async-start(bf16[16,1552,128]{2,1,0:T(8,128)(2,1)} %copy-done), calls=%async_computation | async-start | bytes 12713984 | tf_op jit(solution)/shard_map/all_to_all | solution.py:294
  35.7 16.9 %collective-permute-start.6 = (bf16[16,16,2048]{2,1,0:T(8,128)(2,1)S(1)}, bf16[16,16,2048]{2,1,0:T(8,128)(2,1)S(1)}, u32[]{:S(2)}, u32[]{:S(2)}) collective-permute-start(bf16[16,16,2048]{2,1,0:T(8,128)(2,1)S(1)} %get-tuple-element.20.refs_0_), channel_id=1, source_target_pairs={{0,32},{1,33},{2,34},{3,35},{4,36},{5,37},{6,38},{7,39},{8,40},{9,... | collective-permute-start | bytes 3145736 | tf_op jit(solution)/shard_map/ppermute | solution.py:36
  37.7 15.0 %collective-permute-start.7 = (bf16[16,16,2048]{2,1,0:T(8,128)(2,1)S(1)}, bf16[16,16,2048]{2,1,0:T(8,128)(2,1)S(1)}, u32[]{:S(2)}, u32[]{:S(2)}) collective-permute-start(bf16[16,16,2048]{2,1,0:T(8,128)(2,1)S(1)} %get-tuple-element.20.refs_0_), channel_id=1, source_target_pairs={{0,96},{1,97},{2,98},{3,99},{4,100},{5,101},{6,102},{7,103},{8,104... | collective-permute-start | bytes 3145736 | tf_op jit(solution)/shard_map/ppermute | solution.py:36
  52.6 16.1 %collective-permute-start.8 = (bf16[8,16,2048]{2,1,0:T(8,128)(2,1)S(1)}, bf16[8,16,2048]{2,1,0:T(8,128)(2,1)S(1)}, u32[]{:S(2)}, u32[]{:S(2)}) collective-permute-start(bf16[8,16,2048]{2,1,0:T(8,128)(2,1)S(1)} %slice.21), channel_id=1, source_target_pairs={{0,32},{1,33},{2,34},{3,35},{4,36},{5,37},{6,38},{7,39},{8,40},{9,... | collective-permute-start | bytes 1572872 | tf_op jit(solution)/shard_map/ppermute | solution.py:36
  52.7 16.0 %collective-permute-start.9 = (bf16[8,16,2048]{2,1,0:T(8,128)(2,1)S(1)}, bf16[8,16,2048]{2,1,0:T(8,128)(2,1)S(1)}, u32[]{:S(2)}, u32[]{:S(2)}) collective-permute-start(bf16[8,16,2048]{2,1,0:T(8,128)(2,1)S(1)} %slice.22), channel_id=1, source_target_pairs={{0,96},{1,97},{2,98},{3,99},{4,100},{5,101},{6,102},{7,103},{8,104... | collective-permute-start | bytes 1572872 | tf_op jit(solution)/shard_map/ppermute | solution.py:36
  71.1 32.4 %collective-permute-start.10 = (bf16[64,16,2048]{2,1,0:T(8,128)(2,1)}, bf16[64,16,2048]{2,1,0:T(8,128)(2,1)}, u32[]{:S(2)}, u32[]{:S(2)}) collective-permute-start(bf16[64,16,2048]{2,1,0:T(8,128)(2,1)} %bitcast.4.mine_ref), channel_id=1, source_target_pairs={{0,1},{1,0},{2,3},{3,2},{4,5},{5,4},{6,7},{7,6},{8,9},{9,8},{10,11... | collective-permute-start | bytes 12582920 | tf_op jit(solution)/shard_map/ppermute | solution.py:36
  82.0 81.5 %collective-permute-start.11 = (bf16[16,16,2048]{2,1,0:T(8,128)(2,1)S(1)}, bf16[16,16,2048]{2,1,0:T(8,128)(2,1)S(1)}, u32[]{:S(2)}, u32[]{:S(2)}) collective-permute-start(bf16[16,16,2048]{2,1,0:T(8,128)(2,1)S(1)} %get-tuple-element.29.refs_0_), channel_id=1, source_target_pairs={{0,32},{1,33},{2,34},{3,35},{4,36},{5,37},{6,38},{7,39},{8,40},{9,... | collective-permute-start | bytes 3145736 | tf_op jit(solution)/shard_map/ppermute | solution.py:36
  82.3 81.2 %collective-permute-start.12 = (bf16[16,16,2048]{2,1,0:T(8,128)(2,1)S(1)}, bf16[16,16,2048]{2,1,0:T(8,128)(2,1)}, u32[]{:S(2)}, u32[]{:S(2)}) collective-permute-start(bf16[16,16,2048]{2,1,0:T(8,128)(2,1)S(1)} %get-tuple-element.29.refs_0_), channel_id=1, source_target_pairs={{0,96},{1,97},{2,98},{3,99},{4,100},{5,101},{6,102},{7,103},{8,104... | collective-permute-start | bytes 3145736 | tf_op jit(solution)/shard_map/ppermute | solution.py:36
  85.2 78.2 %collective-permute-start.13 = (bf16[16,16,2048]{2,1,0:T(8,128)(2,1)S(1)}, bf16[16,16,2048]{2,1,0:T(8,128)(2,1)}, u32[]{:S(2)}, u32[]{:S(2)}) collective-permute-start(bf16[16,16,2048]{2,1,0:T(8,128)(2,1)S(1)} %get-tuple-element.29.refs_0_), channel_id=1, source_target_pairs={{0,64},{1,65},{2,66},{3,67},{4,68},{5,69},{6,70},{7,71},{8,72},{9,... | collective-permute-start | bytes 3145736 | tf_op jit(solution)/shard_map/ppermute | solution.py:36
  111.6 58.8 %all-to-all-start.1 = ((bf16[16,128,256]{2,1,0:T(8,128)(2,1)}), bf16[16,128,256]{2,1,0:T(8,128)(2,1)S(1)}, u32[]{:S(2)}, u32[]{:S(2)}) async-start(bf16[16,128,256]{2,1,0:T(8,128)(2,1)} %bitcast.29), calls=%async_computation.1 | async-start | bytes 2097152 | tf_op jit(solution)/shard_map/all_to_all | solution.py:310
  152.3 5.5 %copy-start.2 = (bf16[64,2,16,2048]{3,2,1,0:T(8,128)(2,1)S(1)}, bf16[64,2,16,2048]{3,2,1,0:T(8,128)(2,1)}, u32[]{:S(2)}) copy-start(bf16[64,2,16,2048]{3,2,1,0:T(8,128)(2,1)} %copy-done.1) | copy-start | bytes 25165828
  157.8 5.6 %copy-start.10 = (bf16[2048,512]{1,0:T(8,128)(2,1)}, bf16[2048,512]{1,0:T(8,128)(2,1)S(1)}, u32[]{:S(2)}) copy-start(bf16[2048,512]{1,0:T(8,128)(2,1)S(1)} %place.3) | copy-start | bytes 6291460
  174.7 15.8 %collective-permute-start.14 = (bf16[64,16,2048]{2,1,0:T(8,128)(2,1)}, bf16[64,16,2048]{2,1,0:T(8,128)(2,1)}, u32[]{:S(2)}, u32[]{:S(2)}) collective-permute-start(bf16[64,16,2048]{2,1,0:T(8,128)(2,1)} %bitcast.7.mine_ref), channel_id=1, source_target_pairs={{0,1},{1,0},{2,3},{3,2},{4,5},{5,4},{6,7},{7,6},{8,9},{9,8},{10,11... | collective-permute-start | bytes 12582920 | tf_op jit(solution)/shard_map/ppermute | solution.py:36
  174.7 45.4 %all-to-all-start.2 = ((bf16[16,128,512]{2,1,0:T(8,128)(2,1)}), bf16[16,128,512]{2,1,0:T(8,128)(2,1)S(1)}, u32[]{:S(2)}, u32[]{:S(2)}) async-start(bf16[16,128,512]{2,1,0:T(8,128)(2,1)} %bitcast.28), calls=%async_computation.2 | async-start | bytes 4194304 | tf_op jit(solution)/shard_map/all_to_all | solution.py:310
  223.9 1.2 collective-permute-start.15
  225.2 5.1 %collective-permute-start.16 = (f32[6,6]{0,1:T(8,128)S(1)}, f32[6,6]{0,1:T(8,128)S(1)}, u32[]{:S(2)}, u32[]{:S(2)}) collective-permute-start(f32[6,6]{0,1:T(8,128)S(1)} %fusion.9), channel_id=1, source_target_pairs={{0,2},{1,3},{2,0},{3,1},{4,6},{5,7},{6,4},{7,5},{8,10},{9,11},{10,... | collective-permute-start | bytes 440 | tf_op jit(solution)/shard_map/ppermute | solution.py:36
  230.3 3.6 %collective-permute-start.17 = (f32[6,6]{0,1:T(8,128)S(1)}, f32[6,6]{0,1:T(8,128)S(1)}, u32[]{:S(2)}, u32[]{:S(2)}) collective-permute-start(f32[6,6]{0,1:T(8,128)S(1)} %add.15), channel_id=1, source_target_pairs={{0,4},{1,5},{2,6},{3,7},{4,0},{5,1},{6,2},{7,3},{8,12},{9,13},{10,... | collective-permute-start | bytes 440 | tf_op jit(solution)/shard_map/ppermute | solution.py:36
  233.9 4.8 %collective-permute-start.18 = (f32[6,6]{0,1:T(8,128)S(1)}, f32[6,6]{0,1:T(8,128)S(1)}, u32[]{:S(2)}, u32[]{:S(2)}) collective-permute-start(f32[6,6]{0,1:T(8,128)S(1)} %add.16), channel_id=1, source_target_pairs={{0,12},{1,13},{2,14},{3,15},{4,8},{5,9},{6,10},{7,11},{8,4},{9,5},... | collective-permute-start | bytes 440 | tf_op jit(solution)/shard_map/ppermute | solution.py:36
  (10 other events, 31.6 us)

commit v10 on v8

--- a/solution.py
+++ b/solution.py
@@ -310,9 +310,8 @@
         recv_first, _ = lax.optimization_barrier((recv_first, half))
         start += depth
 
-    _, virt_pieces = lax.optimization_barrier((half, virt_pieces))
+    turned[0], _, virt_pieces = lax.optimization_barrier((turned[0], half, virt_pieces))
     virt_mine = lay(DIRECT, virt_pieces)
-    turned[0], virt_mine = lax.optimization_barrier((turned[0], virt_mine))
     virt_t = merge(virt_mine, other_core(virt_mine))
     virt_half = [
         lax.dot_general(

time: 197 us -> 197 us (level)
  local copies, waits for them, and re-layouts: 23.8 us -> 18.7 us
  waiting for transfers between devices: 91.1 us -> 95 us
  Pallas kernels: 18.2 us -> 21.8 us
  starting transfers between devices: 39.9 us -> 37.1 us
    unnamed x31 -> x27, local copies, waits for them, and re-layouts: 19.5 us -> 14.4 us
    ppermute x13, waiting for transfers between devices: 49.7 us -> 53 us  [permute(): return lax.ppermute(x, AXES, moved(axis, to))]
    all_to_all x2, starting transfers between devices: 10.8 us -> 8.07 us  [shards(): lax.all_to_all(cut, COL, split_axis=0, concat_axis=0, tiled=True)]
    pallas_call x2, Pallas kernels: 2.25 us -> 4.58 us  [lay(): pl.pallas_call(functools.partial(lay_kernel, spots), out_shape=jax.ShapeD...]
  transfers between devices with their start and end apart: 22 -> 22, of which waited for: 13 -> 15; matrix products, arithmetic and copies ran while one was open for 14% -> 14% of each run, Pallas kernels for 8% -> 8%
where the time goes in v10:
time: 197 us; the launch traced here: 196 us
  waiting for transfers between devices  95 us (48%)
  starting transfers between devices  37.1 us (19%)
  Pallas kernels  21.8 us (11%)
  matrix products  20.5 us (10%)
  local copies, waits for them, and re-layouts  18.7 us (9%)
  other arithmetic  2.64 us (1%)
    ppermute x13, waiting for transfers between devices, permute(): return lax.ppermute(x, AXES, moved(axis, to))  53 us
    all_to_all x1, waiting for transfers between devices, shards(): recv = lax.all_to_all(picked, COL, split_axis=0, concat_axis=0, tiled=True)  16.6 us
    all_to_all x2, waiting for transfers between devices, shards(): lax.all_to_all(cut, COL, split_axis=0, concat_axis=0, tiled=True)  15.3 us
    ppermute x13, starting transfers between devices, permute(): return lax.ppermute(x, AXES, moved(axis, to))  14.8 us
    unnamed x27, local copies, waits for them, and re-layouts  14.4 us
    dot_general x2, matrix products, shards(): jnp.dot(occ, dense[-1], preferred_element_type=jnp.float32)  13.4 us
    ppermute x6, waiting for transfers between devices, hop(): return lax.ppermute(x, AXES, pairs)  10.2 us
    ppermute x6, starting transfers between devices, hop(): return lax.ppermute(x, AXES, pairs)  9.51 us
  transfers between devices with their start and end apart: 22, of which 15 were waited for; matrix products, arithmetic and copies ran while one was open for 14% of the time, Pallas kernels for 8%

profile of v10, /device:TPU:2, one launch (start us, length us, event | category | flops | bytes accessed | tf_op | source)
XLA Modules:
  0.0 196.0 jit_solution(18302477757067126229)
XLA Ops:
  7.5 3.2 %collective-permute-done.2 = bf16[1,32,2048]{2,1,0:T(8,128)(2,1)S(1)} collective-permute-done((bf16[1,32,2048]{2,1,0:T(8,128)(2,1)S(1)}, bf16[1,32,2048]{2,1,0:T(8,128)(2,1)S(1)}, u32[]{:S(2)}, u32[]{:S(2)}) %collective-permute-start.2) | collective-permute-done | bytes 131104 | tf_op jit(solution)/shard_map/ppermute | solution.py:153
  22.0 5.7 %collective-permute-done.5 = bf16[4,32,2048]{2,1,0:T(8,128)(2,1)S(1)} collective-permute-done((bf16[4,32,2048]{2,1,0:T(8,128)(2,1)S(1)}, bf16[4,32,2048]{2,1,0:T(8,128)(2,1)S(1)}, u32[]{:S(2)}, u32[]{:S(2)}) %collective-permute-start.5) | collective-permute-done | bytes 524320 | tf_op jit(solution)/shard_map/ppermute | solution.py:153
  28.6 4.7 %all-to-all-start = ((bf16[16,1552,128]{2,1,0:T(8,128)(2,1)}), bf16[16,1552,128]{2,1,0:T(8,128)(2,1)}, u32[]{:S(2)}, u32[]{:S(2)}) async-start(bf16[16,1552,128]{2,1,0:T(8,128)(2,1)} %copy-done), calls=%async_computation | async-start | bytes 12713984 | tf_op jit(solution)/shard_map/all_to_all | solution.py:293
  41.7 23.5 %collective-permute-done.6.refs_1_ = bf16[16,16,2048]{2,1,0:T(8,128)(2,1)S(1)} collective-permute-done((bf16[16,16,2048]{2,1,0:T(8,128)(2,1)S(1)}, bf16[16,16,2048]{2,1,0:T(8,128)(2,1)S(1)}, u32[]{:S(2)}, u32[]{:S(2)}) %collective-permute-start.6) | collective-permute-done | bytes 1048608 | tf_op jit(solution)/shard_map/ppermute | solution.py:36
  65.4 3.3 %collective-permute-start.9 = (bf16[8,16,2048]{2,1,0:T(8,128)(2,1)S(1)}, bf16[8,16,2048]{2,1,0:T(8,128)(2,1)S(1)}, u32[]{:S(2)}, u32[]{:S(2)}) collective-permute-start(bf16[8,16,2048]{2,1,0:T(8,128)(2,1)S(1)} %slice.22), channel_id=1, source_target_pairs={{0,96},{1,97},{2,98},{3,99},{4,100},{5,101},{6,102},{7,103},{8,104... | collective-permute-start | bytes 1572872 | tf_op jit(solution)/shard_map/ppermute | solution.py:36
  68.7 11.5 %collective-permute-done.8.refs_3_ = bf16[8,16,2048]{2,1,0:T(8,128)(2,1)S(1)} collective-permute-done((bf16[8,16,2048]{2,1,0:T(8,128)(2,1)S(1)}, bf16[8,16,2048]{2,1,0:T(8,128)(2,1)S(1)}, u32[]{:S(2)}, u32[]{:S(2)}) %collective-permute-start.8) | collective-permute-done | bytes 524320 | tf_op jit(solution)/shard_map/ppermute | solution.py:36
  80.8 3.2 %collective-permute-start.12 = (bf16[16,16,2048]{2,1,0:T(8,128)(2,1)S(1)}, bf16[16,16,2048]{2,1,0:T(8,128)(2,1)}, u32[]{:S(2)}, u32[]{:S(2)}) collective-permute-start(bf16[16,16,2048]{2,1,0:T(8,128)(2,1)S(1)} %get-tuple-element.35.refs_0_), channel_id=1, source_target_pairs={{0,96},{1,97},{2,98},{3,99},{4,100},{5,101},{6,102},{7,103},{8,104... | collective-permute-start | bytes 3145736 | tf_op jit(solution)/shard_map/ppermute | solution.py:36
  88.5 3.3 %copy-done.1 = bf16[64,2,16,2048]{3,2,1,0:T(8,128)(2,1)} copy-done((bf16[64,2,16,2048]{3,2,1,0:T(8,128)(2,1)}, bf16[64,2,16,2048]{3,2,1,0:T(8,128)(2,1)S(1)}, u32[]{:S(2)}) %copy-start.1) | copy-done | bytes 8388632
  91.7 16.6 %all-to-all-done.refs_0_.refs_1_ = bf16[16,1552,128]{2,1,0:T(8,128)(2,1)} async-done(((bf16[16,1552,128]{2,1,0:T(8,128)(2,1)}), bf16[16,1552,128]{2,1,0:T(8,128)(2,1)}, u32[]{:S(2)}, u32[]{:S(2)}) %all-to-all-start) | async-done | bytes 6357024 | tf_op jit(solution)/shard_map/all_to_all | solution.py:293
  109.5 3.3 %place.2 = bf16[2048,256]{1,0:T(8,128)(2,1)S(1)} custom-call(s32[32]{0:T(128)S(1)} %sub.7.first_ref, bf16[16,1552,128]{2,1,0:T(8,128)(2,1)} %all-to-all-done.refs_0_.refs_1_, bf16[16,1552,128]{2,1,0:T(8,128)(2,1)} %all-to-all-done.refs_0_.refs_1_), custom_call_target="tpu_custom_call" | custom-call | flops 1048576 | bytes 4194304 | tf_op jit(solution)/shard_map/place/pallas_call | solution.py:124
  113.5 3.5 %convolution_convert_fusion.3 = bf16[2048,256]{1,0:T(8,128)(2,1)} fusion(bf16[2048,2048]{1,0:T(8,128)(2,1)S(1)} %bitcast.28, bf16[2048,256]{1,0:T(8,128)(2,1)S(1)} %place.2), kind=kOutput, calls=%fused_computation.3 | convolution fusion | flops 2148007936 | bytes 10485760 | tf_op jit(solution)/shard_map/dot_general | solution.py:307
  117.0 3.8 %all-to-all-start.1 = ((bf16[16,128,256]{2,1,0:T(8,128)(2,1)}), bf16[16,128,256]{2,1,0:T(8,128)(2,1)S(1)}, u32[]{:S(2)}, u32[]{:S(2)}) async-start(bf16[16,128,256]{2,1,0:T(8,128)(2,1)} %bitcast.31), calls=%async_computation.1 | async-start | bytes 2097152 | tf_op jit(solution)/shard_map/all_to_all | solution.py:309
  120.8 5.0 %place.3 = bf16[2048,512]{1,0:T(8,128)(2,1)S(1)} custom-call(s32[32]{0:T(128)S(1)} %sub.7.first_ref, bf16[16,1552,128]{2,1,0:T(8,128)(2,1)} %all-to-all-done.refs_0_.refs_1_, bf16[16,1552,128]{2,1,0:T(8,128)(2,1)} %all-to-all-done.refs_0_.refs_1_), custom_call_target="tpu_custom_call" | custom-call | flops 2097152 | bytes 8388608 | tf_op jit(solution)/shard_map/place/pallas_call | solution.py:124
  125.9 9.9 %convolution_convert_fusion.1 = bf16[2048,512]{1,0:T(8,128)(2,1)} fusion(bf16[2048,2048]{1,0:T(8,128)(2,1)} %bitcast.27, bf16[2048,512]{1,0:T(8,128)(2,1)S(1)} %place.3), kind=kOutput, calls=%fused_computation.1 | convolution fusion | flops 4296015872 | bytes 12582912 | tf_op jit(solution)/shard_map/dot_general | solution.py:307
  135.8 2.9 %all-to-all-done.1.x_ref = bf16[16,128,256]{2,1,0:T(8,128)(2,1)S(1)} async-done(((bf16[16,128,256]{2,1,0:T(8,128)(2,1)}), bf16[16,128,256]{2,1,0:T(8,128)(2,1)S(1)}, u32[]{:S(2)}, u32[]{:S(2)}) %all-to-all-start.1) | async-done | bytes 1048608 | tf_op jit(solution)/shard_map/all_to_all | solution.py:309
  138.7 4.2 %lay.3 = bf16[4,2,4,2,16,2048]{5,4,3,2,1,0:T(8,128)(2,1)} custom-call(bf16[16,16,2048]{2,1,0:T(8,128)(2,1)S(1)} %get-tuple-element.35.refs_0_, bf16[16,16,2048]{2,1,0:T(8,128)(2,1)S(1)} %collective-permute-done.11.refs_1_, bf16[16,16,2048]{2,1,0:T(8,128)(2,1)} %collective-permute-done.12.refs_2_, bf16[16,16,2048]{2,1,0:T(8,128)(2,1)} %collective-permute-done.13.refs_3_), custom_call_target="tpu_custom_call" | custom-call | bytes 8388608 | tf_op jit(solution)/shard_map/lay/pallas_call | solution.py:174
  142.9 4.2 %all-to-all-start.2 = ((bf16[16,128,512]{2,1,0:T(8,128)(2,1)}), bf16[16,128,512]{2,1,0:T(8,128)(2,1)S(1)}, u32[]{:S(2)}, u32[]{:S(2)}) async-start(bf16[16,128,512]{2,1,0:T(8,128)(2,1)} %bitcast.30), calls=%async_computation.2 | async-start | bytes 4194304 | tf_op jit(solution)/shard_map/all_to_all | solution.py:309
  147.1 3.2 %collective-permute-done.14.other_ref = bf16[64,16,2048]{2,1,0:T(8,128)(2,1)} collective-permute-done((bf16[64,16,2048]{2,1,0:T(8,128)(2,1)}, bf16[64,16,2048]{2,1,0:T(8,128)(2,1)}, u32[]{:S(2)}, u32[]{:S(2)}) %collective-permute-start.14) | collective-permute-done | bytes 4194336 | tf_op jit(solution)/shard_map/ppermute | solution.py:36
  150.4 4.1 %merge.3 = bf16[64,2,16,2048]{3,2,1,0:T(8,128)(2,1)S(1)} custom-call(bf16[64,16,2048]{2,1,0:T(8,128)(2,1)} %bitcast.7.mine_ref, bf16[64,16,2048]{2,1,0:T(8,128)(2,1)} %collective-permute-done.14.other_ref), custom_call_target="tpu_custom_call" | custom-call | bytes 16777216 | tf_op jit(solution)/shard_map/merge/pallas_call | solution.py:201
  156.9 4.8 %convolution_convert_fusion.refs_1_ = bf16[512,2048]{1,0:T(8,128)(2,1)S(1)} fusion(bf16[2048,512]{1,0:T(8,128)(2,1)S(1)} %copy-done.11, bf16[2048,2048]{1,0:T(8,128)(2,1)S(1)} %bitcast.24), kind=kOutput, calls=%fused_computation | convolution fusion | flops 4296015872 | bytes 12582912 | tf_op jit(solution)/shard_map/dot_general | solution.py:317
  164.3 12.4 %all-to-all-done.2.x_ref = bf16[16,128,512]{2,1,0:T(8,128)(2,1)S(1)} async-done(((bf16[16,128,512]{2,1,0:T(8,128)(2,1)}), bf16[16,128,512]{2,1,0:T(8,128)(2,1)S(1)}, u32[]{:S(2)}, u32[]{:S(2)}) %all-to-all-start.2) | async-done | bytes 2097184 | tf_op jit(solution)/shard_map/all_to_all | solution.py:309
  182.3 4.6 %collective-permute-done.16 = f32[6,6]{0,1:T(8,128)S(1)} collective-permute-done((f32[6,6]{0,1:T(8,128)S(1)}, f32[6,6]{0,1:T(8,128)S(1)}, u32[]{:S(2)}, u32[]{:S(2)}) %collective-permute-start.16) | collective-permute-done | bytes 176 | tf_op jit(solution)/shard_map/ppermute | solution.py:36
  187.5 3.0 %collective-permute-done.17 = f32[6,6]{0,1:T(8,128)S(1)} collective-permute-done((f32[6,6]{0,1:T(8,128)S(1)}, f32[6,6]{0,1:T(8,128)S(1)}, u32[]{:S(2)}, u32[]{:S(2)}) %collective-permute-start.17) | collective-permute-done | bytes 176 | tf_op jit(solution)/shard_map/ppermute | solution.py:36
  192.1 3.3 %collective-permute-done.18 = f32[6,6]{0,1:T(8,128)S(1)} collective-permute-done((f32[6,6]{0,1:T(8,128)S(1)}, f32[6,6]{0,1:T(8,128)S(1)}, u32[]{:S(2)}, u32[]{:S(2)}) %collective-permute-start.18) | collective-permute-done | bytes 176 | tf_op jit(solution)/shard_map/ppermute | solution.py:36
  (79 shorter events, 48.6 us)
Async XLA Ops:
  0.9 6.2 %collective-permute-start = (bf16[1,32,2048]{2,1,0:T(8,128)(2,1)S(1)}, bf16[1,32,2048]{2,1,0:T(8,128)(2,1)S(1)}, u32[]{:S(2)}, u32[]{:S(2)}) collective-permute-start(bf16[1,32,2048]{2,1,0:T(8,128)(2,1)S(1)} %maximum_bitcast_fusion), channel_id=1, source_target_pairs={{0,4},{1,17},{2,6},{3,19},{4,8},{5,21},{6,10},{7,23},{8,12},{9,25}... | collective-permute-start | bytes 393224 | tf_op jit(solution)/shard_map/ppermute | solution.py:153
  2.5 5.0 %collective-permute-start.1 = (bf16[1,32,2048]{2,1,0:T(8,128)(2,1)S(1)}, bf16[1,32,2048]{2,1,0:T(8,128)(2,1)S(1)}, u32[]{:S(2)}, u32[]{:S(2)}) collective-permute-start(bf16[1,32,2048]{2,1,0:T(8,128)(2,1)S(1)} %maximum_bitcast_fusion), channel_id=1, source_target_pairs={{0,12},{1,19},{2,14},{3,17},{4,0},{5,23},{6,2},{7,21},{8,4},{9,27}... | collective-permute-start | bytes 393224 | tf_op jit(solution)/shard_map/ppermute | solution.py:153
  4.2 6.5 %collective-permute-start.2 = (bf16[1,32,2048]{2,1,0:T(8,128)(2,1)S(1)}, bf16[1,32,2048]{2,1,0:T(8,128)(2,1)S(1)}, u32[]{:S(2)}, u32[]{:S(2)}) collective-permute-start(bf16[1,32,2048]{2,1,0:T(8,128)(2,1)S(1)} %maximum_bitcast_fusion), channel_id=1, source_target_pairs={{0,8},{1,3},{2,10},{3,1},{4,12},{5,7},{6,14},{7,5},{8,0},{9,11},{1... | collective-permute-start | bytes 393224 | tf_op jit(solution)/shard_map/ppermute | solution.py:153
  10.7 11.3 %collective-permute-start.3 = (bf16[4,32,2048]{2,1,0:T(8,128)(2,1)S(1)}, bf16[4,32,2048]{2,1,0:T(8,128)(2,1)S(1)}, u32[]{:S(2)}, u32[]{:S(2)}) collective-permute-start(bf16[4,32,2048]{2,1,0:T(8,128)(2,1)S(1)} %pad_maximum_fusion), channel_id=1, source_target_pairs={{0,16},{1,5},{2,18},{3,7},{4,20},{5,9},{6,22},{7,11},{8,24},{9,13}... | collective-permute-start | bytes 1572872 | tf_op jit(solution)/shard_map/ppermute | solution.py:153
  12.3 9.8 %collective-permute-start.4 = (bf16[4,32,2048]{2,1,0:T(8,128)(2,1)S(1)}, bf16[4,32,2048]{2,1,0:T(8,128)(2,1)S(1)}, u32[]{:S(2)}, u32[]{:S(2)}) collective-permute-start(bf16[4,32,2048]{2,1,0:T(8,128)(2,1)S(1)} %pad_maximum_fusion), channel_id=1, source_target_pairs={{0,18},{1,13},{2,16},{3,15},{4,22},{5,1},{6,20},{7,3},{8,26},{9,5}... | collective-permute-start | bytes 1572872 | tf_op jit(solution)/shard_map/ppermute | solution.py:153
  12.8 14.9 %collective-permute-start.5 = (bf16[4,32,2048]{2,1,0:T(8,128)(2,1)S(1)}, bf16[4,32,2048]{2,1,0:T(8,128)(2,1)S(1)}, u32[]{:S(2)}, u32[]{:S(2)}) collective-permute-start(bf16[4,32,2048]{2,1,0:T(8,128)(2,1)S(1)} %pad_maximum_fusion), channel_id=1, source_target_pairs={{0,2},{1,9},{2,0},{3,11},{4,6},{5,13},{6,4},{7,15},{8,10},{9,1},{1... | collective-permute-start | bytes 1572872 | tf_op jit(solution)/shard_map/ppermute | solution.py:153
  28.6 79.7 %all-to-all-start = ((bf16[16,1552,128]{2,1,0:T(8,128)(2,1)}), bf16[16,1552,128]{2,1,0:T(8,128)(2,1)}, u32[]{:S(2)}, u32[]{:S(2)}) async-start(bf16[16,1552,128]{2,1,0:T(8,128)(2,1)} %copy-done), calls=%async_computation | async-start | bytes 12713984 | tf_op jit(solution)/shard_map/all_to_all | solution.py:293
  37.5 27.7 %collective-permute-start.6 = (bf16[16,16,2048]{2,1,0:T(8,128)(2,1)S(1)}, bf16[16,16,2048]{2,1,0:T(8,128)(2,1)S(1)}, u32[]{:S(2)}, u32[]{:S(2)}) collective-permute-start(bf16[16,16,2048]{2,1,0:T(8,128)(2,1)S(1)} %get-tuple-element.26.refs_0_), channel_id=1, source_target_pairs={{0,32},{1,33},{2,34},{3,35},{4,36},{5,37},{6,38},{7,39},{8,40},{9,... | collective-permute-start | bytes 3145736 | tf_op jit(solution)/shard_map/ppermute | solution.py:36
  39.5 25.8 %collective-permute-start.7 = (bf16[16,16,2048]{2,1,0:T(8,128)(2,1)S(1)}, bf16[16,16,2048]{2,1,0:T(8,128)(2,1)S(1)}, u32[]{:S(2)}, u32[]{:S(2)}) collective-permute-start(bf16[16,16,2048]{2,1,0:T(8,128)(2,1)S(1)} %get-tuple-element.26.refs_0_), channel_id=1, source_target_pairs={{0,96},{1,97},{2,98},{3,99},{4,100},{5,101},{6,102},{7,103},{8,104... | collective-permute-start | bytes 3145736 | tf_op jit(solution)/shard_map/ppermute | solution.py:36
  65.2 14.9 %collective-permute-start.8 = (bf16[8,16,2048]{2,1,0:T(8,128)(2,1)S(1)}, bf16[8,16,2048]{2,1,0:T(8,128)(2,1)S(1)}, u32[]{:S(2)}, u32[]{:S(2)}) collective-permute-start(bf16[8,16,2048]{2,1,0:T(8,128)(2,1)S(1)} %slice.21), channel_id=1, source_target_pairs={{0,32},{1,33},{2,34},{3,35},{4,36},{5,37},{6,38},{7,39},{8,40},{9,... | collective-permute-start | bytes 1572872 | tf_op jit(solution)/shard_map/ppermute | solution.py:36
  65.4 14.8 %collective-permute-start.9 = (bf16[8,16,2048]{2,1,0:T(8,128)(2,1)S(1)}, bf16[8,16,2048]{2,1,0:T(8,128)(2,1)S(1)}, u32[]{:S(2)}, u32[]{:S(2)}) collective-permute-start(bf16[8,16,2048]{2,1,0:T(8,128)(2,1)S(1)} %slice.22), channel_id=1, source_target_pairs={{0,96},{1,97},{2,98},{3,99},{4,100},{5,101},{6,102},{7,103},{8,104... | collective-permute-start | bytes 1572872 | tf_op jit(solution)/shard_map/ppermute | solution.py:36
  80.6 7.2 %collective-permute-start.10 = (bf16[64,16,2048]{2,1,0:T(8,128)(2,1)S(1)}, bf16[64,16,2048]{2,1,0:T(8,128)(2,1)S(1)}, u32[]{:S(2)}, u32[]{:S(2)}) collective-permute-start(bf16[64,16,2048]{2,1,0:T(8,128)(2,1)S(1)} %bitcast.25), channel_id=1, source_target_pairs={{0,1},{1,0},{2,3},{3,2},{4,5},{5,4},{6,7},{7,6},{8,9},{9,8},{10,11... | collective-permute-start | bytes 12582920 | tf_op jit(solution)/shard_map/ppermute | solution.py:36
  80.7 55.1 %collective-permute-start.11 = (bf16[16,16,2048]{2,1,0:T(8,128)(2,1)S(1)}, bf16[16,16,2048]{2,1,0:T(8,128)(2,1)S(1)}, u32[]{:S(2)}, u32[]{:S(2)}) collective-permute-start(bf16[16,16,2048]{2,1,0:T(8,128)(2,1)S(1)} %get-tuple-element.35.refs_0_), channel_id=1, source_target_pairs={{0,32},{1,33},{2,34},{3,35},{4,36},{5,37},{6,38},{7,39},{8,40},{9,... | collective-permute-start | bytes 3145736 | tf_op jit(solution)/shard_map/ppermute | solution.py:36
  80.8 55.0 %collective-permute-start.12 = (bf16[16,16,2048]{2,1,0:T(8,128)(2,1)S(1)}, bf16[16,16,2048]{2,1,0:T(8,128)(2,1)}, u32[]{:S(2)}, u32[]{:S(2)}) collective-permute-start(bf16[16,16,2048]{2,1,0:T(8,128)(2,1)S(1)} %get-tuple-element.35.refs_0_), channel_id=1, source_target_pairs={{0,96},{1,97},{2,98},{3,99},{4,100},{5,101},{6,102},{7,103},{8,104... | collective-permute-start | bytes 3145736 | tf_op jit(solution)/shard_map/ppermute | solution.py:36
  84.0 51.8 %collective-permute-start.13 = (bf16[16,16,2048]{2,1,0:T(8,128)(2,1)S(1)}, bf16[16,16,2048]{2,1,0:T(8,128)(2,1)}, u32[]{:S(2)}, u32[]{:S(2)}) collective-permute-start(bf16[16,16,2048]{2,1,0:T(8,128)(2,1)S(1)} %get-tuple-element.35.refs_0_), channel_id=1, source_target_pairs={{0,64},{1,65},{2,66},{3,67},{4,68},{5,69},{6,70},{7,71},{8,72},{9,... | collective-permute-start | bytes 3145736 | tf_op jit(solution)/shard_map/ppermute | solution.py:36
  117.0 21.7 %all-to-all-start.1 = ((bf16[16,128,256]{2,1,0:T(8,128)(2,1)}), bf16[16,128,256]{2,1,0:T(8,128)(2,1)S(1)}, u32[]{:S(2)}, u32[]{:S(2)}) async-start(bf16[16,128,256]{2,1,0:T(8,128)(2,1)} %bitcast.31), calls=%async_computation.1 | async-start | bytes 2097152 | tf_op jit(solution)/shard_map/all_to_all | solution.py:309
  125.9 9.9 %copy-start.10 = (bf16[2048,512]{1,0:T(8,128)(2,1)}, bf16[2048,512]{1,0:T(8,128)(2,1)S(1)}, u32[]{:S(2)}) copy-start(bf16[2048,512]{1,0:T(8,128)(2,1)S(1)} %place.3) | copy-start | bytes 6291460
  142.9 7.5 %collective-permute-start.14 = (bf16[64,16,2048]{2,1,0:T(8,128)(2,1)}, bf16[64,16,2048]{2,1,0:T(8,128)(2,1)}, u32[]{:S(2)}, u32[]{:S(2)}) collective-permute-start(bf16[64,16,2048]{2,1,0:T(8,128)(2,1)} %bitcast.7.mine_ref), channel_id=1, source_target_pairs={{0,1},{1,0},{2,3},{3,2},{4,5},{5,4},{6,7},{7,6},{8,9},{9,8},{10,11... | collective-permute-start | bytes 12582920 | tf_op jit(solution)/shard_map/ppermute | solution.py:36
  142.9 33.8 %all-to-all-start.2 = ((bf16[16,128,512]{2,1,0:T(8,128)(2,1)}), bf16[16,128,512]{2,1,0:T(8,128)(2,1)S(1)}, u32[]{:S(2)}, u32[]{:S(2)}) async-start(bf16[16,128,512]{2,1,0:T(8,128)(2,1)} %bitcast.30), calls=%async_computation.2 | async-start | bytes 4194304 | tf_op jit(solution)/shard_map/all_to_all | solution.py:309
  147.1 7.4 %copy-start.6 = (bf16[2048,256]{1,0:T(8,128)(2,1)S(1)}, bf16[2048,256]{1,0:T(8,128)(2,1)}, u32[]{:S(2)}) copy-start(bf16[2048,256]{1,0:T(8,128)(2,1)} %copy-done.5) | copy-start | bytes 3145732
  180.5 1.2 collective-permute-start.15
  181.8 5.1 %collective-permute-start.16 = (f32[6,6]{0,1:T(8,128)S(1)}, f32[6,6]{0,1:T(8,128)S(1)}, u32[]{:S(2)}, u32[]{:S(2)}) collective-permute-start(f32[6,6]{0,1:T(8,128)S(1)} %fusion.9), channel_id=1, source_target_pairs={{0,2},{1,3},{2,0},{3,1},{4,6},{5,7},{6,4},{7,5},{8,10},{9,11},{10,... | collective-permute-start | bytes 440 | tf_op jit(solution)/shard_map/ppermute | solution.py:36
  186.9 3.6 %collective-permute-start.17 = (f32[6,6]{0,1:T(8,128)S(1)}, f32[6,6]{0,1:T(8,128)S(1)}, u32[]{:S(2)}, u32[]{:S(2)}) collective-permute-start(f32[6,6]{0,1:T(8,128)S(1)} %add.15), channel_id=1, source_target_pairs={{0,4},{1,5},{2,6},{3,7},{4,0},{5,1},{6,2},{7,3},{8,12},{9,13},{10,... | collective-permute-start | bytes 440 | tf_op jit(solution)/shard_map/ppermute | solution.py:36
  190.5 4.8 %collective-permute-start.18 = (f32[6,6]{0,1:T(8,128)S(1)}, f32[6,6]{0,1:T(8,128)S(1)}, u32[]{:S(2)}, u32[]{:S(2)}) collective-permute-start(f32[6,6]{0,1:T(8,128)S(1)} %add.16), channel_id=1, source_target_pairs={{0,12},{1,13},{2,14},{3,15},{4,8},{5,9},{6,10},{7,11},{8,4},{9,5},... | collective-permute-start | bytes 440 | tf_op jit(solution)/shard_map/ppermute | solution.py:36
  (10 other events, 30.7 us)

commit v11 on v6

--- a/solution.py
+++ b/solution.py
@@ -110,7 +110,7 @@
 
         return carry
 
-    lax.fori_loop(0, slot_refs[0].shape[0], body, 0)
+    lax.fori_loop(0, slot_refs[0].shape[0], body, 0, unroll=4)
     out_ref[...] = total[...].astype(out_ref.dtype)
 
 
@@ -206,57 +206,67 @@
 
 
 def pair_kernel(x_ref, *refs):
-    y_refs, out_ref = refs[:-1], refs[-1]
-    blocks, width, _ = x_ref.shape
-    aux_x = x_ref.shape[2] // width
+    count = (len(refs) - 4) // 2
+    y_refs, out_ref, x_here = refs[:count], refs[count], refs[count + 1]
+    y_here, x_sem, y_sems = refs[count + 2 : -2], refs[-2], refs[-1]
+    blocks, width, columns = x_ref.shape
+    aux_x = columns // width
+    for k in range(blocks):
+        for p in range(aux_x):
+            pltpu.make_async_copy(
+                x_ref.at[k, :, pl.ds(p * width, width)],
+                x_here.at[pl.ds(p * width, width), pl.ds(k * width, width)],
+                x_sem,
+            ).start()
+    loads = [
+        pltpu.make_async_copy(y_ref, here, y_sems.at[i])
+        for i, (y_ref, here) in enumerate(zip(y_refs, y_here, strict=True))
+    ]
+    for load in loads:
+        load.start()
     same = lax.broadcasted_iota(jnp.int32, (width, width), 0) == lax.broadcasted_iota(
         jnp.int32, (width, width), 1
     )
-    x = jnp.concatenate(
-        [
-            jnp.concatenate(
-                [x_ref[k, :, p * width : (p + 1) * width] for k in range(blocks)], axis=1
-            )
-            for p in range(aux_x)
-        ],
-        axis=0,
-    )
+    pltpu.make_async_copy(x_here, x_here, x_sem).wait()
     done = 0
-    for y_ref in y_refs:
+    for load, here in zip(loads, y_here, strict=True):
+        load.wait()
         products = lax.dot_general(
-            x, y_ref[...], (((1,), (1,)), ((), ())), preferred_element_type=jnp.float32
+            x_here[...], here[...], (((1,), (1,)), ((), ())), preferred_element_type=jnp.float32
         )
-        aux_y = y_ref.shape[0] // width
+        aux_y = here.shape[0] // width
         for q in range(aux_y):
             for p in range(aux_x):
                 tile = products[p * width : (p + 1) * width, q * width : (q + 1) * width]
-                tile = jnp.where(same, tile, 0.0).reshape(width // 8, 8, width)
-                out_ref[(done + q) * aux_x + p] = tile.sum(axis=0)
+                out_ref[(done + q) * aux_x + p, :] = jnp.where(same, tile, 0.0).sum(axis=0)
         done += aux_y
 
 
 def pair_sums(x, ys):
-    _, width, _ = x.shape
-    aux_x, aux_y = x.shape[2] // width, sum(y.shape[0] for y in ys) // width
+    blocks, width, columns = x.shape
+    aux_x, aux_y = columns // width, sum(y.shape[0] for y in ys) // width
     sums = pl.pallas_call(
         pair_kernel,
-        out_shape=jax.ShapeDtypeStruct((aux_y * aux_x, 8, width), jnp.float32),
-        in_specs=[pl.BlockSpec(memory_space=pltpu.VMEM)] * (1 + len(ys)),
+        out_shape=jax.ShapeDtypeStruct((aux_y * aux_x, width), jnp.float32),
+        in_specs=[pl.BlockSpec(memory_space=pl.ANY)] * (1 + len(ys)),
         out_specs=pl.BlockSpec(memory_space=pltpu.VMEM),
-        compiler_params=pltpu.CompilerParams(vmem_limit_bytes=16 * 1024 * 1024),
+        scratch_shapes=[pltpu.VMEM((columns, blocks * width), x.dtype)]
+        + [pltpu.VMEM(y.shape, y.dtype) for y in ys]
+        + [pltpu.SemaphoreType.DMA, pltpu.SemaphoreType.DMA((len(ys),))],
+        compiler_params=pltpu.CompilerParams(vmem_limit_bytes=60 * 1024 * 1024),
         cost_estimate=pl.CostEstimate(
             flops=2 * x.size * aux_y, bytes_accessed=6 * x.size, transcendentals=0
         ),
         name="pair",
     )(x, *ys)
-    return sums.sum(axis=(1, 2)).reshape(aux_y, aux_x).T
+    return sums.sum(axis=1).reshape(aux_y, aux_x).T
 
 
 def col_sum(x):
     x = x + other_core(x)
     x = x + permute(x, "xh", lambda k: 1 - k)
     x = x + permute(x, "y", lambda k: k ^ 1)
-    return x + permute(x, "y", lambda k: k ^ 2)
+    return x + permute(x, "y", lambda k: 3 - k)
 
 
 def shards(tensor_blocks, block_list, occ_green, virt_green):

time: 196 us -> 198 us (1.010)
  local copies, waits for them, and re-layouts: 15.4 us -> 10.3 us
  Pallas kernels: 19.4 us -> 24.3 us
  waiting for transfers between devices: 99.3 us -> 96 us
  matrix products: 22.2 us -> 24.3 us
  starting transfers between devices: 35.8 us -> 37.8 us
    pallas_call x2, Pallas kernels: 3.59 us -> 9.33 us  [pair_sums(): pl.pallas_call(pair_kernel, out_shape=jax.ShapeDtypeStruct((aux_y * aux_x...]
    unnamed x27 -> x15, local copies, waits for them, and re-layouts: 12.3 us -> 8.34 us
    all_to_all x2, waiting for transfers between devices: 17.4 us -> 13.8 us  [shards(): lax.all_to_all(cut, COL, split_axis=0, concat_axis=0, tiled=True)]
    dot_general x2, matrix products: 6.96 us -> 9.1 us  [shards(): lax.dot_general(d, virt_t, (((0,), (0,)), ((), ())), preferred_element_ty...]
  transfers between devices with their start and end apart: 29 -> 29, of which waited for: 17 -> 17; matrix products, arithmetic and copies ran while one was open for 13% -> 14% of each run, Pallas kernels for 9% -> 10%
where the time goes in v11:
time: 198 us; the launch traced here: 197 us
  waiting for transfers between devices  96 us (48%)
  starting transfers between devices  37.8 us (19%)
  Pallas kernels  24.3 us (12%)
  matrix products  24.3 us (12%)
  local copies, waits for them, and re-layouts  10.3 us (5%)
  other arithmetic  3.86 us (2%)
    ppermute x20, waiting for transfers between devices, permute(): return lax.ppermute(x, AXES, moved(axis, to))  55.5 us
    all_to_all x1, waiting for transfers between devices, shards(): recv = lax.all_to_all(picked, COL, split_axis=0, concat_axis=0, tiled=True)  16.3 us
    dot_general x2, matrix products, shards(): jnp.dot(occ, dense[-1], preferred_element_type=jnp.float32)  15.2 us
    ppermute x20, starting transfers between devices, permute(): return lax.ppermute(x, AXES, moved(axis, to))  14.5 us
    all_to_all x2, waiting for transfers between devices, shards(): lax.all_to_all(cut, COL, split_axis=0, concat_axis=0, tiled=True)  13.8 us
    ppermute x6, waiting for transfers between devices, hop(): return lax.ppermute(x, AXES, pairs)  10.3 us
    ppermute x6, starting transfers between devices, hop(): return lax.ppermute(x, AXES, pairs)  9.53 us
    pallas_call x2, Pallas kernels, pair_sums(): pl.pallas_call(pair_kernel, out_shape=jax.ShapeDtypeStruct((aux_y * aux_x...  9.33 us
  transfers between devices with their start and end apart: 29, of which 17 were waited for; matrix products, arithmetic and copies ran while one was open for 14% of the time, Pallas kernels for 10%

profile of v11, /device:TPU:2, one launch (start us, length us, event | category | flops | bytes accessed | tf_op | source)
XLA Modules:
  0.0 196.9 jit_solution(6740912329037624818)
XLA Ops:
  22.8 5.1 %collective-permute-done.4 = bf16[4,32,2048]{2,1,0:T(8,128)(2,1)S(1)} collective-permute-done((bf16[4,32,2048]{2,1,0:T(8,128)(2,1)S(1)}, bf16[4,32,2048]{2,1,0:T(8,128)(2,1)S(1)}, u32[]{:S(2)}, u32[]{:S(2)}) %collective-permute-start.4) | collective-permute-done | bytes 524320 | tf_op jit(solution)/shard_map/ppermute | solution.py:153
  27.9 4.7 %all-to-all-start = ((bf16[16,1552,128]{2,1,0:T(8,128)(2,1)}), bf16[16,1552,128]{2,1,0:T(8,128)(2,1)}, u32[]{:S(2)}, u32[]{:S(2)}) async-start(bf16[16,1552,128]{2,1,0:T(8,128)(2,1)} %copy-done), calls=%async_computation | async-start | bytes 12713984 | tf_op jit(solution)/shard_map/all_to_all | solution.py:284
  33.0 4.1 %collective-permute-start.7 = (bf16[16,16,2048]{2,1,0:T(8,128)(2,1)S(1)}, bf16[16,16,2048]{2,1,0:T(8,128)(2,1)S(1)}, u32[]{:S(2)}, u32[]{:S(2)}) collective-permute-start(bf16[16,16,2048]{2,1,0:T(8,128)(2,1)S(1)} %get-tuple-element.29.refs_0_), channel_id=1, source_target_pairs={{0,96},{1,97},{2,98},{3,99},{4,100},{5,101},{6,102},{7,103},{8,104... | collective-permute-start | bytes 3145736 | tf_op jit(solution)/shard_map/ppermute | solution.py:36
  37.1 22.8 %collective-permute-done.7.refs_2_ = bf16[16,16,2048]{2,1,0:T(8,128)(2,1)S(1)} collective-permute-done((bf16[16,16,2048]{2,1,0:T(8,128)(2,1)S(1)}, bf16[16,16,2048]{2,1,0:T(8,128)(2,1)S(1)}, u32[]{:S(2)}, u32[]{:S(2)}) %collective-permute-start.7) | collective-permute-done | bytes 1048608 | tf_op jit(solution)/shard_map/ppermute | solution.py:36
  60.0 3.8 %collective-permute-start.9 = (bf16[8,16,2048]{2,1,0:T(8,128)(2,1)S(1)}, bf16[8,16,2048]{2,1,0:T(8,128)(2,1)S(1)}, u32[]{:S(2)}, u32[]{:S(2)}) collective-permute-start(bf16[8,16,2048]{2,1,0:T(8,128)(2,1)S(1)} %slice.22), channel_id=1, source_target_pairs={{0,96},{1,97},{2,98},{3,99},{4,100},{5,101},{6,102},{7,103},{8,104... | collective-permute-start | bytes 1572872 | tf_op jit(solution)/shard_map/ppermute | solution.py:36
  63.9 10.7 %collective-permute-done.9.refs_4_ = bf16[8,16,2048]{2,1,0:T(8,128)(2,1)S(1)} collective-permute-done((bf16[8,16,2048]{2,1,0:T(8,128)(2,1)S(1)}, bf16[8,16,2048]{2,1,0:T(8,128)(2,1)S(1)}, u32[]{:S(2)}, u32[]{:S(2)}) %collective-permute-start.9) | collective-permute-done | bytes 524320 | tf_op jit(solution)/shard_map/ppermute | solution.py:36
  74.6 3.5 %collective-permute-done.8.refs_3_ = bf16[8,16,2048]{2,1,0:T(8,128)(2,1)S(1)} collective-permute-done((bf16[8,16,2048]{2,1,0:T(8,128)(2,1)S(1)}, bf16[8,16,2048]{2,1,0:T(8,128)(2,1)S(1)}, u32[]{:S(2)}, u32[]{:S(2)}) %collective-permute-start.8) | collective-permute-done | bytes 524320 | tf_op jit(solution)/shard_map/ppermute | solution.py:36
  79.2 5.4 %collective-permute-done.13.refs_8_ = bf16[8,16,2048]{2,1,0:T(8,128)(2,1)S(1)} collective-permute-done((bf16[8,16,2048]{2,1,0:T(8,128)(2,1)S(1)}, bf16[8,16,2048]{2,1,0:T(8,128)(2,1)S(1)}, u32[]{:S(2)}, u32[]{:S(2)}) %collective-permute-start.13) | collective-permute-done | bytes 524320 | tf_op jit(solution)/shard_map/ppermute | solution.py:36
  91.3 16.3 %all-to-all-done.refs_0_.refs_1_ = bf16[16,1552,128]{2,1,0:T(8,128)(2,1)} async-done(((bf16[16,1552,128]{2,1,0:T(8,128)(2,1)}), bf16[16,1552,128]{2,1,0:T(8,128)(2,1)}, u32[]{:S(2)}, u32[]{:S(2)}) %all-to-all-start) | async-done | bytes 6357024 | tf_op jit(solution)/shard_map/all_to_all | solution.py:284
  108.8 4.9 %place.2 = bf16[2048,384]{1,0:T(8,128)(2,1)S(1)} custom-call(s32[32]{0:T(128)S(1)} %sub.7.first_ref, bf16[16,1552,128]{2,1,0:T(8,128)(2,1)} %all-to-all-done.refs_0_.refs_1_, bf16[16,1552,128]{2,1,0:T(8,128)(2,1)} %all-to-all-done.refs_0_.refs_1_), custom_call_target="tpu_custom_call" | custom-call | flops 1572864 | bytes 6291456 | tf_op jit(solution)/shard_map/place/pallas_call | solution.py:124
  113.7 5.6 %convolution_convert_fusion.3 = bf16[2048,384]{1,0:T(8,128)(2,1)} fusion(bf16[2048,2048]{1,0:T(8,128)(2,1)S(1)} %bitcast.22, bf16[2048,384]{1,0:T(8,128)(2,1)S(1)} %place.2), kind=kOutput, calls=%fused_computation.3 | convolution fusion | flops 3222011904 | bytes 11534336 | tf_op jit(solution)/shard_map/dot_general | solution.py:297
  119.3 4.6 %all-to-all-start.1 = ((bf16[16,128,384]{2,1,0:T(8,128)(2,1)}), bf16[16,128,384]{2,1,0:T(8,128)(2,1)}, u32[]{:S(2)}, u32[]{:S(2)}) async-start(bf16[16,128,384]{2,1,0:T(8,128)(2,1)} %bitcast.27), calls=%async_computation.1 | async-start | bytes 3145728 | tf_op jit(solution)/shard_map/all_to_all | solution.py:299
  123.9 4.3 %place.3 = bf16[2048,384]{1,0:T(8,128)(2,1)S(1)} custom-call(s32[32]{0:T(128)S(1)} %sub.7.first_ref, bf16[16,1552,128]{2,1,0:T(8,128)(2,1)} %all-to-all-done.refs_0_.refs_1_, bf16[16,1552,128]{2,1,0:T(8,128)(2,1)} %all-to-all-done.refs_0_.refs_1_), custom_call_target="tpu_custom_call" | custom-call | flops 1572864 | bytes 6291456 | tf_op jit(solution)/shard_map/place/pallas_call | solution.py:124
  128.2 9.7 %convolution_convert_fusion.2 = bf16[2048,384]{1,0:T(8,128)(2,1)} fusion(bf16[2048,2048]{1,0:T(8,128)(2,1)} %bitcast.21, bf16[2048,384]{1,0:T(8,128)(2,1)S(1)} %place.3), kind=kOutput, calls=%fused_computation.2 | convolution fusion | flops 3222011904 | bytes 11534336 | tf_op jit(solution)/shard_map/dot_general | solution.py:297
  139.0 8.5 %all-to-all-done.1.x_ref = bf16[16,128,384]{2,1,0:T(8,128)(2,1)} async-done(((bf16[16,128,384]{2,1,0:T(8,128)(2,1)}), bf16[16,128,384]{2,1,0:T(8,128)(2,1)}, u32[]{:S(2)}, u32[]{:S(2)}) %all-to-all-start.1) | async-done | bytes 1572896 | tf_op jit(solution)/shard_map/all_to_all | solution.py:299
  147.5 4.4 %all-to-all-start.2 = ((bf16[16,128,384]{2,1,0:T(8,128)(2,1)}), bf16[16,128,384]{2,1,0:T(8,128)(2,1)}, u32[]{:S(2)}, u32[]{:S(2)}) async-start(bf16[16,128,384]{2,1,0:T(8,128)(2,1)} %bitcast.26), calls=%async_computation.2 | async-start | bytes 3145728 | tf_op jit(solution)/shard_map/all_to_all | solution.py:299
  152.0 3.8 %lay.3 = bf16[4,2,4,2,2,16,2048]{6,5,4,3,2,1,0:T(8,128)(2,1)S(1)} custom-call(bf16[16,16,2048]{2,1,0:T(8,128)(2,1)S(1)} %get-tuple-element.36.refs_0_, bf16[16,16,2048]{2,1,0:T(8,128)(2,1)} %collective-permute-done.15.refs_1_, bf16[16,16,2048]{2,1,0:T(8,128)(2,1)} %collective-permute-done.16.refs_2_, bf16[16,16,2048]{2,1,0:T(8,128)(2,1)} %collective-permute-done.17.refs_3_, ...), custom_call_target="tpu_custom_call" | custom-call | bytes 16777216 | tf_op jit(solution)/shard_map/lay/pallas_call | solution.py:175
  155.8 4.5 %convolution_convert_fusion.refs_1_ = bf16[384,2048]{1,0:T(8,128)(2,1)} fusion(bf16[2048,384]{1,0:T(8,128)(2,1)S(1)} %copy-done.5, bf16[2048,2048]{1,0:T(8,128)(2,1)S(1)} %bitcast.23), kind=kOutput, calls=%fused_computation | convolution fusion | flops 3222011904 | bytes 11534336 | tf_op jit(solution)/shard_map/dot_general | solution.py:307
  160.3 4.6 %convolution_convert_fusion.1.refs_0_ = bf16[384,2048]{1,0:T(8,128)(2,1)} fusion(bf16[2048,384]{1,0:T(8,128)(2,1)S(1)} %place.2, bf16[2048,2048]{1,0:T(8,128)(2,1)S(1)} %bitcast.24), kind=kOutput, calls=%fused_computation.1 | convolution fusion | flops 3222011904 | bytes 11534336 | tf_op jit(solution)/shard_map/dot_general | solution.py:307
  164.9 4.7 %pair.2 = f32[18,128]{1,0:T(8,128)} custom-call(bf16[16,128,384]{2,1,0:T(8,128)(2,1)} %all-to-all-done.1.x_ref, bf16[384,2048]{1,0:T(8,128)(2,1)} %convolution_convert_fusion.1.refs_0_, bf16[384,2048]{1,0:T(8,128)(2,1)} %convolution_convert_fusion.refs_1_), custom_call_target="tpu_custom_call" | custom-call | flops 9437184 | bytes 4718592 | tf_op jit(solution)/shard_map/pair/pallas_call | solution.py:248
  170.4 5.3 %all-to-all-done.2.x_ref = bf16[16,128,384]{2,1,0:T(8,128)(2,1)} async-done(((bf16[16,128,384]{2,1,0:T(8,128)(2,1)}), bf16[16,128,384]{2,1,0:T(8,128)(2,1)}, u32[]{:S(2)}, u32[]{:S(2)}) %all-to-all-start.2) | async-done | bytes 1572896 | tf_op jit(solution)/shard_map/all_to_all | solution.py:299
  175.7 4.7 %pair.3 = f32[18,128]{1,0:T(8,128)} custom-call(bf16[16,128,384]{2,1,0:T(8,128)(2,1)} %all-to-all-done.2.x_ref, bf16[384,2048]{1,0:T(8,128)(2,1)} %convolution_convert_fusion.1.refs_0_, bf16[384,2048]{1,0:T(8,128)(2,1)} %convolution_convert_fusion.refs_1_), custom_call_target="tpu_custom_call" | custom-call | flops 9437184 | bytes 4718592 | tf_op jit(solution)/shard_map/pair/pallas_call | solution.py:248
  183.3 4.5 %collective-permute-done.23 = f32[6,6]{0,1:T(8,128)S(1)} collective-permute-done((f32[6,6]{0,1:T(8,128)S(1)}, f32[6,6]{0,1:T(8,128)S(1)}, u32[]{:S(2)}, u32[]{:S(2)}) %collective-permute-start.23) | collective-permute-done | bytes 176 | tf_op jit(solution)/shard_map/ppermute | solution.py:36
  192.9 3.3 %collective-permute-done.25 = f32[6,6]{0,1:T(8,128)S(1)} collective-permute-done((f32[6,6]{0,1:T(8,128)S(1)}, f32[6,6]{0,1:T(8,128)S(1)}, u32[]{:S(2)}, u32[]{:S(2)}) %collective-permute-start.25) | collective-permute-done | bytes 176 | tf_op jit(solution)/shard_map/ppermute | solution.py:36
  (79 shorter events, 43.0 us)
Async XLA Ops:
  0.9 6.6 %collective-permute-start.2 = (bf16[1,32,2048]{2,1,0:T(8,128)(2,1)S(1)}, bf16[1,32,2048]{2,1,0:T(8,128)(2,1)S(1)}, u32[]{:S(2)}, u32[]{:S(2)}) collective-permute-start(bf16[1,32,2048]{2,1,0:T(8,128)(2,1)S(1)} %maximum_bitcast_fusion), channel_id=1, source_target_pairs={{0,8},{1,3},{2,10},{3,1},{4,12},{5,7},{6,14},{7,5},{8,0},{9,11},{1... | collective-permute-start | bytes 393224 | tf_op jit(solution)/shard_map/ppermute | solution.py:153
  5.2 6.2 %collective-permute-start = (bf16[1,32,2048]{2,1,0:T(8,128)(2,1)S(1)}, bf16[1,32,2048]{2,1,0:T(8,128)(2,1)S(1)}, u32[]{:S(2)}, u32[]{:S(2)}) collective-permute-start(bf16[1,32,2048]{2,1,0:T(8,128)(2,1)S(1)} %maximum_bitcast_fusion), channel_id=1, source_target_pairs={{0,4},{1,17},{2,6},{3,19},{4,8},{5,21},{6,10},{7,23},{8,12},{9,25}... | collective-permute-start | bytes 393224 | tf_op jit(solution)/shard_map/ppermute | solution.py:153
  11.5 11.3 %collective-permute-start.5 = (bf16[4,32,2048]{2,1,0:T(8,128)(2,1)S(1)}, bf16[4,32,2048]{2,1,0:T(8,128)(2,1)S(1)}, u32[]{:S(2)}, u32[]{:S(2)}) collective-permute-start(bf16[4,32,2048]{2,1,0:T(8,128)(2,1)S(1)} %pad_maximum_fusion), channel_id=1, source_target_pairs={{0,2},{1,9},{2,0},{3,11},{4,6},{5,13},{6,4},{7,15},{8,10},{9,1},{1... | collective-permute-start | bytes 1572872 | tf_op jit(solution)/shard_map/ppermute | solution.py:153
  13.7 14.2 %collective-permute-start.4 = (bf16[4,32,2048]{2,1,0:T(8,128)(2,1)S(1)}, bf16[4,32,2048]{2,1,0:T(8,128)(2,1)S(1)}, u32[]{:S(2)}, u32[]{:S(2)}) collective-permute-start(bf16[4,32,2048]{2,1,0:T(8,128)(2,1)S(1)} %pad_maximum_fusion), channel_id=1, source_target_pairs={{0,18},{1,13},{2,16},{3,15},{4,22},{5,1},{6,20},{7,3},{8,26},{9,5}... | collective-permute-start | bytes 1572872 | tf_op jit(solution)/shard_map/ppermute | solution.py:153
  15.1 12.8 %collective-permute-start.3 = (bf16[4,32,2048]{2,1,0:T(8,128)(2,1)S(1)}, bf16[4,32,2048]{2,1,0:T(8,128)(2,1)S(1)}, u32[]{:S(2)}, u32[]{:S(2)}) collective-permute-start(bf16[4,32,2048]{2,1,0:T(8,128)(2,1)S(1)} %pad_maximum_fusion), channel_id=1, source_target_pairs={{0,16},{1,5},{2,18},{3,7},{4,20},{5,9},{6,22},{7,11},{8,24},{9,13}... | collective-permute-start | bytes 1572872 | tf_op jit(solution)/shard_map/ppermute | solution.py:153
  27.9 79.7 %all-to-all-start = ((bf16[16,1552,128]{2,1,0:T(8,128)(2,1)}), bf16[16,1552,128]{2,1,0:T(8,128)(2,1)}, u32[]{:S(2)}, u32[]{:S(2)}) async-start(bf16[16,1552,128]{2,1,0:T(8,128)(2,1)} %copy-done), calls=%async_computation | async-start | bytes 12713984 | tf_op jit(solution)/shard_map/all_to_all | solution.py:284
  33.0 26.9 %collective-permute-start.7 = (bf16[16,16,2048]{2,1,0:T(8,128)(2,1)S(1)}, bf16[16,16,2048]{2,1,0:T(8,128)(2,1)S(1)}, u32[]{:S(2)}, u32[]{:S(2)}) collective-permute-start(bf16[16,16,2048]{2,1,0:T(8,128)(2,1)S(1)} %get-tuple-element.29.refs_0_), channel_id=1, source_target_pairs={{0,96},{1,97},{2,98},{3,99},{4,100},{5,101},{6,102},{7,103},{8,104... | collective-permute-start | bytes 3145736 | tf_op jit(solution)/shard_map/ppermute | solution.py:36
  37.1 26.6 %collective-permute-start.6 = (bf16[16,16,2048]{2,1,0:T(8,128)(2,1)S(1)}, bf16[16,16,2048]{2,1,0:T(8,128)(2,1)S(1)}, u32[]{:S(2)}, u32[]{:S(2)}) collective-permute-start(bf16[16,16,2048]{2,1,0:T(8,128)(2,1)S(1)} %get-tuple-element.29.refs_0_), channel_id=1, source_target_pairs={{0,32},{1,33},{2,34},{3,35},{4,36},{5,37},{6,38},{7,39},{8,40},{9,... | collective-permute-start | bytes 3145736 | tf_op jit(solution)/shard_map/ppermute | solution.py:36
  60.0 14.6 %collective-permute-start.9 = (bf16[8,16,2048]{2,1,0:T(8,128)(2,1)S(1)}, bf16[8,16,2048]{2,1,0:T(8,128)(2,1)S(1)}, u32[]{:S(2)}, u32[]{:S(2)}) collective-permute-start(bf16[8,16,2048]{2,1,0:T(8,128)(2,1)S(1)} %slice.22), channel_id=1, source_target_pairs={{0,96},{1,97},{2,98},{3,99},{4,100},{5,101},{6,102},{7,103},{8,104... | collective-permute-start | bytes 1572872 | tf_op jit(solution)/shard_map/ppermute | solution.py:36
  63.8 14.3 %collective-permute-start.8 = (bf16[8,16,2048]{2,1,0:T(8,128)(2,1)S(1)}, bf16[8,16,2048]{2,1,0:T(8,128)(2,1)S(1)}, u32[]{:S(2)}, u32[]{:S(2)}) collective-permute-start(bf16[8,16,2048]{2,1,0:T(8,128)(2,1)S(1)} %slice.21), channel_id=1, source_target_pairs={{0,32},{1,33},{2,34},{3,35},{4,36},{5,37},{6,38},{7,39},{8,40},{9,... | collective-permute-start | bytes 1572872 | tf_op jit(solution)/shard_map/ppermute | solution.py:36
  78.1 8.2 %collective-permute-start.10 = (bf16[16,16,2048]{2,1,0:T(8,128)(2,1)S(1)}, bf16[16,16,2048]{2,1,0:T(8,128)(2,1)S(1)}, u32[]{:S(2)}, u32[]{:S(2)}) collective-permute-start(bf16[16,16,2048]{2,1,0:T(8,128)(2,1)S(1)} %get-tuple-element.29.refs_0_), channel_id=1, source_target_pairs={{0,1},{1,0},{2,3},{3,2},{4,5},{5,4},{6,7},{7,6},{8,9},{9,8},{10,11... | collective-permute-start | bytes 3145736 | tf_op jit(solution)/shard_map/ppermute | solution.py:36
  78.1 9.2 %collective-permute-start.11 = (bf16[16,16,2048]{2,1,0:T(8,128)(2,1)S(1)}, bf16[16,16,2048]{2,1,0:T(8,128)(2,1)S(1)}, u32[]{:S(2)}, u32[]{:S(2)}) collective-permute-start(bf16[16,16,2048]{2,1,0:T(8,128)(2,1)S(1)} %collective-permute-done.6.refs_1_), channel_id=1, source_target_pairs={{0,1},{1,0},{2,3},{3,2},{4,5},{5,4},{6,7},{7,6},{8,9},{9,8},{10,11... | collective-permute-start | bytes 3145736 | tf_op jit(solution)/shard_map/ppermute | solution.py:36
  78.6 8.7 %collective-permute-start.12 = (bf16[16,16,2048]{2,1,0:T(8,128)(2,1)S(1)}, bf16[16,16,2048]{2,1,0:T(8,128)(2,1)S(1)}, u32[]{:S(2)}, u32[]{:S(2)}) collective-permute-start(bf16[16,16,2048]{2,1,0:T(8,128)(2,1)S(1)} %collective-permute-done.7.refs_2_), channel_id=1, source_target_pairs={{0,1},{1,0},{2,3},{3,2},{4,5},{5,4},{6,7},{7,6},{8,9},{9,8},{10,11... | collective-permute-start | bytes 3145736 | tf_op jit(solution)/shard_map/ppermute | solution.py:36
  78.6 5.9 %collective-permute-start.13 = (bf16[8,16,2048]{2,1,0:T(8,128)(2,1)S(1)}, bf16[8,16,2048]{2,1,0:T(8,128)(2,1)S(1)}, u32[]{:S(2)}, u32[]{:S(2)}) collective-permute-start(bf16[8,16,2048]{2,1,0:T(8,128)(2,1)S(1)} %collective-permute-done.8.refs_3_), channel_id=1, source_target_pairs={{0,1},{1,0},{2,3},{3,2},{4,5},{5,4},{6,7},{7,6},{8,9},{9,8},{10,11... | collective-permute-start | bytes 1572872 | tf_op jit(solution)/shard_map/ppermute | solution.py:36
  79.1 6.1 %collective-permute-start.14 = (bf16[8,16,2048]{2,1,0:T(8,128)(2,1)S(1)}, bf16[8,16,2048]{2,1,0:T(8,128)(2,1)S(1)}, u32[]{:S(2)}, u32[]{:S(2)}) collective-permute-start(bf16[8,16,2048]{2,1,0:T(8,128)(2,1)S(1)} %collective-permute-done.9.refs_4_), channel_id=1, source_target_pairs={{0,1},{1,0},{2,3},{3,2},{4,5},{5,4},{6,7},{7,6},{8,9},{9,8},{10,11... | collective-permute-start | bytes 1572872 | tf_op jit(solution)/shard_map/ppermute | solution.py:36
  84.5 53.3 %collective-permute-start.17 = (bf16[16,16,2048]{2,1,0:T(8,128)(2,1)S(1)}, bf16[16,16,2048]{2,1,0:T(8,128)(2,1)}, u32[]{:S(2)}, u32[]{:S(2)}) collective-permute-start(bf16[16,16,2048]{2,1,0:T(8,128)(2,1)S(1)} %get-tuple-element.36.refs_0_), channel_id=1, source_target_pairs={{0,64},{1,65},{2,66},{3,67},{4,68},{5,69},{6,70},{7,71},{8,72},{9,... | collective-permute-start | bytes 3145736 | tf_op jit(solution)/shard_map/ppermute | solution.py:36
  85.3 52.6 %collective-permute-start.16 = (bf16[16,16,2048]{2,1,0:T(8,128)(2,1)S(1)}, bf16[16,16,2048]{2,1,0:T(8,128)(2,1)}, u32[]{:S(2)}, u32[]{:S(2)}) collective-permute-start(bf16[16,16,2048]{2,1,0:T(8,128)(2,1)S(1)} %get-tuple-element.36.refs_0_), channel_id=1, source_target_pairs={{0,96},{1,97},{2,98},{3,99},{4,100},{5,101},{6,102},{7,103},{8,104... | collective-permute-start | bytes 3145736 | tf_op jit(solution)/shard_map/ppermute | solution.py:36
  86.3 51.6 %collective-permute-start.15 = (bf16[16,16,2048]{2,1,0:T(8,128)(2,1)S(1)}, bf16[16,16,2048]{2,1,0:T(8,128)(2,1)}, u32[]{:S(2)}, u32[]{:S(2)}) collective-permute-start(bf16[16,16,2048]{2,1,0:T(8,128)(2,1)S(1)} %get-tuple-element.36.refs_0_), channel_id=1, source_target_pairs={{0,32},{1,33},{2,34},{3,35},{4,36},{5,37},{6,38},{7,39},{8,40},{9,... | collective-permute-start | bytes 3145736 | tf_op jit(solution)/shard_map/ppermute | solution.py:36
  119.3 28.2 %all-to-all-start.1 = ((bf16[16,128,384]{2,1,0:T(8,128)(2,1)}), bf16[16,128,384]{2,1,0:T(8,128)(2,1)}, u32[]{:S(2)}, u32[]{:S(2)}) async-start(bf16[16,128,384]{2,1,0:T(8,128)(2,1)} %bitcast.27), calls=%async_computation.1 | async-start | bytes 3145728 | tf_op jit(solution)/shard_map/all_to_all | solution.py:299
  137.9 14.1 %collective-permute-start.18 = (bf16[16,16,2048]{2,1,0:T(8,128)(2,1)S(1)}, bf16[16,16,2048]{2,1,0:T(8,128)(2,1)}, u32[]{:S(2)}, u32[]{:S(2)}) collective-permute-start(bf16[16,16,2048]{2,1,0:T(8,128)(2,1)S(1)} %get-tuple-element.36.refs_0_), channel_id=1, source_target_pairs={{0,1},{1,0},{2,3},{3,2},{4,5},{5,4},{6,7},{7,6},{8,9},{9,8},{10,11... | collective-permute-start | bytes 3145736 | tf_op jit(solution)/shard_map/ppermute | solution.py:36
  138.0 13.9 %collective-permute-start.19 = (bf16[16,16,2048]{2,1,0:T(8,128)(2,1)}, bf16[16,16,2048]{2,1,0:T(8,128)(2,1)}, u32[]{:S(2)}, u32[]{:S(2)}) collective-permute-start(bf16[16,16,2048]{2,1,0:T(8,128)(2,1)} %collective-permute-done.15.refs_1_), channel_id=1, source_target_pairs={{0,1},{1,0},{2,3},{3,2},{4,5},{5,4},{6,7},{7,6},{8,9},{9,8},{10,11... | collective-permute-start | bytes 3145736 | tf_op jit(solution)/shard_map/ppermute | solution.py:36
  138.4 13.5 %collective-permute-start.20 = (bf16[16,16,2048]{2,1,0:T(8,128)(2,1)}, bf16[16,16,2048]{2,1,0:T(8,128)(2,1)}, u32[]{:S(2)}, u32[]{:S(2)}) collective-permute-start(bf16[16,16,2048]{2,1,0:T(8,128)(2,1)} %collective-permute-done.16.refs_2_), channel_id=1, source_target_pairs={{0,1},{1,0},{2,3},{3,2},{4,5},{5,4},{6,7},{7,6},{8,9},{9,8},{10,11... | collective-permute-start | bytes 3145736 | tf_op jit(solution)/shard_map/ppermute | solution.py:36
  138.5 13.4 %collective-permute-start.21 = (bf16[16,16,2048]{2,1,0:T(8,128)(2,1)}, bf16[16,16,2048]{2,1,0:T(8,128)(2,1)}, u32[]{:S(2)}, u32[]{:S(2)}) collective-permute-start(bf16[16,16,2048]{2,1,0:T(8,128)(2,1)} %collective-permute-done.17.refs_3_), channel_id=1, source_target_pairs={{0,1},{1,0},{2,3},{3,2},{4,5},{5,4},{6,7},{7,6},{8,9},{9,8},{10,11... | collective-permute-start | bytes 3145736 | tf_op jit(solution)/shard_map/ppermute | solution.py:36
  147.5 28.2 %all-to-all-start.2 = ((bf16[16,128,384]{2,1,0:T(8,128)(2,1)}), bf16[16,128,384]{2,1,0:T(8,128)(2,1)}, u32[]{:S(2)}, u32[]{:S(2)}) async-start(bf16[16,128,384]{2,1,0:T(8,128)(2,1)} %bitcast.26), calls=%async_computation.2 | async-start | bytes 3145728 | tf_op jit(solution)/shard_map/all_to_all | solution.py:299
  (11 other events, 46.4 us)

commit v12 on v6

--- a/solution.py
+++ b/solution.py
@@ -110,7 +110,7 @@
 
         return carry
 
-    lax.fori_loop(0, slot_refs[0].shape[0], body, 0)
+    lax.fori_loop(0, slot_refs[0].shape[0], body, 0, unroll=True)
     out_ref[...] = total[...].astype(out_ref.dtype)
 
 
@@ -256,7 +256,7 @@
     x = x + other_core(x)
     x = x + permute(x, "xh", lambda k: 1 - k)
     x = x + permute(x, "y", lambda k: k ^ 1)
-    return x + permute(x, "y", lambda k: k ^ 2)
+    return x + permute(x, "y", lambda k: 3 - k)
 
 
 def shards(tensor_blocks, block_list, occ_green, virt_green):

time: 196 us -> 195 us (level)
  no operation moved by 1% of the time
where the time goes in v12:
time: 195 us
  waiting for transfers between devices  98.8 us (51%)
  starting transfers between devices  36.3 us (19%)
  matrix products  22.2 us (11%)
  Pallas kernels  19 us (10%)
  local copies, waits for them, and re-layouts  15.4 us (8%)
  other arithmetic  2.64 us (1%)
    ppermute x20, waiting for transfers between devices, permute(): return lax.ppermute(x, AXES, moved(axis, to))  55.5 us
    all_to_all x2, waiting for transfers between devices, shards(): lax.all_to_all(cut, COL, split_axis=0, concat_axis=0, tiled=True)  17.7 us
    all_to_all x1, waiting for transfers between devices, shards(): recv = lax.all_to_all(picked, COL, split_axis=0, concat_axis=0, tiled=True)  15.3 us
    dot_general x2, matrix products, shards(): jnp.dot(occ, dense[-1], preferred_element_type=jnp.float32)  15.2 us
    ppermute x20, starting transfers between devices, permute(): return lax.ppermute(x, AXES, moved(axis, to))  14.5 us
    unnamed x27, local copies, waits for them, and re-layouts  12.3 us
    ppermute x6, waiting for transfers between devices, hop(): return lax.ppermute(x, AXES, pairs)  10.3 us
    ppermute x6, starting transfers between devices, hop(): return lax.ppermute(x, AXES, pairs)  9.53 us
  transfers between devices with their start and end apart: 29, of which 17 were waited for; matrix products, arithmetic and copies ran while one was open for 13% of the time, Pallas kernels for 9%

profile of v12, /device:TPU:2, one launch (start us, length us, event | category | flops | bytes accessed | tf_op | source)
XLA Modules:
  0.0 194.6 jit_solution(14711497409938928901)
XLA Ops:
  0.9 3.3 %collective-permute-start.2 = (bf16[1,32,2048]{2,1,0:T(8,128)(2,1)S(1)}, bf16[1,32,2048]{2,1,0:T(8,128)(2,1)S(1)}, u32[]{:S(2)}, u32[]{:S(2)}) collective-permute-start(bf16[1,32,2048]{2,1,0:T(8,128)(2,1)S(1)} %maximum_bitcast_fusion), channel_id=1, source_target_pairs={{0,8},{1,3},{2,10},{3,1},{4,12},{5,7},{6,14},{7,5},{8,0},{9,11},{1... | collective-permute-start | bytes 393224 | tf_op jit(solution)/shard_map/ppermute | solution.py:153
  22.8 5.1 %collective-permute-done.4 = bf16[4,32,2048]{2,1,0:T(8,128)(2,1)S(1)} collective-permute-done((bf16[4,32,2048]{2,1,0:T(8,128)(2,1)S(1)}, bf16[4,32,2048]{2,1,0:T(8,128)(2,1)S(1)}, u32[]{:S(2)}, u32[]{:S(2)}) %collective-permute-start.4) | collective-permute-done | bytes 524320 | tf_op jit(solution)/shard_map/ppermute | solution.py:153
  27.9 4.7 %all-to-all-start = ((bf16[16,1552,128]{2,1,0:T(8,128)(2,1)}), bf16[16,1552,128]{2,1,0:T(8,128)(2,1)}, u32[]{:S(2)}, u32[]{:S(2)}) async-start(bf16[16,1552,128]{2,1,0:T(8,128)(2,1)} %copy-done), calls=%async_computation | async-start | bytes 12713984 | tf_op jit(solution)/shard_map/all_to_all | solution.py:274
  34.0 4.0 %collective-permute-start.7 = (bf16[16,16,2048]{2,1,0:T(8,128)(2,1)S(1)}, bf16[16,16,2048]{2,1,0:T(8,128)(2,1)S(1)}, u32[]{:S(2)}, u32[]{:S(2)}) collective-permute-start(bf16[16,16,2048]{2,1,0:T(8,128)(2,1)S(1)} %get-tuple-element.29.refs_0_), channel_id=1, source_target_pairs={{0,96},{1,97},{2,98},{3,99},{4,100},{5,101},{6,102},{7,103},{8,104... | collective-permute-start | bytes 3145736 | tf_op jit(solution)/shard_map/ppermute | solution.py:36
  38.1 22.8 %collective-permute-done.7.refs_2_ = bf16[16,16,2048]{2,1,0:T(8,128)(2,1)S(1)} collective-permute-done((bf16[16,16,2048]{2,1,0:T(8,128)(2,1)S(1)}, bf16[16,16,2048]{2,1,0:T(8,128)(2,1)S(1)}, u32[]{:S(2)}, u32[]{:S(2)}) %collective-permute-start.7) | collective-permute-done | bytes 1048608 | tf_op jit(solution)/shard_map/ppermute | solution.py:36
  60.9 3.8 %collective-permute-start.9 = (bf16[8,16,2048]{2,1,0:T(8,128)(2,1)S(1)}, bf16[8,16,2048]{2,1,0:T(8,128)(2,1)S(1)}, u32[]{:S(2)}, u32[]{:S(2)}) collective-permute-start(bf16[8,16,2048]{2,1,0:T(8,128)(2,1)S(1)} %slice.22), channel_id=1, source_target_pairs={{0,96},{1,97},{2,98},{3,99},{4,100},{5,101},{6,102},{7,103},{8,104... | collective-permute-start | bytes 1572872 | tf_op jit(solution)/shard_map/ppermute | solution.py:36
  64.8 10.7 %collective-permute-done.9.refs_4_ = bf16[8,16,2048]{2,1,0:T(8,128)(2,1)S(1)} collective-permute-done((bf16[8,16,2048]{2,1,0:T(8,128)(2,1)S(1)}, bf16[8,16,2048]{2,1,0:T(8,128)(2,1)S(1)}, u32[]{:S(2)}, u32[]{:S(2)}) %collective-permute-start.9) | collective-permute-done | bytes 524320 | tf_op jit(solution)/shard_map/ppermute | solution.py:36
  75.6 3.5 %collective-permute-done.8.refs_3_ = bf16[8,16,2048]{2,1,0:T(8,128)(2,1)S(1)} collective-permute-done((bf16[8,16,2048]{2,1,0:T(8,128)(2,1)S(1)}, bf16[8,16,2048]{2,1,0:T(8,128)(2,1)S(1)}, u32[]{:S(2)}, u32[]{:S(2)}) %collective-permute-start.8) | collective-permute-done | bytes 524320 | tf_op jit(solution)/shard_map/ppermute | solution.py:36
  80.1 5.4 %collective-permute-done.13.refs_8_ = bf16[8,16,2048]{2,1,0:T(8,128)(2,1)S(1)} collective-permute-done((bf16[8,16,2048]{2,1,0:T(8,128)(2,1)S(1)}, bf16[8,16,2048]{2,1,0:T(8,128)(2,1)S(1)}, u32[]{:S(2)}, u32[]{:S(2)}) %collective-permute-start.13) | collective-permute-done | bytes 524320 | tf_op jit(solution)/shard_map/ppermute | solution.py:36
  92.3 15.3 %all-to-all-done.refs_0_.refs_1_ = bf16[16,1552,128]{2,1,0:T(8,128)(2,1)} async-done(((bf16[16,1552,128]{2,1,0:T(8,128)(2,1)}), bf16[16,1552,128]{2,1,0:T(8,128)(2,1)}, u32[]{:S(2)}, u32[]{:S(2)}) %all-to-all-start) | async-done | bytes 6357024 | tf_op jit(solution)/shard_map/all_to_all | solution.py:274
  108.8 4.8 %place.2 = bf16[2048,384]{1,0:T(8,128)(2,1)S(1)} custom-call(s32[32]{0:T(128)S(1)} %sub.7.first_ref, bf16[16,1552,128]{2,1,0:T(8,128)(2,1)} %all-to-all-done.refs_0_.refs_1_, bf16[16,1552,128]{2,1,0:T(8,128)(2,1)} %all-to-all-done.refs_0_.refs_1_), custom_call_target="tpu_custom_call" | custom-call | flops 1572864 | bytes 6291456 | tf_op jit(solution)/shard_map/place/pallas_call | solution.py:124
  113.6 5.6 %convolution_convert_fusion.3 = bf16[2048,384]{1,0:T(8,128)(2,1)} fusion(bf16[2048,2048]{1,0:T(8,128)(2,1)S(1)} %bitcast.22, bf16[2048,384]{1,0:T(8,128)(2,1)S(1)} %place.2), kind=kOutput, calls=%fused_computation.3 | convolution fusion | flops 3222011904 | bytes 11534336 | tf_op jit(solution)/shard_map/dot_general | solution.py:287
  119.2 3.9 %all-to-all-start.1 = ((bf16[16,128,384]{2,1,0:T(8,128)(2,1)}), bf16[16,128,384]{2,1,0:T(8,128)(2,1)S(1)}, u32[]{:S(2)}, u32[]{:S(2)}) async-start(bf16[16,128,384]{2,1,0:T(8,128)(2,1)} %bitcast.5), calls=%async_computation.1 | async-start | bytes 3145728 | tf_op jit(solution)/shard_map/all_to_all | solution.py:289
  123.1 4.1 %place.3 = bf16[2048,384]{1,0:T(8,128)(2,1)S(1)} custom-call(s32[32]{0:T(128)S(1)} %sub.7.first_ref, bf16[16,1552,128]{2,1,0:T(8,128)(2,1)} %all-to-all-done.refs_0_.refs_1_, bf16[16,1552,128]{2,1,0:T(8,128)(2,1)} %all-to-all-done.refs_0_.refs_1_), custom_call_target="tpu_custom_call" | custom-call | flops 1572864 | bytes 6291456 | tf_op jit(solution)/shard_map/place/pallas_call | solution.py:124
  127.3 9.6 %convolution_convert_fusion.2 = bf16[2048,384]{1,0:T(8,128)(2,1)} fusion(bf16[2048,2048]{1,0:T(8,128)(2,1)} %bitcast.21, bf16[2048,384]{1,0:T(8,128)(2,1)S(1)} %place.3), kind=kOutput, calls=%fused_computation.2 | convolution fusion | flops 3222011904 | bytes 11534336 | tf_op jit(solution)/shard_map/dot_general | solution.py:287
  138.0 8.6 %all-to-all-done.1.x_ref = bf16[16,128,384]{2,1,0:T(8,128)(2,1)S(1)} async-done(((bf16[16,128,384]{2,1,0:T(8,128)(2,1)}), bf16[16,128,384]{2,1,0:T(8,128)(2,1)S(1)}, u32[]{:S(2)}, u32[]{:S(2)}) %all-to-all-start.1) | async-done | bytes 1572896 | tf_op jit(solution)/shard_map/all_to_all | solution.py:289
  146.6 3.7 %all-to-all-start.2 = ((bf16[16,128,384]{2,1,0:T(8,128)(2,1)}), bf16[16,128,384]{2,1,0:T(8,128)(2,1)S(1)}, u32[]{:S(2)}, u32[]{:S(2)}) async-start(bf16[16,128,384]{2,1,0:T(8,128)(2,1)} %bitcast.26), calls=%async_computation.2 | async-start | bytes 3145728 | tf_op jit(solution)/shard_map/all_to_all | solution.py:289
  150.4 4.4 %lay.3 = bf16[4,2,4,2,2,16,2048]{6,5,4,3,2,1,0:T(8,128)(2,1)S(1)} custom-call(bf16[16,16,2048]{2,1,0:T(8,128)(2,1)} %get-tuple-element.36.refs_0_, bf16[16,16,2048]{2,1,0:T(8,128)(2,1)} %collective-permute-done.15.refs_1_, bf16[16,16,2048]{2,1,0:T(8,128)(2,1)} %collective-permute-done.16.refs_2_, bf16[16,16,2048]{2,1,0:T(8,128)(2,1)} %collective-permute-done.17.refs_3_, ...), custom_call_target="tpu_custom_call" | custom-call | bytes 16777216 | tf_op jit(solution)/shard_map/lay/pallas_call | solution.py:175
  154.8 3.5 %convolution_convert_fusion.refs_1_ = bf16[384,2048]{1,0:T(8,128)(2,1)S(1)} fusion(bf16[2048,384]{1,0:T(8,128)(2,1)S(1)} %copy-done.11, bf16[2048,2048]{1,0:T(8,128)(2,1)S(1)} %bitcast.23), kind=kOutput, calls=%fused_computation | convolution fusion | flops 3222011904 | bytes 11534336 | tf_op jit(solution)/shard_map/dot_general | solution.py:297
  158.4 3.5 %convolution_convert_fusion.1.refs_0_ = bf16[384,2048]{1,0:T(8,128)(2,1)S(1)} fusion(bf16[2048,384]{1,0:T(8,128)(2,1)S(1)} %copy-done.9, bf16[2048,2048]{1,0:T(8,128)(2,1)S(1)} %bitcast.24), kind=kOutput, calls=%fused_computation.1 | convolution fusion | flops 3222011904 | bytes 11534336 | tf_op jit(solution)/shard_map/dot_general | solution.py:297
  165.0 9.1 %all-to-all-done.2.x_ref = bf16[16,128,384]{2,1,0:T(8,128)(2,1)S(1)} async-done(((bf16[16,128,384]{2,1,0:T(8,128)(2,1)}), bf16[16,128,384]{2,1,0:T(8,128)(2,1)S(1)}, u32[]{:S(2)}, u32[]{:S(2)}) %all-to-all-start.2) | async-done | bytes 1572896 | tf_op jit(solution)/shard_map/all_to_all | solution.py:289
  181.1 4.5 %collective-permute-done.23 = f32[6,6]{0,1:T(8,128)S(1)} collective-permute-done((f32[6,6]{0,1:T(8,128)S(1)}, f32[6,6]{0,1:T(8,128)S(1)}, u32[]{:S(2)}, u32[]{:S(2)}) %collective-permute-start.23) | collective-permute-done | bytes 176 | tf_op jit(solution)/shard_map/ppermute | solution.py:36
  185.8 3.3 %collective-permute-done.24 = f32[6,6]{0,1:T(8,128)S(1)} collective-permute-done((f32[6,6]{0,1:T(8,128)S(1)}, f32[6,6]{0,1:T(8,128)S(1)}, u32[]{:S(2)}, u32[]{:S(2)}) %collective-permute-start.24) | collective-permute-done | bytes 176 | tf_op jit(solution)/shard_map/ppermute | solution.py:36
  190.6 3.3 %collective-permute-done.25 = f32[6,6]{0,1:T(8,128)S(1)} collective-permute-done((f32[6,6]{0,1:T(8,128)S(1)}, f32[6,6]{0,1:T(8,128)S(1)}, u32[]{:S(2)}, u32[]{:S(2)}) %collective-permute-start.25) | collective-permute-done | bytes 176 | tf_op jit(solution)/shard_map/ppermute | solution.py:36
  (91 shorter events, 43.8 us)
Async XLA Ops:
  0.9 6.6 %collective-permute-start.2 = (bf16[1,32,2048]{2,1,0:T(8,128)(2,1)S(1)}, bf16[1,32,2048]{2,1,0:T(8,128)(2,1)S(1)}, u32[]{:S(2)}, u32[]{:S(2)}) collective-permute-start(bf16[1,32,2048]{2,1,0:T(8,128)(2,1)S(1)} %maximum_bitcast_fusion), channel_id=1, source_target_pairs={{0,8},{1,3},{2,10},{3,1},{4,12},{5,7},{6,14},{7,5},{8,0},{9,11},{1... | collective-permute-start | bytes 393224 | tf_op jit(solution)/shard_map/ppermute | solution.py:153
  5.2 6.2 %collective-permute-start = (bf16[1,32,2048]{2,1,0:T(8,128)(2,1)S(1)}, bf16[1,32,2048]{2,1,0:T(8,128)(2,1)S(1)}, u32[]{:S(2)}, u32[]{:S(2)}) collective-permute-start(bf16[1,32,2048]{2,1,0:T(8,128)(2,1)S(1)} %maximum_bitcast_fusion), channel_id=1, source_target_pairs={{0,4},{1,17},{2,6},{3,19},{4,8},{5,21},{6,10},{7,23},{8,12},{9,25}... | collective-permute-start | bytes 393224 | tf_op jit(solution)/shard_map/ppermute | solution.py:153
  11.5 11.3 %collective-permute-start.5 = (bf16[4,32,2048]{2,1,0:T(8,128)(2,1)S(1)}, bf16[4,32,2048]{2,1,0:T(8,128)(2,1)S(1)}, u32[]{:S(2)}, u32[]{:S(2)}) collective-permute-start(bf16[4,32,2048]{2,1,0:T(8,128)(2,1)S(1)} %pad_maximum_fusion), channel_id=1, source_target_pairs={{0,2},{1,9},{2,0},{3,11},{4,6},{5,13},{6,4},{7,15},{8,10},{9,1},{1... | collective-permute-start | bytes 1572872 | tf_op jit(solution)/shard_map/ppermute | solution.py:153
  13.7 14.2 %collective-permute-start.4 = (bf16[4,32,2048]{2,1,0:T(8,128)(2,1)S(1)}, bf16[4,32,2048]{2,1,0:T(8,128)(2,1)S(1)}, u32[]{:S(2)}, u32[]{:S(2)}) collective-permute-start(bf16[4,32,2048]{2,1,0:T(8,128)(2,1)S(1)} %pad_maximum_fusion), channel_id=1, source_target_pairs={{0,18},{1,13},{2,16},{3,15},{4,22},{5,1},{6,20},{7,3},{8,26},{9,5}... | collective-permute-start | bytes 1572872 | tf_op jit(solution)/shard_map/ppermute | solution.py:153
  15.1 12.8 %collective-permute-start.3 = (bf16[4,32,2048]{2,1,0:T(8,128)(2,1)S(1)}, bf16[4,32,2048]{2,1,0:T(8,128)(2,1)S(1)}, u32[]{:S(2)}, u32[]{:S(2)}) collective-permute-start(bf16[4,32,2048]{2,1,0:T(8,128)(2,1)S(1)} %pad_maximum_fusion), channel_id=1, source_target_pairs={{0,16},{1,5},{2,18},{3,7},{4,20},{5,9},{6,22},{7,11},{8,24},{9,13}... | collective-permute-start | bytes 1572872 | tf_op jit(solution)/shard_map/ppermute | solution.py:153
  27.9 79.7 %all-to-all-start = ((bf16[16,1552,128]{2,1,0:T(8,128)(2,1)}), bf16[16,1552,128]{2,1,0:T(8,128)(2,1)}, u32[]{:S(2)}, u32[]{:S(2)}) async-start(bf16[16,1552,128]{2,1,0:T(8,128)(2,1)} %copy-done), calls=%async_computation | async-start | bytes 12713984 | tf_op jit(solution)/shard_map/all_to_all | solution.py:274
  34.0 26.9 %collective-permute-start.7 = (bf16[16,16,2048]{2,1,0:T(8,128)(2,1)S(1)}, bf16[16,16,2048]{2,1,0:T(8,128)(2,1)S(1)}, u32[]{:S(2)}, u32[]{:S(2)}) collective-permute-start(bf16[16,16,2048]{2,1,0:T(8,128)(2,1)S(1)} %get-tuple-element.29.refs_0_), channel_id=1, source_target_pairs={{0,96},{1,97},{2,98},{3,99},{4,100},{5,101},{6,102},{7,103},{8,104... | collective-permute-start | bytes 3145736 | tf_op jit(solution)/shard_map/ppermute | solution.py:36
  38.1 26.6 %collective-permute-start.6 = (bf16[16,16,2048]{2,1,0:T(8,128)(2,1)S(1)}, bf16[16,16,2048]{2,1,0:T(8,128)(2,1)S(1)}, u32[]{:S(2)}, u32[]{:S(2)}) collective-permute-start(bf16[16,16,2048]{2,1,0:T(8,128)(2,1)S(1)} %get-tuple-element.29.refs_0_), channel_id=1, source_target_pairs={{0,32},{1,33},{2,34},{3,35},{4,36},{5,37},{6,38},{7,39},{8,40},{9,... | collective-permute-start | bytes 3145736 | tf_op jit(solution)/shard_map/ppermute | solution.py:36
  60.9 14.6 %collective-permute-start.9 = (bf16[8,16,2048]{2,1,0:T(8,128)(2,1)S(1)}, bf16[8,16,2048]{2,1,0:T(8,128)(2,1)S(1)}, u32[]{:S(2)}, u32[]{:S(2)}) collective-permute-start(bf16[8,16,2048]{2,1,0:T(8,128)(2,1)S(1)} %slice.22), channel_id=1, source_target_pairs={{0,96},{1,97},{2,98},{3,99},{4,100},{5,101},{6,102},{7,103},{8,104... | collective-permute-start | bytes 1572872 | tf_op jit(solution)/shard_map/ppermute | solution.py:36
  64.7 14.3 %collective-permute-start.8 = (bf16[8,16,2048]{2,1,0:T(8,128)(2,1)S(1)}, bf16[8,16,2048]{2,1,0:T(8,128)(2,1)S(1)}, u32[]{:S(2)}, u32[]{:S(2)}) collective-permute-start(bf16[8,16,2048]{2,1,0:T(8,128)(2,1)S(1)} %slice.21), channel_id=1, source_target_pairs={{0,32},{1,33},{2,34},{3,35},{4,36},{5,37},{6,38},{7,39},{8,40},{9,... | collective-permute-start | bytes 1572872 | tf_op jit(solution)/shard_map/ppermute | solution.py:36
  79.1 8.2 %collective-permute-start.10 = (bf16[16,16,2048]{2,1,0:T(8,128)(2,1)S(1)}, bf16[16,16,2048]{2,1,0:T(8,128)(2,1)S(1)}, u32[]{:S(2)}, u32[]{:S(2)}) collective-permute-start(bf16[16,16,2048]{2,1,0:T(8,128)(2,1)S(1)} %get-tuple-element.29.refs_0_), channel_id=1, source_target_pairs={{0,1},{1,0},{2,3},{3,2},{4,5},{5,4},{6,7},{7,6},{8,9},{9,8},{10,11... | collective-permute-start | bytes 3145736 | tf_op jit(solution)/shard_map/ppermute | solution.py:36
  79.1 9.2 %collective-permute-start.11 = (bf16[16,16,2048]{2,1,0:T(8,128)(2,1)S(1)}, bf16[16,16,2048]{2,1,0:T(8,128)(2,1)S(1)}, u32[]{:S(2)}, u32[]{:S(2)}) collective-permute-start(bf16[16,16,2048]{2,1,0:T(8,128)(2,1)S(1)} %collective-permute-done.6.refs_1_), channel_id=1, source_target_pairs={{0,1},{1,0},{2,3},{3,2},{4,5},{5,4},{6,7},{7,6},{8,9},{9,8},{10,11... | collective-permute-start | bytes 3145736 | tf_op jit(solution)/shard_map/ppermute | solution.py:36
  79.6 8.7 %collective-permute-start.12 = (bf16[16,16,2048]{2,1,0:T(8,128)(2,1)S(1)}, bf16[16,16,2048]{2,1,0:T(8,128)(2,1)S(1)}, u32[]{:S(2)}, u32[]{:S(2)}) collective-permute-start(bf16[16,16,2048]{2,1,0:T(8,128)(2,1)S(1)} %collective-permute-done.7.refs_2_), channel_id=1, source_target_pairs={{0,1},{1,0},{2,3},{3,2},{4,5},{5,4},{6,7},{7,6},{8,9},{9,8},{10,11... | collective-permute-start | bytes 3145736 | tf_op jit(solution)/shard_map/ppermute | solution.py:36
  79.6 5.9 %collective-permute-start.13 = (bf16[8,16,2048]{2,1,0:T(8,128)(2,1)S(1)}, bf16[8,16,2048]{2,1,0:T(8,128)(2,1)S(1)}, u32[]{:S(2)}, u32[]{:S(2)}) collective-permute-start(bf16[8,16,2048]{2,1,0:T(8,128)(2,1)S(1)} %collective-permute-done.8.refs_3_), channel_id=1, source_target_pairs={{0,1},{1,0},{2,3},{3,2},{4,5},{5,4},{6,7},{7,6},{8,9},{9,8},{10,11... | collective-permute-start | bytes 1572872 | tf_op jit(solution)/shard_map/ppermute | solution.py:36
  80.1 6.1 %collective-permute-start.14 = (bf16[8,16,2048]{2,1,0:T(8,128)(2,1)S(1)}, bf16[8,16,2048]{2,1,0:T(8,128)(2,1)S(1)}, u32[]{:S(2)}, u32[]{:S(2)}) collective-permute-start(bf16[8,16,2048]{2,1,0:T(8,128)(2,1)S(1)} %collective-permute-done.9.refs_4_), channel_id=1, source_target_pairs={{0,1},{1,0},{2,3},{3,2},{4,5},{5,4},{6,7},{7,6},{8,9},{9,8},{10,11... | collective-permute-start | bytes 1572872 | tf_op jit(solution)/shard_map/ppermute | solution.py:36
  85.5 51.4 %collective-permute-start.17 = (bf16[16,16,2048]{2,1,0:T(8,128)(2,1)}, bf16[16,16,2048]{2,1,0:T(8,128)(2,1)}, u32[]{:S(2)}, u32[]{:S(2)}) collective-permute-start(bf16[16,16,2048]{2,1,0:T(8,128)(2,1)} %get-tuple-element.36.refs_0_), channel_id=1, source_target_pairs={{0,64},{1,65},{2,66},{3,67},{4,68},{5,69},{6,70},{7,71},{8,72},{9,... | collective-permute-start | bytes 3145736 | tf_op jit(solution)/shard_map/ppermute | solution.py:36
  86.2 50.7 %collective-permute-start.16 = (bf16[16,16,2048]{2,1,0:T(8,128)(2,1)}, bf16[16,16,2048]{2,1,0:T(8,128)(2,1)}, u32[]{:S(2)}, u32[]{:S(2)}) collective-permute-start(bf16[16,16,2048]{2,1,0:T(8,128)(2,1)} %get-tuple-element.36.refs_0_), channel_id=1, source_target_pairs={{0,96},{1,97},{2,98},{3,99},{4,100},{5,101},{6,102},{7,103},{8,104... | collective-permute-start | bytes 3145736 | tf_op jit(solution)/shard_map/ppermute | solution.py:36
  87.2 49.7 %collective-permute-start.15 = (bf16[16,16,2048]{2,1,0:T(8,128)(2,1)}, bf16[16,16,2048]{2,1,0:T(8,128)(2,1)}, u32[]{:S(2)}, u32[]{:S(2)}) collective-permute-start(bf16[16,16,2048]{2,1,0:T(8,128)(2,1)} %get-tuple-element.36.refs_0_), channel_id=1, source_target_pairs={{0,32},{1,33},{2,34},{3,35},{4,36},{5,37},{6,38},{7,39},{8,40},{9,... | collective-permute-start | bytes 3145736 | tf_op jit(solution)/shard_map/ppermute | solution.py:36
  119.2 27.4 %all-to-all-start.1 = ((bf16[16,128,384]{2,1,0:T(8,128)(2,1)}), bf16[16,128,384]{2,1,0:T(8,128)(2,1)S(1)}, u32[]{:S(2)}, u32[]{:S(2)}) async-start(bf16[16,128,384]{2,1,0:T(8,128)(2,1)} %bitcast.5), calls=%async_computation.1 | async-start | bytes 3145728 | tf_op jit(solution)/shard_map/all_to_all | solution.py:289
  136.9 13.5 %collective-permute-start.18 = (bf16[16,16,2048]{2,1,0:T(8,128)(2,1)}, bf16[16,16,2048]{2,1,0:T(8,128)(2,1)}, u32[]{:S(2)}, u32[]{:S(2)}) collective-permute-start(bf16[16,16,2048]{2,1,0:T(8,128)(2,1)} %get-tuple-element.36.refs_0_), channel_id=1, source_target_pairs={{0,1},{1,0},{2,3},{3,2},{4,5},{5,4},{6,7},{7,6},{8,9},{9,8},{10,11... | collective-permute-start | bytes 3145736 | tf_op jit(solution)/shard_map/ppermute | solution.py:36
  137.1 13.3 %collective-permute-start.19 = (bf16[16,16,2048]{2,1,0:T(8,128)(2,1)}, bf16[16,16,2048]{2,1,0:T(8,128)(2,1)}, u32[]{:S(2)}, u32[]{:S(2)}) collective-permute-start(bf16[16,16,2048]{2,1,0:T(8,128)(2,1)} %collective-permute-done.15.refs_1_), channel_id=1, source_target_pairs={{0,1},{1,0},{2,3},{3,2},{4,5},{5,4},{6,7},{7,6},{8,9},{9,8},{10,11... | collective-permute-start | bytes 3145736 | tf_op jit(solution)/shard_map/ppermute | solution.py:36
  137.5 12.9 %collective-permute-start.20 = (bf16[16,16,2048]{2,1,0:T(8,128)(2,1)}, bf16[16,16,2048]{2,1,0:T(8,128)(2,1)}, u32[]{:S(2)}, u32[]{:S(2)}) collective-permute-start(bf16[16,16,2048]{2,1,0:T(8,128)(2,1)} %collective-permute-done.16.refs_2_), channel_id=1, source_target_pairs={{0,1},{1,0},{2,3},{3,2},{4,5},{5,4},{6,7},{7,6},{8,9},{9,8},{10,11... | collective-permute-start | bytes 3145736 | tf_op jit(solution)/shard_map/ppermute | solution.py:36
  137.6 12.8 %collective-permute-start.21 = (bf16[16,16,2048]{2,1,0:T(8,128)(2,1)}, bf16[16,16,2048]{2,1,0:T(8,128)(2,1)}, u32[]{:S(2)}, u32[]{:S(2)}) collective-permute-start(bf16[16,16,2048]{2,1,0:T(8,128)(2,1)} %collective-permute-done.17.refs_3_), channel_id=1, source_target_pairs={{0,1},{1,0},{2,3},{3,2},{4,5},{5,4},{6,7},{7,6},{8,9},{9,8},{10,11... | collective-permute-start | bytes 3145736 | tf_op jit(solution)/shard_map/ppermute | solution.py:36
  146.6 27.4 %all-to-all-start.2 = ((bf16[16,128,384]{2,1,0:T(8,128)(2,1)}), bf16[16,128,384]{2,1,0:T(8,128)(2,1)S(1)}, u32[]{:S(2)}, u32[]{:S(2)}) async-start(bf16[16,128,384]{2,1,0:T(8,128)(2,1)} %bitcast.26), calls=%async_computation.2 | async-start | bytes 3145728 | tf_op jit(solution)/shard_map/all_to_all | solution.py:289
  (17 other events, 63.5 us)

commit v13 on v12

--- a/solution.py
+++ b/solution.py
@@ -299,6 +299,7 @@
         ).astype(jnp.bfloat16)
         for d in dense
     ]
+    virt_half = [jnp.concatenate(virt_half, axis=0)]
     sums = jnp.concatenate([pair_sums(x, virt_half) for x in turned], axis=0)
     return (col_sum(sums) / float(basis_total))[None]
 

time: 195 us -> 194 us (level)
  local copies, waits for them, and re-layouts: 15.4 us -> 11.3 us
  waiting for transfers between devices: 98.8 us -> 101 us
    unnamed x27 -> x23, local copies, waits for them, and re-layouts: 12.3 us -> 9.36 us
  transfers between devices with their start and end apart: 29 -> 29, of which waited for: 17 -> 17; matrix products, arithmetic and copies ran while one was open for 13% -> 13% of each run, Pallas kernels for 9% -> 8%
where the time goes in v13:
time: 194 us
  waiting for transfers between devices  101 us (52%)
  starting transfers between devices  37 us (19%)
  matrix products  22.1 us (11%)
  Pallas kernels  19 us (10%)
  local copies, waits for them, and re-layouts  11.3 us (6%)
  other arithmetic  3.04 us (2%)
    ppermute x20, waiting for transfers between devices, permute(): return lax.ppermute(x, AXES, moved(axis, to))  55.5 us
    all_to_all x2, waiting for transfers between devices, shards(): lax.all_to_all(cut, COL, split_axis=0, concat_axis=0, tiled=True)  18.5 us
    all_to_all x1, waiting for transfers between devices, shards(): recv = lax.all_to_all(picked, COL, split_axis=0, concat_axis=0, tiled=True)  16.3 us
    dot_general x2, matrix products, shards(): jnp.dot(occ, dense[-1], preferred_element_type=jnp.float32)  15.2 us
    ppermute x20, starting transfers between devices, permute(): return lax.ppermute(x, AXES, moved(axis, to))  14.5 us
    ppermute x6, waiting for transfers between devices, hop(): return lax.ppermute(x, AXES, pairs)  10.3 us
    ppermute x6, starting transfers between devices, hop(): return lax.ppermute(x, AXES, pairs)  9.53 us
    unnamed x23, local copies, waits for them, and re-layouts  9.36 us
  transfers between devices with their start and end apart: 29, of which 17 were waited for; matrix products, arithmetic and copies ran while one was open for 13% of the time, Pallas kernels for 8%

profile of v13, /device:TPU:2, one launch (start us, length us, event | category | flops | bytes accessed | tf_op | source)
XLA Modules:
  0.0 193.6 jit_solution(13977026477091457902)
XLA Ops:
  0.9 3.3 %collective-permute-start.2 = (bf16[1,32,2048]{2,1,0:T(8,128)(2,1)S(1)}, bf16[1,32,2048]{2,1,0:T(8,128)(2,1)S(1)}, u32[]{:S(2)}, u32[]{:S(2)}) collective-permute-start(bf16[1,32,2048]{2,1,0:T(8,128)(2,1)S(1)} %maximum_bitcast_fusion), channel_id=1, source_target_pairs={{0,8},{1,3},{2,10},{3,1},{4,12},{5,7},{6,14},{7,5},{8,0},{9,11},{1... | collective-permute-start | bytes 393224 | tf_op jit(solution)/shard_map/ppermute | solution.py:153
  22.8 5.1 %collective-permute-done.4 = bf16[4,32,2048]{2,1,0:T(8,128)(2,1)S(1)} collective-permute-done((bf16[4,32,2048]{2,1,0:T(8,128)(2,1)S(1)}, bf16[4,32,2048]{2,1,0:T(8,128)(2,1)S(1)}, u32[]{:S(2)}, u32[]{:S(2)}) %collective-permute-start.4) | collective-permute-done | bytes 524320 | tf_op jit(solution)/shard_map/ppermute | solution.py:153
  27.9 4.7 %all-to-all-start = ((bf16[16,1552,128]{2,1,0:T(8,128)(2,1)}), bf16[16,1552,128]{2,1,0:T(8,128)(2,1)}, u32[]{:S(2)}, u32[]{:S(2)}) async-start(bf16[16,1552,128]{2,1,0:T(8,128)(2,1)} %copy-done), calls=%async_computation | async-start | bytes 12713984 | tf_op jit(solution)/shard_map/all_to_all | solution.py:274
  33.0 4.1 %collective-permute-start.7 = (bf16[16,16,2048]{2,1,0:T(8,128)(2,1)S(1)}, bf16[16,16,2048]{2,1,0:T(8,128)(2,1)S(1)}, u32[]{:S(2)}, u32[]{:S(2)}) collective-permute-start(bf16[16,16,2048]{2,1,0:T(8,128)(2,1)S(1)} %get-tuple-element.29.refs_0_), channel_id=1, source_target_pairs={{0,96},{1,97},{2,98},{3,99},{4,100},{5,101},{6,102},{7,103},{8,104... | collective-permute-start | bytes 3145736 | tf_op jit(solution)/shard_map/ppermute | solution.py:36
  37.1 22.8 %collective-permute-done.7.refs_2_ = bf16[16,16,2048]{2,1,0:T(8,128)(2,1)S(1)} collective-permute-done((bf16[16,16,2048]{2,1,0:T(8,128)(2,1)S(1)}, bf16[16,16,2048]{2,1,0:T(8,128)(2,1)S(1)}, u32[]{:S(2)}, u32[]{:S(2)}) %collective-permute-start.7) | collective-permute-done | bytes 1048608 | tf_op jit(solution)/shard_map/ppermute | solution.py:36
  59.9 3.8 %collective-permute-start.9 = (bf16[8,16,2048]{2,1,0:T(8,128)(2,1)S(1)}, bf16[8,16,2048]{2,1,0:T(8,128)(2,1)S(1)}, u32[]{:S(2)}, u32[]{:S(2)}) collective-permute-start(bf16[8,16,2048]{2,1,0:T(8,128)(2,1)S(1)} %slice.22), channel_id=1, source_target_pairs={{0,96},{1,97},{2,98},{3,99},{4,100},{5,101},{6,102},{7,103},{8,104... | collective-permute-start | bytes 1572872 | tf_op jit(solution)/shard_map/ppermute | solution.py:36
  63.8 10.7 %collective-permute-done.9.refs_4_ = bf16[8,16,2048]{2,1,0:T(8,128)(2,1)S(1)} collective-permute-done((bf16[8,16,2048]{2,1,0:T(8,128)(2,1)S(1)}, bf16[8,16,2048]{2,1,0:T(8,128)(2,1)S(1)}, u32[]{:S(2)}, u32[]{:S(2)}) %collective-permute-start.9) | collective-permute-done | bytes 524320 | tf_op jit(solution)/shard_map/ppermute | solution.py:36
  74.6 3.5 %collective-permute-done.8.refs_3_ = bf16[8,16,2048]{2,1,0:T(8,128)(2,1)S(1)} collective-permute-done((bf16[8,16,2048]{2,1,0:T(8,128)(2,1)S(1)}, bf16[8,16,2048]{2,1,0:T(8,128)(2,1)S(1)}, u32[]{:S(2)}, u32[]{:S(2)}) %collective-permute-start.8) | collective-permute-done | bytes 524320 | tf_op jit(solution)/shard_map/ppermute | solution.py:36
  79.1 5.4 %collective-permute-done.13.refs_8_ = bf16[8,16,2048]{2,1,0:T(8,128)(2,1)S(1)} collective-permute-done((bf16[8,16,2048]{2,1,0:T(8,128)(2,1)S(1)}, bf16[8,16,2048]{2,1,0:T(8,128)(2,1)S(1)}, u32[]{:S(2)}, u32[]{:S(2)}) %collective-permute-start.13) | collective-permute-done | bytes 524320 | tf_op jit(solution)/shard_map/ppermute | solution.py:36
  91.3 16.3 %all-to-all-done.refs_0_.refs_1_ = bf16[16,1552,128]{2,1,0:T(8,128)(2,1)} async-done(((bf16[16,1552,128]{2,1,0:T(8,128)(2,1)}), bf16[16,1552,128]{2,1,0:T(8,128)(2,1)}, u32[]{:S(2)}, u32[]{:S(2)}) %all-to-all-start) | async-done | bytes 6357024 | tf_op jit(solution)/shard_map/all_to_all | solution.py:274
  108.8 4.8 %place.2 = bf16[2048,384]{1,0:T(8,128)(2,1)S(1)} custom-call(s32[32]{0:T(128)S(1)} %sub.7.first_ref, bf16[16,1552,128]{2,1,0:T(8,128)(2,1)} %all-to-all-done.refs_0_.refs_1_, bf16[16,1552,128]{2,1,0:T(8,128)(2,1)} %all-to-all-done.refs_0_.refs_1_), custom_call_target="tpu_custom_call" | custom-call | flops 1572864 | bytes 6291456 | tf_op jit(solution)/shard_map/place/pallas_call | solution.py:124
  113.6 5.6 %convolution_convert_fusion.3 = bf16[2048,384]{1,0:T(8,128)(2,1)} fusion(bf16[2048,2048]{1,0:T(8,128)(2,1)S(1)} %bitcast.22, bf16[2048,384]{1,0:T(8,128)(2,1)S(1)} %place.2), kind=kOutput, calls=%fused_computation.4 | convolution fusion | flops 3222011904 | bytes 11534336 | tf_op jit(solution)/shard_map/dot_general | solution.py:287
  119.2 3.9 %all-to-all-start.1 = ((bf16[16,128,384]{2,1,0:T(8,128)(2,1)}), bf16[16,128,384]{2,1,0:T(8,128)(2,1)S(1)}, u32[]{:S(2)}, u32[]{:S(2)}) async-start(bf16[16,128,384]{2,1,0:T(8,128)(2,1)} %bitcast.27), calls=%async_computation.1 | async-start | bytes 3145728 | tf_op jit(solution)/shard_map/all_to_all | solution.py:289
  123.1 4.1 %place.3 = bf16[2048,384]{1,0:T(8,128)(2,1)S(1)} custom-call(s32[32]{0:T(128)S(1)} %sub.7.first_ref, bf16[16,1552,128]{2,1,0:T(8,128)(2,1)} %all-to-all-done.refs_0_.refs_1_, bf16[16,1552,128]{2,1,0:T(8,128)(2,1)} %all-to-all-done.refs_0_.refs_1_), custom_call_target="tpu_custom_call" | custom-call | flops 1572864 | bytes 6291456 | tf_op jit(solution)/shard_map/place/pallas_call | solution.py:124
  127.2 9.6 %convolution_convert_fusion.2 = bf16[2048,384]{1,0:T(8,128)(2,1)} fusion(bf16[2048,2048]{1,0:T(8,128)(2,1)} %bitcast.21, bf16[2048,384]{1,0:T(8,128)(2,1)S(1)} %place.3), kind=kOutput, calls=%fused_computation.3 | convolution fusion | flops 3222011904 | bytes 11534336 | tf_op jit(solution)/shard_map/dot_general | solution.py:287
  138.0 8.6 %all-to-all-done.1.x_ref = bf16[16,128,384]{2,1,0:T(8,128)(2,1)S(1)} async-done(((bf16[16,128,384]{2,1,0:T(8,128)(2,1)}), bf16[16,128,384]{2,1,0:T(8,128)(2,1)S(1)}, u32[]{:S(2)}, u32[]{:S(2)}) %all-to-all-start.1) | async-done | bytes 1572896 | tf_op jit(solution)/shard_map/all_to_all | solution.py:289
  146.6 4.4 %all-to-all-start.2 = ((bf16[16,128,384]{2,1,0:T(8,128)(2,1)}), bf16[16,128,384]{2,1,0:T(8,128)(2,1)}, u32[]{:S(2)}, u32[]{:S(2)}) async-start(bf16[16,128,384]{2,1,0:T(8,128)(2,1)} %bitcast.26), calls=%async_computation.2 | async-start | bytes 3145728 | tf_op jit(solution)/shard_map/all_to_all | solution.py:289
  151.1 3.8 %lay.3 = bf16[4,2,4,2,2,16,2048]{6,5,4,3,2,1,0:T(8,128)(2,1)S(1)} custom-call(bf16[16,16,2048]{2,1,0:T(8,128)(2,1)S(1)} %get-tuple-element.36.refs_0_, bf16[16,16,2048]{2,1,0:T(8,128)(2,1)} %collective-permute-done.15.refs_1_, bf16[16,16,2048]{2,1,0:T(8,128)(2,1)} %collective-permute-done.16.refs_2_, bf16[16,16,2048]{2,1,0:T(8,128)(2,1)} %collective-permute-done.17.refs_3_, ...), custom_call_target="tpu_custom_call" | custom-call | bytes 16777216 | tf_op jit(solution)/shard_map/lay/pallas_call | solution.py:175
  154.9 3.5 %convolution_convert_fusion = bf16[384,2048]{1,0:T(8,128)(2,1)S(1)} fusion(bf16[2048,384]{1,0:T(8,128)(2,1)S(1)} %copy-done.9, bf16[2048,2048]{1,0:T(8,128)(2,1)S(1)} %bitcast.23), kind=kOutput, calls=%fused_computation.1 | convolution fusion | flops 3222011904 | bytes 11534336 | tf_op jit(solution)/shard_map/dot_general | solution.py:297
  158.4 3.5 %convolution_convert_fusion.1 = bf16[384,2048]{1,0:T(8,128)(2,1)S(1)} fusion(bf16[2048,384]{1,0:T(8,128)(2,1)S(1)} %copy-done.7, bf16[2048,2048]{1,0:T(8,128)(2,1)S(1)} %bitcast.24), kind=kOutput, calls=%fused_computation.2 | convolution fusion | flops 3222011904 | bytes 11534336 | tf_op jit(solution)/shard_map/dot_general | solution.py:297
  164.9 9.9 %all-to-all-done.2.x_ref = bf16[16,128,384]{2,1,0:T(8,128)(2,1)} async-done(((bf16[16,128,384]{2,1,0:T(8,128)(2,1)}), bf16[16,128,384]{2,1,0:T(8,128)(2,1)}, u32[]{:S(2)}, u32[]{:S(2)}) %all-to-all-start.2) | async-done | bytes 1572896 | tf_op jit(solution)/shard_map/all_to_all | solution.py:289
  180.0 4.5 %collective-permute-done.23 = f32[6,6]{0,1:T(8,128)S(1)} collective-permute-done((f32[6,6]{0,1:T(8,128)S(1)}, f32[6,6]{0,1:T(8,128)S(1)}, u32[]{:S(2)}, u32[]{:S(2)}) %collective-permute-start.23) | collective-permute-done | bytes 176 | tf_op jit(solution)/shard_map/ppermute | solution.py:36
  184.8 3.3 %collective-permute-done.24 = f32[6,6]{0,1:T(8,128)S(1)} collective-permute-done((f32[6,6]{0,1:T(8,128)S(1)}, f32[6,6]{0,1:T(8,128)S(1)}, u32[]{:S(2)}, u32[]{:S(2)}) %collective-permute-start.24) | collective-permute-done | bytes 176 | tf_op jit(solution)/shard_map/ppermute | solution.py:36
  189.6 3.3 %collective-permute-done.25 = f32[6,6]{0,1:T(8,128)S(1)} collective-permute-done((f32[6,6]{0,1:T(8,128)S(1)}, f32[6,6]{0,1:T(8,128)S(1)}, u32[]{:S(2)}, u32[]{:S(2)}) %collective-permute-start.25) | collective-permute-done | bytes 176 | tf_op jit(solution)/shard_map/ppermute | solution.py:36
  (88 shorter events, 40.8 us)
Async XLA Ops:
  0.9 6.6 %collective-permute-start.2 = (bf16[1,32,2048]{2,1,0:T(8,128)(2,1)S(1)}, bf16[1,32,2048]{2,1,0:T(8,128)(2,1)S(1)}, u32[]{:S(2)}, u32[]{:S(2)}) collective-permute-start(bf16[1,32,2048]{2,1,0:T(8,128)(2,1)S(1)} %maximum_bitcast_fusion), channel_id=1, source_target_pairs={{0,8},{1,3},{2,10},{3,1},{4,12},{5,7},{6,14},{7,5},{8,0},{9,11},{1... | collective-permute-start | bytes 393224 | tf_op jit(solution)/shard_map/ppermute | solution.py:153
  5.2 6.2 %collective-permute-start = (bf16[1,32,2048]{2,1,0:T(8,128)(2,1)S(1)}, bf16[1,32,2048]{2,1,0:T(8,128)(2,1)S(1)}, u32[]{:S(2)}, u32[]{:S(2)}) collective-permute-start(bf16[1,32,2048]{2,1,0:T(8,128)(2,1)S(1)} %maximum_bitcast_fusion), channel_id=1, source_target_pairs={{0,4},{1,17},{2,6},{3,19},{4,8},{5,21},{6,10},{7,23},{8,12},{9,25}... | collective-permute-start | bytes 393224 | tf_op jit(solution)/shard_map/ppermute | solution.py:153
  11.5 11.3 %collective-permute-start.5 = (bf16[4,32,2048]{2,1,0:T(8,128)(2,1)S(1)}, bf16[4,32,2048]{2,1,0:T(8,128)(2,1)S(1)}, u32[]{:S(2)}, u32[]{:S(2)}) collective-permute-start(bf16[4,32,2048]{2,1,0:T(8,128)(2,1)S(1)} %pad_maximum_fusion.1), channel_id=1, source_target_pairs={{0,2},{1,9},{2,0},{3,11},{4,6},{5,13},{6,4},{7,15},{8,10},{9,1},{1... | collective-permute-start | bytes 1572872 | tf_op jit(solution)/shard_map/ppermute | solution.py:153
  13.7 14.2 %collective-permute-start.4 = (bf16[4,32,2048]{2,1,0:T(8,128)(2,1)S(1)}, bf16[4,32,2048]{2,1,0:T(8,128)(2,1)S(1)}, u32[]{:S(2)}, u32[]{:S(2)}) collective-permute-start(bf16[4,32,2048]{2,1,0:T(8,128)(2,1)S(1)} %pad_maximum_fusion.1), channel_id=1, source_target_pairs={{0,18},{1,13},{2,16},{3,15},{4,22},{5,1},{6,20},{7,3},{8,26},{9,5}... | collective-permute-start | bytes 1572872 | tf_op jit(solution)/shard_map/ppermute | solution.py:153
  15.1 12.8 %collective-permute-start.3 = (bf16[4,32,2048]{2,1,0:T(8,128)(2,1)S(1)}, bf16[4,32,2048]{2,1,0:T(8,128)(2,1)S(1)}, u32[]{:S(2)}, u32[]{:S(2)}) collective-permute-start(bf16[4,32,2048]{2,1,0:T(8,128)(2,1)S(1)} %pad_maximum_fusion.1), channel_id=1, source_target_pairs={{0,16},{1,5},{2,18},{3,7},{4,20},{5,9},{6,22},{7,11},{8,24},{9,13}... | collective-permute-start | bytes 1572872 | tf_op jit(solution)/shard_map/ppermute | solution.py:153
  27.9 79.7 %all-to-all-start = ((bf16[16,1552,128]{2,1,0:T(8,128)(2,1)}), bf16[16,1552,128]{2,1,0:T(8,128)(2,1)}, u32[]{:S(2)}, u32[]{:S(2)}) async-start(bf16[16,1552,128]{2,1,0:T(8,128)(2,1)} %copy-done), calls=%async_computation | async-start | bytes 12713984 | tf_op jit(solution)/shard_map/all_to_all | solution.py:274
  33.0 26.9 %collective-permute-start.7 = (bf16[16,16,2048]{2,1,0:T(8,128)(2,1)S(1)}, bf16[16,16,2048]{2,1,0:T(8,128)(2,1)S(1)}, u32[]{:S(2)}, u32[]{:S(2)}) collective-permute-start(bf16[16,16,2048]{2,1,0:T(8,128)(2,1)S(1)} %get-tuple-element.29.refs_0_), channel_id=1, source_target_pairs={{0,96},{1,97},{2,98},{3,99},{4,100},{5,101},{6,102},{7,103},{8,104... | collective-permute-start | bytes 3145736 | tf_op jit(solution)/shard_map/ppermute | solution.py:36
  37.1 26.6 %collective-permute-start.6 = (bf16[16,16,2048]{2,1,0:T(8,128)(2,1)S(1)}, bf16[16,16,2048]{2,1,0:T(8,128)(2,1)S(1)}, u32[]{:S(2)}, u32[]{:S(2)}) collective-permute-start(bf16[16,16,2048]{2,1,0:T(8,128)(2,1)S(1)} %get-tuple-element.29.refs_0_), channel_id=1, source_target_pairs={{0,32},{1,33},{2,34},{3,35},{4,36},{5,37},{6,38},{7,39},{8,40},{9,... | collective-permute-start | bytes 3145736 | tf_op jit(solution)/shard_map/ppermute | solution.py:36
  59.9 14.6 %collective-permute-start.9 = (bf16[8,16,2048]{2,1,0:T(8,128)(2,1)S(1)}, bf16[8,16,2048]{2,1,0:T(8,128)(2,1)S(1)}, u32[]{:S(2)}, u32[]{:S(2)}) collective-permute-start(bf16[8,16,2048]{2,1,0:T(8,128)(2,1)S(1)} %slice.22), channel_id=1, source_target_pairs={{0,96},{1,97},{2,98},{3,99},{4,100},{5,101},{6,102},{7,103},{8,104... | collective-permute-start | bytes 1572872 | tf_op jit(solution)/shard_map/ppermute | solution.py:36
  63.7 14.3 %collective-permute-start.8 = (bf16[8,16,2048]{2,1,0:T(8,128)(2,1)S(1)}, bf16[8,16,2048]{2,1,0:T(8,128)(2,1)S(1)}, u32[]{:S(2)}, u32[]{:S(2)}) collective-permute-start(bf16[8,16,2048]{2,1,0:T(8,128)(2,1)S(1)} %slice.21), channel_id=1, source_target_pairs={{0,32},{1,33},{2,34},{3,35},{4,36},{5,37},{6,38},{7,39},{8,40},{9,... | collective-permute-start | bytes 1572872 | tf_op jit(solution)/shard_map/ppermute | solution.py:36
  78.1 8.2 %collective-permute-start.10 = (bf16[16,16,2048]{2,1,0:T(8,128)(2,1)S(1)}, bf16[16,16,2048]{2,1,0:T(8,128)(2,1)S(1)}, u32[]{:S(2)}, u32[]{:S(2)}) collective-permute-start(bf16[16,16,2048]{2,1,0:T(8,128)(2,1)S(1)} %get-tuple-element.29.refs_0_), channel_id=1, source_target_pairs={{0,1},{1,0},{2,3},{3,2},{4,5},{5,4},{6,7},{7,6},{8,9},{9,8},{10,11... | collective-permute-start | bytes 3145736 | tf_op jit(solution)/shard_map/ppermute | solution.py:36
  78.1 9.2 %collective-permute-start.11 = (bf16[16,16,2048]{2,1,0:T(8,128)(2,1)S(1)}, bf16[16,16,2048]{2,1,0:T(8,128)(2,1)S(1)}, u32[]{:S(2)}, u32[]{:S(2)}) collective-permute-start(bf16[16,16,2048]{2,1,0:T(8,128)(2,1)S(1)} %collective-permute-done.6.refs_1_), channel_id=1, source_target_pairs={{0,1},{1,0},{2,3},{3,2},{4,5},{5,4},{6,7},{7,6},{8,9},{9,8},{10,11... | collective-permute-start | bytes 3145736 | tf_op jit(solution)/shard_map/ppermute | solution.py:36
  78.6 8.7 %collective-permute-start.12 = (bf16[16,16,2048]{2,1,0:T(8,128)(2,1)S(1)}, bf16[16,16,2048]{2,1,0:T(8,128)(2,1)S(1)}, u32[]{:S(2)}, u32[]{:S(2)}) collective-permute-start(bf16[16,16,2048]{2,1,0:T(8,128)(2,1)S(1)} %collective-permute-done.7.refs_2_), channel_id=1, source_target_pairs={{0,1},{1,0},{2,3},{3,2},{4,5},{5,4},{6,7},{7,6},{8,9},{9,8},{10,11... | collective-permute-start | bytes 3145736 | tf_op jit(solution)/shard_map/ppermute | solution.py:36
  78.6 5.9 %collective-permute-start.13 = (bf16[8,16,2048]{2,1,0:T(8,128)(2,1)S(1)}, bf16[8,16,2048]{2,1,0:T(8,128)(2,1)S(1)}, u32[]{:S(2)}, u32[]{:S(2)}) collective-permute-start(bf16[8,16,2048]{2,1,0:T(8,128)(2,1)S(1)} %collective-permute-done.8.refs_3_), channel_id=1, source_target_pairs={{0,1},{1,0},{2,3},{3,2},{4,5},{5,4},{6,7},{7,6},{8,9},{9,8},{10,11... | collective-permute-start | bytes 1572872 | tf_op jit(solution)/shard_map/ppermute | solution.py:36
  79.1 6.1 %collective-permute-start.14 = (bf16[8,16,2048]{2,1,0:T(8,128)(2,1)S(1)}, bf16[8,16,2048]{2,1,0:T(8,128)(2,1)S(1)}, u32[]{:S(2)}, u32[]{:S(2)}) collective-permute-start(bf16[8,16,2048]{2,1,0:T(8,128)(2,1)S(1)} %collective-permute-done.9.refs_4_), channel_id=1, source_target_pairs={{0,1},{1,0},{2,3},{3,2},{4,5},{5,4},{6,7},{7,6},{8,9},{9,8},{10,11... | collective-permute-start | bytes 1572872 | tf_op jit(solution)/shard_map/ppermute | solution.py:36
  84.5 52.4 %collective-permute-start.17 = (bf16[16,16,2048]{2,1,0:T(8,128)(2,1)S(1)}, bf16[16,16,2048]{2,1,0:T(8,128)(2,1)}, u32[]{:S(2)}, u32[]{:S(2)}) collective-permute-start(bf16[16,16,2048]{2,1,0:T(8,128)(2,1)S(1)} %get-tuple-element.36.refs_0_), channel_id=1, source_target_pairs={{0,64},{1,65},{2,66},{3,67},{4,68},{5,69},{6,70},{7,71},{8,72},{9,... | collective-permute-start | bytes 3145736 | tf_op jit(solution)/shard_map/ppermute | solution.py:36
  85.3 51.6 %collective-permute-start.16 = (bf16[16,16,2048]{2,1,0:T(8,128)(2,1)S(1)}, bf16[16,16,2048]{2,1,0:T(8,128)(2,1)}, u32[]{:S(2)}, u32[]{:S(2)}) collective-permute-start(bf16[16,16,2048]{2,1,0:T(8,128)(2,1)S(1)} %get-tuple-element.36.refs_0_), channel_id=1, source_target_pairs={{0,96},{1,97},{2,98},{3,99},{4,100},{5,101},{6,102},{7,103},{8,104... | collective-permute-start | bytes 3145736 | tf_op jit(solution)/shard_map/ppermute | solution.py:36
  86.3 50.6 %collective-permute-start.15 = (bf16[16,16,2048]{2,1,0:T(8,128)(2,1)S(1)}, bf16[16,16,2048]{2,1,0:T(8,128)(2,1)}, u32[]{:S(2)}, u32[]{:S(2)}) collective-permute-start(bf16[16,16,2048]{2,1,0:T(8,128)(2,1)S(1)} %get-tuple-element.36.refs_0_), channel_id=1, source_target_pairs={{0,32},{1,33},{2,34},{3,35},{4,36},{5,37},{6,38},{7,39},{8,40},{9,... | collective-permute-start | bytes 3145736 | tf_op jit(solution)/shard_map/ppermute | solution.py:36
  119.2 27.4 %all-to-all-start.1 = ((bf16[16,128,384]{2,1,0:T(8,128)(2,1)}), bf16[16,128,384]{2,1,0:T(8,128)(2,1)S(1)}, u32[]{:S(2)}, u32[]{:S(2)}) async-start(bf16[16,128,384]{2,1,0:T(8,128)(2,1)} %bitcast.27), calls=%async_computation.1 | async-start | bytes 3145728 | tf_op jit(solution)/shard_map/all_to_all | solution.py:289
  136.9 14.1 %collective-permute-start.18 = (bf16[16,16,2048]{2,1,0:T(8,128)(2,1)S(1)}, bf16[16,16,2048]{2,1,0:T(8,128)(2,1)}, u32[]{:S(2)}, u32[]{:S(2)}) collective-permute-start(bf16[16,16,2048]{2,1,0:T(8,128)(2,1)S(1)} %get-tuple-element.36.refs_0_), channel_id=1, source_target_pairs={{0,1},{1,0},{2,3},{3,2},{4,5},{5,4},{6,7},{7,6},{8,9},{9,8},{10,11... | collective-permute-start | bytes 3145736 | tf_op jit(solution)/shard_map/ppermute | solution.py:36
  137.1 14.0 %collective-permute-start.19 = (bf16[16,16,2048]{2,1,0:T(8,128)(2,1)}, bf16[16,16,2048]{2,1,0:T(8,128)(2,1)}, u32[]{:S(2)}, u32[]{:S(2)}) collective-permute-start(bf16[16,16,2048]{2,1,0:T(8,128)(2,1)} %collective-permute-done.15.refs_1_), channel_id=1, source_target_pairs={{0,1},{1,0},{2,3},{3,2},{4,5},{5,4},{6,7},{7,6},{8,9},{9,8},{10,11... | collective-permute-start | bytes 3145736 | tf_op jit(solution)/shard_map/ppermute | solution.py:36
  137.5 13.6 %collective-permute-start.20 = (bf16[16,16,2048]{2,1,0:T(8,128)(2,1)}, bf16[16,16,2048]{2,1,0:T(8,128)(2,1)}, u32[]{:S(2)}, u32[]{:S(2)}) collective-permute-start(bf16[16,16,2048]{2,1,0:T(8,128)(2,1)} %collective-permute-done.16.refs_2_), channel_id=1, source_target_pairs={{0,1},{1,0},{2,3},{3,2},{4,5},{5,4},{6,7},{7,6},{8,9},{9,8},{10,11... | collective-permute-start | bytes 3145736 | tf_op jit(solution)/shard_map/ppermute | solution.py:36
  137.6 13.5 %collective-permute-start.21 = (bf16[16,16,2048]{2,1,0:T(8,128)(2,1)}, bf16[16,16,2048]{2,1,0:T(8,128)(2,1)}, u32[]{:S(2)}, u32[]{:S(2)}) collective-permute-start(bf16[16,16,2048]{2,1,0:T(8,128)(2,1)} %collective-permute-done.17.refs_3_), channel_id=1, source_target_pairs={{0,1},{1,0},{2,3},{3,2},{4,5},{5,4},{6,7},{7,6},{8,9},{9,8},{10,11... | collective-permute-start | bytes 3145736 | tf_op jit(solution)/shard_map/ppermute | solution.py:36
  146.6 28.2 %all-to-all-start.2 = ((bf16[16,128,384]{2,1,0:T(8,128)(2,1)}), bf16[16,128,384]{2,1,0:T(8,128)(2,1)}, u32[]{:S(2)}, u32[]{:S(2)}) async-start(bf16[16,128,384]{2,1,0:T(8,128)(2,1)} %bitcast.26), calls=%async_computation.2 | async-start | bytes 3145728 | tf_op jit(solution)/shard_map/all_to_all | solution.py:289
  (15 other events, 65.1 us)
